TPU v7x, 32 devices: a whole 2x2x4 slice. The times are simulated.
32 devices in a mesh: img: 16 (over z, y, core), cap: 2 (over x).
Axes of the slice: x: 2, y: 2, z: 4, core: 2. Of those that a mesh axis runs over, the one named last changes fastest.
Arguments:
- feats_img: bfloat16 [12288, 768], P(('img', 'cap')), may hold values from -6 to 6
- feats_cap: bfloat16 [12288, 768], P(('img', 'cap')), may hold values from -6 to 6
- cot_img: bfloat16 [12288, 512], P(('img', 'cap')), may hold values from -60 to 60
- cot_cap: bfloat16 [12288, 512], P(('img', 'cap')), may hold values from -60 to 60
- w_in: bfloat16 [2048, 768], replicated, may hold values from -0.21875 to 0.21875
- b_in: float32 [2048], replicated, may hold values from -3 to 3
- w_out: bfloat16 [2048, 512], replicated, may hold values from -0.125 to 0.125
- tile_seed: int32 [96, 4], P(('img', 'cap')), may hold values from 0 to 16777214
- tile_cols: int32 [96, 4], P(('img', 'cap')), may hold values from 0 to 95, as said below
- tile_count: int32 [96], P(('img', 'cap')), may hold values from 1 to 4, as said below
Outputs:
- grad_feats_img: bfloat16 [12288, 768], P(('img', 'cap'))
- grad_feats_cap: bfloat16 [12288, 768], P(('img', 'cap'))
- grad_w_in: float32 [2048, 768], P(('img', 'cap'))
- grad_w_out: float32 [2048, 512], P(('img', 'cap'))
- grad_b_in: float32 [2048], P(('img', 'cap'))
Inputs may be any that keep to these rules, and one draw needn't show every extreme that they name: `tile_cols`: slot 0 of image tile t holds t itself; the other slots hold distinct caption tiles within 3 tiles of t; slot 1 of tile 96 - 4 holds the next tile and slot 1 of tile 96 - 3 the previous one. `tile_count`: the largest count, 4, is reached on some device in every draw, among others on tiles 96 - 4 and 93.
All inputs are finite; a program needn't handle non-finite values.
Results may differ from a plain program's by a relative error of at most 0.0061.
Values may be sent and summed in bfloat16 or wider, within the bound.
No kernel may reach another device: no remote copies, remote signals or barrier semaphores. Data moves between devices by JAX's collectives and lax.ppermute only.
A program may use at most 64 MiB of HBM per device.

v0:
```python
import math

import jax
import jax.numpy as jnp
from jax import lax
from jax.sharding import PartitionSpec as P

TILE = 128
HOPS = 2


ALPHA = 0.1


def shifted(array, axis, by):
    count = lax.axis_size(axis)
    pairs = [(i, i + by) for i in range(count) if 0 <= i + by < count]
    return lax.ppermute(array, axis, pairs)


def with_halo(array, sides, width):
    for axis, dim in sides:
        count, length = (lax.axis_size(axis), array.shape[dim])
        up = [(i, (i + 1) % count) for i in range(count - 1)]
        down = [(j, i) for i, j in up]
        last = lax.slice_in_dim(array, length - width, length, axis=dim)
        initial = lax.slice_in_dim(array, 0, width, axis=dim)
        before = lax.ppermute(last, axis, up)
        after = lax.ppermute(initial, axis, down)
        array = jnp.concatenate([before, array, after], axis=dim)
    return array


def tile_patterns(seeds, counts):
    row_index = lax.broadcasted_iota(jnp.int32, (TILE, TILE), 0)
    col_index = lax.broadcasted_iota(jnp.int32, (TILE, TILE), 1)
    index_of_slot = lax.broadcasted_iota(jnp.int32, seeds.shape, 1)
    mixed = seeds[:, :, None, None] + row_index * 40503 + col_index * 9973
    mixed = mixed * 668265261
    mixed = jnp.bitwise_xor(mixed, jnp.right_shift(mixed, 15))
    mixed = mixed * 374761393
    mixed = jnp.bitwise_xor(mixed, jnp.right_shift(mixed, 13))
    has_edge = jnp.bitwise_and(mixed, 15) == 0
    on_diagonal = (row_index == col_index)[None, None] & (index_of_slot == 0)[:, :, None, None]
    is_live = (index_of_slot < counts[:, None])[:, :, None, None]
    return jnp.where(is_live & (has_edge | on_diagonal), 1.0, 0.0).astype(jnp.bfloat16)


def gelu_parts(preact):
    normal_cdf = 0.5 * (1.0 + jax.scipy.special.erf(preact * 0.7071067811865476))
    normal_pdf = jnp.exp(-0.5 * preact * preact) * 0.3989422804014327
    return (preact * normal_cdf, normal_cdf + preact * normal_pdf)


def per_device(
    feats_img, feats_cap, cot_img, cot_cap, w_in, b_in, w_out, tile_seed, tile_cols, tile_count
):
    local_rows = feats_img.shape[0]
    width = cot_img.shape[1]
    local_tiles = local_rows // TILE
    first_tile = lax.axis_index(("img", "cap")) * local_tiles
    sparsity_layout = tile_patterns(tile_seed, tile_count)
    placed = tile_cols - first_tile + local_tiles
    top_slots = jnp.max(tile_count)
    col_part = jnp.sum(sparsity_layout, axis=2, dtype=jnp.float32)
    degree_wide = jnp.zeros((3 * local_tiles, TILE), jnp.float32).at[placed].add(col_part)
    from_next = shifted(degree_wide[:local_tiles], ("img", "cap"), -1)
    from_prev = shifted(degree_wide[2 * local_tiles :], ("img", "cap"), 1)
    degree_cap = degree_wide[local_tiles : 2 * local_tiles] + from_next + from_prev
    degree_img = jnp.sum(sparsity_layout, axis=(1, 3), dtype=jnp.float32).reshape(local_rows)
    norm_img = lax.rsqrt(degree_img)[:, None]
    norm_cap = lax.rsqrt(degree_cap.reshape(local_rows))[:, None]
    flow_img = cot_img.astype(jnp.float32)
    flow_cap = cot_cap.astype(jnp.float32)
    sum_img = jnp.zeros_like(flow_img)
    sum_cap = jnp.zeros_like(flow_cap)
    for hop_index in range(HOPS):
        sum_img = sum_img + flow_img
        sum_cap = sum_cap + flow_cap
        one_state_img = (flow_img * norm_img).astype(jnp.bfloat16)
        state_cap = (flow_cap * norm_cap).astype(jnp.bfloat16)
        one_cap_wide = with_halo(state_cap, ((("img", "cap"), 0),), local_rows)
        block_groups = one_cap_wide.reshape(3 * local_tiles, TILE, width)

        def image_add_slot(index_of_slot, running_totals):
            slot_pattern = lax.dynamic_index_in_dim(
                sparsity_layout, index_of_slot, 1, keepdims=False
            )
            slot_place = lax.dynamic_index_in_dim(placed, index_of_slot, 1, keepdims=False)
            selected_entries = jnp.take(block_groups, slot_place, axis=0)
            return running_totals + jnp.einsum(
                "jrc,jcf->jrf", slot_pattern, selected_entries, preferred_element_type=jnp.float32
            )

        running_totals = lax.fori_loop(
            0, top_slots, image_add_slot, jnp.zeros((local_tiles, TILE, width), jnp.float32)
        )
        new_img = (1.0 - ALPHA) * norm_img * running_totals.reshape(local_rows, width)
        pushed_block_groups = one_state_img.reshape(local_tiles, TILE, width)

        def pushed_add_slot(index_of_slot, running_totals):
            slot_pattern = lax.dynamic_index_in_dim(
                sparsity_layout, index_of_slot, 1, keepdims=False
            )
            slot_place = lax.dynamic_index_in_dim(placed, index_of_slot, 1, keepdims=False)
            contribution = jnp.einsum(
                "jrc,jrf->jcf",
                slot_pattern,
                pushed_block_groups,
                preferred_element_type=jnp.float32,
            )
            return running_totals.at[slot_place].add(contribution)

        partial_sums = lax.fori_loop(
            0, top_slots, pushed_add_slot, jnp.zeros((3 * local_tiles, TILE, width), jnp.float32)
        )
        sums_next = shifted(partial_sums[:local_tiles], ("img", "cap"), -1)
        sums_prev = shifted(partial_sums[2 * local_tiles :], ("img", "cap"), 1)
        summed = partial_sums[local_tiles : 2 * local_tiles] + sums_next + sums_prev
        new_cap = (1.0 - ALPHA) * norm_cap * summed.reshape(local_rows, width)
        flow_img = new_img
        flow_cap = new_cap
    logit_img = (ALPHA * sum_img + flow_img).astype(jnp.bfloat16)
    logit_cap = (ALPHA * sum_cap + flow_cap).astype(jnp.bfloat16)
    feats = jnp.concatenate([feats_img, feats_cap], axis=0)
    logit_gradient = jnp.concatenate([logit_img, logit_cap], axis=0)
    preact = (
        lax.dot_general(feats, w_in, (((1,), (1,)), ((), ())), preferred_element_type=jnp.float32)
        + b_in
    )
    gelu_value, gelu_slope = gelu_parts(preact)
    hidden_act = gelu_value.astype(jnp.bfloat16)
    hidden_grad = lax.dot_general(
        logit_gradient, w_out, (((1,), (1,)), ((), ())), preferred_element_type=jnp.float32
    )
    preact_grad = (hidden_grad * gelu_slope).astype(jnp.bfloat16)
    feat_grad = jnp.dot(preact_grad, w_in, preferred_element_type=jnp.float32).astype(jnp.bfloat16)
    grad_scale = 1.0 / math.sqrt(2 * local_rows * lax.axis_size("img") * lax.axis_size("cap"))
    part_in = (
        lax.dot_general(
            preact_grad, feats, (((0,), (0,)), ((), ())), preferred_element_type=jnp.float32
        )
        * grad_scale
    )
    part_out = (
        lax.dot_general(
            hidden_act, logit_gradient, (((0,), (0,)), ((), ())), preferred_element_type=jnp.float32
        )
        * grad_scale
    )
    part_bias = jnp.sum(preact_grad, axis=0, dtype=jnp.float32) * grad_scale
    grad_w_in, grad_w_out, grad_b_in = (
        lax.psum_scatter(part_in, ("img", "cap"), scatter_dimension=0, tiled=True),
        lax.psum_scatter(part_out, ("img", "cap"), scatter_dimension=0, tiled=True),
        lax.psum_scatter(part_bias, ("img", "cap"), scatter_dimension=0, tiled=True),
    )
    return (feat_grad[:local_rows], feat_grad[local_rows:], grad_w_in, grad_w_out, grad_b_in)


def solution(mesh):
    in_specs = (
        P(("img", "cap"), None),
        P(("img", "cap"), None),
        P(("img", "cap"), None),
        P(("img", "cap"), None),
        P(),
        P(),
        P(),
        P(("img", "cap"), None),
        P(("img", "cap"), None),
        P(("img", "cap")),
    )
    out_specs = (
        P(("img", "cap"), None),
        P(("img", "cap"), None),
        P(("img", "cap"), None),
        P(("img", "cap"), None),
        P(("img", "cap")),
    )
    return jax.shard_map(
        per_device, mesh=mesh, in_specs=in_specs, out_specs=out_specs, check_vma=False
    )
```

profile of v0, /device:TPU:0, one launch (start us, length us, event | category | flops | bytes accessed | tf_op | source)
XLA Modules:
  0.0 476.2 jit_solution(15353611689633235397)
XLA Ops:
  13.6 6.0 %collective-permute-start.1 = (f32[3,128]{1,0:T(4,128)}, f32[3,128]{1,0:T(4,128)}, u32[]{:S(2)}, u32[]{:S(2)}) collective-permute-start(f32[3,128]{1,0:T(4,128)} %get-tuple-element.244), channel_id=1, source_target_pairs={{0,1},{1,2},{2,3},{3,4},{4,5},{5,6},{6,7},{7,8},{8,9},{9,10},{10,1... | collective-permute-start | bytes 4616 | tf_op jit(solution)/shard_map/ppermute | solution.py:18
  26.5 3.8 collective-permute-start.2
  33.3 24.3 %while.41 = (s32[]{:T(128)}, f32[9,128,512]{2,1,0:T(8,128)}, s32[]{:T(128)}, s32[3,4]{0,1:T(4,128)S(1)}, bf16[3,4,128,128]{2,3,0,1:T(8,128)(2,1)}, /*index=5*/bf...) while((s32[]{:T(128)}, f32[9,128,512]{2,1,0:T(8,128)}, s32[]{:T(128)}, s32[3,4]{0,1:T(4,128)S(1)}, ...), condition=%wide.region_8.10_spmd, body=%wide.region_6.9_spmd.sunk | while | flops 50528268 | bytes 3637419 | solution.py:114
  36.1 3.2 scatter_fusion
  42.1 3.1 scatter_fusion
  47.9 3.1 scatter_fusion
  53.8 3.1 scatter_fusion
  57.6 2.8 fusion.52
  61.8 5.5 %collective-permute-start.5 = (f32[3,128,512]{2,1,0:T(8,128)}, f32[3,128,512]{2,1,0:T(8,128)}, u32[]{:S(2)}, u32[]{:S(2)}) collective-permute-start(f32[3,128,512]{2,1,0:T(8,128)} %get-tuple-element.235), channel_id=1, source_target_pairs={{0,1},{1,2},{2,3},{3,4},{4,5},{5,6},{6,7},{7,8},{8,9},{9,10},{10,1... | collective-permute-start | bytes 2359304 | tf_op jit(solution)/shard_map/ppermute | solution.py:18
  71.4 20.7 %while.40 = (s32[]{:T(128)}, f32[3,128,512]{2,1,0:T(8,128)}, s32[]{:T(128)}, bf16[3,4,128,128]{3,2,0,1:T(8,128)(2,1)}, s32[3,4]{0,1:T(4,128)S(1)}, /*index=5*/bf...) while((s32[]{:T(128)}, f32[3,128,512]{2,1,0:T(8,128)}, s32[]{:T(128)}, ...), condition=%wide.region_5.7_spmd, body=%wide.region_4.6_spmd.sunk | while | flops 50725912 | bytes 2855101 | solution.py:95
  95.3 24.4 %while.43 = (s32[]{:T(128)}, f32[9,128,512]{2,1,0:T(8,128)}, s32[]{:T(128)}, s32[3,4]{0,1:T(4,128)S(1)}, bf16[3,4,128,128]{2,3,0,1:T(8,128)(2,1)}, /*index=5*/bf...) while((s32[]{:T(128)}, f32[9,128,512]{2,1,0:T(8,128)}, s32[]{:T(128)}, ...), condition=%wide.region_13.15_spmd, body=%wide.region_11.14_spmd.sunk | while | flops 50528268 | bytes 3637419 | solution.py:114
  98.1 3.3 scatter_fusion.1
  104.1 3.1 scatter_fusion.1
  110.0 3.1 scatter_fusion.1
  115.9 3.1 scatter_fusion.1
  122.6 4.6 collective-permute-start.9
  129.7 5.5 %collective-permute-done.8 = f32[3,128,512]{2,1,0:T(8,128)S(1)} collective-permute-done((f32[3,128,512]{2,1,0:T(8,128)S(1)}, f32[3,128,512]{2,1,0:T(8,128)S(1)}, u32[]{:S(2)}, u32[]{:S(2)}) %collective-permute-start.8) | collective-permute-done | bytes 786464 | tf_op jit(solution)/shard_map/ppermute | solution.py:18
  135.2 10.6 %collective-permute-done.9 = f32[3,128,512]{2,1,0:T(8,128)S(1)} collective-permute-done((f32[3,128,512]{2,1,0:T(8,128)S(1)}, f32[3,128,512]{2,1,0:T(8,128)S(1)}, u32[]{:S(2)}, u32[]{:S(2)}) %collective-permute-start.9) | collective-permute-done | bytes 786464 | tf_op jit(solution)/shard_map/ppermute | solution.py:18
  148.2 5.1 %collective-permute-start.6 = (bf16[384,512]{1,0:T(8,128)(2,1)S(1)}, bf16[384,512]{1,0:T(8,128)(2,1)}, u32[]{:S(2)}, u32[]{:S(2)}) collective-permute-start(bf16[384,512]{1,0:T(8,128)(2,1)S(1)} %get-tuple-element.240), channel_id=1, source_target_pairs={{0,1},{1,2},{2,3},{3,4},{4,5},{5,6},{6,7},{7,8},{8,9},{9,10},{10,1... | collective-permute-start | bytes 1179656 | tf_op jit(solution)/shard_map/ppermute | solution.py:28
  154.7 4.6 fusion.56
  160.7 8.7 %collective-permute-done.7 = bf16[384,512]{1,0:T(8,128)(2,1)} collective-permute-done((bf16[384,512]{1,0:T(8,128)(2,1)S(1)}, bf16[384,512]{1,0:T(8,128)(2,1)}, u32[]{:S(2)}, u32[]{:S(2)}) %collective-permute-start.7) | collective-permute-done | bytes 393248 | tf_op jit(solution)/shard_map/ppermute | solution.py:29
  172.6 20.8 %while.42 = (s32[]{:T(128)}, f32[3,128,512]{2,1,0:T(8,128)}, s32[]{:T(128)}, bf16[3,4,128,128]{3,2,0,1:T(8,128)(2,1)}, s32[3,4]{0,1:T(4,128)S(1)}, /*index=5*/bf...) while((s32[]{:T(128)}, f32[3,128,512]{2,1,0:T(8,128)}, s32[]{:T(128)}, ...), condition=%wide.region_10.12_spmd, body=%wide.region_9.11_spmd.sunk | while | flops 50725912 | bytes 2855101 | solution.py:95
  175.2 2.4 convolution_add_fusion.5
  185.2 2.4 convolution_add_fusion.5
  190.3 2.4 convolution_add_fusion.5
  196.0 5.3 %convolution_multiply_fusion.1 = f32[2048,512]{1,0:T(8,128)} fusion(f32[768,2048]{1,0:T(8,128)} %fusion.56, f32[2048]{0:T(1024)S(1)} %copy-done.13, bf16[384,512]{1,0:T(8,128)(2,1)S(1)} %copy-done.5, bf16[384,512]{1,0:T(8,128)(2,1)S(1)} %fusion.33), kind=kOutput, calls=%fused_computation.50 | convolution fusion | flops 1622671360 | bytes 11280384 | tf_op jit(solution)/shard_map/dot_general | solution.py:146
  202.0 6.2 %convert_reduce_fusion = (f32[2048]{0:T(1024)S(1)}, bf16[768,2048]{1,0:T(8,128)(2,1)S(1)}) fusion(f32[768,2048]{1,0:T(8,128)} %fusion.56, f32[2048]{0:T(1024)S(1)} %copy-done.14, bf16[2048,512]{1,0:T(8,128)(2,1)} %param.26, bf16[384,512]{1,0:T(8,128)(2,1)S(1)} %copy-done.5, bf16[384,512]{1,0:T(8,128)(2,1)} %copy-done.6), kind=kOutput, calls=%fused_computation.46 | convolution fusion | flops 1632630784 | bytes 12337152 | tf_op jit(solution)/shard_map/dot_general | solution.py:133
  210.0 4.6 convolution_multiply_fusion
  214.6 50.9 %all-reduce = f32[2048]{0:T(1024)S(1)} all-reduce(f32[2048]{0:T(1024)S(1)} %broadcast_multiply_fusion), channel_id=4, replica_groups=mesh['img'=16,'cap'=2] {'img','cap'}, use_global_device_ids=true, to_apply=%region_17.19.clone | all-reduce | flops 2048 | bytes 16384
  266.1 4.5 convolution_convert_fusion
  271.7 80.4 %reduce-scatter.5.cloned.1.call-done = f32[64,512]{1,0:T(8,128)} async-done(((f32[2048,512]{1,0:T(8,128)}), f32[64,512]{1,0:T(8,128)}) %reduce-scatter.5.cloned.1.call-update) | async-done | bytes 131088 | tf_op jit(solution)/shard_map/reduce_scatter | solution.py:154
  352.1 117.3 %reduce-scatter.3.cloned.1.call-done = f32[64,768]{1,0:T(8,128)} async-done(((f32[2048,768]{1,0:T(8,128)}), f32[64,768]{1,0:T(8,128)}) %reduce-scatter.3.cloned.1.call-update) | async-done | bytes 196624 | tf_op jit(solution)/shard_map/reduce_scatter | solution.py:153
  (131 shorter events, 88.5 us)
Async XLA Ops:
  7.2 147.5 %copy-start = (bf16[2048,768]{1,0:T(8,128)(2,1)S(1)}, bf16[2048,768]{1,0:T(8,128)(2,1)}, u32[]{:S(2)}) copy-start(bf16[2048,768]{1,0:T(8,128)(2,1)} %param.24) | copy-start | bytes 9437188
  7.2 344.9 %reduce-scatter.5.cloned.1.call-start = ((), (), s32[]{:S(2)}) async-start(), calls=%async_computation.3 | async-start | bytes 4325376 | tf_op jit(solution)/shard_map/reduce_scatter | solution.py:154
  12.3 10.4 %collective-permute-start = (f32[3,128]{1,0:T(4,128)}, f32[3,128]{1,0:T(4,128)}, u32[]{:S(2)}, u32[]{:S(2)}) collective-permute-start(f32[3,128]{1,0:T(4,128)} %get-tuple-element.243), channel_id=1, source_target_pairs={{1,0},{2,1},{3,2},{4,3},{5,4},{6,5},{7,6},{8,7},{9,8},{10,9},{11,1... | collective-permute-start | bytes 4616 | tf_op jit(solution)/shard_map/ppermute | solution.py:18
  13.6 9.1 %collective-permute-start.1 = (f32[3,128]{1,0:T(4,128)}, f32[3,128]{1,0:T(4,128)}, u32[]{:S(2)}, u32[]{:S(2)}) collective-permute-start(f32[3,128]{1,0:T(4,128)} %get-tuple-element.244), channel_id=1, source_target_pairs={{0,1},{1,2},{2,3},{3,4},{4,5},{5,6},{6,7},{7,8},{8,9},{9,10},{10,1... | collective-permute-start | bytes 4616 | tf_op jit(solution)/shard_map/ppermute | solution.py:18
  24.1 0.6 copy-start.9
  26.5 41.6 %collective-permute-start.2 = (bf16[384,512]{1,0:T(8,128)(2,1)}, bf16[384,512]{1,0:T(8,128)(2,1)}, u32[]{:S(2)}, u32[]{:S(2)}) collective-permute-start(bf16[384,512]{1,0:T(8,128)(2,1)} %fusion.35), channel_id=1, source_target_pairs={{0,1},{1,2},{2,3},{3,4},{4,5},{5,6},{6,7},{7,8},{8,9},{9,10},{10,1... | collective-permute-start | bytes 1179656 | tf_op jit(solution)/shard_map/ppermute | solution.py:28
  30.3 37.8 %collective-permute-start.3 = (bf16[384,512]{1,0:T(8,128)(2,1)}, bf16[384,512]{1,0:T(8,128)(2,1)}, u32[]{:S(2)}, u32[]{:S(2)}) collective-permute-start(bf16[384,512]{1,0:T(8,128)(2,1)} %fusion.35), channel_id=1, source_target_pairs={{1,0},{2,1},{3,2},{4,3},{5,4},{6,5},{7,6},{8,7},{9,8},{10,9},{11,1... | collective-permute-start | bytes 1179656 | tf_op jit(solution)/shard_map/ppermute | solution.py:29
  57.6 9.6 %copy-start.1 = (bf16[3,4,128,128]{2,3,0,1:T(8,128)(2,1)S(1)}, bf16[3,4,128,128]{2,3,0,1:T(8,128)(2,1)}, u32[]{:S(2)}) copy-start(bf16[3,4,128,128]{2,3,0,1:T(8,128)(2,1)} %get-tuple-element.524) | copy-start | bytes 1179652
  60.5 66.9 %collective-permute-start.4 = (f32[3,128,512]{2,1,0:T(8,128)}, f32[3,128,512]{2,1,0:T(8,128)}, u32[]{:S(2)}, u32[]{:S(2)}) collective-permute-start(f32[3,128,512]{2,1,0:T(8,128)} %get-tuple-element.234), channel_id=1, source_target_pairs={{1,0},{2,1},{3,2},{4,3},{5,4},{6,5},{7,6},{8,7},{9,8},{10,9},{11,1... | collective-permute-start | bytes 2359304 | tf_op jit(solution)/shard_map/ppermute | solution.py:18
  61.8 65.6 %collective-permute-start.5 = (f32[3,128,512]{2,1,0:T(8,128)}, f32[3,128,512]{2,1,0:T(8,128)}, u32[]{:S(2)}, u32[]{:S(2)}) collective-permute-start(f32[3,128,512]{2,1,0:T(8,128)} %get-tuple-element.235), channel_id=1, source_target_pairs={{0,1},{1,2},{2,3},{3,4},{4,5},{5,6},{6,7},{7,8},{8,9},{9,10},{10,1... | collective-permute-start | bytes 2359304 | tf_op jit(solution)/shard_map/ppermute | solution.py:18
  119.7 7.5 %copy-start.3 = (bf16[384,768]{1,0:T(8,128)(2,1)S(1)}, bf16[384,768]{1,0:T(8,128)(2,1)}, u32[]{:S(2)}) copy-start(bf16[384,768]{1,0:T(8,128)(2,1)} %param.20) | copy-start | bytes 1769476
  119.7 7.6 %copy-start.4 = (bf16[384,768]{1,0:T(8,128)(2,1)S(1)}, bf16[384,768]{1,0:T(8,128)(2,1)}, u32[]{:S(2)}) copy-start(bf16[384,768]{1,0:T(8,128)(2,1)} %param.21) | copy-start | bytes 1769476
  121.3 13.9 %collective-permute-start.8 = (f32[3,128,512]{2,1,0:T(8,128)S(1)}, f32[3,128,512]{2,1,0:T(8,128)S(1)}, u32[]{:S(2)}, u32[]{:S(2)}) collective-permute-start(f32[3,128,512]{2,1,0:T(8,128)S(1)} %get-tuple-element.236), channel_id=1, source_target_pairs={{1,0},{2,1},{3,2},{4,3},{5,4},{6,5},{7,6},{8,7},{9,8},{10,9},{11,1... | collective-permute-start | bytes 2359304 | tf_op jit(solution)/shard_map/ppermute | solution.py:18
  122.6 23.2 %collective-permute-start.9 = (f32[3,128,512]{2,1,0:T(8,128)S(1)}, f32[3,128,512]{2,1,0:T(8,128)S(1)}, u32[]{:S(2)}, u32[]{:S(2)}) collective-permute-start(f32[3,128,512]{2,1,0:T(8,128)S(1)} %get-tuple-element.237), channel_id=1, source_target_pairs={{0,1},{1,2},{2,3},{3,4},{4,5},{5,6},{6,7},{7,8},{8,9},{9,10},{10,1... | collective-permute-start | bytes 2359304 | tf_op jit(solution)/shard_map/ppermute | solution.py:18
  127.3 27.3 %copy-start.7 = (bf16[768,768]{1,0:T(8,128)(2,1)}, bf16[768,768]{1,0:T(8,128)(2,1)S(1)}, u32[]{:S(2)}) copy-start(bf16[768,768]{1,0:T(8,128)(2,1)S(1)} %constant_dynamic-update-slice_fusion) | copy-start | bytes 3538948
  129.6 17.5 %copy-start.2 = (bf16[384,512]{1,0:T(8,128)(2,1)S(1)}, bf16[384,512]{1,0:T(8,128)(2,1)}, u32[]{:S(2)}) copy-start(bf16[384,512]{1,0:T(8,128)(2,1)} %param.23) | copy-start | bytes 1179652
  129.6 17.5 %copy-start.10 = (f32[384]{0:T(512)S(1)}, f32[384]{0:T(512)}, u32[]{:S(2)}) copy-start(f32[384]{0:T(512)} %copy-done.9) | copy-start | bytes 4612
  129.7 17.5 %copy-start.11 = (f32[384]{0:T(512)S(1)}, f32[384]{0:T(512)}, u32[]{:S(2)}) copy-start(f32[384]{0:T(512)} %get-tuple-element.232) | copy-start | bytes 4612
  148.2 12.5 %collective-permute-start.6 = (bf16[384,512]{1,0:T(8,128)(2,1)S(1)}, bf16[384,512]{1,0:T(8,128)(2,1)}, u32[]{:S(2)}, u32[]{:S(2)}) collective-permute-start(bf16[384,512]{1,0:T(8,128)(2,1)S(1)} %get-tuple-element.240), channel_id=1, source_target_pairs={{0,1},{1,2},{2,3},{3,4},{4,5},{5,6},{6,7},{7,8},{8,9},{9,10},{10,1... | collective-permute-start | bytes 1179656 | tf_op jit(solution)/shard_map/ppermute | solution.py:28
  153.4 16.0 %collective-permute-start.7 = (bf16[384,512]{1,0:T(8,128)(2,1)S(1)}, bf16[384,512]{1,0:T(8,128)(2,1)}, u32[]{:S(2)}, u32[]{:S(2)}) collective-permute-start(bf16[384,512]{1,0:T(8,128)(2,1)S(1)} %get-tuple-element.240), channel_id=1, source_target_pairs={{1,0},{2,1},{3,2},{4,3},{5,4},{6,5},{7,6},{8,7},{9,8},{10,9},{11,1... | collective-permute-start | bytes 1179656 | tf_op jit(solution)/shard_map/ppermute | solution.py:29
  172.6 20.8 %copy-start.12 = (f32[384]{0:T(512)S(1)}, f32[384]{0:T(512)}, u32[]{:S(2)}) copy-start(f32[384]{0:T(512)} %broadcast_multiply_fusion.3) | copy-start | bytes 4612
  193.4 2.6 copy-start.5
  193.4 2.5 copy-start.13
  195.2 0.7 copy-start.6
  201.3 0.7 copy-start.14
  201.3 268.1 %reduce-scatter.3.cloned.1.call-start = ((), (), s32[]{:S(2)}) async-start(), calls=%async_computation.2 | async-start | bytes 6488064 | tf_op jit(solution)/shard_map/reduce_scatter | solution.py:153
  202.0 8.0 %copy-start.8 = (bf16[768,768]{1,0:T(8,128)(2,1)S(1)}, bf16[768,768]{1,0:T(8,128)(2,1)}, u32[]{:S(2)}) copy-start(bf16[768,768]{1,0:T(8,128)(2,1)} %copy-done.7) | copy-start | bytes 3538948
  208.2 1.8 copy-start.15
Sparse Core Ops, SparseCore 0:
  201.4 150.6 reduce-scatter.4
  358.3 111.0 reduce-scatter.2
where the time goes:
time: 480 us; the launch traced here: 476 us
  waiting for transfers between devices  223 us (46%)
  matrix products  61 us (13%)
  blocking collectives  50.9 us (11%)
  other arithmetic  47.1 us (10%)
  local copies, waits for them, and re-layouts  33.5 us (7%)
  starting transfers between devices  31.6 us (7%)
  loops' own time  14.4 us (3%)
  between operations  14.4 us (3%)
    reduce_scatter x1, waiting for transfers between devices, per_device(): lax.psum_scatter(part_in, ('img', 'cap'), scatter_dimension=0, tiled=True)  117 us
    reduce_scatter x1, waiting for transfers between devices, per_device(): lax.psum_scatter(part_out, ('img', 'cap'), scatter_dimension=0, tiled=True)  80.4 us
    unnamed x1, blocking collectives  50.9 us
    scatter-add x8, other arithmetic, pushed_add_slot(): return running_totals.at[slot_place].add(contribution)  25.1 us
    ppermute x6, starting transfers between devices, shifted(): return lax.ppermute(array, axis, pairs)  19.9 us
    dot_general x8, matrix products, image_add_slot(): jnp.einsum('jrc,jcf->jrf', slot_pattern, selected_entries, preferred_elem...  19.4 us
    dot_general x8, matrix products, pushed_add_slot(): jnp.einsum('jrc,jrf->jcf', slot_pattern, pushed_block_groups, preferred_e...  16.4 us
    ppermute x6, waiting for transfers between devices, shifted(): return lax.ppermute(array, axis, pairs)  16.1 us
  transfers between devices with their start and end apart: 12, of which 6 were waited for; matrix products, arithmetic and copies ran while one was open for 21% of the time, Pallas kernels for 0%

commit v1 on v0

v1 whole, which is shorter than its diff:
```python
import math

import jax
import jax.numpy as jnp
from jax import lax
from jax.experimental import pallas as pl
from jax.experimental.pallas import tpu as pltpu
from jax.sharding import PartitionSpec as P

TILE = 128
ALPHA = 0.1
AXES = ("img", "cap")
F32 = jnp.float32
BF16 = jnp.bfloat16


def gelu_parts(preact):
    normal_cdf = 0.5 * (1.0 + jax.scipy.special.erf(preact * 0.7071067811865476))
    normal_pdf = jnp.exp(-0.5 * preact * preact) * 0.3989422804014327
    return (preact * normal_cdf, normal_cdf + preact * normal_pdf)


def tiles_kernel(seed_ref, place_ref, count_ref, pat_ref, pat_t_ref, nimg_ref, ncap_ref, deg_ref, *, tiles, slots):
    all_tiles, mid = 7 * tiles, 5 * tiles
    deg_ref[...] = jnp.zeros_like(deg_ref)
    row = lax.broadcasted_iota(jnp.int32, (TILE, TILE), 0)
    col = lax.broadcasted_iota(jnp.int32, (TILE, TILE), 1)
    first, second = jnp.int32(668265261), jnp.int32(374761393)
    base = (row * 40503 + col * 9973) * first
    base_t = (col * 40503 + row * 9973) * first
    off_diag = row - col

    def pattern(start, seed, live, s):
        mixed = start + seed * first
        mixed = jnp.bitwise_xor(mixed, jnp.right_shift(mixed, 15))
        mixed = mixed * second
        mixed = jnp.bitwise_xor(mixed, jnp.right_shift(mixed, 13))
        edge = jnp.bitwise_and(mixed, 15) == jnp.where(live, 0, 16)
        if s == 0:
            edge = edge | (off_diag == jnp.where(live, 0, TILE))
        return jnp.where(edge, 1.0, 0.0)

    def one(q, full):
        total = None
        for s in range(slots):
            live = s < count_ref[q]
            seed = seed_ref[q * slots + s]
            e = pattern(base, seed, live, s)
            c = place_ref[q * slots + s]
            deg_ref[c] += jnp.sum(e, axis=0, keepdims=True)
            if full:
                m = q - tiles
                pat_ref[m, :, pl.ds(s * TILE, TILE)] = e.astype(BF16)
                pat_t_ref[m, pl.ds(s * TILE, TILE), :] = pattern(base_t, seed, live, s).astype(BF16)
                total = e if total is None else total + e
        if full:
            d = jnp.sum(total, axis=1, keepdims=True)
            n = jnp.where(d > 0.0, lax.rsqrt(d), 0.0)
            nimg_ref[q - tiles] = jnp.broadcast_to(n, (TILE, TILE))

    def edge_body(q, c):
        one(q, False)
        return c

    def mid_body(q, c):
        one(q, True)
        return c

    lax.fori_loop(0, tiles, edge_body, 0)
    lax.fori_loop(tiles, tiles + mid, mid_body, 0)
    lax.fori_loop(tiles + mid, all_tiles, edge_body, 0)
    for m in range(mid):
        d = deg_ref[m + 2 * tiles]
        n = jnp.where(d > 0.0, lax.rsqrt(d), 0.0)
        ncap_ref[m] = jnp.broadcast_to(n, (TILE, TILE)).T


def make_tiles(seeds, places, counts, tiles, slots):
    mid = 5 * tiles
    smem = pl.BlockSpec(memory_space=pltpu.SMEM)
    vmem = pl.BlockSpec(memory_space=pltpu.VMEM)
    return pl.pallas_call(
        lambda *r: tiles_kernel(*r, tiles=tiles, slots=slots),
        out_shape=(
            jax.ShapeDtypeStruct((mid, TILE, slots * TILE), BF16),
            jax.ShapeDtypeStruct((mid, slots * TILE, TILE), BF16),
            jax.ShapeDtypeStruct((mid, TILE, TILE), F32),
            jax.ShapeDtypeStruct((mid, TILE, TILE), F32),
        ),
        in_specs=[smem] * 3,
        out_specs=(vmem,) * 4,
        scratch_shapes=[pltpu.VMEM((9 * tiles, 1, TILE), F32)],
        compiler_params=pltpu.CompilerParams(vmem_limit_bytes=40 << 20),
        name="tiles",
    )(seeds, places, counts)


def hops_kernel(
    place_ref, base_ref, own_img, own_cap, low, high, mate, far, pat_ref, pat_t_ref, nimg_ref, ncap_ref,
    out_img, out_cap, img0, cap0, img1, cap1, acc, acc2, keep_img, keep_cap, *, tiles, slots, width,
):
    mid = 5 * tiles
    near = 3 * tiles
    keep = 1.0 - ALPHA

    def wide(n_ref, m):
        n = n_ref[m]
        return jnp.concatenate([n] * (width // TILE), axis=1)

    def scale(rows_img, rows_cap, base):
        for t in range(tiles):
            m = base + t
            img0[m] = (rows_img(t).astype(F32) * wide(nimg_ref, m)).astype(BF16)
            cap0[m] = (rows_cap(t).astype(F32) * wide(ncap_ref, m)).astype(BF16)

    def both(ref):
        return (lambda t: ref[pl.ds(t * TILE, TILE), :]), (lambda t: ref[pl.ds((tiles + t) * TILE, TILE), :])

    scale(lambda t: own_img[pl.ds(t * TILE, TILE), :], lambda t: own_cap[pl.ds(t * TILE, TILE), :], 2 * tiles)
    scale(*both(low), 0)
    scale(*both(high), 4 * tiles)
    scale(*both(mate), base_ref[0])
    scale(*both(far), base_ref[1])
    acc[...] = jnp.zeros_like(acc)
    acc2[...] = jnp.zeros_like(acc2)

    def push(q, state, target, lo, count):
        r = jnp.dot(pat_t_ref[q], state, preferred_element_type=F32)
        for s in range(slots):
            c = place_ref[q * slots + s] - lo
            c = jnp.where((c >= 0) & (c < count), c, count)
            target[c] += r[s * TILE : (s + 1) * TILE]

    def pull(q, source, lo):
        total = None
        for s in range(slots):
            c = place_ref[q * slots + s] - lo
            r = jnp.dot(pat_ref[q, :, pl.ds(s * TILE, TILE)], source[c], preferred_element_type=F32)
            total = r if total is None else total + r
        return total

    def push1(q, c):
        push(q, img0[q], acc, tiles, near)
        return c

    lax.fori_loop(0, mid, push1, 0)

    def pull1(q, c):
        n = wide(nimg_ref, q)
        flow = keep * n * pull(q, cap0, 0)
        img1[q - tiles] = (flow * n).astype(BF16)
        keep_img[q - tiles] = flow
        return c

    lax.fori_loop(tiles, tiles + near, pull1, 0)

    def finish1(m, c):
        n = wide(ncap_ref, m + tiles)
        flow = keep * n * acc[m]
        cap1[m] = (flow * n).astype(BF16)
        keep_cap[m] = flow
        return c

    lax.fori_loop(0, near, finish1, 0)

    def push2(q, c):
        push(q, img1[q - tiles], acc2, 2 * tiles, tiles)
        return c

    lax.fori_loop(tiles, tiles + near, push2, 0)
    for t in range(tiles):
        q = 2 * tiles + t
        rows = pl.ds(t * TILE, TILE)
        flow = keep * wide(nimg_ref, q) * pull(q, cap1, tiles)
        out_img[rows, :] = (ALPHA * (own_img[rows, :].astype(F32) + keep_img[tiles + t]) + flow).astype(BF16)
        flow = keep * wide(ncap_ref, q) * acc2[t]
        out_cap[rows, :] = (ALPHA * (own_cap[rows, :].astype(F32) + keep_cap[tiles + t]) + flow).astype(BF16)


def propagate(places, bases, own_img, own_cap, low, high, mate, far, pats, tiles, slots):
    width = own_img.shape[1]
    smem = pl.BlockSpec(memory_space=pltpu.SMEM)
    vmem = pl.BlockSpec(memory_space=pltpu.VMEM)
    mid, near = 5 * tiles, 3 * tiles
    return pl.pallas_call(
        lambda *r: hops_kernel(*r, tiles=tiles, slots=slots, width=width),
        out_shape=(jax.ShapeDtypeStruct(own_img.shape, BF16),) * 2,
        in_specs=[smem] * 2 + [vmem] * 10,
        out_specs=(vmem,) * 2,
        scratch_shapes=[
            pltpu.VMEM((mid, TILE, width), BF16),
            pltpu.VMEM((mid, TILE, width), BF16),
            pltpu.VMEM((near, TILE, width), BF16),
            pltpu.VMEM((near, TILE, width), BF16),
            pltpu.VMEM((near + 1, TILE, width), F32),
            pltpu.VMEM((tiles + 1, TILE, width), F32),
            pltpu.VMEM((near, TILE, width), F32),
            pltpu.VMEM((near, TILE, width), F32),
        ],
        compiler_params=pltpu.CompilerParams(vmem_limit_bytes=56 << 20),
        name="hops",
    )(places, bases, own_img, own_cap, low, high, mate, far, *pats)


def moved(array, count, by):
    return lax.ppermute(array, AXES, [(i, i + by) for i in range(count) if 0 <= i + by < count])


def flipped(array, count, mask):
    return lax.ppermute(array, AXES, [(i, i ^ mask) for i in range(count)])


def halve(array, axis, count, mask):
    kept = lax.index_in_dim(array, 0, axis, keepdims=False)
    sent = lax.index_in_dim(array, 1, axis, keepdims=False)
    return (kept.astype(F32) + flipped(sent, count, mask).astype(F32)).astype(BF16)


def scattered(part, count, bits, order):
    rows, lanes = part.shape[1:]
    part = part.reshape((2,) * len(bits) + (rows, lanes))
    left = list(bits)
    for bit in order:
        part = halve(part, left.index(bit), count, 1 << bit)
        left.remove(bit)
    part = part.reshape((4, rows, lanes))
    got = [flipped(part[k], count, ((k >> 1) << left[0]) | ((k & 1) << left[1])) for k in range(1, 4)]
    total = part[0].astype(F32)
    for piece in got:
        total = total + piece.astype(F32)
    return total


def per_device(
    feats_img, feats_cap, cot_img, cot_cap, w_in, b_in, w_out, tile_seed, tile_cols, tile_count
):
    local_rows = feats_img.shape[0]
    tiles = local_rows // TILE
    slots = tile_seed.shape[1]
    hid, f_in = w_in.shape
    n_img, n_cap = lax.axis_size("img"), lax.axis_size("cap")
    count = n_img * n_cap
    me = lax.axis_index(AXES)

    meta = jnp.concatenate([tile_seed, tile_cols, tile_count[:, None]], axis=1)
    bands = [moved(meta, count, by) for by in (3, 2, 1)] + [meta] + [moved(meta, count, -by) for by in (1, 2, 3)]
    block = jnp.concatenate([cot_img, cot_cap], axis=0)
    mate = flipped(block, count, 1)
    low = moved(block, count, 2)
    high = moved(block, count, -2)
    far = lax.ppermute(
        mate,
        AXES,
        [(i, i + 2) for i in range(0, count - 2, 2)] + [(i, i - 2) for i in range(3, count, 2)],
    )
    wide = jnp.concatenate(bands, axis=0)
    frame = jnp.arange(7 * tiles, dtype=jnp.int32)[:, None]
    counts = wide[:, 2 * slots]
    seeds = wide[:, :slots].reshape(-1)
    places = jnp.where(counts[:, None] > 0, wide[:, slots : 2 * slots] - (me - 3) * tiles, frame)
    pats = make_tiles(seeds, (places + tiles).reshape(-1), counts, tiles, slots)

    m = count.bit_length() - 1
    a = n_cap.bit_length() - 1
    cap_bits = list(range(a))
    img_bits = list(range(a + 1, m - 2))
    bits = [a] + cap_bits + img_bits + [m - 1, m - 2]
    pos = jnp.arange(count, dtype=jnp.int32)
    order = jnp.zeros_like(pos)
    for k, bit in enumerate(bits):
        order = order | (((pos >> (m - 1 - k)) & 1) << bit)
    order = order ^ me
    rows = hid // count
    w_in_p = jnp.take(w_in.reshape(count, rows, f_in), order, axis=0).reshape(hid, f_in)
    w_out_p = jnp.take(w_out.reshape(count, rows, -1), order, axis=0).reshape(hid, -1)
    b_in_p = jnp.take(b_in.reshape(count, rows), order, axis=0).reshape(hid)

    feats = jnp.concatenate([feats_img, feats_cap], axis=0)
    preact = (
        lax.dot_general(feats, w_in_p, (((1,), (1,)), ((), ())), preferred_element_type=F32) + b_in_p
    )
    gelu_value, gelu_slope = gelu_parts(preact)
    hidden_act = gelu_value.astype(BF16)
    gelu_slope = lax.optimization_barrier(gelu_slope)

    even = (me & 1) == 0
    bases = jnp.where(even, jnp.array([3, 1]), jnp.array([1, 3])).astype(jnp.int32) * tiles
    mid_places = (places - tiles)[tiles : 6 * tiles].reshape(-1)
    logit_img, logit_cap = propagate(
        mid_places, bases, cot_img, cot_cap, low, high, mate, far, pats, tiles, slots
    )
    logit_gradient = jnp.concatenate([logit_img, logit_cap], axis=0)
    over_rows = (((0,), (0,)), ((), ()))
    part_out = lax.dot_general(hidden_act, logit_gradient, over_rows, preferred_element_type=F32).astype(BF16)
    hidden_grad = lax.dot_general(
        logit_gradient, w_out_p, (((1,), (1,)), ((), ())), preferred_element_type=F32
    )
    preact_grad = (hidden_grad * gelu_slope).astype(BF16)
    part_in = lax.dot_general(preact_grad, feats, over_rows, preferred_element_type=F32).astype(BF16)
    part_bias = jnp.sum(preact_grad, axis=0, dtype=F32).astype(BF16)
    packed = jnp.concatenate([part_out, jnp.broadcast_to(part_bias[:, None], (hid, TILE))], axis=1)
    feat_grad = jnp.dot(preact_grad, w_in_p, preferred_element_type=F32).astype(BF16)

    grad_scale = 1.0 / math.sqrt(2 * local_rows * count)
    g_out = scattered(packed.reshape(count, rows, -1), count, bits, [a] + img_bits + cap_bits) * grad_scale
    g_in = scattered(part_in.reshape(count, rows, f_in), count, bits, [a] + cap_bits + img_bits) * grad_scale
    width = cot_img.shape[1]
    return (feat_grad[:local_rows], feat_grad[local_rows:], g_in, g_out[:, :width], g_out[:, width])


def solution(mesh):
    rows = P(("img", "cap"), None)
    in_specs = (rows, rows, rows, rows, P(), P(), P(), rows, rows, P(("img", "cap")))
    out_specs = (rows, rows, rows, rows, P(("img", "cap")))
    return jax.shard_map(
        per_device, mesh=mesh, in_specs=in_specs, out_specs=out_specs, check_vma=False
    )
```

time: 480 us -> 171 us (0.36)
  waiting for transfers between devices: 223 us -> 38.7 us
  blocking collectives: 50.9 us -> 0 us
  matrix products: 61 us -> 24 us
  other arithmetic: 47.1 us -> 14.1 us
  Pallas kernels: 0 us -> 21.9 us
  loops' own time: 14.4 us -> 0 us
  between operations: 14.4 us -> 1 us
  starting transfers between devices: 31.6 us -> 40.9 us
    reduce_scatter x2 -> x0, waiting for transfers between devices: 198 us -> none  [the longest x1 117 us: per_device(): lax.psum_scatter(part_in, ('img', 'cap'), scatter_dimension=0, tiled=True)]
    unnamed x1 -> x0, blocking collectives: 50.9 us -> none
    dot_general x21 -> x5, matrix products: 61 us -> 24 us  [the longest x1 8.71 us: per_device(): lax.dot_general(feats, w_in_p, (((1,), (1,)), ((), ())), preferred_elemen...]
    scatter-add x9 -> x0, other arithmetic: 25.8 us -> none  [the longest x8 25.1 us: pushed_add_slot(): return running_totals.at[slot_place].add(contribution)]
    pallas_call x0 -> x2, Pallas kernels: none -> 21.9 us  [the longest x1 15.9 us: propagate(): pl.pallas_call(lambda *r: hops_kernel(*r, tiles=tiles, slots=slots, width...]
    another operation x4 -> x0, loops' own time: 14.4 us -> none  [the longest x2 7.27 us: per_device(): lax.fori_loop(0, top_slots, image_add_slot, jnp.zeros((local_tiles, TILE,...]
    ppermute x10 -> x22, waiting for transfers between devices: 25.7 us -> 38.7 us  [the longest x13 32.2 us: flipped(): return lax.ppermute(array, AXES, [(i, i ^ mask) for i in range(count)])]
    ppermute x10 -> x22, starting transfers between devices: 31.5 us -> 40.9 us  [the longest x8 19.1 us: moved(): lax.ppermute(array, AXES, [(i, i + by) for i in range(count) if 0 <= i +...]
  transfers between devices with their start and end apart: 12 -> 22, of which waited for: 6 -> 8; matrix products, arithmetic and copies ran while one was open for 21% -> 27% of each run, Pallas kernels for 0% -> 4%
where the time goes in v1:
time: 171 us; the launch traced here: 170 us
  starting transfers between devices  40.9 us (24%)
  waiting for transfers between devices  38.7 us (23%)
  local copies, waits for them, and re-layouts  29.5 us (17%)
  matrix products  24 us (14%)
  Pallas kernels  21.9 us (13%)
  other arithmetic  14.1 us (8%)
    ppermute x13, waiting for transfers between devices, flipped(): return lax.ppermute(array, AXES, [(i, i ^ mask) for i in range(count)])  32.2 us
    ppermute x8, starting transfers between devices, moved(): lax.ppermute(array, AXES, [(i, i + by) for i in range(count) if 0 <= i +...  19.1 us
    ppermute x13, starting transfers between devices, flipped(): return lax.ppermute(array, AXES, [(i, i ^ mask) for i in range(count)])  18 us
    pallas_call x1, Pallas kernels, propagate(): pl.pallas_call(lambda *r: hops_kernel(*r, tiles=tiles, slots=slots, width...  15.9 us
    dot_general x1, matrix products, per_device(): lax.dot_general(feats, w_in_p, (((1,), (1,)), ((), ())), preferred_elemen...  8.71 us
    unnamed x35, local copies, waits for them, and re-layouts  8.34 us
    ppermute x8, waiting for transfers between devices, moved(): lax.ppermute(array, AXES, [(i, i + by) for i in range(count) if 0 <= i +...  6.5 us
    pallas_call x1, Pallas kernels, make_tiles(): pl.pallas_call(lambda *r: tiles_kernel(*r, tiles=tiles, slots=slots), out...  5.99 us
  transfers between devices with their start and end apart: 22, of which 8 were waited for; matrix products, arithmetic and copies ran while one was open for 27% of the time, Pallas kernels for 4%

profile of v1, /device:TPU:0, one launch (start us, length us, event | category | flops | bytes accessed | tf_op | source)
XLA Modules:
  0.0 170.2 jit_solution(2087317070533105407)
XLA Ops:
  2.4 4.3 %collective-permute-start = (s32[3,9]{1,0:T(4,128)S(1)}, s32[3,9]{1,0:T(4,128)S(1)}, u32[]{:S(2)}, u32[]{:S(2)}) collective-permute-start(s32[3,9]{1,0:T(4,128)S(1)} %pad_add_fusion), channel_id=1, source_target_pairs={{0,3},{1,4},{2,5},{3,6},{4,7},{5,8},{6,9},{7,10},{8,11},{9,12},{10... | collective-permute-start | bytes 332 | tf_op jit(solution)/shard_map/ppermute | solution.py:206
  6.7 3.5 %collective-permute-start.1 = (s32[3,9]{1,0:T(4,128)S(1)}, s32[3,9]{1,0:T(4,128)S(1)}, u32[]{:S(2)}, u32[]{:S(2)}) collective-permute-start(s32[3,9]{1,0:T(4,128)S(1)} %pad_add_fusion), channel_id=1, source_target_pairs={{0,2},{1,3},{2,4},{3,5},{4,6},{5,7},{6,8},{7,9},{8,10},{9,11},{10,... | collective-permute-start | bytes 332 | tf_op jit(solution)/shard_map/ppermute | solution.py:206
  10.2 1.8 %constant_dynamic-update-slice_fusion.1 = bf16[768,512]{1,0:T(8,128)(2,1)} fusion(bf16[384,512]{1,0:T(8,128)(2,1)} %r_2_.1), kind=kLoop, calls=%fused_computation.62 | loop fusion | bytes 786432
  12.0 1.8 %constant_dynamic-update-slice_fusion = bf16[768,512]{1,0:T(8,128)(2,1)} fusion(bf16[768,512]{1,0:T(8,128)(2,1)} %constant_dynamic-update-slice_fusion.1, bf16[384,512]{1,0:T(8,128)(2,1)} %r_3_.1), kind=kLoop, calls=%fused_computation.61 | loop fusion | bytes 786432 | tf_op jit(solution)/shard_map/concatenate | solution.py:247
  13.8 4.6 %collective-permute-start.6 = (bf16[768,512]{1,0:T(8,128)(2,1)}, bf16[768,512]{1,0:T(8,128)(2,1)}, u32[]{:S(2)}, u32[]{:S(2)}) collective-permute-start(bf16[768,512]{1,0:T(8,128)(2,1)} %constant_dynamic-update-slice_fusion), channel_id=1, source_target_pairs={{0,2},{1,3},{2,4},{3,5},{4,6},{5,7},{6,8},{7,9},{8,10},{9,11},{10,... | collective-permute-start | bytes 2359304 | tf_op jit(solution)/shard_map/ppermute | solution.py:206
  20.7 2.4 %gather_fusion.1 = bf16[32,64,768]{2,1,0:T(8,128)(2,1)} fusion(bf16[32,64,768]{2,1,0:T(8,128)(2,1)S(1)} %bitcast.77, s32[1024]{0:T(1024)S(1)} %pad_clamp_fusion), kind=kCustom, calls=%fused_computation.1 | custom fusion | bytes 6291584 | tf_op jit(solution)/shard_map/jit(_take)/gather | solution.py:274
  23.7 3.3 %bitcast_select_fusion = bf16[2048,768]{1,0:T(8,128)(2,1)} fusion(bf16[32,64,768]{2,1,0:T(8,128)(2,1)} %gather_fusion.1, pred[2048]{0:T(1024)(128)(4,1)S(1)} %broadcast_in_dim.65), kind=kLoop, calls=%fused_computation.15 | loop fusion | flops 1572864 | bytes 6293504 | tf_op jit(solution)/shard_map/jit(_take)/select_n | solution.py:274
  27.9 2.3 %gather_fusion = bf16[32,64,512]{2,1,0:T(8,128)(2,1)S(1)} fusion(bf16[32,64,512]{2,1,0:T(8,128)(2,1)} %bitcast.82, s32[1024]{0:T(1024)S(1)} %pad_clamp_fusion), kind=kCustom, calls=%fused_computation | custom fusion | bytes 4194432 | tf_op jit(solution)/shard_map/jit(_take)/gather | solution.py:275
  32.8 8.7 %fusion.3 = (f32[768,2048]{1,0:T(8,128)}, f32[768,2048]{1,0:T(8,128)}) fusion(f32[2048]{0:T(1024)S(1)} %broadcast_select_fusion, bf16[768,768]{1,0:T(8,128)(2,1)} %constant_dynamic-update-slice_fusion.4, bf16[2048,768]{1,0:T(8,128)(2,1)} %bitcast_select_fusion), kind=kOutput, calls=%fused_computation.7 | convolution fusion | flops 2430074880 | bytes 16916480 | tf_op jit(solution)/shard_map/dot_general | solution.py:280
  41.5 3.9 %collective-permute-start.9 = (bf16[768,512]{1,0:T(8,128)(2,1)}, bf16[768,512]{1,0:T(8,128)(2,1)}, u32[]{:S(2)}, u32[]{:S(2)}) collective-permute-start(bf16[768,512]{1,0:T(8,128)(2,1)} %collective-permute-done.8.r_6_), channel_id=1, source_target_pairs={{0,2},{2,4},{4,6},{6,8},{8,10},{10,12},{12,14},{14,16},{16,18},{18... | collective-permute-start | bytes 2359304 | tf_op jit(solution)/shard_map/ppermute | solution.py:251
  49.9 2.9 %collective-permute-done.3 = s32[3,9]{1,0:T(4,128)S(1)} collective-permute-done((s32[3,9]{1,0:T(4,128)S(1)}, s32[3,9]{1,0:T(4,128)S(1)}, u32[]{:S(2)}, u32[]{:S(2)}) %collective-permute-start.3) | collective-permute-done | bytes 140 | tf_op jit(solution)/shard_map/ppermute | solution.py:206
  54.2 3.6 %collective-permute-done.5 = s32[3,9]{1,0:T(4,128)S(1)} collective-permute-done((s32[3,9]{1,0:T(4,128)S(1)}, s32[3,9]{1,0:T(4,128)S(1)}, u32[]{:S(2)}, u32[]{:S(2)}) %collective-permute-start.5) | collective-permute-done | bytes 140 | tf_op jit(solution)/shard_map/ppermute | solution.py:206
  59.3 6.0 %tiles.1 = (bf16[15,128,512]{2,1,0:T(8,128)(2,1)S(1)}, bf16[15,512,128]{2,1,0:T(8,128)(2,1)S(1)}, f32[15,128,128]{2,1,0:T(8,128)S(1)}, f32[15,128,128]{2,1,0:T(8,128)S(1)}) custom-call(s32[84]{0:T(128)S(1)} %reshape.167.r_0_, s32[84]{0:T(128)S(1)} %reshape.168.r_1_, s32[21]{0:T(128)S(1)} %slice_reduce_fusion.1.r_2_), custom_call_target="tpu_custom_call" | custom-call | tf_op jit(solution)/shard_map/tiles/pallas_call | solution.py:82
  69.8 15.9 %hops.1 = (bf16[384,512]{1,0:T(8,128)(2,1)}, bf16[384,512]{1,0:T(8,128)(2,1)}) custom-call(s32[60]{0:T(128)} %reshape.166.r_0_, s32[2]{0:T(128)} %fusion.21.r_1_, bf16[384,512]{1,0:T(8,128)(2,1)} %r_2_.1, bf16[384,512]{1,0:T(8,128)(2,1)} %r_3_.1, bf16[768,512]{1,0:T(8,128)(2,1)} %collective-permute-done.6.r_4_, ...), custom_call_target="tpu_custom_call" | custom-call | tf_op jit(solution)/shard_map/hops/pallas_call | solution.py:185
  88.0 4.3 %fusion.7 = bf16[2048,512]{0,1:T(8,128)(2,1)S(1)} fusion(bf16[768,512]{1,0:T(8,128)(2,1)S(1)} %constant_dynamic-update-slice_fusion.2, f32[768,2048]{1,0:T(8,128)} %get-tuple-element.33, f32[2048]{0:T(1024)S(1)} %broadcast_select_fusion), kind=kOutput, calls=%fused_computation.17 | convolution fusion | flops 1621098496 | bytes 9183232 | tf_op jit(solution)/shard_map/dot_general | solution.py:294
  92.4 3.5 %fusion.56 = (bf16[2048]{0:T(1024)(128)(2,1)S(1)}, bf16[768,2048]{1,0:T(8,128)(2,1)}) fusion(f32[768,2048]{1,0:T(8,128)S(1)} %bitcast.80, bf16[768,512]{1,0:T(8,128)(2,1)S(1)} %constant_dynamic-update-slice_fusion.2, bf16[2048,512]{1,0:T(8,128)(2,1)S(1)} %copy-done.6), kind=kOutput, calls=%fused_computation.122 | convolution fusion | flops 1615329280 | bytes 12324864 | tf_op jit(solution)/shard_map/dot_general | solution.py:295
  97.4 2.4 %copy.23 = bf16[1024,640]{1,0:T(8,128)(2,1)} copy(bf16[1024,640]{0,1:T(8,128)(2,1)} %get-tuple-element.21) | data formatting | bytes 2621440 | tf_op jit(solution)/shard_map/slice | solution.py:215
  101.3 4.9 %convolution_convert_fusion = bf16[2048,768]{1,0:T(8,128)(2,1)S(1)} fusion(bf16[768,2048]{1,0:T(8,128)(2,1)} %get-tuple-element.35, bf16[768,768]{1,0:T(8,128)(2,1)} %constant_dynamic-update-slice_fusion.4), kind=kOutput, calls=%fused_computation.11 | convolution fusion | flops 2417491968 | bytes 7471104 | tf_op jit(solution)/shard_map/dot_general | solution.py:299
  106.2 1.9 %fusion.54 = (bf16[1024,768]{1,0:T(8,128)(2,1)}, bf16[1024,768]{1,0:T(8,128)(2,1)}) fusion(bf16[2048,768]{1,0:T(8,128)(2,1)S(1)} %convolution_convert_fusion), kind=kLoop, calls=%fused_computation.120 | loop fusion | bytes 6291456 | tf_op jit(solution)/shard_map/slice | solution.py:215
  108.1 2.1 %copy.22 = f32[1024,640]{1,0:T(8,128)} copy(f32[1024,640]{0,1:T(8,128)S(1)} %get-tuple-element.22) | data formatting | bytes 5242880 | tf_op jit(solution)/shard_map/convert_element_type | solution.py:216
  110.2 2.5 %add_convert_fusion = bf16[2,2,2,2,64,640]{5,4,3,2,1,0:T(8,128)(2,1)S(1)} fusion(f32[2,2,2,2,64,640]{5,4,3,2,1,0:T(8,128)} %bitcast.78, bf16[2,2,2,2,64,640]{5,4,3,2,1,0:T(8,128)(2,1)} %collective-permute-done.16), kind=kLoop, calls=%fused_computation.20 | loop fusion | flops 1966080 | bytes 5242880 | tf_op jit(solution)/shard_map/convert_element_type | solution.py:216
  112.8 3.1 %collective-permute-start.17 = (bf16[2,2,2,64,640]{4,3,2,1,0:T(8,128)(2,1)S(1)}, bf16[2,2,2,64,640]{4,3,2,1,0:T(8,128)(2,1)S(1)}, u32[]{:S(2)}, u32[]{:S(2)}) collective-permute-start(bf16[2,2,2,64,640]{4,3,2,1,0:T(8,128)(2,1)S(1)} %slice_bitcast_fusion.2), channel_id=1, source_target_pairs={{0,4},{1,5},{2,6},{3,7},{4,0},{5,1},{6,2},{7,3},{8,12},{9,13},{10,... | collective-permute-start | bytes 1966088 | tf_op jit(solution)/shard_map/ppermute | solution.py:210
  115.9 2.0 %fusion.5 = bf16[2,2,2,2,64,768]{5,4,3,2,1,0:T(8,128)(2,1)S(1)} fusion(bf16[2,2,2,2,64,768]{5,4,3,2,1,0:T(8,128)(2,1)S(1)} %bitcast.81, bf16[2,2,2,2,64,768]{5,4,3,2,1,0:T(8,128)(2,1)} %collective-permute-done.10), kind=kLoop, calls=%fused_computation.14 | loop fusion | flops 3145728 | bytes 4718592 | tf_op jit(solution)/shard_map/convert_element_type | solution.py:216
  118.0 2.1 %collective-permute-start.11 = (bf16[2,2,2,64,768]{4,3,2,1,0:T(8,128)(2,1)S(1)}, bf16[2,2,2,64,768]{4,3,2,1,0:T(8,128)(2,1)S(1)}, u32[]{:S(2)}, u32[]{:S(2)}) collective-permute-start(bf16[2,2,2,64,768]{4,3,2,1,0:T(8,128)(2,1)S(1)} %slice_bitcast_fusion), channel_id=1, source_target_pairs={{0,1},{1,0},{2,3},{3,2},{4,5},{5,4},{6,7},{7,6},{8,9},{9,8},{10,11... | collective-permute-start | bytes 2359304 | tf_op jit(solution)/shard_map/ppermute | solution.py:210
  120.1 11.2 %collective-permute-done.17 = bf16[2,2,2,64,640]{4,3,2,1,0:T(8,128)(2,1)S(1)} collective-permute-done((bf16[2,2,2,64,640]{4,3,2,1,0:T(8,128)(2,1)S(1)}, bf16[2,2,2,64,640]{4,3,2,1,0:T(8,128)(2,1)S(1)}, u32[]{:S(2)}, u32[]{:S(2)}) %collective-permute-start.17) | collective-permute-done | bytes 655392 | tf_op jit(solution)/shard_map/ppermute | solution.py:210
  131.5 2.1 %collective-permute-start.18 = (bf16[2,2,64,640]{3,2,1,0:T(8,128)(2,1)S(1)}, bf16[2,2,64,640]{3,2,1,0:T(8,128)(2,1)S(1)}, u32[]{:S(2)}, u32[]{:S(2)}) collective-permute-start(bf16[2,2,64,640]{3,2,1,0:T(8,128)(2,1)S(1)} %slice_bitcast_fusion.6), channel_id=1, source_target_pairs={{0,1},{1,0},{2,3},{3,2},{4,5},{5,4},{6,7},{7,6},{8,9},{9,8},{10,11... | collective-permute-start | bytes 983048 | tf_op jit(solution)/shard_map/ppermute | solution.py:210
  133.6 2.6 %convolution_convert_fusion.1 = bf16[768,768]{1,0:T(8,128)(2,1)S(1)} fusion(bf16[768,2048]{1,0:T(8,128)(2,1)S(1)} %copy-done.9, bf16[2048,768]{1,0:T(8,128)(2,1)S(1)} %copy-done.8), kind=kOutput, calls=%fused_computation.24 | convolution fusion | flops 2416508928 | bytes 7471104 | tf_op jit(solution)/shard_map/dot_general | solution.py:302
  136.2 8.8 %collective-permute-done.18 = bf16[2,2,64,640]{3,2,1,0:T(8,128)(2,1)S(1)} collective-permute-done((bf16[2,2,64,640]{3,2,1,0:T(8,128)(2,1)S(1)}, bf16[2,2,64,640]{3,2,1,0:T(8,128)(2,1)S(1)}, u32[]{:S(2)}, u32[]{:S(2)}) %collective-permute-start.18) | collective-permute-done | bytes 327712 | tf_op jit(solution)/shard_map/ppermute | solution.py:210
  151.4 4.5 %collective-permute-done.20 = bf16[64,640]{1,0:T(8,128)(2,1)S(1)} collective-permute-done((bf16[64,640]{1,0:T(8,128)(2,1)S(1)}, bf16[64,640]{1,0:T(8,128)(2,1)S(1)}, u32[]{:S(2)}, u32[]{:S(2)}) %collective-permute-start.20) | collective-permute-done | bytes 81952 | tf_op jit(solution)/shard_map/ppermute | solution.py:210
  156.6 3.2 %collective-permute-done.12 = bf16[2,2,64,768]{3,2,1,0:T(8,128)(2,1)S(1)} collective-permute-done((bf16[2,2,64,768]{3,2,1,0:T(8,128)(2,1)S(1)}, bf16[2,2,64,768]{3,2,1,0:T(8,128)(2,1)S(1)}, u32[]{:S(2)}, u32[]{:S(2)}) %collective-permute-start.12) | collective-permute-done | bytes 393248 | tf_op jit(solution)/shard_map/ppermute | solution.py:210
  160.7 2.3 %collective-permute-start.14 = (bf16[64,768]{1,0:T(8,128)(2,1)S(1)}, bf16[64,768]{1,0:T(8,128)(2,1)S(1)}, u32[]{:S(2)}, u32[]{:S(2)}) collective-permute-start(bf16[64,768]{1,0:T(8,128)(2,1)S(1)} %get-tuple-element.27), channel_id=1, source_target_pairs={{0,16},{1,17},{2,18},{3,19},{4,20},{5,21},{6,22},{7,23},{8,24},{9,... | collective-permute-start | bytes 294920 | tf_op jit(solution)/shard_map/ppermute | solution.py:210
  165.1 3.2 %collective-permute-done.14 = bf16[64,768]{1,0:T(8,128)(2,1)S(1)} collective-permute-done((bf16[64,768]{1,0:T(8,128)(2,1)S(1)}, bf16[64,768]{1,0:T(8,128)(2,1)S(1)}, u32[]{:S(2)}, u32[]{:S(2)}) %collective-permute-start.14) | collective-permute-done | bytes 98336 | tf_op jit(solution)/shard_map/ppermute | solution.py:210
  (104 shorter events, 37.3 us)
Async XLA Ops:
  0.6 20.1 %copy-start = (bf16[2048,768]{1,0:T(8,128)(2,1)S(1)}, bf16[2048,768]{1,0:T(8,128)(2,1)}, u32[]{:S(2)}) copy-start(bf16[2048,768]{1,0:T(8,128)(2,1)} %param.16) | copy-start | bytes 9437188
  2.4 43.6 %collective-permute-start = (s32[3,9]{1,0:T(4,128)S(1)}, s32[3,9]{1,0:T(4,128)S(1)}, u32[]{:S(2)}, u32[]{:S(2)}) collective-permute-start(s32[3,9]{1,0:T(4,128)S(1)} %pad_add_fusion), channel_id=1, source_target_pairs={{0,3},{1,4},{2,5},{3,6},{4,7},{5,8},{6,9},{7,10},{8,11},{9,12},{10... | collective-permute-start | bytes 332 | tf_op jit(solution)/shard_map/ppermute | solution.py:206
  6.7 40.6 %collective-permute-start.1 = (s32[3,9]{1,0:T(4,128)S(1)}, s32[3,9]{1,0:T(4,128)S(1)}, u32[]{:S(2)}, u32[]{:S(2)}) collective-permute-start(s32[3,9]{1,0:T(4,128)S(1)} %pad_add_fusion), channel_id=1, source_target_pairs={{0,2},{1,3},{2,4},{3,5},{4,6},{5,7},{6,8},{7,9},{8,10},{9,11},{10,... | collective-permute-start | bytes 332 | tf_op jit(solution)/shard_map/ppermute | solution.py:206
  13.8 27.7 %collective-permute-start.8 = (bf16[768,512]{1,0:T(8,128)(2,1)}, bf16[768,512]{1,0:T(8,128)(2,1)}, u32[]{:S(2)}, u32[]{:S(2)}) collective-permute-start(bf16[768,512]{1,0:T(8,128)(2,1)} %constant_dynamic-update-slice_fusion), channel_id=1, source_target_pairs={{0,1},{1,0},{2,3},{3,2},{4,5},{5,4},{6,7},{7,6},{8,9},{9,8},{10,11... | collective-permute-start | bytes 2359304 | tf_op jit(solution)/shard_map/ppermute | solution.py:210
  13.8 56.0 %collective-permute-start.6 = (bf16[768,512]{1,0:T(8,128)(2,1)}, bf16[768,512]{1,0:T(8,128)(2,1)}, u32[]{:S(2)}, u32[]{:S(2)}) collective-permute-start(bf16[768,512]{1,0:T(8,128)(2,1)} %constant_dynamic-update-slice_fusion), channel_id=1, source_target_pairs={{0,2},{1,3},{2,4},{3,5},{4,6},{5,7},{6,8},{7,9},{8,10},{9,11},{10,... | collective-permute-start | bytes 2359304 | tf_op jit(solution)/shard_map/ppermute | solution.py:206
  18.4 51.4 %collective-permute-start.7 = (bf16[768,512]{1,0:T(8,128)(2,1)}, bf16[768,512]{1,0:T(8,128)(2,1)}, u32[]{:S(2)}, u32[]{:S(2)}) collective-permute-start(bf16[768,512]{1,0:T(8,128)(2,1)} %constant_dynamic-update-slice_fusion), channel_id=1, source_target_pairs={{2,0},{3,1},{4,2},{5,3},{6,4},{7,5},{8,6},{9,7},{10,8},{11,9},{12,... | collective-permute-start | bytes 2359304 | tf_op jit(solution)/shard_map/ppermute | solution.py:206
  32.8 12.6 %copy-start.12 = (s32[2]{0:T(128)S(1)}, s32[2]{0:T(128)}, u32[]{:S(2)}) copy-start(s32[2]{0:T(128)} %constant.88.clone) | copy-start | bytes 28
  32.8 12.6 %copy-start.13 = (s32[2]{0:T(128)S(1)}, s32[2]{0:T(128)}, u32[]{:S(2)}) copy-start(s32[2]{0:T(128)} %constant.89.clone) | copy-start | bytes 28
  41.5 28.3 %collective-permute-start.9 = (bf16[768,512]{1,0:T(8,128)(2,1)}, bf16[768,512]{1,0:T(8,128)(2,1)}, u32[]{:S(2)}, u32[]{:S(2)}) collective-permute-start(bf16[768,512]{1,0:T(8,128)(2,1)} %collective-permute-done.8.r_6_), channel_id=1, source_target_pairs={{0,2},{2,4},{4,6},{6,8},{8,10},{10,12},{12,14},{14,16},{16,18},{18... | collective-permute-start | bytes 2359304 | tf_op jit(solution)/shard_map/ppermute | solution.py:251
  46.0 2.6 %collective-permute-start.2 = (s32[3,9]{1,0:T(4,128)S(1)}, s32[3,9]{1,0:T(4,128)S(1)}, u32[]{:S(2)}, u32[]{:S(2)}) collective-permute-start(s32[3,9]{1,0:T(4,128)S(1)} %pad_add_fusion), channel_id=1, source_target_pairs={{0,1},{1,2},{2,3},{3,4},{4,5},{5,6},{6,7},{7,8},{8,9},{9,10},{10,1... | collective-permute-start | bytes 332 | tf_op jit(solution)/shard_map/ppermute | solution.py:206
  47.3 5.5 %collective-permute-start.3 = (s32[3,9]{1,0:T(4,128)S(1)}, s32[3,9]{1,0:T(4,128)S(1)}, u32[]{:S(2)}, u32[]{:S(2)}) collective-permute-start(s32[3,9]{1,0:T(4,128)S(1)} %pad_add_fusion), channel_id=1, source_target_pairs={{1,0},{2,1},{3,2},{4,3},{5,4},{6,5},{7,6},{8,7},{9,8},{10,9},{11,1... | collective-permute-start | bytes 332 | tf_op jit(solution)/shard_map/ppermute | solution.py:206
  48.6 5.6 %collective-permute-start.4 = (s32[3,9]{1,0:T(4,128)S(1)}, s32[3,9]{1,0:T(4,128)S(1)}, u32[]{:S(2)}, u32[]{:S(2)}) collective-permute-start(s32[3,9]{1,0:T(4,128)S(1)} %pad_add_fusion), channel_id=1, source_target_pairs={{2,0},{3,1},{4,2},{5,3},{6,4},{7,5},{8,6},{9,7},{10,8},{11,9},{12,... | collective-permute-start | bytes 332 | tf_op jit(solution)/shard_map/ppermute | solution.py:206
  52.7 5.1 %collective-permute-start.5 = (s32[3,9]{1,0:T(4,128)S(1)}, s32[3,9]{1,0:T(4,128)S(1)}, u32[]{:S(2)}, u32[]{:S(2)}) collective-permute-start(s32[3,9]{1,0:T(4,128)S(1)} %pad_add_fusion), channel_id=1, source_target_pairs={{3,0},{4,1},{5,2},{6,3},{7,4},{8,5},{9,6},{10,7},{11,8},{12,9},{13... | collective-permute-start | bytes 332 | tf_op jit(solution)/shard_map/ppermute | solution.py:206
  86.8 5.6 %slice-start = ((s8[6291456]{0:T(1024)(128)(4,1)}), s8[4194304]{0:T(1024)(128)(4,1)S(1)}, s32[]{:S(2)}) async-start(s8[6291456]{0:T(1024)(128)(4,1)} %bitcast.79), calls=%async_computation | async-start | bytes 8388608
  87.9 4.4 %copy-start.6 = (bf16[2048,512]{1,0:T(8,128)(2,1)S(1)}, bf16[2048,512]{1,0:T(8,128)(2,1)}, u32[]{:S(2)}) copy-start(bf16[2048,512]{1,0:T(8,128)(2,1)} %bitcast_select_fusion.1) | copy-start | bytes 6291460
  87.9 4.5 %slice-start.1 = ((s8[6291456]{0:T(1024)(128)(4,1)}), s8[2097152]{0:T(1024)(128)(4,1)S(1)}, s32[]{:S(2)}) async-start(s8[6291456]{0:T(1024)(128)(4,1)} %bitcast.79), calls=%async_computation.1 | async-start | bytes 4194304
  99.8 10.3 %collective-permute-start.16 = (bf16[2,2,2,2,64,640]{5,4,3,2,1,0:T(8,128)(2,1)}, bf16[2,2,2,2,64,640]{5,4,3,2,1,0:T(8,128)(2,1)}, u32[]{:S(2)}, u32[]{:S(2)}) collective-permute-start(bf16[2,2,2,2,64,640]{5,4,3,2,1,0:T(8,128)(2,1)} %bitcast.85), channel_id=1, source_target_pairs={{0,2},{1,3},{2,0},{3,1},{4,6},{5,7},{6,4},{7,5},{8,10},{9,11},{10,... | collective-permute-start | bytes 3932168 | tf_op jit(solution)/shard_map/ppermute | solution.py:210
  108.1 7.8 %collective-permute-start.10 = (bf16[2,2,2,2,64,768]{5,4,3,2,1,0:T(8,128)(2,1)}, bf16[2,2,2,2,64,768]{5,4,3,2,1,0:T(8,128)(2,1)}, u32[]{:S(2)}, u32[]{:S(2)}) collective-permute-start(bf16[2,2,2,2,64,768]{5,4,3,2,1,0:T(8,128)(2,1)} %bitcast.7), channel_id=1, source_target_pairs={{0,2},{1,3},{2,0},{3,1},{4,6},{5,7},{6,4},{7,5},{8,10},{9,11},{10,... | collective-permute-start | bytes 4718600 | tf_op jit(solution)/shard_map/ppermute | solution.py:210
  110.2 5.8 %copy-start.7 = (bf16[1024,768]{1,0:T(8,128)(2,1)S(1)}, bf16[1024,768]{1,0:T(8,128)(2,1)}, u32[]{:S(2)}) copy-start(bf16[1024,768]{1,0:T(8,128)(2,1)} %get-tuple-element.20) | copy-start | bytes 4718596
  112.8 18.5 %collective-permute-start.17 = (bf16[2,2,2,64,640]{4,3,2,1,0:T(8,128)(2,1)S(1)}, bf16[2,2,2,64,640]{4,3,2,1,0:T(8,128)(2,1)S(1)}, u32[]{:S(2)}, u32[]{:S(2)}) collective-permute-start(bf16[2,2,2,64,640]{4,3,2,1,0:T(8,128)(2,1)S(1)} %slice_bitcast_fusion.2), channel_id=1, source_target_pairs={{0,4},{1,5},{2,6},{3,7},{4,0},{5,1},{6,2},{7,3},{8,12},{9,13},{10,... | collective-permute-start | bytes 1966088 | tf_op jit(solution)/shard_map/ppermute | solution.py:210
  115.9 17.7 %copy-start.9 = (bf16[768,2048]{1,0:T(8,128)(2,1)S(1)}, bf16[768,2048]{1,0:T(8,128)(2,1)}, u32[]{:S(2)}) copy-start(bf16[768,2048]{1,0:T(8,128)(2,1)} %get-tuple-element.35) | copy-start | bytes 9437188
  118.0 15.6 %copy-start.8 = (bf16[2048,768]{1,0:T(8,128)(2,1)S(1)}, bf16[2048,768]{1,0:T(8,128)(2,1)}, u32[]{:S(2)}) copy-start(bf16[2048,768]{1,0:T(8,128)(2,1)} %bitcast_select_fusion) | copy-start | bytes 9437188
  118.0 31.6 %collective-permute-start.11 = (bf16[2,2,2,64,768]{4,3,2,1,0:T(8,128)(2,1)S(1)}, bf16[2,2,2,64,768]{4,3,2,1,0:T(8,128)(2,1)S(1)}, u32[]{:S(2)}, u32[]{:S(2)}) collective-permute-start(bf16[2,2,2,64,768]{4,3,2,1,0:T(8,128)(2,1)S(1)} %slice_bitcast_fusion), channel_id=1, source_target_pairs={{0,1},{1,0},{2,3},{3,2},{4,5},{5,4},{6,7},{7,6},{8,9},{9,8},{10,11... | collective-permute-start | bytes 2359304 | tf_op jit(solution)/shard_map/ppermute | solution.py:210
  131.5 13.5 %collective-permute-start.18 = (bf16[2,2,64,640]{3,2,1,0:T(8,128)(2,1)S(1)}, bf16[2,2,64,640]{3,2,1,0:T(8,128)(2,1)S(1)}, u32[]{:S(2)}, u32[]{:S(2)}) collective-permute-start(bf16[2,2,64,640]{3,2,1,0:T(8,128)(2,1)S(1)} %slice_bitcast_fusion.6), channel_id=1, source_target_pairs={{0,1},{1,0},{2,3},{3,2},{4,5},{5,4},{6,7},{7,6},{8,9},{9,8},{10,11... | collective-permute-start | bytes 983048 | tf_op jit(solution)/shard_map/ppermute | solution.py:210
  145.2 6.2 %collective-permute-start.19 = (bf16[64,640]{1,0:T(8,128)(2,1)S(1)}, bf16[64,640]{1,0:T(8,128)(2,1)S(1)}, u32[]{:S(2)}, u32[]{:S(2)}) collective-permute-start(bf16[64,640]{1,0:T(8,128)(2,1)S(1)} %get-tuple-element.28), channel_id=1, source_target_pairs={{0,8},{1,9},{2,10},{3,11},{4,12},{5,13},{6,14},{7,15},{8,0},{9,1},... | collective-permute-start | bytes 245768 | tf_op jit(solution)/shard_map/ppermute | solution.py:210
  146.8 9.1 %collective-permute-start.20 = (bf16[64,640]{1,0:T(8,128)(2,1)S(1)}, bf16[64,640]{1,0:T(8,128)(2,1)S(1)}, u32[]{:S(2)}, u32[]{:S(2)}) collective-permute-start(bf16[64,640]{1,0:T(8,128)(2,1)S(1)} %get-tuple-element.30), channel_id=1, source_target_pairs={{0,16},{1,17},{2,18},{3,19},{4,20},{5,21},{6,22},{7,23},{8,24},{9,... | collective-permute-start | bytes 245768 | tf_op jit(solution)/shard_map/ppermute | solution.py:210
  147.9 8.0 %collective-permute-start.21 = (bf16[64,640]{1,0:T(8,128)(2,1)S(1)}, bf16[64,640]{1,0:T(8,128)(2,1)S(1)}, u32[]{:S(2)}, u32[]{:S(2)}) collective-permute-start(bf16[64,640]{1,0:T(8,128)(2,1)S(1)} %get-tuple-element.29), channel_id=1, source_target_pairs={{0,24},{1,25},{2,26},{3,27},{4,28},{5,29},{6,30},{7,31},{8,16},{9,... | collective-permute-start | bytes 245768 | tf_op jit(solution)/shard_map/ppermute | solution.py:210
  149.8 20.3 %copy-start.1 = (bf16[2048,768]{1,0:T(8,128)(2,1)S(1)}, bf16[2048,768]{1,0:T(8,128)(2,1)}, u32[]{:S(2)}) copy-start(bf16[2048,768]{1,0:T(8,128)(2,1)} %param.16) | copy-start | bytes 9437188
  149.9 10.0 %collective-permute-start.12 = (bf16[2,2,64,768]{3,2,1,0:T(8,128)(2,1)S(1)}, bf16[2,2,64,768]{3,2,1,0:T(8,128)(2,1)S(1)}, u32[]{:S(2)}, u32[]{:S(2)}) collective-permute-start(bf16[2,2,64,768]{3,2,1,0:T(8,128)(2,1)S(1)} %slice_bitcast_fusion.4), channel_id=1, source_target_pairs={{0,4},{1,5},{2,6},{3,7},{4,0},{5,1},{6,2},{7,3},{8,12},{9,13},{10,... | collective-permute-start | bytes 1179656 | tf_op jit(solution)/shard_map/ppermute | solution.py:210
  160.0 5.1 %collective-permute-start.13 = (bf16[64,768]{1,0:T(8,128)(2,1)S(1)}, bf16[64,768]{1,0:T(8,128)(2,1)S(1)}, u32[]{:S(2)}, u32[]{:S(2)}) collective-permute-start(bf16[64,768]{1,0:T(8,128)(2,1)S(1)} %get-tuple-element.25), channel_id=1, source_target_pairs={{0,8},{1,9},{2,10},{3,11},{4,12},{5,13},{6,14},{7,15},{8,0},{9,1},... | collective-permute-start | bytes 294920 | tf_op jit(solution)/shard_map/ppermute | solution.py:210
  160.7 7.5 %collective-permute-start.14 = (bf16[64,768]{1,0:T(8,128)(2,1)S(1)}, bf16[64,768]{1,0:T(8,128)(2,1)S(1)}, u32[]{:S(2)}, u32[]{:S(2)}) collective-permute-start(bf16[64,768]{1,0:T(8,128)(2,1)S(1)} %get-tuple-element.27), channel_id=1, source_target_pairs={{0,16},{1,17},{2,18},{3,19},{4,20},{5,21},{6,22},{7,23},{8,24},{9,... | collective-permute-start | bytes 294920 | tf_op jit(solution)/shard_map/ppermute | solution.py:210
  163.0 6.5 %collective-permute-start.15 = (bf16[64,768]{1,0:T(8,128)(2,1)S(1)}, bf16[64,768]{1,0:T(8,128)(2,1)S(1)}, u32[]{:S(2)}, u32[]{:S(2)}) collective-permute-start(bf16[64,768]{1,0:T(8,128)(2,1)S(1)} %get-tuple-element.26), channel_id=1, source_target_pairs={{0,24},{1,25},{2,26},{3,27},{4,28},{5,29},{6,30},{7,31},{8,16},{9,... | collective-permute-start | bytes 294920 | tf_op jit(solution)/shard_map/ppermute | solution.py:210
  (6 other events, 9.6 us)

commit v2 on v1

--- a/solution.py
+++ b/solution.py
@@ -96,12 +96,18 @@
 
 
 def hops_kernel(
-    place_ref, base_ref, own_img, own_cap, low, high, mate, far, pat_ref, pat_t_ref, nimg_ref, ncap_ref,
-    out_img, out_cap, img0, cap0, img1, cap1, acc, acc2, keep_img, keep_cap, *, tiles, slots, width,
+    place_ref, base_ref, own_img, own_cap, low_hbm, high_hbm, mate_hbm, far_hbm, pat_ref, pat_t_ref, nimg_ref, ncap_ref,
+    out_ref, bands, img0, cap0, img1, cap1, acc, acc2, keep_img, keep_cap, sems, *, tiles, slots, width,
 ):
     mid = 5 * tiles
     near = 3 * tiles
     keep = 1.0 - ALPHA
+    copies = [
+        pltpu.make_async_copy(src, bands.at[k], sems.at[k])
+        for k, src in enumerate((low_hbm, high_hbm, mate_hbm, far_hbm))
+    ]
+    for copy in copies:
+        copy.start()
 
     def wide(n_ref, m):
         n = n_ref[m]
@@ -113,16 +119,15 @@
             img0[m] = (rows_img(t).astype(F32) * wide(nimg_ref, m)).astype(BF16)
             cap0[m] = (rows_cap(t).astype(F32) * wide(ncap_ref, m)).astype(BF16)
 
-    def both(ref):
-        return (lambda t: ref[pl.ds(t * TILE, TILE), :]), (lambda t: ref[pl.ds((tiles + t) * TILE, TILE), :])
-
-    scale(lambda t: own_img[pl.ds(t * TILE, TILE), :], lambda t: own_cap[pl.ds(t * TILE, TILE), :], 2 * tiles)
-    scale(*both(low), 0)
-    scale(*both(high), 4 * tiles)
-    scale(*both(mate), base_ref[0])
-    scale(*both(far), base_ref[1])
+    def both(k):
+        return (lambda t: bands[k, pl.ds(t * TILE, TILE), :]), (lambda t: bands[k, pl.ds((tiles + t) * TILE, TILE), :])
+
     acc[...] = jnp.zeros_like(acc)
     acc2[...] = jnp.zeros_like(acc2)
+    scale(lambda t: own_img[pl.ds(t * TILE, TILE), :], lambda t: own_cap[pl.ds(t * TILE, TILE), :], 2 * tiles)
+    for k, base in enumerate((0, 4 * tiles, base_ref[0], base_ref[1])):
+        copies[k].wait()
+        scale(*both(k), base)
 
     def push(q, state, target, lo, count):
         r = jnp.dot(pat_t_ref[q], state, preferred_element_type=F32)
@@ -172,22 +177,26 @@
         q = 2 * tiles + t
         rows = pl.ds(t * TILE, TILE)
         flow = keep * wide(nimg_ref, q) * pull(q, cap1, tiles)
-        out_img[rows, :] = (ALPHA * (own_img[rows, :].astype(F32) + keep_img[tiles + t]) + flow).astype(BF16)
+        out_ref[rows, :] = (ALPHA * (own_img[rows, :].astype(F32) + keep_img[tiles + t]) + flow).astype(BF16)
         flow = keep * wide(ncap_ref, q) * acc2[t]
-        out_cap[rows, :] = (ALPHA * (own_cap[rows, :].astype(F32) + keep_cap[tiles + t]) + flow).astype(BF16)
+        out_ref[pl.ds((tiles + t) * TILE, TILE), :] = (
+            ALPHA * (own_cap[rows, :].astype(F32) + keep_cap[tiles + t]) + flow
+        ).astype(BF16)
 
 
 def propagate(places, bases, own_img, own_cap, low, high, mate, far, pats, tiles, slots):
     width = own_img.shape[1]
     smem = pl.BlockSpec(memory_space=pltpu.SMEM)
     vmem = pl.BlockSpec(memory_space=pltpu.VMEM)
+    hbm = pl.BlockSpec(memory_space=pl.ANY)
     mid, near = 5 * tiles, 3 * tiles
     return pl.pallas_call(
         lambda *r: hops_kernel(*r, tiles=tiles, slots=slots, width=width),
-        out_shape=(jax.ShapeDtypeStruct(own_img.shape, BF16),) * 2,
-        in_specs=[smem] * 2 + [vmem] * 10,
-        out_specs=(vmem,) * 2,
+        out_shape=jax.ShapeDtypeStruct(low.shape, BF16),
+        in_specs=[smem] * 2 + [vmem] * 2 + [hbm] * 4 + [vmem] * 4,
+        out_specs=vmem,
         scratch_shapes=[
+            pltpu.VMEM((4,) + low.shape, BF16),
             pltpu.VMEM((mid, TILE, width), BF16),
             pltpu.VMEM((mid, TILE, width), BF16),
             pltpu.VMEM((near, TILE, width), BF16),
@@ -196,12 +205,92 @@
             pltpu.VMEM((tiles + 1, TILE, width), F32),
             pltpu.VMEM((near, TILE, width), F32),
             pltpu.VMEM((near, TILE, width), F32),
+            pltpu.SemaphoreType.DMA((4,)),
         ],
         compiler_params=pltpu.CompilerParams(vmem_limit_bytes=56 << 20),
         name="hops",
     )(places, bases, own_img, own_cap, low, high, mate, far, *pats)
 
 
+BLOCK = 64
+GROUP = 4
+
+
+def grouped(width):
+    return [
+        pl.BlockSpec((BLOCK, width), lambda i, order, k=k: (order[i * GROUP + k], 0)) for k in range(GROUP)
+    ]
+
+
+def stacked(refs):
+    return jnp.concatenate([r[...] for r in refs], axis=0)
+
+
+def whole(shape):
+    return pl.BlockSpec(shape, lambda i, order: (0,) * len(shape))
+
+
+def out_kernel(order_ref, *refs):
+    act, (logit_ref, part_ref) = refs[:GROUP], refs[GROUP:]
+    part_ref[...] = jnp.dot(stacked(act), logit_ref[...], preferred_element_type=F32).astype(BF16)
+
+
+def in_kernel(order_ref, *refs):
+    slope, w_out = refs[:GROUP], refs[GROUP : 2 * GROUP]
+    logit_ref, feats_ref, part_ref, grad_ref = refs[2 * GROUP :]
+    hidden = lax.dot_general(
+        stacked(w_out), logit_ref[...], (((1,), (1,)), ((), ())), preferred_element_type=F32
+    )
+    grad = (hidden * stacked(slope)).astype(BF16)
+    grad_ref[...] = grad
+    f_in = feats_ref.shape[1]
+    part_ref[:, :f_in] = jnp.dot(grad, feats_ref[...], preferred_element_type=F32).astype(BF16)
+    bias = jnp.sum(grad.astype(F32), axis=1, keepdims=True)
+    part_ref[:, f_in:] = jnp.broadcast_to(bias, (bias.shape[0], TILE)).astype(BF16)
+
+
+def feat_kernel(order_ref, *refs):
+    w_in = refs[:GROUP]
+    grad_ref, img_ref, cap_ref, acc_ref = refs[GROUP:]
+    i = pl.program_id(0)
+
+    @pl.when(i == 0)
+    def _():
+        acc_ref[...] = jnp.zeros_like(acc_ref)
+
+    acc_ref[...] += lax.dot_general(
+        grad_ref[...], stacked(w_in), (((0,), (0,)), ((), ())), preferred_element_type=F32
+    )
+
+    @pl.when(i == pl.num_programs(0) - 1)
+    def _():
+        half = img_ref.shape[0]
+        img_ref[...] = acc_ref[:half].astype(BF16)
+        cap_ref[...] = acc_ref[half:].astype(BF16)
+
+
+def over_hidden(kernel, name, order, in_specs, out_specs, out_shape, scratch, args):
+    return pl.pallas_call(
+        kernel,
+        out_shape=out_shape,
+        grid_spec=pltpu.PrefetchScalarGridSpec(
+            num_scalar_prefetch=1,
+            grid=(order.shape[0] // GROUP,),
+            in_specs=in_specs,
+            out_specs=out_specs,
+            scratch_shapes=scratch,
+        ),
+        compiler_params=pltpu.CompilerParams(
+            dimension_semantics=("arbitrary",), vmem_limit_bytes=40 << 20
+        ),
+        name=name,
+    )(order, *args)
+
+
+def rows_of(width):
+    return pl.BlockSpec((GROUP * BLOCK, width), lambda i, order: (i, 0))
+
+
 def moved(array, count, by):
     return lax.ppermute(array, AXES, [(i, i + by) for i in range(count) if 0 <= i + by < count])
 
@@ -216,9 +305,12 @@
     return (kept.astype(F32) + flipped(sent, count, mask).astype(F32)).astype(BF16)
 
 
+def nearest_pair(count, by):
+    return [(i, i + by) for i in range(0, count - by, 2)] + [(i, i - by) for i in range(by + 1, count, 2)]
+
+
 def scattered(part, count, bits, order):
-    rows, lanes = part.shape[1:]
-    part = part.reshape((2,) * len(bits) + (rows, lanes))
+    rows, lanes = part.shape[-2:]
     left = list(bits)
     for bit in order:
         part = halve(part, left.index(bit), count, 1 << bit)
@@ -242,18 +334,23 @@
     count = n_img * n_cap
     me = lax.axis_index(AXES)
 
-    meta = jnp.concatenate([tile_seed, tile_cols, tile_count[:, None]], axis=1)
-    bands = [moved(meta, count, by) for by in (3, 2, 1)] + [meta] + [moved(meta, count, -by) for by in (1, 2, 3)]
     block = jnp.concatenate([cot_img, cot_cap], axis=0)
     mate = flipped(block, count, 1)
     low = moved(block, count, 2)
     high = moved(block, count, -2)
-    far = lax.ppermute(
-        mate,
-        AXES,
-        [(i, i + 2) for i in range(0, count - 2, 2)] + [(i, i - 2) for i in range(3, count, 2)],
-    )
-    wide = jnp.concatenate(bands, axis=0)
+    far = lax.ppermute(mate, AXES, nearest_pair(count, 2))
+    even = (me & 1) == 0
+    meta = jnp.concatenate([tile_seed, tile_cols, tile_count[:, None]], axis=1)
+    other = flipped(meta, count, 1)
+    pair = jnp.where(even, jnp.concatenate([meta, other]), jnp.concatenate([other, meta]))
+    pair_low = moved(pair, count, 2)
+    pair_high = moved(pair, count, -2)
+    pair_far = lax.ppermute(pair, AXES, nearest_pair(count, 4))
+    wide = jnp.where(
+        even,
+        jnp.concatenate([pair_far[tiles:], pair_low, pair, pair_high]),
+        jnp.concatenate([pair_low, pair, pair_high, pair_far[:tiles]]),
+    )
     frame = jnp.arange(7 * tiles, dtype=jnp.int32)[:, None]
     counts = wide[:, 2 * slots]
     seeds = wide[:, :slots].reshape(-1)
@@ -271,41 +368,54 @@
         order = order | (((pos >> (m - 1 - k)) & 1) << bit)
     order = order ^ me
     rows = hid // count
-    w_in_p = jnp.take(w_in.reshape(count, rows, f_in), order, axis=0).reshape(hid, f_in)
-    w_out_p = jnp.take(w_out.reshape(count, rows, -1), order, axis=0).reshape(hid, -1)
-    b_in_p = jnp.take(b_in.reshape(count, rows), order, axis=0).reshape(hid)
+    if rows % BLOCK:
+        w_in, w_out, b_in = [
+            jnp.take(v.reshape((count, rows) + v.shape[1:]), order, axis=0).reshape(v.shape) for v in (w_in, w_out, b_in)
+        ]
+        order = jnp.arange(hid // BLOCK, dtype=jnp.int32)
+    else:
+        order = (order[:, None] * (rows // BLOCK) + jnp.arange(rows // BLOCK, dtype=jnp.int32)).reshape(-1)
 
     feats = jnp.concatenate([feats_img, feats_cap], axis=0)
-    preact = (
-        lax.dot_general(feats, w_in_p, (((1,), (1,)), ((), ())), preferred_element_type=F32) + b_in_p
-    )
+    across = (((1,), (1,)), ((), ()))
+    preact = lax.dot_general(w_in, feats, across, preferred_element_type=F32) + b_in[:, None]
     gelu_value, gelu_slope = gelu_parts(preact)
-    hidden_act = gelu_value.astype(BF16)
-    gelu_slope = lax.optimization_barrier(gelu_slope)
-
-    even = (me & 1) == 0
+    hidden_act, gelu_slope = lax.optimization_barrier((gelu_value.astype(BF16), gelu_slope))
+
     bases = jnp.where(even, jnp.array([3, 1]), jnp.array([1, 3])).astype(jnp.int32) * tiles
     mid_places = (places - tiles)[tiles : 6 * tiles].reshape(-1)
-    logit_img, logit_cap = propagate(
-        mid_places, bases, cot_img, cot_cap, low, high, mate, far, pats, tiles, slots
-    )
-    logit_gradient = jnp.concatenate([logit_img, logit_cap], axis=0)
-    over_rows = (((0,), (0,)), ((), ()))
-    part_out = lax.dot_general(hidden_act, logit_gradient, over_rows, preferred_element_type=F32).astype(BF16)
-    hidden_grad = lax.dot_general(
-        logit_gradient, w_out_p, (((1,), (1,)), ((), ())), preferred_element_type=F32
-    )
-    preact_grad = (hidden_grad * gelu_slope).astype(BF16)
-    part_in = lax.dot_general(preact_grad, feats, over_rows, preferred_element_type=F32).astype(BF16)
-    part_bias = jnp.sum(preact_grad, axis=0, dtype=F32).astype(BF16)
-    packed = jnp.concatenate([part_out, jnp.broadcast_to(part_bias[:, None], (hid, TILE))], axis=1)
-    feat_grad = jnp.dot(preact_grad, w_in_p, preferred_element_type=F32).astype(BF16)
-
-    grad_scale = 1.0 / math.sqrt(2 * local_rows * count)
-    g_out = scattered(packed.reshape(count, rows, -1), count, bits, [a] + img_bits + cap_bits) * grad_scale
-    g_in = scattered(part_in.reshape(count, rows, f_in), count, bits, [a] + cap_bits + img_bits) * grad_scale
+    logit = propagate(mid_places, bases, cot_img, cot_cap, low, high, mate, far, pats, tiles, slots)
+
     width = cot_img.shape[1]
-    return (feat_grad[:local_rows], feat_grad[local_rows:], g_in, g_out[:, :width], g_out[:, width])
+    nodes = 2 * local_rows
+    part_out = over_hidden(
+        out_kernel, "part_out", order, grouped(nodes) + [whole(logit.shape)], rows_of(width),
+        jax.ShapeDtypeStruct((hid, width), BF16), [], [hidden_act] * GROUP + [logit],
+    )
+    part_in, preact_grad = over_hidden(
+        in_kernel, "part_in", order,
+        grouped(nodes) + grouped(width) + [whole(logit.shape), whole(feats.shape)],
+        (rows_of(f_in + TILE), rows_of(nodes)),
+        (jax.ShapeDtypeStruct((hid, f_in + TILE), BF16), jax.ShapeDtypeStruct((hid, nodes), BF16)),
+        [], [gelu_slope] * GROUP + [w_out] * GROUP + [logit, feats],
+    )
+    grad_img, grad_cap = over_hidden(
+        feat_kernel, "feat_grad", order, grouped(f_in) + [rows_of(nodes)],
+        (whole((local_rows, f_in)),) * 2, (jax.ShapeDtypeStruct((local_rows, f_in), BF16),) * 2,
+        [pltpu.VMEM((nodes, f_in), F32)], [w_in] * GROUP + [preact_grad],
+    )
+
+    grad_scale = 1.0 / math.sqrt(nodes * count)
+    blocked = (2,) * m + (rows,)
+    rest = bits[1:]
+    g_out = halve(part_out.reshape(blocked + (width,)), 0, count, 1 << a)
+    g_in = halve(part_in.reshape(blocked + (f_in + TILE,)), 0, count, 1 << a)
+    cut = f_in // 2
+    g_out = scattered(g_out, count, rest, img_bits + cap_bits) * grad_scale
+    g_a = scattered(g_in[..., :cut], count, rest, img_bits + cap_bits) * grad_scale
+    g_b = scattered(g_in[..., cut:], count, rest, cap_bits + img_bits) * grad_scale
+    g_in = jnp.concatenate([g_a, g_b[:, : f_in - cut]], axis=1)
+    return (grad_img, grad_cap, g_in, g_out, g_b[:, f_in - cut])
 
 
 def solution(mesh):

time: 171 us -> 145 us (0.85)
  Pallas kernels: 21.9 us -> 41.6 us
  matrix products: 24 us -> 6.61 us
  local copies, waits for them, and re-layouts: 29.5 us -> 15.5 us
  other arithmetic: 14.1 us -> 4.57 us
  waiting for transfers between devices: 38.7 us -> 32.9 us
    pallas_call x0 -> x3, Pallas kernels: none -> 19.2 us  [over_hidden(): pl.pallas_call(kernel, out_shape=out_shape, grid_spec=pltpu.PrefetchScala...]
    dot_general x5 -> x1, matrix products: 24 us -> 6.61 us  [per_device(): lax.dot_general(w_in, feats, across, preferred_element_type=F32)]
    ppermute x8 -> x4, starting transfers between devices: 19.1 us -> 6.2 us  [moved(): lax.ppermute(array, AXES, [(i, i + by) for i in range(count) if 0 <= i +...]
    ppermute x13 -> x19, starting transfers between devices: 18 us -> 26.2 us  [flipped(): return lax.ppermute(array, AXES, [(i, i ^ mask) for i in range(count)])]
    ppermute x8 -> x4, waiting for transfers between devices: 6.5 us -> 0.01 us  [moved(): lax.ppermute(array, AXES, [(i, i + by) for i in range(count) if 0 <= i +...]
    ppermute x1 -> x2, starting transfers between devices: 3.91 us -> 9.36 us  [the longest x1 5.69 us: per_device(): far = lax.ppermute(mate, AXES, nearest_pair(count, 2))]
    gather x4 -> x0, local copies, waits for them, and re-layouts: 5.29 us -> none  [the longest x1 2.38 us: per_device(): jnp.take(w_in.reshape(count, rows, f_in), order, axis=0).reshape(hid, f_in)]
    select_n x4 -> x2, other arithmetic: 5.04 us -> 0.09 us  [the longest x1 0.08 us: per_device(): jnp.where(even, jnp.concatenate([meta, other]), jnp.concatenate([other, m...]
  transfers between devices with their start and end apart: 22 -> 25, of which waited for: 8 -> 12; matrix products, arithmetic and copies ran while one was open for 27% -> 10% of each run, Pallas kernels for 4% -> 15%
where the time goes in v2:
time: 145 us; the launch traced here: 144 us
  starting transfers between devices  41.8 us (29%)
  Pallas kernels  41.6 us (29%)
  waiting for transfers between devices  32.9 us (23%)
  local copies, waits for them, and re-layouts  15.5 us (11%)
  matrix products  6.61 us (5%)
  other arithmetic  4.57 us (3%)
    ppermute x19, waiting for transfers between devices, flipped(): return lax.ppermute(array, AXES, [(i, i ^ mask) for i in range(count)])  32.8 us
    ppermute x19, starting transfers between devices, flipped(): return lax.ppermute(array, AXES, [(i, i ^ mask) for i in range(count)])  26.2 us
    pallas_call x3, Pallas kernels, over_hidden(): pl.pallas_call(kernel, out_shape=out_shape, grid_spec=pltpu.PrefetchScala...  19.2 us
    pallas_call x1, Pallas kernels, propagate(): pl.pallas_call(lambda *r: hops_kernel(*r, tiles=tiles, slots=slots, width...  16.4 us
    unnamed x32, local copies, waits for them, and re-layouts  9.58 us
    dot_general x1, matrix products, per_device(): lax.dot_general(w_in, feats, across, preferred_element_type=F32)  6.61 us
    ppermute x4, starting transfers between devices, moved(): lax.ppermute(array, AXES, [(i, i + by) for i in range(count) if 0 <= i +...  6.2 us
    pallas_call x1, Pallas kernels, make_tiles(): pl.pallas_call(lambda *r: tiles_kernel(*r, tiles=tiles, slots=slots), out...  5.99 us
  transfers between devices with their start and end apart: 25, of which 12 were waited for; matrix products, arithmetic and copies ran while one was open for 10% of the time, Pallas kernels for 15%

profile of v2, /device:TPU:0, one launch (start us, length us, event | category | flops | bytes accessed | tf_op | source)
XLA Modules:
  0.0 144.0 jit_solution(13605696496930248732)
XLA Ops:
  0.7 1.9 %constant_dynamic-update-slice_fusion.3 = bf16[768,512]{1,0:T(8,128)(2,1)} fusion(bf16[384,512]{1,0:T(8,128)(2,1)} %r_2_.1), kind=kLoop, calls=%fused_computation.73 | loop fusion | bytes 786432
  2.6 1.8 %constant_dynamic-update-slice_fusion.2 = bf16[768,512]{1,0:T(8,128)(2,1)} fusion(bf16[768,512]{1,0:T(8,128)(2,1)} %constant_dynamic-update-slice_fusion.3, bf16[384,512]{1,0:T(8,128)(2,1)} %r_3_.1), kind=kLoop, calls=%fused_computation.72 | loop fusion | bytes 786432 | tf_op jit(solution)/shard_map/concatenate | solution.py:337
  4.3 2.9 %collective-permute-start.6 = (bf16[768,512]{1,0:T(8,128)(2,1)}, bf16[768,512]{1,0:T(8,128)(2,1)}, u32[]{:S(2)}, u32[]{:S(2)}) collective-permute-start(bf16[768,512]{1,0:T(8,128)(2,1)} %constant_dynamic-update-slice_fusion.2), channel_id=1, source_target_pairs={{0,1},{1,0},{2,3},{3,2},{4,5},{5,4},{6,7},{7,6},{8,9},{9,8},{10,11... | collective-permute-start | bytes 2359304 | tf_op jit(solution)/shard_map/ppermute | solution.py:299
  7.3 2.3 %collective-permute-start.4 = (bf16[768,512]{1,0:T(8,128)(2,1)}, bf16[768,512]{1,0:T(8,128)(2,1)}, u32[]{:S(2)}, u32[]{:S(2)}) collective-permute-start(bf16[768,512]{1,0:T(8,128)(2,1)} %constant_dynamic-update-slice_fusion.2), channel_id=1, source_target_pairs={{0,2},{1,3},{2,4},{3,5},{4,6},{5,7},{6,8},{7,9},{8,10},{9,11},{10,... | collective-permute-start | bytes 2359304 | tf_op jit(solution)/shard_map/ppermute | solution.py:295
  9.6 1.3 collective-permute-start.5
  15.0 6.6 %fusion.3 = (f32[2048,768]{1,0:T(8,128)}, bf16[2048,768]{1,0:T(8,128)(2,1)}) fusion(f32[2048]{0:T(1024)S(1)} %copy-done.14, bf16[768,768]{1,0:T(8,128)(2,1)S(1)} %constant_dynamic-update-slice_fusion.refs_9_, bf16[2048,768]{1,0:T(8,128)(2,1)S(1)} %copy-done), kind=kOutput, calls=%fused_computation.4 | convolution fusion | flops 2433220608 | bytes 13770752 | tf_op jit(solution)/shard_map/dot_general | solution.py:381
  22.2 3.0 %collective-permute-done = s32[3,9]{1,0:T(4,128)S(1)} collective-permute-done((s32[3,9]{1,0:T(4,128)S(1)}, s32[3,9]{1,0:T(4,128)S(1)}, u32[]{:S(2)}, u32[]{:S(2)}) %collective-permute-start) | collective-permute-done | bytes 140 | tf_op jit(solution)/shard_map/ppermute | solution.py:299
  25.2 3.7 %collective-permute-start.1 = (s32[6,9]{1,0:T(8,128)S(1)}, s32[6,9]{1,0:T(8,128)S(1)}, u32[]{:S(2)}, u32[]{:S(2)}) collective-permute-start(s32[6,9]{1,0:T(8,128)S(1)} %add_select_fusion.1), channel_id=1, source_target_pairs={{0,4},{2,6},{4,8},{6,10},{8,12},{10,14},{12,16},{14,18},{16,20},{1... | collective-permute-start | bytes 656 | tf_op jit(solution)/shard_map/ppermute | solution.py:348
  28.9 1.3 collective-permute-start.2
  30.2 1.3 collective-permute-start.3
  31.5 5.7 %collective-permute-start.7 = (bf16[768,512]{1,0:T(8,128)(2,1)}, bf16[768,512]{1,0:T(8,128)(2,1)}, u32[]{:S(2)}, u32[]{:S(2)}) collective-permute-start(bf16[768,512]{1,0:T(8,128)(2,1)} %collective-permute-done.6.r_6_), channel_id=1, source_target_pairs={{0,2},{2,4},{4,6},{6,8},{8,10},{10,12},{12,14},{14,16},{16,18},{18... | collective-permute-start | bytes 2359304 | tf_op jit(solution)/shard_map/ppermute | solution.py:341
  38.5 6.0 %tiles.1 = (bf16[15,128,512]{2,1,0:T(8,128)(2,1)S(1)}, bf16[15,512,128]{2,1,0:T(8,128)(2,1)S(1)}, f32[15,128,128]{2,1,0:T(8,128)S(1)}, f32[15,128,128]{2,1,0:T(8,128)S(1)}) custom-call(s32[84]{0:T(128)S(1)} %reshape.62.r_0_, s32[84]{0:T(128)S(1)} %reshape.63.r_1_, s32[21]{0:T(128)S(1)} %slice_reduce_fusion.1.r_2_), custom_call_target="tpu_custom_call" | custom-call | tf_op jit(solution)/shard_map/tiles/pallas_call | solution.py:82
  44.5 1.3 copy-done.6
  45.8 1.4 copy-done.7
  49.1 16.4 %hops.1.refs_8_.refs_4_ = bf16[768,512]{1,0:T(8,128)(2,1)} custom-call(s32[60]{0:T(128)} %reshape.61.r_0_, s32[2]{0:T(128)} %fusion.26.r_1_, bf16[384,512]{1,0:T(8,128)(2,1)} %r_2_.1, bf16[384,512]{1,0:T(8,128)(2,1)} %r_3_.1, bf16[768,512]{1,0:T(8,128)(2,1)} %collective-permute-done.4.r_4_, bf16[768,512]{1,0:T(8,128)(2,1)} %collective-permute-done.5.r_5_, ...), custom_call_target="tpu_custom_call" | custom-call | tf_op jit(solution)/shard_map/hops/pallas_call | solution.py:193
  65.5 1.1 copy-done.3
  66.7 3.5 %part_out.1 = bf16[2048,512]{1,0:T(8,128)(2,1)S(1)} custom-call(s32[32]{0:T(128)S(1)} %fusion.39.order_ref, bf16[2048,768]{1,0:T(8,128)(2,1)S(1)} %copy-done.1, bf16[2048,768]{1,0:T(8,128)(2,1)S(1)} %copy-done.1, bf16[2048,768]{1,0:T(8,128)(2,1)S(1)} %copy-done.1, bf16[2048,768]{1,0:T(8,128)(2,1)S(1)} %copy-done.1, bf16[768,512]{1,0:T(8,128)(2,1)S(1)} %copy-done.3), custom_call_target="tpu_custom_call" | custom-call | tf_op jit(solution)/shard_map/part_out/pallas_call | solution.py:273
  72.1 9.6 %part_in.1 = (bf16[2048,896]{1,0:T(8,128)(2,1)S(1)}, bf16[2048,768]{1,0:T(8,128)(2,1)S(1)}) custom-call(s32[32]{0:T(128)S(1)} %fusion.39.order_ref, f32[2048,768]{1,0:T(8,128)} %get-tuple-element.15.refs_0_.refs_1_.refs_2_.refs_3_, f32[2048,768]{1,0:T(8,128)} %get-tuple-element.15.refs_0_.refs_1_.refs_2_.refs_3_, ...), custom_call_target="tpu_custom_call" | custom-call | tf_op jit(solution)/shard_map/part_in/pallas_call | solution.py:273
  83.3 2.5 %collective-permute-start.20 = (bf16[2,2,2,64,512]{4,3,2,1,0:T(8,128)(2,1)S(1)}, bf16[2,2,2,64,512]{4,3,2,1,0:T(8,128)(2,1)S(1)}, u32[]{:S(2)}, u32[]{:S(2)}) collective-permute-start(bf16[2,2,2,64,512]{4,3,2,1,0:T(8,128)(2,1)S(1)} %slice_bitcast_fusion), channel_id=1, source_target_pairs={{0,4},{1,5},{2,6},{3,7},{4,0},{5,1},{6,2},{7,3},{8,12},{9,13},{10,... | collective-permute-start | bytes 1572872 | tf_op jit(solution)/shard_map/ppermute | solution.py:299
  85.8 12.1 %collective-permute-done.20 = bf16[2,2,2,64,512]{4,3,2,1,0:T(8,128)(2,1)S(1)} collective-permute-done((bf16[2,2,2,64,512]{4,3,2,1,0:T(8,128)(2,1)S(1)}, bf16[2,2,2,64,512]{4,3,2,1,0:T(8,128)(2,1)S(1)}, u32[]{:S(2)}, u32[]{:S(2)}) %collective-permute-start.20) | collective-permute-done | bytes 524320 | tf_op jit(solution)/shard_map/ppermute | solution.py:299
  98.8 6.1 %feat_grad.1 = (bf16[384,768]{1,0:T(8,128)(2,1)}, bf16[384,768]{1,0:T(8,128)(2,1)}) custom-call(s32[32]{0:T(128)S(1)} %fusion.39.order_ref, bf16[2048,768]{1,0:T(8,128)(2,1)S(1)} %copy-done, bf16[2048,768]{1,0:T(8,128)(2,1)S(1)} %copy-done, bf16[2048,768]{1,0:T(8,128)(2,1)S(1)} %copy-done, bf16[2048,768]{1,0:T(8,128)(2,1)S(1)} %copy-done, ...), custom_call_target="tpu_custom_call" | custom-call | tf_op jit(solution)/shard_map/feat_grad/pallas_call | solution.py:273
  105.9 1.6 %collective-permute-start.22 = (bf16[64,512]{1,0:T(8,128)(2,1)S(1)}, bf16[64,512]{1,0:T(8,128)(2,1)S(1)}, u32[]{:S(2)}, u32[]{:S(2)}) collective-permute-start(bf16[64,512]{1,0:T(8,128)(2,1)S(1)} %get-tuple-element.33), channel_id=1, source_target_pairs={{0,8},{1,9},{2,10},{3,11},{4,12},{5,13},{6,14},{7,15},{8,0},{9,1},... | collective-permute-start | bytes 196616 | tf_op jit(solution)/shard_map/ppermute | solution.py:299
  107.6 2.6 %collective-permute-start.23 = (bf16[64,512]{1,0:T(8,128)(2,1)S(1)}, bf16[64,512]{1,0:T(8,128)(2,1)S(1)}, u32[]{:S(2)}, u32[]{:S(2)}) collective-permute-start(bf16[64,512]{1,0:T(8,128)(2,1)S(1)} %get-tuple-element.35), channel_id=1, source_target_pairs={{0,16},{1,17},{2,18},{3,19},{4,20},{5,21},{6,22},{7,23},{8,24},{9,... | collective-permute-start | bytes 196616 | tf_op jit(solution)/shard_map/ppermute | solution.py:299
  111.0 1.5 %collective-permute-start.9 = (bf16[2,2,2,64,384]{4,3,2,1,0:T(8,128)(2,1)S(1)}, bf16[2,2,2,64,384]{4,3,2,1,0:T(8,128)(2,1)S(1)}, u32[]{:S(2)}, u32[]{:S(2)}) collective-permute-start(bf16[2,2,2,64,384]{4,3,2,1,0:T(8,128)(2,1)S(1)} %slice_bitcast_fusion.4), channel_id=1, source_target_pairs={{0,4},{1,5},{2,6},{3,7},{4,0},{5,1},{6,2},{7,3},{8,12},{9,13},{10,... | collective-permute-start | bytes 1179656 | tf_op jit(solution)/shard_map/ppermute | solution.py:299
  114.1 2.1 %collective-permute-done.24 = bf16[64,512]{1,0:T(8,128)(2,1)S(1)} collective-permute-done((bf16[64,512]{1,0:T(8,128)(2,1)S(1)}, bf16[64,512]{1,0:T(8,128)(2,1)S(1)}, u32[]{:S(2)}, u32[]{:S(2)}) %collective-permute-start.24) | collective-permute-done | bytes 65568 | tf_op jit(solution)/shard_map/ppermute | solution.py:299
  116.9 3.2 %collective-permute-done.9 = bf16[2,2,2,64,384]{4,3,2,1,0:T(8,128)(2,1)S(1)} collective-permute-done((bf16[2,2,2,64,384]{4,3,2,1,0:T(8,128)(2,1)S(1)}, bf16[2,2,2,64,384]{4,3,2,1,0:T(8,128)(2,1)S(1)}, u32[]{:S(2)}, u32[]{:S(2)}) %collective-permute-start.9) | collective-permute-done | bytes 393248 | tf_op jit(solution)/shard_map/ppermute | solution.py:299
  121.2 4.6 %collective-permute-done.14 = bf16[2,2,2,64,512]{4,3,2,1,0:T(8,128)(2,1)S(1)} collective-permute-done((bf16[2,2,2,64,512]{4,3,2,1,0:T(8,128)(2,1)S(1)}, bf16[2,2,2,64,512]{4,3,2,1,0:T(8,128)(2,1)S(1)}, u32[]{:S(2)}, u32[]{:S(2)}) %collective-permute-start.14) | collective-permute-done | bytes 524320 | tf_op jit(solution)/shard_map/ppermute | solution.py:299
  125.9 1.2 collective-permute-start.15
  128.7 3.3 %collective-permute-start.12 = (bf16[64,384]{1,0:T(8,128)(2,1)S(1)}, bf16[64,384]{1,0:T(8,128)(2,1)S(1)}, u32[]{:S(2)}, u32[]{:S(2)}) collective-permute-start(bf16[64,384]{1,0:T(8,128)(2,1)S(1)} %get-tuple-element.41), channel_id=1, source_target_pairs={{0,16},{1,17},{2,18},{3,19},{4,20},{5,21},{6,22},{7,23},{8,24},{9,... | collective-permute-start | bytes 147464 | tf_op jit(solution)/shard_map/ppermute | solution.py:299
  133.2 3.3 %collective-permute-start.17 = (bf16[64,512]{1,0:T(8,128)(2,1)S(1)}, bf16[64,512]{1,0:T(8,128)(2,1)S(1)}, u32[]{:S(2)}, u32[]{:S(2)}) collective-permute-start(bf16[64,512]{1,0:T(8,128)(2,1)S(1)} %get-tuple-element.38), channel_id=1, source_target_pairs={{0,16},{1,17},{2,18},{3,19},{4,20},{5,21},{6,22},{7,23},{8,24},{9,... | collective-permute-start | bytes 196616 | tf_op jit(solution)/shard_map/ppermute | solution.py:299
  138.0 1.8 %collective-permute-done.17 = bf16[64,512]{1,0:T(8,128)(2,1)S(1)} collective-permute-done((bf16[64,512]{1,0:T(8,128)(2,1)S(1)}, bf16[64,512]{1,0:T(8,128)(2,1)S(1)}, u32[]{:S(2)}, u32[]{:S(2)}) %collective-permute-start.17) | collective-permute-done | bytes 65568 | tf_op jit(solution)/shard_map/ppermute | solution.py:299
  139.8 2.8 %collective-permute-done.18 = bf16[64,512]{1,0:T(8,128)(2,1)S(1)} collective-permute-done((bf16[64,512]{1,0:T(8,128)(2,1)S(1)}, bf16[64,512]{1,0:T(8,128)(2,1)S(1)}, u32[]{:S(2)}, u32[]{:S(2)}) %collective-permute-start.18) | collective-permute-done | bytes 65568 | tf_op jit(solution)/shard_map/ppermute | solution.py:299
  (97 shorter events, 23.2 us)
Async XLA Ops:
  0.6 14.3 %copy-start = (bf16[2048,768]{1,0:T(8,128)(2,1)S(1)}, bf16[2048,768]{1,0:T(8,128)(2,1)}, u32[]{:S(2)}) copy-start(bf16[2048,768]{1,0:T(8,128)(2,1)} %refs_3_.1) | copy-start | bytes 9437188
  0.6 14.3 %copy-start.14 = (f32[2048]{0:T(1024)S(1)}, f32[2048]{0:T(1024)}, u32[]{:S(2)}) copy-start(f32[2048]{0:T(1024)} %param.17) | copy-start | bytes 24580
  4.3 27.2 %collective-permute-start.6 = (bf16[768,512]{1,0:T(8,128)(2,1)}, bf16[768,512]{1,0:T(8,128)(2,1)}, u32[]{:S(2)}, u32[]{:S(2)}) collective-permute-start(bf16[768,512]{1,0:T(8,128)(2,1)} %constant_dynamic-update-slice_fusion.2), channel_id=1, source_target_pairs={{0,1},{1,0},{2,3},{3,2},{4,5},{5,4},{6,7},{7,6},{8,9},{9,8},{10,11... | collective-permute-start | bytes 2359304 | tf_op jit(solution)/shard_map/ppermute | solution.py:299
  7.3 41.8 %collective-permute-start.4 = (bf16[768,512]{1,0:T(8,128)(2,1)}, bf16[768,512]{1,0:T(8,128)(2,1)}, u32[]{:S(2)}, u32[]{:S(2)}) collective-permute-start(bf16[768,512]{1,0:T(8,128)(2,1)} %constant_dynamic-update-slice_fusion.2), channel_id=1, source_target_pairs={{0,2},{1,3},{2,4},{3,5},{4,6},{5,7},{6,8},{7,9},{8,10},{9,11},{10,... | collective-permute-start | bytes 2359304 | tf_op jit(solution)/shard_map/ppermute | solution.py:295
  9.6 39.5 %collective-permute-start.5 = (bf16[768,512]{1,0:T(8,128)(2,1)}, bf16[768,512]{1,0:T(8,128)(2,1)}, u32[]{:S(2)}, u32[]{:S(2)}) collective-permute-start(bf16[768,512]{1,0:T(8,128)(2,1)} %constant_dynamic-update-slice_fusion.2), channel_id=1, source_target_pairs={{2,0},{3,1},{4,2},{5,3},{6,4},{7,5},{8,6},{9,7},{10,8},{11,9},{12,... | collective-permute-start | bytes 2359304 | tf_op jit(solution)/shard_map/ppermute | solution.py:295
  12.4 12.7 %collective-permute-start = (s32[3,9]{1,0:T(4,128)S(1)}, s32[3,9]{1,0:T(4,128)S(1)}, u32[]{:S(2)}, u32[]{:S(2)}) collective-permute-start(s32[3,9]{1,0:T(4,128)S(1)} %pad_add_fusion), channel_id=1, source_target_pairs={{0,1},{1,0},{2,3},{3,2},{4,5},{5,4},{6,7},{7,6},{8,9},{9,8},{10,11... | collective-permute-start | bytes 332 | tf_op jit(solution)/shard_map/ppermute | solution.py:299
  14.9 6.7 %copy-start.12 = (s32[2]{0:T(128)S(1)}, s32[2]{0:T(128)}, u32[]{:S(2)}) copy-start(s32[2]{0:T(128)} %constant.13.clone) | copy-start | bytes 28
  15.0 6.7 %copy-start.13 = (s32[2]{0:T(128)S(1)}, s32[2]{0:T(128)}, u32[]{:S(2)}) copy-start(s32[2]{0:T(128)} %constant.14.clone) | copy-start | bytes 28
  15.0 10.2 %copy-start.10 = (s32[3,4]{1,0:T(4,128)S(1)}, s32[3,4]{1,0:T(4,128)}, u32[]{:S(2)}) copy-start(s32[3,4]{1,0:T(4,128)} %param.20) | copy-start | bytes 148
  15.0 10.2 %copy-start.11 = (s32[3,4]{1,0:T(4,128)S(1)}, s32[3,4]{1,0:T(4,128)}, u32[]{:S(2)}) copy-start(s32[3,4]{1,0:T(4,128)} %param.19) | copy-start | bytes 148
  25.2 5.0 %collective-permute-start.1 = (s32[6,9]{1,0:T(8,128)S(1)}, s32[6,9]{1,0:T(8,128)S(1)}, u32[]{:S(2)}, u32[]{:S(2)}) collective-permute-start(s32[6,9]{1,0:T(8,128)S(1)} %add_select_fusion.1), channel_id=1, source_target_pairs={{0,4},{2,6},{4,8},{6,10},{8,12},{10,14},{12,16},{14,18},{16,20},{1... | collective-permute-start | bytes 656 | tf_op jit(solution)/shard_map/ppermute | solution.py:348
  28.9 8.3 %collective-permute-start.2 = (s32[6,9]{1,0:T(8,128)S(1)}, s32[6,9]{1,0:T(8,128)S(1)}, u32[]{:S(2)}, u32[]{:S(2)}) collective-permute-start(s32[6,9]{1,0:T(8,128)S(1)} %add_select_fusion.1), channel_id=1, source_target_pairs={{0,2},{1,3},{2,4},{3,5},{4,6},{5,7},{6,8},{7,9},{8,10},{9,11},{10,... | collective-permute-start | bytes 656 | tf_op jit(solution)/shard_map/ppermute | solution.py:295
  30.2 7.0 %collective-permute-start.3 = (s32[6,9]{1,0:T(8,128)S(1)}, s32[6,9]{1,0:T(8,128)S(1)}, u32[]{:S(2)}, u32[]{:S(2)}) collective-permute-start(s32[6,9]{1,0:T(8,128)S(1)} %add_select_fusion.1), channel_id=1, source_target_pairs={{2,0},{3,1},{4,2},{5,3},{6,4},{7,5},{8,6},{9,7},{10,8},{11,9},{12,... | collective-permute-start | bytes 656 | tf_op jit(solution)/shard_map/ppermute | solution.py:295
  31.5 17.6 %collective-permute-start.7 = (bf16[768,512]{1,0:T(8,128)(2,1)}, bf16[768,512]{1,0:T(8,128)(2,1)}, u32[]{:S(2)}, u32[]{:S(2)}) collective-permute-start(bf16[768,512]{1,0:T(8,128)(2,1)} %collective-permute-done.6.r_6_), channel_id=1, source_target_pairs={{0,2},{2,4},{4,6},{6,8},{8,10},{10,12},{12,14},{14,16},{16,18},{18... | collective-permute-start | bytes 2359304 | tf_op jit(solution)/shard_map/ppermute | solution.py:341
  49.1 16.4 %copy-start.1 = (bf16[2048,768]{1,0:T(8,128)(2,1)S(1)}, bf16[2048,768]{1,0:T(8,128)(2,1)}, u32[]{:S(2)}) copy-start(bf16[2048,768]{1,0:T(8,128)(2,1)} %get-tuple-element.24.refs_0_.refs_1_.refs_2_.refs_3_) | copy-start | bytes 9437188
  70.4 12.5 %collective-permute-start.19 = (bf16[2,2,2,2,64,512]{5,4,3,2,1,0:T(8,128)(2,1)S(1)}, bf16[2,2,2,2,64,512]{5,4,3,2,1,0:T(8,128)(2,1)S(1)}, u32[]{:S(2)}, u32[]{:S(2)}) collective-permute-start(bf16[2,2,2,2,64,512]{5,4,3,2,1,0:T(8,128)(2,1)S(1)} %bitcast.114), channel_id=1, source_target_pairs={{0,2},{1,3},{2,0},{3,1},{4,6},{5,7},{6,4},{7,5},{8,10},{9,11},{10,... | collective-permute-start | bytes 3145736 | tf_op jit(solution)/shard_map/ppermute | solution.py:299
  82.0 28.4 %collective-permute-start.8 = (bf16[2,2,2,2,64,896]{5,4,3,2,1,0:T(8,128)(2,1)S(1)}, bf16[2,2,2,2,64,896]{5,4,3,2,1,0:T(8,128)(2,1)S(1)}, u32[]{:S(2)}, u32[]{:S(2)}) collective-permute-start(bf16[2,2,2,2,64,896]{5,4,3,2,1,0:T(8,128)(2,1)S(1)} %bitcast.109), channel_id=1, source_target_pairs={{0,2},{1,3},{2,0},{3,1},{4,6},{5,7},{6,4},{7,5},{8,10},{9,11},{10,... | collective-permute-start | bytes 5505032 | tf_op jit(solution)/shard_map/ppermute | solution.py:299
  83.3 14.6 %collective-permute-start.20 = (bf16[2,2,2,64,512]{4,3,2,1,0:T(8,128)(2,1)S(1)}, bf16[2,2,2,64,512]{4,3,2,1,0:T(8,128)(2,1)S(1)}, u32[]{:S(2)}, u32[]{:S(2)}) collective-permute-start(bf16[2,2,2,64,512]{4,3,2,1,0:T(8,128)(2,1)S(1)} %slice_bitcast_fusion), channel_id=1, source_target_pairs={{0,4},{1,5},{2,6},{3,7},{4,0},{5,1},{6,2},{7,3},{8,12},{9,13},{10,... | collective-permute-start | bytes 1572872 | tf_op jit(solution)/shard_map/ppermute | solution.py:299
  98.1 7.8 %collective-permute-start.21 = (bf16[2,2,64,512]{3,2,1,0:T(8,128)(2,1)S(1)}, bf16[2,2,64,512]{3,2,1,0:T(8,128)(2,1)S(1)}, u32[]{:S(2)}, u32[]{:S(2)}) collective-permute-start(bf16[2,2,64,512]{3,2,1,0:T(8,128)(2,1)S(1)} %slice_bitcast_fusion.6), channel_id=1, source_target_pairs={{0,1},{1,0},{2,3},{3,2},{4,5},{5,4},{6,7},{7,6},{8,9},{9,8},{10,11... | collective-permute-start | bytes 786440 | tf_op jit(solution)/shard_map/ppermute | solution.py:299
  105.9 7.5 %collective-permute-start.22 = (bf16[64,512]{1,0:T(8,128)(2,1)S(1)}, bf16[64,512]{1,0:T(8,128)(2,1)S(1)}, u32[]{:S(2)}, u32[]{:S(2)}) collective-permute-start(bf16[64,512]{1,0:T(8,128)(2,1)S(1)} %get-tuple-element.33), channel_id=1, source_target_pairs={{0,8},{1,9},{2,10},{3,11},{4,12},{5,13},{6,14},{7,15},{8,0},{9,1},... | collective-permute-start | bytes 196616 | tf_op jit(solution)/shard_map/ppermute | solution.py:299
  107.6 6.6 %collective-permute-start.23 = (bf16[64,512]{1,0:T(8,128)(2,1)S(1)}, bf16[64,512]{1,0:T(8,128)(2,1)S(1)}, u32[]{:S(2)}, u32[]{:S(2)}) collective-permute-start(bf16[64,512]{1,0:T(8,128)(2,1)S(1)} %get-tuple-element.35), channel_id=1, source_target_pairs={{0,16},{1,17},{2,18},{3,19},{4,20},{5,21},{6,22},{7,23},{8,24},{9,... | collective-permute-start | bytes 196616 | tf_op jit(solution)/shard_map/ppermute | solution.py:299
  110.1 6.1 %collective-permute-start.24 = (bf16[64,512]{1,0:T(8,128)(2,1)S(1)}, bf16[64,512]{1,0:T(8,128)(2,1)S(1)}, u32[]{:S(2)}, u32[]{:S(2)}) collective-permute-start(bf16[64,512]{1,0:T(8,128)(2,1)S(1)} %get-tuple-element.34), channel_id=1, source_target_pairs={{0,24},{1,25},{2,26},{3,27},{4,28},{5,29},{6,30},{7,31},{8,16},{9,... | collective-permute-start | bytes 196616 | tf_op jit(solution)/shard_map/ppermute | solution.py:299
  111.0 9.1 %collective-permute-start.9 = (bf16[2,2,2,64,384]{4,3,2,1,0:T(8,128)(2,1)S(1)}, bf16[2,2,2,64,384]{4,3,2,1,0:T(8,128)(2,1)S(1)}, u32[]{:S(2)}, u32[]{:S(2)}) collective-permute-start(bf16[2,2,2,64,384]{4,3,2,1,0:T(8,128)(2,1)S(1)} %slice_bitcast_fusion.4), channel_id=1, source_target_pairs={{0,4},{1,5},{2,6},{3,7},{4,0},{5,1},{6,2},{7,3},{8,12},{9,13},{10,... | collective-permute-start | bytes 1179656 | tf_op jit(solution)/shard_map/ppermute | solution.py:299
  112.6 13.2 %collective-permute-start.14 = (bf16[2,2,2,64,512]{4,3,2,1,0:T(8,128)(2,1)S(1)}, bf16[2,2,2,64,512]{4,3,2,1,0:T(8,128)(2,1)S(1)}, u32[]{:S(2)}, u32[]{:S(2)}) collective-permute-start(bf16[2,2,2,64,512]{4,3,2,1,0:T(8,128)(2,1)S(1)} %slice_bitcast_fusion.2), channel_id=1, source_target_pairs={{0,1},{1,0},{2,3},{3,2},{4,5},{5,4},{6,7},{7,6},{8,9},{9,8},{10,11... | collective-permute-start | bytes 1572872 | tf_op jit(solution)/shard_map/ppermute | solution.py:299
  120.3 7.6 %collective-permute-start.10 = (bf16[2,2,64,384]{3,2,1,0:T(8,128)(2,1)S(1)}, bf16[2,2,64,384]{3,2,1,0:T(8,128)(2,1)S(1)}, u32[]{:S(2)}, u32[]{:S(2)}) collective-permute-start(bf16[2,2,64,384]{3,2,1,0:T(8,128)(2,1)S(1)} %slice_bitcast_fusion.10), channel_id=1, source_target_pairs={{0,1},{1,0},{2,3},{3,2},{4,5},{5,4},{6,7},{7,6},{8,9},{9,8},{10,11... | collective-permute-start | bytes 589832 | tf_op jit(solution)/shard_map/ppermute | solution.py:299
  125.9 6.5 %collective-permute-start.15 = (bf16[2,2,64,512]{3,2,1,0:T(8,128)(2,1)S(1)}, bf16[2,2,64,512]{3,2,1,0:T(8,128)(2,1)S(1)}, u32[]{:S(2)}, u32[]{:S(2)}) collective-permute-start(bf16[2,2,64,512]{3,2,1,0:T(8,128)(2,1)S(1)} %slice_bitcast_fusion.8), channel_id=1, source_target_pairs={{0,4},{1,5},{2,6},{3,7},{4,0},{5,1},{6,2},{7,3},{8,12},{9,13},{10,... | collective-permute-start | bytes 786440 | tf_op jit(solution)/shard_map/ppermute | solution.py:299
  127.9 8.6 %collective-permute-start.11 = (bf16[64,384]{1,0:T(8,128)(2,1)S(1)}, bf16[64,384]{1,0:T(8,128)(2,1)S(1)}, u32[]{:S(2)}, u32[]{:S(2)}) collective-permute-start(bf16[64,384]{1,0:T(8,128)(2,1)S(1)} %get-tuple-element.39), channel_id=1, source_target_pairs={{0,8},{1,9},{2,10},{3,11},{4,12},{5,13},{6,14},{7,15},{8,0},{9,1},... | collective-permute-start | bytes 147464 | tf_op jit(solution)/shard_map/ppermute | solution.py:299
  128.7 8.4 %collective-permute-start.12 = (bf16[64,384]{1,0:T(8,128)(2,1)S(1)}, bf16[64,384]{1,0:T(8,128)(2,1)S(1)}, u32[]{:S(2)}, u32[]{:S(2)}) collective-permute-start(bf16[64,384]{1,0:T(8,128)(2,1)S(1)} %get-tuple-element.41), channel_id=1, source_target_pairs={{0,16},{1,17},{2,18},{3,19},{4,20},{5,21},{6,22},{7,23},{8,24},{9,... | collective-permute-start | bytes 147464 | tf_op jit(solution)/shard_map/ppermute | solution.py:299
  132.0 6.0 %collective-permute-start.13 = (bf16[64,384]{1,0:T(8,128)(2,1)S(1)}, bf16[64,384]{1,0:T(8,128)(2,1)S(1)}, u32[]{:S(2)}, u32[]{:S(2)}) collective-permute-start(bf16[64,384]{1,0:T(8,128)(2,1)S(1)} %get-tuple-element.40), channel_id=1, source_target_pairs={{0,24},{1,25},{2,26},{3,27},{4,28},{5,29},{6,30},{7,31},{8,16},{9,... | collective-permute-start | bytes 147464 | tf_op jit(solution)/shard_map/ppermute | solution.py:299
  132.5 5.6 %collective-permute-start.16 = (bf16[64,512]{1,0:T(8,128)(2,1)S(1)}, bf16[64,512]{1,0:T(8,128)(2,1)S(1)}, u32[]{:S(2)}, u32[]{:S(2)}) collective-permute-start(bf16[64,512]{1,0:T(8,128)(2,1)S(1)} %get-tuple-element.36), channel_id=1, source_target_pairs={{0,8},{1,9},{2,10},{3,11},{4,12},{5,13},{6,14},{7,15},{8,0},{9,1},... | collective-permute-start | bytes 196616 | tf_op jit(solution)/shard_map/ppermute | solution.py:299
  133.2 6.6 %collective-permute-start.17 = (bf16[64,512]{1,0:T(8,128)(2,1)S(1)}, bf16[64,512]{1,0:T(8,128)(2,1)S(1)}, u32[]{:S(2)}, u32[]{:S(2)}) collective-permute-start(bf16[64,512]{1,0:T(8,128)(2,1)S(1)} %get-tuple-element.38), channel_id=1, source_target_pairs={{0,16},{1,17},{2,18},{3,19},{4,20},{5,21},{6,22},{7,23},{8,24},{9,... | collective-permute-start | bytes 196616 | tf_op jit(solution)/shard_map/ppermute | solution.py:299
  136.5 6.1 %collective-permute-start.18 = (bf16[64,512]{1,0:T(8,128)(2,1)S(1)}, bf16[64,512]{1,0:T(8,128)(2,1)S(1)}, u32[]{:S(2)}, u32[]{:S(2)}) collective-permute-start(bf16[64,512]{1,0:T(8,128)(2,1)S(1)} %get-tuple-element.37), channel_id=1, source_target_pairs={{0,24},{1,25},{2,26},{3,27},{4,28},{5,29},{6,30},{7,31},{8,16},{9,... | collective-permute-start | bytes 196616 | tf_op jit(solution)/shard_map/ppermute | solution.py:299
  (8 other events, 15.9 us)

commit v3 on v2

--- a/solution.py
+++ b/solution.py
@@ -9,6 +9,7 @@
 
 TILE = 128
 ALPHA = 0.1
+SHORT = pl.CostEstimate(flops=1, transcendentals=0, bytes_accessed=1)
 AXES = ("img", "cap")
 F32 = jnp.float32
 BF16 = jnp.bfloat16
@@ -90,7 +91,8 @@
         in_specs=[smem] * 3,
         out_specs=(vmem,) * 4,
         scratch_shapes=[pltpu.VMEM((9 * tiles, 1, TILE), F32)],
-        compiler_params=pltpu.CompilerParams(vmem_limit_bytes=40 << 20),
+        compiler_params=pltpu.CompilerParams(vmem_limit_bytes=28 << 20),
+        cost_estimate=SHORT,
         name="tiles",
     )(seeds, places, counts)
 
@@ -148,7 +150,7 @@
         push(q, img0[q], acc, tiles, near)
         return c
 
-    lax.fori_loop(0, mid, push1, 0)
+    lax.fori_loop(0, mid, push1, 0, unroll=3)
 
     def pull1(q, c):
         n = wide(nimg_ref, q)
@@ -157,7 +159,7 @@
         keep_img[q - tiles] = flow
         return c
 
-    lax.fori_loop(tiles, tiles + near, pull1, 0)
+    lax.fori_loop(tiles, tiles + near, pull1, 0, unroll=3)
 
     def finish1(m, c):
         n = wide(ncap_ref, m + tiles)
@@ -166,13 +168,13 @@
         keep_cap[m] = flow
         return c
 
-    lax.fori_loop(0, near, finish1, 0)
+    lax.fori_loop(0, near, finish1, 0, unroll=3)
 
     def push2(q, c):
         push(q, img1[q - tiles], acc2, 2 * tiles, tiles)
         return c
 
-    lax.fori_loop(tiles, tiles + near, push2, 0)
+    lax.fori_loop(tiles, tiles + near, push2, 0, unroll=3)
     for t in range(tiles):
         q = 2 * tiles + t
         rows = pl.ds(t * TILE, TILE)
@@ -188,7 +190,7 @@
     width = own_img.shape[1]
     smem = pl.BlockSpec(memory_space=pltpu.SMEM)
     vmem = pl.BlockSpec(memory_space=pltpu.VMEM)
-    hbm = pl.BlockSpec(memory_space=pl.ANY)
+    hbm = pl.BlockSpec(memory_space=pltpu.HBM)
     mid, near = 5 * tiles, 3 * tiles
     return pl.pallas_call(
         lambda *r: hops_kernel(*r, tiles=tiles, slots=slots, width=width),
@@ -207,7 +209,8 @@
             pltpu.VMEM((near, TILE, width), F32),
             pltpu.SemaphoreType.DMA((4,)),
         ],
-        compiler_params=pltpu.CompilerParams(vmem_limit_bytes=56 << 20),
+        compiler_params=pltpu.CompilerParams(vmem_limit_bytes=32 << 20),
+        cost_estimate=SHORT,
         name="hops",
     )(places, bases, own_img, own_cap, low, high, mate, far, *pats)
 
@@ -251,18 +254,20 @@
 
 def feat_kernel(order_ref, *refs):
     w_in = refs[:GROUP]
-    grad_ref, img_ref, cap_ref, acc_ref = refs[GROUP:]
+    kept_ref, sent_ref, img_ref, cap_ref, acc_ref = refs[GROUP:]
     i = pl.program_id(0)
+    steps = pl.num_programs(0)
 
     @pl.when(i == 0)
     def _():
         acc_ref[...] = jnp.zeros_like(acc_ref)
 
+    grad = jnp.where(i < steps // 2, kept_ref[...], sent_ref[...])
     acc_ref[...] += lax.dot_general(
-        grad_ref[...], stacked(w_in), (((0,), (0,)), ((), ())), preferred_element_type=F32
+        grad, stacked(w_in), (((0,), (0,)), ((), ())), preferred_element_type=F32
     )
 
-    @pl.when(i == pl.num_programs(0) - 1)
+    @pl.when(i == steps - 1)
     def _():
         half = img_ref.shape[0]
         img_ref[...] = acc_ref[:half].astype(BF16)
@@ -281,16 +286,53 @@
             scratch_shapes=scratch,
         ),
         compiler_params=pltpu.CompilerParams(
-            dimension_semantics=("arbitrary",), vmem_limit_bytes=40 << 20
+            dimension_semantics=("arbitrary",), vmem_limit_bytes=28 << 20
         ),
+        cost_estimate=SHORT,
         name=name,
     )(order, *args)
 
 
+def rows_of_half(width, half, side):
+    steps = half // GROUP
+    if side:
+        return pl.BlockSpec((GROUP * BLOCK, width), lambda i, order: (jnp.maximum(i - steps, 0), 0))
+    return pl.BlockSpec((GROUP * BLOCK, width), lambda i, order: (jnp.minimum(i, steps - 1), 0))
+
+
 def rows_of(width):
     return pl.BlockSpec((GROUP * BLOCK, width), lambda i, order: (i, 0))
 
 
+def stack_kernel(top_ref, bottom_ref, out_ref, sems):
+    half = top_ref.shape[0]
+    copies = [
+        pltpu.make_async_copy(src, out_ref.at[pl.ds(k * half, half)], sems.at[k])
+        for k, src in enumerate((top_ref, bottom_ref))
+    ]
+    for copy in copies:
+        copy.start()
+    for copy in copies:
+        copy.wait()
+
+
+def stack(top, bottom):
+    hbm = pl.BlockSpec(memory_space=pltpu.HBM)
+    return pl.pallas_call(
+        stack_kernel,
+        out_shape=jax.ShapeDtypeStruct((2 * top.shape[0], top.shape[1]), top.dtype),
+        in_specs=[hbm] * 2,
+        out_specs=hbm,
+        scratch_shapes=[pltpu.SemaphoreType.DMA((2,))],
+        cost_estimate=SHORT,
+        name="stack",
+    )(top, bottom)
+
+
+def after(value, *done):
+    return lax.optimization_barrier((value,) + done)[0]
+
+
 def moved(array, count, by):
     return lax.ppermute(array, AXES, [(i, i + by) for i in range(count) if 0 <= i + by < count])
 
@@ -299,28 +341,49 @@
     return lax.ppermute(array, AXES, [(i, i ^ mask) for i in range(count)])
 
 
-def halve(array, axis, count, mask):
-    kept = lax.index_in_dim(array, 0, axis, keepdims=False)
-    sent = lax.index_in_dim(array, 1, axis, keepdims=False)
-    return (kept.astype(F32) + flipped(sent, count, mask).astype(F32)).astype(BF16)
+def added(kept, came):
+    return (kept.astype(F32) + came.astype(F32)).astype(BF16)
+
+
+def parts(array, axis):
+    return lax.index_in_dim(array, 0, axis, keepdims=False), lax.index_in_dim(array, 1, axis, keepdims=False)
+
+
+def meet(values, owners):
+    for owner, value in zip(owners, lax.optimization_barrier(tuple(values))):
+        owner.part = value
 
 
 def nearest_pair(count, by):
     return [(i, i + by) for i in range(0, count - by, 2)] + [(i, i - by) for i in range(by + 1, count, 2)]
 
 
-def scattered(part, count, bits, order):
-    rows, lanes = part.shape[-2:]
-    left = list(bits)
-    for bit in order:
-        part = halve(part, left.index(bit), count, 1 << bit)
-        left.remove(bit)
-    part = part.reshape((4, rows, lanes))
-    got = [flipped(part[k], count, ((k >> 1) << left[0]) | ((k & 1) << left[1])) for k in range(1, 4)]
-    total = part[0].astype(F32)
-    for piece in got:
-        total = total + piece.astype(F32)
-    return total
+class Reduction:
+
+    def __init__(self, part, count, bits, order):
+        self.part, self.count, self.left, self.order = part, count, list(bits), list(order)
+
+    def start(self):
+        bit = self.order.pop(0)
+        self.kept, sent = parts(self.part, self.left.index(bit))
+        self.left.remove(bit)
+        self.came = flipped(sent, self.count, 1 << bit)
+
+    def finish(self):
+        self.part = added(self.kept, self.came)
+        return self.part
+
+    def start_last(self):
+        part = self.part.reshape((4,) + self.part.shape[-2:])
+        hi, lo = self.left
+        self.own = part[0]
+        self.got = [flipped(part[k], self.count, ((k >> 1) << hi) | ((k & 1) << lo)) for k in range(1, 4)]
+
+    def result(self):
+        total = self.own.astype(F32)
+        for piece in self.got:
+            total = total + piece.astype(F32)
+        return total
 
 
 def per_device(
@@ -334,14 +397,14 @@
     count = n_img * n_cap
     me = lax.axis_index(AXES)
 
-    block = jnp.concatenate([cot_img, cot_cap], axis=0)
+    even = (me & 1) == 0
+    meta = jnp.concatenate([tile_seed, tile_cols, tile_count[:, None]], axis=1)
+    other = flipped(meta, count, 1)
+    block = stack(cot_img, cot_cap)
     mate = flipped(block, count, 1)
     low = moved(block, count, 2)
     high = moved(block, count, -2)
     far = lax.ppermute(mate, AXES, nearest_pair(count, 2))
-    even = (me & 1) == 0
-    meta = jnp.concatenate([tile_seed, tile_cols, tile_count[:, None]], axis=1)
-    other = flipped(meta, count, 1)
     pair = jnp.where(even, jnp.concatenate([meta, other]), jnp.concatenate([other, meta]))
     pair_low = moved(pair, count, 2)
     pair_high = moved(pair, count, -2)
@@ -388,32 +451,57 @@
 
     width = cot_img.shape[1]
     nodes = 2 * local_rows
-    part_out = over_hidden(
-        out_kernel, "part_out", order, grouped(nodes) + [whole(logit.shape)], rows_of(width),
-        jax.ShapeDtypeStruct((hid, width), BF16), [], [hidden_act] * GROUP + [logit],
+    half = order.shape[0] // 2
+    blocked = (2,) * (m - 1) + (rows,)
+
+    def out_half(order, logit):
+        return over_hidden(
+            out_kernel, "part_out", order, grouped(nodes) + [whole(logit.shape)], rows_of(width),
+            jax.ShapeDtypeStruct((hid // 2, width), BF16), [], [hidden_act] * GROUP + [logit],
+        ).reshape(blocked + (width,))
+
+    def in_half(order, logit):
+        part, grad = over_hidden(
+            in_kernel, "part_in", order,
+            grouped(nodes) + grouped(width) + [whole(logit.shape), whole(feats.shape)],
+            (rows_of(f_in + TILE), rows_of(nodes)),
+            (jax.ShapeDtypeStruct((hid // 2, f_in + TILE), BF16), jax.ShapeDtypeStruct((hid // 2, nodes), BF16)),
+            [], [gelu_slope] * GROUP + [w_out] * GROUP + [logit, feats],
+        )
+        return part.reshape(blocked + (f_in + TILE,)), grad
+
+    core = 1 << a
+    rest = bits[1:]
+    out_sent = out_half(order[half:], logit)
+    out_came = flipped(out_sent, count, core)
+    out_kept = out_half(order[:half], after(logit, out_sent))
+    r_out = Reduction(added(out_kept, out_came), count, rest, img_bits + cap_bits)
+    r_out.start()
+    in_sent, grad_sent = in_half(order[half:], after(logit, r_out.part))
+    in_came = flipped(in_sent, count, core)
+    in_kept, grad_kept = in_half(order[:half], after(logit, grad_sent))
+    g_in = added(in_kept, in_came)
+    cut = f_in // 3
+    r_a = Reduction(g_in[..., :cut], count, rest, img_bits + cap_bits)
+    r_b = Reduction(g_in[..., cut:], count, rest, cap_bits + img_bits)
+    r_a.start()
+    r_b.start()
+    grad_kept = after(grad_kept, g_in)
+    grad_img, grad_cap = over_hidden(
+        feat_kernel, "feat_grad", order, grouped(f_in) + [rows_of_half(nodes, half, 0), rows_of_half(nodes, half, 1)],
+        (whole((local_rows, f_in)),) * 2, (jax.ShapeDtypeStruct((local_rows, f_in), BF16),) * 2,
+        [pltpu.VMEM((nodes, f_in), F32)], [w_in] * GROUP + [grad_kept, grad_sent],
     )
-    part_in, preact_grad = over_hidden(
-        in_kernel, "part_in", order,
-        grouped(nodes) + grouped(width) + [whole(logit.shape), whole(feats.shape)],
-        (rows_of(f_in + TILE), rows_of(nodes)),
-        (jax.ShapeDtypeStruct((hid, f_in + TILE), BF16), jax.ShapeDtypeStruct((hid, nodes), BF16)),
-        [], [gelu_slope] * GROUP + [w_out] * GROUP + [logit, feats],
-    )
-    grad_img, grad_cap = over_hidden(
-        feat_kernel, "feat_grad", order, grouped(f_in) + [rows_of(nodes)],
-        (whole((local_rows, f_in)),) * 2, (jax.ShapeDtypeStruct((local_rows, f_in), BF16),) * 2,
-        [pltpu.VMEM((nodes, f_in), F32)], [w_in] * GROUP + [preact_grad],
-    )
-
+    chunks = (r_out, r_a, r_b)
+    for _ in range(m - 4):
+        meet([r.finish() for r in chunks], chunks)
+        for r in chunks:
+            r.start()
+    meet([r.finish() for r in chunks], chunks)
+    for r in chunks:
+        r.start_last()
     grad_scale = 1.0 / math.sqrt(nodes * count)
-    blocked = (2,) * m + (rows,)
-    rest = bits[1:]
-    g_out = halve(part_out.reshape(blocked + (width,)), 0, count, 1 << a)
-    g_in = halve(part_in.reshape(blocked + (f_in + TILE,)), 0, count, 1 << a)
-    cut = f_in // 2
-    g_out = scattered(g_out, count, rest, img_bits + cap_bits) * grad_scale
-    g_a = scattered(g_in[..., :cut], count, rest, img_bits + cap_bits) * grad_scale
-    g_b = scattered(g_in[..., cut:], count, rest, cap_bits + img_bits) * grad_scale
+    g_out, g_b, g_a = [r.result() * grad_scale for r in (r_out, r_b, r_a)]
     g_in = jnp.concatenate([g_a, g_b[:, : f_in - cut]], axis=1)
     return (grad_img, grad_cap, g_in, g_out, g_b[:, f_in - cut])
 

time: 145 us -> 163 us (1.12)
  Pallas kernels: 41.6 us -> 61 us
  waiting for transfers between devices: 32.9 us -> 22.4 us
  local copies, waits for them, and re-layouts: 15.5 us -> 21.5 us
  other arithmetic: 4.57 us -> 8.49 us
  starting transfers between devices: 41.8 us -> 40 us
    pallas_call x0 -> x1, Pallas kernels: none -> 24.9 us  [stack(): pl.pallas_call(stack_kernel, out_shape=jax.ShapeDtypeStruct((2 * top.shap...]
    ppermute x19, waiting for transfers between devices: 32.8 us -> 22.4 us  [flipped(): return lax.ppermute(array, AXES, [(i, i ^ mask) for i in range(count)])]
    pallas_call x1, Pallas kernels: 16.4 us -> 9.63 us  [propagate(): pl.pallas_call(lambda *r: hops_kernel(*r, tiles=tiles, slots=slots, width...]
    unnamed x32 -> x37, local copies, waits for them, and re-layouts: 9.58 us -> 15.2 us
    ppermute x19, starting transfers between devices: 26.2 us -> 22.2 us  [flipped(): return lax.ppermute(array, AXES, [(i, i ^ mask) for i in range(count)])]
    ppermute x4, starting transfers between devices: 6.2 us -> 10.1 us  [moved(): lax.ppermute(array, AXES, [(i, i + by) for i in range(count) if 0 <= i +...]
    concatenate x1 -> x0, local copies, waits for them, and re-layouts: 1.76 us -> none  [per_device(): block = jnp.concatenate([cot_img, cot_cap], axis=0)]
    pallas_call x3 -> x5, Pallas kernels: 19.2 us -> 20.4 us  [over_hidden(): pl.pallas_call(kernel, out_shape=out_shape, grid_spec=pltpu.PrefetchScala...]
  transfers between devices with their start and end apart: 25 -> 25, of which waited for: 12 -> 9; matrix products, arithmetic and copies ran while one was open for 10% -> 14% of each run, Pallas kernels for 15% -> 12%
where the time goes in v3:
time: 163 us; the launch traced here: 162 us
  Pallas kernels  61 us (37%)
  starting transfers between devices  40 us (25%)
  waiting for transfers between devices  22.4 us (14%)
  local copies, waits for them, and re-layouts  21.5 us (13%)
  other arithmetic  8.49 us (5%)
  matrix products  7.8 us (5%)
    pallas_call x1, Pallas kernels, stack(): pl.pallas_call(stack_kernel, out_shape=jax.ShapeDtypeStruct((2 * top.shap...  24.9 us
    ppermute x19, waiting for transfers between devices, flipped(): return lax.ppermute(array, AXES, [(i, i ^ mask) for i in range(count)])  22.4 us
    ppermute x19, starting transfers between devices, flipped(): return lax.ppermute(array, AXES, [(i, i ^ mask) for i in range(count)])  22.2 us
    pallas_call x5, Pallas kernels, over_hidden(): pl.pallas_call(kernel, out_shape=out_shape, grid_spec=pltpu.PrefetchScala...  20.4 us
    unnamed x37, local copies, waits for them, and re-layouts  15.2 us
    ppermute x4, starting transfers between devices, moved(): lax.ppermute(array, AXES, [(i, i + by) for i in range(count) if 0 <= i +...  10.1 us
    pallas_call x1, Pallas kernels, propagate(): pl.pallas_call(lambda *r: hops_kernel(*r, tiles=tiles, slots=slots, width...  9.63 us
    dot_general x1, matrix products, per_device(): lax.dot_general(w_in, feats, across, preferred_element_type=F32)  7.8 us
  transfers between devices with their start and end apart: 25, of which 9 were waited for; matrix products, arithmetic and copies ran while one was open for 14% of the time, Pallas kernels for 12%

profile of v3, /device:TPU:0, one launch (start us, length us, event | category | flops | bytes accessed | tf_op | source)
XLA Modules:
  0.0 162.2 jit_solution(5620865318745423001)
XLA Ops:
  0.6 24.9 %stack.1 = bf16[768,512]{1,0:T(8,128)(2,1)} custom-call(bf16[384,512]{1,0:T(8,128)(2,1)} %r_2_.1, bf16[384,512]{1,0:T(8,128)(2,1)} %r_3_.1), custom_call_target="tpu_custom_call" | custom-call | flops 1 | bytes 1 | tf_op jit(solution)/shard_map/stack/pallas_call | solution.py:321
  25.6 3.0 %collective-permute-start.6 = (bf16[768,512]{1,0:T(8,128)(2,1)}, bf16[768,512]{1,0:T(8,128)(2,1)}, u32[]{:S(2)}, u32[]{:S(2)}) collective-permute-start(bf16[768,512]{1,0:T(8,128)(2,1)} %stack.1), channel_id=1, source_target_pairs={{0,1},{1,0},{2,3},{3,2},{4,5},{5,4},{6,7},{7,6},{8,9},{9,8},{10,11... | collective-permute-start | bytes 2359304 | tf_op jit(solution)/shard_map/ppermute | solution.py:341
  29.9 3.9 %collective-permute-start.4 = (bf16[768,512]{1,0:T(8,128)(2,1)}, bf16[768,512]{1,0:T(8,128)(2,1)}, u32[]{:S(2)}, u32[]{:S(2)}) collective-permute-start(bf16[768,512]{1,0:T(8,128)(2,1)} %stack.1), channel_id=1, source_target_pairs={{0,2},{1,3},{2,4},{3,5},{4,6},{5,7},{6,8},{7,9},{8,10},{9,11},{10,... | collective-permute-start | bytes 2359304 | tf_op jit(solution)/shard_map/ppermute | solution.py:337
  34.5 1.4 pad_add_fusion
  35.9 1.9 %constant_dynamic-update-slice_fusion.1 = bf16[768,768]{1,0:T(8,128)(2,1)} fusion(bf16[384,768]{1,0:T(8,128)(2,1)} %param.12), kind=kLoop, calls=%fused_computation.69 | loop fusion | bytes 1179648
  38.7 7.8 %fusion.3 = (f32[2048,768]{1,0:T(8,128)}, bf16[2048,768]{1,0:T(8,128)(2,1)S(1)}) fusion(f32[2048]{0:T(1024)} %param.17, bf16[768,768]{1,0:T(8,128)(2,1)} %constant_dynamic-update-slice_fusion.refs_9_, bf16[2048,768]{1,0:T(8,128)(2,1)} %refs_3_.1), kind=kOutput, calls=%fused_computation.4 | convolution fusion | flops 2433220608 | bytes 13770752 | tf_op jit(solution)/shard_map/dot_general | solution.py:444
  48.6 3.1 %collective-permute-start.1 = (s32[6,9]{1,0:T(8,128)S(1)}, s32[6,9]{1,0:T(8,128)S(1)}, u32[]{:S(2)}, u32[]{:S(2)}) collective-permute-start(s32[6,9]{1,0:T(8,128)S(1)} %add_select_fusion.1), channel_id=1, source_target_pairs={{0,4},{2,6},{4,8},{6,10},{8,12},{10,14},{12,16},{14,18},{16,20},{1... | collective-permute-start | bytes 656 | tf_op jit(solution)/shard_map/ppermute | solution.py:411
  53.0 3.7 %collective-permute-start.2 = (s32[6,9]{1,0:T(8,128)S(1)}, s32[6,9]{1,0:T(8,128)S(1)}, u32[]{:S(2)}, u32[]{:S(2)}) collective-permute-start(s32[6,9]{1,0:T(8,128)S(1)} %add_select_fusion.1), channel_id=1, source_target_pairs={{0,2},{1,3},{2,4},{3,5},{4,6},{5,7},{6,8},{7,9},{8,10},{9,11},{10,... | collective-permute-start | bytes 656 | tf_op jit(solution)/shard_map/ppermute | solution.py:337
  56.7 4.6 %collective-permute-start.7 = (bf16[768,512]{1,0:T(8,128)(2,1)}, bf16[768,512]{1,0:T(8,128)(2,1)}, u32[]{:S(2)}, u32[]{:S(2)}) collective-permute-start(bf16[768,512]{1,0:T(8,128)(2,1)} %collective-permute-done.6.r_6_), channel_id=1, source_target_pairs={{0,2},{2,4},{4,6},{6,8},{8,10},{10,12},{12,14},{14,16},{16,18},{18... | collective-permute-start | bytes 2359304 | tf_op jit(solution)/shard_map/ppermute | solution.py:407
  65.8 6.0 %tiles.1 = (bf16[15,128,512]{2,1,0:T(8,128)(2,1)S(1)}, bf16[15,512,128]{2,1,0:T(8,128)(2,1)S(1)}, f32[15,128,128]{2,1,0:T(8,128)S(1)}, f32[15,128,128]{2,1,0:T(8,128)S(1)}) custom-call(s32[84]{0:T(128)S(1)} %copy-done.13, s32[84]{0:T(128)S(1)} %reshape.61.r_1_, s32[21]{0:T(128)S(1)} %slice_reduce_fusion.1.r_2_), custom_call_target="tpu_custom_call" | custom-call | flops 1 | bytes 1 | tf_op jit(solution)/shard_map/tiles/pallas_call | solution.py:83
  71.8 1.4 copy-done.2
  73.2 1.3 copy-done.4
  78.6 1.5 copy-done.3
  80.1 1.5 copy-done.5
  85.7 9.6 %hops.1.refs_4_.refs_8_ = bf16[768,512]{1,0:T(8,128)(2,1)S(1)} custom-call(s32[60]{0:T(128)S(1)} %reshape.59.r_0_, s32[2]{0:T(128)S(1)} %copy-done.12, bf16[384,512]{1,0:T(8,128)(2,1)S(1)} %copy-done.6, bf16[384,512]{1,0:T(8,128)(2,1)S(1)} %copy-done.7, bf16[768,512]{1,0:T(8,128)(2,1)} %collective-permute-done.4.r_4_, ...), custom_call_target="tpu_custom_call" | custom-call | flops 1 | bytes 1 | tf_op jit(solution)/shard_map/hops/pallas_call | solution.py:195
  95.4 2.0 %part_out.2 = bf16[1024,512]{1,0:T(8,128)(2,1)S(1)} custom-call(s32[16]{0:T(128)S(1)} %get-tuple-element.65.order_ref, bf16[2048,768]{1,0:T(8,128)(2,1)S(1)} %get-tuple-element.32.refs_0_.refs_1_.refs_2_.refs_3_, bf16[2048,768]{1,0:T(8,128)(2,1)S(1)} %get-tuple-element.32.refs_0_.refs_1_.refs_2_.refs_3_, ...), custom_call_target="tpu_custom_call" | custom-call | flops 1 | bytes 1 | tf_op jit(solution)/shard_map/part_out/pallas_call | solution.py:278
  97.5 2.0 %part_out.3 = bf16[1024,512]{1,0:T(8,128)(2,1)S(1)} custom-call(s32[16]{0:T(128)S(1)} %get-tuple-element.66.order_ref, bf16[2048,768]{1,0:T(8,128)(2,1)S(1)} %get-tuple-element.32.refs_0_.refs_1_.refs_2_.refs_3_, bf16[2048,768]{1,0:T(8,128)(2,1)S(1)} %get-tuple-element.32.refs_0_.refs_1_.refs_2_.refs_3_, ...), custom_call_target="tpu_custom_call" | custom-call | flops 1 | bytes 1 | tf_op jit(solution)/shard_map/part_out/pallas_call | solution.py:278
  101.3 5.0 %part_in.2 = (bf16[1024,896]{1,0:T(8,128)(2,1)S(1)}, bf16[1024,768]{1,0:T(8,128)(2,1)S(1)}) custom-call(s32[16]{0:T(128)S(1)} %get-tuple-element.65.order_ref, f32[2048,768]{1,0:T(8,128)S(1)} %bitcast.102, f32[2048,768]{1,0:T(8,128)S(1)} %bitcast.102, f32[2048,768]{1,0:T(8,128)S(1)} %bitcast.102, f32[2048,768]{1,0:T(8,128)S(1)} %bitcast.102, ...), custom_call_target="tpu_custom_call" | custom-call | flops 1 | bytes 1 | tf_op jit(solution)/shard_map/part_in/pallas_call | solution.py:278
  108.2 5.0 %part_in.3 = (bf16[1024,896]{1,0:T(8,128)(2,1)S(1)}, bf16[1024,768]{1,0:T(8,128)(2,1)S(1)}) custom-call(s32[16]{0:T(128)S(1)} %get-tuple-element.66.order_ref, f32[2048,768]{1,0:T(8,128)S(1)} %bitcast.102, f32[2048,768]{1,0:T(8,128)S(1)} %bitcast.102, f32[2048,768]{1,0:T(8,128)S(1)} %bitcast.102, f32[2048,768]{1,0:T(8,128)S(1)} %bitcast.102, ...), custom_call_target="tpu_custom_call" | custom-call | flops 1 | bytes 1 | tf_op jit(solution)/shard_map/part_in/pallas_call | solution.py:278
  115.1 6.7 %collective-permute-done.10 = bf16[2,2,2,64,512]{4,3,2,1,0:T(8,128)(2,1)S(1)} collective-permute-done((bf16[2,2,2,64,512]{4,3,2,1,0:T(8,128)(2,1)S(1)}, bf16[2,2,2,64,512]{4,3,2,1,0:T(8,128)(2,1)S(1)}, u32[]{:S(2)}, u32[]{:S(2)}) %collective-permute-start.10) | collective-permute-done | bytes 524320 | tf_op jit(solution)/shard_map/ppermute | solution.py:341
  122.0 6.3 %feat_grad.1 = (bf16[384,768]{1,0:T(8,128)(2,1)}, bf16[384,768]{1,0:T(8,128)(2,1)}) custom-call(s32[32]{0:T(128)S(1)} %fusion.39.order_ref, bf16[2048,768]{1,0:T(8,128)(2,1)S(1)} %copy-done.1, bf16[2048,768]{1,0:T(8,128)(2,1)S(1)} %copy-done.1, bf16[2048,768]{1,0:T(8,128)(2,1)S(1)} %copy-done.1, bf16[2048,768]{1,0:T(8,128)(2,1)S(1)} %copy-done.1, ...), custom_call_target="tpu_custom_call" | custom-call | flops 1 | bytes 1 | tf_op jit(solution)/shard_map/feat_grad/pallas_call | solution.py:278
  128.3 2.0 %collective-permute-done.12 = bf16[2,2,2,64,640]{4,3,2,1,0:T(8,128)(2,1)S(1)} collective-permute-done((bf16[2,2,2,64,640]{4,3,2,1,0:T(8,128)(2,1)S(1)}, bf16[2,2,2,64,640]{4,3,2,1,0:T(8,128)(2,1)S(1)}, u32[]{:S(2)}, u32[]{:S(2)}) %collective-permute-start.12) | collective-permute-done | bytes 655392 | tf_op jit(solution)/shard_map/ppermute | solution.py:341
  133.7 3.4 %collective-permute-done.14 = bf16[2,2,64,256]{3,2,1,0:T(8,128)(2,1)S(1)} collective-permute-done((bf16[2,2,64,256]{3,2,1,0:T(8,128)(2,1)S(1)}, bf16[2,2,64,256]{3,2,1,0:T(8,128)(2,1)S(1)}, u32[]{:S(2)}, u32[]{:S(2)}) %collective-permute-start.14) | collective-permute-done | bytes 131104 | tf_op jit(solution)/shard_map/ppermute | solution.py:341
  137.1 3.4 %collective-permute-done.13 = bf16[2,2,64,512]{3,2,1,0:T(8,128)(2,1)S(1)} collective-permute-done((bf16[2,2,64,512]{3,2,1,0:T(8,128)(2,1)S(1)}, bf16[2,2,64,512]{3,2,1,0:T(8,128)(2,1)S(1)}, u32[]{:S(2)}, u32[]{:S(2)}) %collective-permute-start.13) | collective-permute-done | bytes 262176 | tf_op jit(solution)/shard_map/ppermute | solution.py:341
  140.8 1.6 %collective-permute-start.16 = (bf16[64,256]{1,0:T(8,128)(2,1)S(1)}, bf16[64,256]{1,0:T(8,128)(2,1)S(1)}, u32[]{:S(2)}, u32[]{:S(2)}) collective-permute-start(bf16[64,256]{1,0:T(8,128)(2,1)S(1)} %get-tuple-element.59), channel_id=1, source_target_pairs={{0,8},{1,9},{2,10},{3,11},{4,12},{5,13},{6,14},{7,15},{8,0},{9,1},... | collective-permute-start | bytes 98312 | tf_op jit(solution)/shard_map/ppermute | solution.py:341
  142.5 2.5 %collective-permute-start.18 = (bf16[64,256]{1,0:T(8,128)(2,1)S(1)}, bf16[64,256]{1,0:T(8,128)(2,1)S(1)}, u32[]{:S(2)}, u32[]{:S(2)}) collective-permute-start(bf16[64,256]{1,0:T(8,128)(2,1)S(1)} %get-tuple-element.60), channel_id=1, source_target_pairs={{0,24},{1,25},{2,26},{3,27},{4,28},{5,29},{6,30},{7,31},{8,16},{9,... | collective-permute-start | bytes 98312 | tf_op jit(solution)/shard_map/ppermute | solution.py:341
  145.0 2.0 %collective-permute-start.22 = (bf16[64,512]{1,0:T(8,128)(2,1)S(1)}, bf16[64,512]{1,0:T(8,128)(2,1)S(1)}, u32[]{:S(2)}, u32[]{:S(2)}) collective-permute-start(bf16[64,512]{1,0:T(8,128)(2,1)S(1)} %get-tuple-element.56), channel_id=1, source_target_pairs={{0,8},{1,9},{2,10},{3,11},{4,12},{5,13},{6,14},{7,15},{8,0},{9,1},... | collective-permute-start | bytes 196616 | tf_op jit(solution)/shard_map/ppermute | solution.py:341
  147.0 2.5 %collective-permute-start.24 = (bf16[64,512]{1,0:T(8,128)(2,1)S(1)}, bf16[64,512]{1,0:T(8,128)(2,1)S(1)}, u32[]{:S(2)}, u32[]{:S(2)}) collective-permute-start(bf16[64,512]{1,0:T(8,128)(2,1)S(1)} %get-tuple-element.57), channel_id=1, source_target_pairs={{0,24},{1,25},{2,26},{3,27},{4,28},{5,29},{6,30},{7,31},{8,16},{9,... | collective-permute-start | bytes 196616 | tf_op jit(solution)/shard_map/ppermute | solution.py:341
  149.6 1.9 %collective-permute-start.19 = (bf16[64,640]{1,0:T(8,128)(2,1)S(1)}, bf16[64,640]{1,0:T(8,128)(2,1)S(1)}, u32[]{:S(2)}, u32[]{:S(2)}) collective-permute-start(bf16[64,640]{1,0:T(8,128)(2,1)S(1)} %get-tuple-element.53), channel_id=1, source_target_pairs={{0,8},{1,9},{2,10},{3,11},{4,12},{5,13},{6,14},{7,15},{8,0},{9,1},... | collective-permute-start | bytes 245768 | tf_op jit(solution)/shard_map/ppermute | solution.py:341
  151.5 2.5 %collective-permute-start.21 = (bf16[64,640]{1,0:T(8,128)(2,1)S(1)}, bf16[64,640]{1,0:T(8,128)(2,1)S(1)}, u32[]{:S(2)}, u32[]{:S(2)}) collective-permute-start(bf16[64,640]{1,0:T(8,128)(2,1)S(1)} %get-tuple-element.54), channel_id=1, source_target_pairs={{0,24},{1,25},{2,26},{3,27},{4,28},{5,29},{6,30},{7,31},{8,16},{9,... | collective-permute-start | bytes 245768 | tf_op jit(solution)/shard_map/ppermute | solution.py:341
  154.1 2.9 %collective-permute-done.23 = bf16[64,512]{1,0:T(8,128)(2,1)S(1)} collective-permute-done((bf16[64,512]{1,0:T(8,128)(2,1)S(1)}, bf16[64,512]{1,0:T(8,128)(2,1)S(1)}, u32[]{:S(2)}, u32[]{:S(2)}) %collective-permute-start.23) | collective-permute-done | bytes 65568 | tf_op jit(solution)/shard_map/ppermute | solution.py:341
  157.8 3.0 %collective-permute-done.20 = bf16[64,640]{1,0:T(8,128)(2,1)S(1)} collective-permute-done((bf16[64,640]{1,0:T(8,128)(2,1)S(1)}, bf16[64,640]{1,0:T(8,128)(2,1)S(1)}, u32[]{:S(2)}, u32[]{:S(2)}) %collective-permute-start.20) | collective-permute-done | bytes 81952 | tf_op jit(solution)/shard_map/ppermute | solution.py:341
  (104 shorter events, 30.8 us)
Async XLA Ops:
  0.6 37.2 %copy-start.14 = (bf16[384,768]{1,0:T(8,128)(2,1)S(1)}, bf16[384,768]{1,0:T(8,128)(2,1)}, u32[]{:S(2)}) copy-start(bf16[384,768]{1,0:T(8,128)(2,1)} %param.13) | copy-start | bytes 1769476
  25.6 31.1 %collective-permute-start.6 = (bf16[768,512]{1,0:T(8,128)(2,1)}, bf16[768,512]{1,0:T(8,128)(2,1)}, u32[]{:S(2)}, u32[]{:S(2)}) collective-permute-start(bf16[768,512]{1,0:T(8,128)(2,1)} %stack.1), channel_id=1, source_target_pairs={{0,1},{1,0},{2,3},{3,2},{4,5},{5,4},{6,7},{7,6},{8,9},{9,8},{10,11... | collective-permute-start | bytes 2359304 | tf_op jit(solution)/shard_map/ppermute | solution.py:341
  28.6 49.9 %collective-permute-start.5 = (bf16[768,512]{1,0:T(8,128)(2,1)}, bf16[768,512]{1,0:T(8,128)(2,1)}, u32[]{:S(2)}, u32[]{:S(2)}) collective-permute-start(bf16[768,512]{1,0:T(8,128)(2,1)} %stack.1), channel_id=1, source_target_pairs={{2,0},{3,1},{4,2},{5,3},{6,4},{7,5},{8,6},{9,7},{10,8},{11,9},{12,... | collective-permute-start | bytes 2359304 | tf_op jit(solution)/shard_map/ppermute | solution.py:337
  29.9 48.7 %collective-permute-start.4 = (bf16[768,512]{1,0:T(8,128)(2,1)}, bf16[768,512]{1,0:T(8,128)(2,1)}, u32[]{:S(2)}, u32[]{:S(2)}) collective-permute-start(bf16[768,512]{1,0:T(8,128)(2,1)} %stack.1), channel_id=1, source_target_pairs={{0,2},{1,3},{2,4},{3,5},{4,6},{5,7},{6,8},{7,9},{8,10},{9,11},{10,... | collective-permute-start | bytes 2359304 | tf_op jit(solution)/shard_map/ppermute | solution.py:337
  35.9 11.9 %collective-permute-start = (s32[3,9]{1,0:T(4,128)}, s32[3,9]{1,0:T(4,128)}, u32[]{:S(2)}, u32[]{:S(2)}) collective-permute-start(s32[3,9]{1,0:T(4,128)} %pad_add_fusion), channel_id=1, source_target_pairs={{0,1},{1,0},{2,3},{3,2},{4,5},{5,4},{6,7},{7,6},{8,9},{9,8},{10,11... | collective-permute-start | bytes 332 | tf_op jit(solution)/shard_map/ppermute | solution.py:341
  38.7 39.9 %copy-start.6 = (bf16[384,512]{1,0:T(8,128)(2,1)S(1)}, bf16[384,512]{1,0:T(8,128)(2,1)}, u32[]{:S(2)}) copy-start(bf16[384,512]{1,0:T(8,128)(2,1)} %r_2_.1) | copy-start | bytes 1179652
  48.6 4.4 %collective-permute-start.1 = (s32[6,9]{1,0:T(8,128)S(1)}, s32[6,9]{1,0:T(8,128)S(1)}, u32[]{:S(2)}, u32[]{:S(2)}) collective-permute-start(s32[6,9]{1,0:T(8,128)S(1)} %add_select_fusion.1), channel_id=1, source_target_pairs={{0,4},{2,6},{4,8},{6,10},{8,12},{10,14},{12,16},{14,18},{16,20},{1... | collective-permute-start | bytes 656 | tf_op jit(solution)/shard_map/ppermute | solution.py:411
  51.7 9.6 %collective-permute-start.3 = (s32[6,9]{1,0:T(8,128)S(1)}, s32[6,9]{1,0:T(8,128)S(1)}, u32[]{:S(2)}, u32[]{:S(2)}) collective-permute-start(s32[6,9]{1,0:T(8,128)S(1)} %add_select_fusion.1), channel_id=1, source_target_pairs={{2,0},{3,1},{4,2},{5,3},{6,4},{7,5},{8,6},{9,7},{10,8},{11,9},{12,... | collective-permute-start | bytes 656 | tf_op jit(solution)/shard_map/ppermute | solution.py:337
  53.0 8.3 %collective-permute-start.2 = (s32[6,9]{1,0:T(8,128)S(1)}, s32[6,9]{1,0:T(8,128)S(1)}, u32[]{:S(2)}, u32[]{:S(2)}) collective-permute-start(s32[6,9]{1,0:T(8,128)S(1)} %add_select_fusion.1), channel_id=1, source_target_pairs={{0,2},{1,3},{2,4},{3,5},{4,6},{5,7},{6,8},{7,9},{8,10},{9,11},{10,... | collective-permute-start | bytes 656 | tf_op jit(solution)/shard_map/ppermute | solution.py:337
  56.7 21.9 %collective-permute-start.7 = (bf16[768,512]{1,0:T(8,128)(2,1)}, bf16[768,512]{1,0:T(8,128)(2,1)}, u32[]{:S(2)}, u32[]{:S(2)}) collective-permute-start(bf16[768,512]{1,0:T(8,128)(2,1)} %collective-permute-done.6.r_6_), channel_id=1, source_target_pairs={{0,2},{2,4},{4,6},{6,8},{8,10},{10,12},{12,14},{14,16},{16,18},{18... | collective-permute-start | bytes 2359304 | tf_op jit(solution)/shard_map/ppermute | solution.py:407
  78.6 1.5 copy-start.3
  97.4 2.7 %collective-permute-start.8 = (bf16[2,2,2,2,64,512]{5,4,3,2,1,0:T(8,128)(2,1)S(1)}, bf16[2,2,2,2,64,512]{5,4,3,2,1,0:T(8,128)(2,1)S(1)}, u32[]{:S(2)}, u32[]{:S(2)}) collective-permute-start(bf16[2,2,2,2,64,512]{5,4,3,2,1,0:T(8,128)(2,1)S(1)} %bitcast.105), channel_id=1, source_target_pairs={{0,2},{1,3},{2,0},{3,1},{4,6},{5,7},{6,4},{7,5},{8,10},{9,11},{10,... | collective-permute-start | bytes 3145736 | tf_op jit(solution)/shard_map/ppermute | solution.py:341
  97.5 3.0 %slice-start = ((s8[6291456]{0:T(1024)(128)(4,1)}), s8[4194304]{0:T(1024)(128)(4,1)S(1)}, s32[]{:S(2)}) async-start(s8[6291456]{0:T(1024)(128)(4,1)} %bitcast.101), calls=%async_computation | async-start | bytes 8388608
  97.5 3.0 %slice-start.1 = ((s8[6291456]{0:T(1024)(128)(4,1)}), s8[2097152]{0:T(1024)(128)(4,1)S(1)}, s32[]{:S(2)}) async-start(s8[6291456]{0:T(1024)(128)(4,1)} %bitcast.101), calls=%async_computation.1 | async-start | bytes 4194304
  99.6 1.8 %copy-start = (bf16[2048,512]{1,0:T(8,128)(2,1)S(1)}, bf16[2048,512]{1,0:T(8,128)(2,1)}, u32[]{:S(2)}) copy-start(bf16[2048,512]{1,0:T(8,128)(2,1)} %refs_7_.3) | copy-start | bytes 6291460
  106.4 6.9 %collective-permute-start.9 = (bf16[2,2,2,2,64,896]{5,4,3,2,1,0:T(8,128)(2,1)S(1)}, bf16[2,2,2,2,64,896]{5,4,3,2,1,0:T(8,128)(2,1)S(1)}, u32[]{:S(2)}, u32[]{:S(2)}) collective-permute-start(bf16[2,2,2,2,64,896]{5,4,3,2,1,0:T(8,128)(2,1)S(1)} %bitcast.106), channel_id=1, source_target_pairs={{0,2},{1,3},{2,0},{3,1},{4,6},{5,7},{6,4},{7,5},{8,10},{9,11},{10,... | collective-permute-start | bytes 5505032 | tf_op jit(solution)/shard_map/ppermute | solution.py:341
  107.0 14.9 %collective-permute-start.10 = (bf16[2,2,2,64,512]{4,3,2,1,0:T(8,128)(2,1)S(1)}, bf16[2,2,2,64,512]{4,3,2,1,0:T(8,128)(2,1)S(1)}, u32[]{:S(2)}, u32[]{:S(2)}) collective-permute-start(bf16[2,2,2,64,512]{4,3,2,1,0:T(8,128)(2,1)S(1)} %slice_bitcast_fusion.2), channel_id=1, source_target_pairs={{0,4},{1,5},{2,6},{3,7},{4,0},{5,1},{6,2},{7,3},{8,12},{9,13},{10,... | collective-permute-start | bytes 1572872 | tf_op jit(solution)/shard_map/ppermute | solution.py:341
  113.8 8.1 %copy-start.1 = (bf16[2048,768]{1,0:T(8,128)(2,1)S(1)}, bf16[2048,768]{1,0:T(8,128)(2,1)}, u32[]{:S(2)}) copy-start(bf16[2048,768]{1,0:T(8,128)(2,1)} %refs_3_.1) | copy-start | bytes 9437188
  113.9 16.5 %collective-permute-start.12 = (bf16[2,2,2,64,640]{4,3,2,1,0:T(8,128)(2,1)S(1)}, bf16[2,2,2,64,640]{4,3,2,1,0:T(8,128)(2,1)S(1)}, u32[]{:S(2)}, u32[]{:S(2)}) collective-permute-start(bf16[2,2,2,64,640]{4,3,2,1,0:T(8,128)(2,1)S(1)} %slice_bitcast_fusion), channel_id=1, source_target_pairs={{0,1},{1,0},{2,3},{3,2},{4,5},{5,4},{6,7},{7,6},{8,9},{9,8},{10,11... | collective-permute-start | bytes 1966088 | tf_op jit(solution)/shard_map/ppermute | solution.py:341
  115.0 13.2 %collective-permute-start.11 = (bf16[2,2,2,64,256]{4,3,2,1,0:T(8,128)(2,1)S(1)}, bf16[2,2,2,64,256]{4,3,2,1,0:T(8,128)(2,1)S(1)}, u32[]{:S(2)}, u32[]{:S(2)}) collective-permute-start(bf16[2,2,2,64,256]{4,3,2,1,0:T(8,128)(2,1)S(1)} %slice_bitcast_fusion.5), channel_id=1, source_target_pairs={{0,4},{1,5},{2,6},{3,7},{4,0},{5,1},{6,2},{7,3},{8,12},{9,13},{10,... | collective-permute-start | bytes 786440 | tf_op jit(solution)/shard_map/ppermute | solution.py:341
  130.5 6.5 %collective-permute-start.14 = (bf16[2,2,64,256]{3,2,1,0:T(8,128)(2,1)S(1)}, bf16[2,2,64,256]{3,2,1,0:T(8,128)(2,1)S(1)}, u32[]{:S(2)}, u32[]{:S(2)}) collective-permute-start(bf16[2,2,64,256]{3,2,1,0:T(8,128)(2,1)S(1)} %slice_bitcast_fusion.8), channel_id=1, source_target_pairs={{0,1},{1,0},{2,3},{3,2},{4,5},{5,4},{6,7},{7,6},{8,9},{9,8},{10,11... | collective-permute-start | bytes 393224 | tf_op jit(solution)/shard_map/ppermute | solution.py:341
  131.7 8.8 %collective-permute-start.13 = (bf16[2,2,64,512]{3,2,1,0:T(8,128)(2,1)S(1)}, bf16[2,2,64,512]{3,2,1,0:T(8,128)(2,1)S(1)}, u32[]{:S(2)}, u32[]{:S(2)}) collective-permute-start(bf16[2,2,64,512]{3,2,1,0:T(8,128)(2,1)S(1)} %slice_bitcast_fusion.7), channel_id=1, source_target_pairs={{0,1},{1,0},{2,3},{3,2},{4,5},{5,4},{6,7},{7,6},{8,9},{9,8},{10,11... | collective-permute-start | bytes 786440 | tf_op jit(solution)/shard_map/ppermute | solution.py:341
  132.8 8.0 %collective-permute-start.15 = (bf16[2,2,64,640]{3,2,1,0:T(8,128)(2,1)S(1)}, bf16[2,2,64,640]{3,2,1,0:T(8,128)(2,1)S(1)}, u32[]{:S(2)}, u32[]{:S(2)}) collective-permute-start(bf16[2,2,64,640]{3,2,1,0:T(8,128)(2,1)S(1)} %slice_bitcast_fusion.4), channel_id=1, source_target_pairs={{0,4},{1,5},{2,6},{3,7},{4,0},{5,1},{6,2},{7,3},{8,12},{9,13},{10,... | collective-permute-start | bytes 983048 | tf_op jit(solution)/shard_map/ppermute | solution.py:341
  140.8 8.6 %collective-permute-start.16 = (bf16[64,256]{1,0:T(8,128)(2,1)S(1)}, bf16[64,256]{1,0:T(8,128)(2,1)S(1)}, u32[]{:S(2)}, u32[]{:S(2)}) collective-permute-start(bf16[64,256]{1,0:T(8,128)(2,1)S(1)} %get-tuple-element.59), channel_id=1, source_target_pairs={{0,8},{1,9},{2,10},{3,11},{4,12},{5,13},{6,14},{7,15},{8,0},{9,1},... | collective-permute-start | bytes 98312 | tf_op jit(solution)/shard_map/ppermute | solution.py:341
  142.5 7.1 %collective-permute-start.18 = (bf16[64,256]{1,0:T(8,128)(2,1)S(1)}, bf16[64,256]{1,0:T(8,128)(2,1)S(1)}, u32[]{:S(2)}, u32[]{:S(2)}) collective-permute-start(bf16[64,256]{1,0:T(8,128)(2,1)S(1)} %get-tuple-element.60), channel_id=1, source_target_pairs={{0,24},{1,25},{2,26},{3,27},{4,28},{5,29},{6,30},{7,31},{8,16},{9,... | collective-permute-start | bytes 98312 | tf_op jit(solution)/shard_map/ppermute | solution.py:341
  145.0 6.5 %collective-permute-start.17 = (bf16[64,256]{1,0:T(8,128)(2,1)S(1)}, bf16[64,256]{1,0:T(8,128)(2,1)S(1)}, u32[]{:S(2)}, u32[]{:S(2)}) collective-permute-start(bf16[64,256]{1,0:T(8,128)(2,1)S(1)} %get-tuple-element.61), channel_id=1, source_target_pairs={{0,16},{1,17},{2,18},{3,19},{4,20},{5,21},{6,22},{7,23},{8,24},{9,... | collective-permute-start | bytes 98312 | tf_op jit(solution)/shard_map/ppermute | solution.py:341
  145.0 9.0 %collective-permute-start.22 = (bf16[64,512]{1,0:T(8,128)(2,1)S(1)}, bf16[64,512]{1,0:T(8,128)(2,1)S(1)}, u32[]{:S(2)}, u32[]{:S(2)}) collective-permute-start(bf16[64,512]{1,0:T(8,128)(2,1)S(1)} %get-tuple-element.56), channel_id=1, source_target_pairs={{0,8},{1,9},{2,10},{3,11},{4,12},{5,13},{6,14},{7,15},{8,0},{9,1},... | collective-permute-start | bytes 196616 | tf_op jit(solution)/shard_map/ppermute | solution.py:341
  147.0 7.1 %collective-permute-start.24 = (bf16[64,512]{1,0:T(8,128)(2,1)S(1)}, bf16[64,512]{1,0:T(8,128)(2,1)S(1)}, u32[]{:S(2)}, u32[]{:S(2)}) collective-permute-start(bf16[64,512]{1,0:T(8,128)(2,1)S(1)} %get-tuple-element.57), channel_id=1, source_target_pairs={{0,24},{1,25},{2,26},{3,27},{4,28},{5,29},{6,30},{7,31},{8,16},{9,... | collective-permute-start | bytes 196616 | tf_op jit(solution)/shard_map/ppermute | solution.py:341
  149.5 7.4 %collective-permute-start.23 = (bf16[64,512]{1,0:T(8,128)(2,1)S(1)}, bf16[64,512]{1,0:T(8,128)(2,1)S(1)}, u32[]{:S(2)}, u32[]{:S(2)}) collective-permute-start(bf16[64,512]{1,0:T(8,128)(2,1)S(1)} %get-tuple-element.58), channel_id=1, source_target_pairs={{0,16},{1,17},{2,18},{3,19},{4,20},{5,21},{6,22},{7,23},{8,24},{9,... | collective-permute-start | bytes 196616 | tf_op jit(solution)/shard_map/ppermute | solution.py:341
  149.6 8.1 %collective-permute-start.19 = (bf16[64,640]{1,0:T(8,128)(2,1)S(1)}, bf16[64,640]{1,0:T(8,128)(2,1)S(1)}, u32[]{:S(2)}, u32[]{:S(2)}) collective-permute-start(bf16[64,640]{1,0:T(8,128)(2,1)S(1)} %get-tuple-element.53), channel_id=1, source_target_pairs={{0,8},{1,9},{2,10},{3,11},{4,12},{5,13},{6,14},{7,15},{8,0},{9,1},... | collective-permute-start | bytes 245768 | tf_op jit(solution)/shard_map/ppermute | solution.py:341
  151.5 6.3 %collective-permute-start.21 = (bf16[64,640]{1,0:T(8,128)(2,1)S(1)}, bf16[64,640]{1,0:T(8,128)(2,1)S(1)}, u32[]{:S(2)}, u32[]{:S(2)}) collective-permute-start(bf16[64,640]{1,0:T(8,128)(2,1)S(1)} %get-tuple-element.54), channel_id=1, source_target_pairs={{0,24},{1,25},{2,26},{3,27},{4,28},{5,29},{6,30},{7,31},{8,16},{9,... | collective-permute-start | bytes 245768 | tf_op jit(solution)/shard_map/ppermute | solution.py:341
  154.0 6.9 %collective-permute-start.20 = (bf16[64,640]{1,0:T(8,128)(2,1)S(1)}, bf16[64,640]{1,0:T(8,128)(2,1)S(1)}, u32[]{:S(2)}, u32[]{:S(2)}) collective-permute-start(bf16[64,640]{1,0:T(8,128)(2,1)S(1)} %get-tuple-element.55), channel_id=1, source_target_pairs={{0,16},{1,17},{2,18},{3,19},{4,20},{5,21},{6,22},{7,23},{8,24},{9,... | collective-permute-start | bytes 245768 | tf_op jit(solution)/shard_map/ppermute | solution.py:341
  (11 other events, 11.8 us)

commit v4 on v3

--- a/solution.py
+++ b/solution.py
@@ -21,7 +21,8 @@
     return (preact * normal_cdf, normal_cdf + preact * normal_pdf)
 
 
-def tiles_kernel(seed_ref, place_ref, count_ref, pat_ref, pat_t_ref, nimg_ref, ncap_ref, deg_ref, *, tiles, slots):
+def tiles_kernel(seed_ref, place_ref, count_ref, *refs, tiles, slots):
+    outs, (pat_ref, pat_t_ref, nimg_ref, ncap_ref, deg_ref, sems) = refs[:4], refs[4:]
     all_tiles, mid = 7 * tiles, 5 * tiles
     deg_ref[...] = jnp.zeros_like(deg_ref)
     row = lax.broadcasted_iota(jnp.int32, (TILE, TILE), 0)
@@ -69,45 +70,60 @@
 
     lax.fori_loop(0, tiles, edge_body, 0)
     lax.fori_loop(tiles, tiles + mid, mid_body, 0)
+    copies = [
+        pltpu.make_async_copy(src, dst, sems.at[k])
+        for k, (src, dst) in enumerate(zip((pat_ref, pat_t_ref, nimg_ref, ncap_ref), outs))
+    ]
+    for copy in copies[:3]:
+        copy.start()
     lax.fori_loop(tiles + mid, all_tiles, edge_body, 0)
     for m in range(mid):
         d = deg_ref[m + 2 * tiles]
         n = jnp.where(d > 0.0, lax.rsqrt(d), 0.0)
         ncap_ref[m] = jnp.broadcast_to(n, (TILE, TILE)).T
+    copies[3].start()
+    for copy in copies:
+        copy.wait()
+
+
+def table_shapes(tiles, slots):
+    mid = 5 * tiles
+    return (
+        ((mid, TILE, slots * TILE), BF16),
+        ((mid, slots * TILE, TILE), BF16),
+        ((mid, TILE, TILE), F32),
+        ((mid, TILE, TILE), F32),
+    )
 
 
 def make_tiles(seeds, places, counts, tiles, slots):
-    mid = 5 * tiles
     smem = pl.BlockSpec(memory_space=pltpu.SMEM)
-    vmem = pl.BlockSpec(memory_space=pltpu.VMEM)
+    hbm = pl.BlockSpec(memory_space=pltpu.HBM)
+    tables = table_shapes(tiles, slots)
     return pl.pallas_call(
         lambda *r: tiles_kernel(*r, tiles=tiles, slots=slots),
-        out_shape=(
-            jax.ShapeDtypeStruct((mid, TILE, slots * TILE), BF16),
-            jax.ShapeDtypeStruct((mid, slots * TILE, TILE), BF16),
-            jax.ShapeDtypeStruct((mid, TILE, TILE), F32),
-            jax.ShapeDtypeStruct((mid, TILE, TILE), F32),
-        ),
+        out_shape=tuple(jax.ShapeDtypeStruct(*t) for t in tables),
         in_specs=[smem] * 3,
-        out_specs=(vmem,) * 4,
-        scratch_shapes=[pltpu.VMEM((9 * tiles, 1, TILE), F32)],
-        compiler_params=pltpu.CompilerParams(vmem_limit_bytes=28 << 20),
+        out_specs=(hbm,) * 4,
+        scratch_shapes=[pltpu.VMEM(*t) for t in tables]
+        + [pltpu.VMEM((9 * tiles, 1, TILE), F32), pltpu.SemaphoreType.DMA((4,))],
+        compiler_params=pltpu.CompilerParams(vmem_limit_bytes=16 << 20),
         cost_estimate=SHORT,
         name="tiles",
     )(seeds, places, counts)
 
 
 def hops_kernel(
-    place_ref, base_ref, own_img, own_cap, low_hbm, high_hbm, mate_hbm, far_hbm, pat_ref, pat_t_ref, nimg_ref, ncap_ref,
-    out_ref, bands, img0, cap0, img1, cap1, acc, acc2, keep_img, keep_cap, sems, *, tiles, slots, width,
+    place_ref, base_ref, own_hbm, low_hbm, high_hbm, mate_hbm, far_hbm, pat_hbm, pat_t_hbm, nimg_hbm, ncap_hbm,
+    out_ref, bands, pat_ref, pat_t_ref, nimg_ref, ncap_ref, img0, cap0, img1, cap1, acc, acc2, keep_img, keep_cap,
+    sems, *, tiles, slots, width,
 ):
     mid = 5 * tiles
     near = 3 * tiles
     keep = 1.0 - ALPHA
-    copies = [
-        pltpu.make_async_copy(src, bands.at[k], sems.at[k])
-        for k, src in enumerate((low_hbm, high_hbm, mate_hbm, far_hbm))
-    ]
+    sources = (own_hbm, nimg_hbm, ncap_hbm, low_hbm, high_hbm, mate_hbm, far_hbm, pat_t_hbm, pat_hbm)
+    targets = (bands.at[0], nimg_ref, ncap_ref) + tuple(bands.at[k] for k in range(1, 5)) + (pat_t_ref, pat_ref)
+    copies = [pltpu.make_async_copy(s, t, sems.at[k]) for k, (s, t) in enumerate(zip(sources, targets))]
     for copy in copies:
         copy.start()
 
@@ -115,21 +131,22 @@
         n = n_ref[m]
         return jnp.concatenate([n] * (width // TILE), axis=1)
 
-    def scale(rows_img, rows_cap, base):
+    def scale(k, base):
         for t in range(tiles):
             m = base + t
-            img0[m] = (rows_img(t).astype(F32) * wide(nimg_ref, m)).astype(BF16)
-            cap0[m] = (rows_cap(t).astype(F32) * wide(ncap_ref, m)).astype(BF16)
-
-    def both(k):
-        return (lambda t: bands[k, pl.ds(t * TILE, TILE), :]), (lambda t: bands[k, pl.ds((tiles + t) * TILE, TILE), :])
+            img0[m] = (bands[k, pl.ds(t * TILE, TILE), :].astype(F32) * wide(nimg_ref, m)).astype(BF16)
+            cap0[m] = (bands[k, pl.ds((tiles + t) * TILE, TILE), :].astype(F32) * wide(ncap_ref, m)).astype(BF16)
 
     acc[...] = jnp.zeros_like(acc)
     acc2[...] = jnp.zeros_like(acc2)
-    scale(lambda t: own_img[pl.ds(t * TILE, TILE), :], lambda t: own_cap[pl.ds(t * TILE, TILE), :], 2 * tiles)
-    for k, base in enumerate((0, 4 * tiles, base_ref[0], base_ref[1])):
-        copies[k].wait()
-        scale(*both(k), base)
+    for copy in copies[:3]:
+        copy.wait()
+    for k, base in enumerate((2 * tiles, 0, 4 * tiles, base_ref[0], base_ref[1])):
+        if k:
+            copies[2 + k].wait()
+        scale(k, base)
+    for copy in copies[7:]:
+        copy.wait()
 
     def push(q, state, target, lo, count):
         r = jnp.dot(pat_t_ref[q], state, preferred_element_type=F32)
@@ -179,26 +196,26 @@
         q = 2 * tiles + t
         rows = pl.ds(t * TILE, TILE)
         flow = keep * wide(nimg_ref, q) * pull(q, cap1, tiles)
-        out_ref[rows, :] = (ALPHA * (own_img[rows, :].astype(F32) + keep_img[tiles + t]) + flow).astype(BF16)
+        out_ref[rows, :] = (ALPHA * (bands[0, rows, :].astype(F32) + keep_img[tiles + t]) + flow).astype(BF16)
         flow = keep * wide(ncap_ref, q) * acc2[t]
-        out_ref[pl.ds((tiles + t) * TILE, TILE), :] = (
-            ALPHA * (own_cap[rows, :].astype(F32) + keep_cap[tiles + t]) + flow
-        ).astype(BF16)
-
-
-def propagate(places, bases, own_img, own_cap, low, high, mate, far, pats, tiles, slots):
-    width = own_img.shape[1]
+        rows = pl.ds((tiles + t) * TILE, TILE)
+        out_ref[rows, :] = (ALPHA * (bands[0, rows, :].astype(F32) + keep_cap[tiles + t]) + flow).astype(BF16)
+
+
+def propagate(places, bases, own, low, high, mate, far, tables, tiles, slots):
+    width = own.shape[1]
     smem = pl.BlockSpec(memory_space=pltpu.SMEM)
     vmem = pl.BlockSpec(memory_space=pltpu.VMEM)
     hbm = pl.BlockSpec(memory_space=pltpu.HBM)
     mid, near = 5 * tiles, 3 * tiles
     return pl.pallas_call(
         lambda *r: hops_kernel(*r, tiles=tiles, slots=slots, width=width),
-        out_shape=jax.ShapeDtypeStruct(low.shape, BF16),
-        in_specs=[smem] * 2 + [vmem] * 2 + [hbm] * 4 + [vmem] * 4,
+        out_shape=jax.ShapeDtypeStruct(own.shape, BF16),
+        in_specs=[smem] * 2 + [hbm] * 9,
         out_specs=vmem,
         scratch_shapes=[
-            pltpu.VMEM((4,) + low.shape, BF16),
+            pltpu.VMEM((5,) + own.shape, BF16),
+            *[pltpu.VMEM(*t) for t in table_shapes(tiles, slots)],
             pltpu.VMEM((mid, TILE, width), BF16),
             pltpu.VMEM((mid, TILE, width), BF16),
             pltpu.VMEM((near, TILE, width), BF16),
@@ -207,12 +224,12 @@
             pltpu.VMEM((tiles + 1, TILE, width), F32),
             pltpu.VMEM((near, TILE, width), F32),
             pltpu.VMEM((near, TILE, width), F32),
-            pltpu.SemaphoreType.DMA((4,)),
+            pltpu.SemaphoreType.DMA((9,)),
         ],
-        compiler_params=pltpu.CompilerParams(vmem_limit_bytes=32 << 20),
+        compiler_params=pltpu.CompilerParams(vmem_limit_bytes=34 << 20),
         cost_estimate=SHORT,
         name="hops",
-    )(places, bases, own_img, own_cap, low, high, mate, far, *pats)
+    )(places, bases, own, low, high, mate, far, *tables)
 
 
 BLOCK = 64
@@ -304,26 +321,19 @@
     return pl.BlockSpec((GROUP * BLOCK, width), lambda i, order: (i, 0))
 
 
-def stack_kernel(top_ref, bottom_ref, out_ref, sems):
+def stack_kernel(top_ref, bottom_ref, out_ref):
     half = top_ref.shape[0]
-    copies = [
-        pltpu.make_async_copy(src, out_ref.at[pl.ds(k * half, half)], sems.at[k])
-        for k, src in enumerate((top_ref, bottom_ref))
-    ]
-    for copy in copies:
-        copy.start()
-    for copy in copies:
-        copy.wait()
+    out_ref[:half] = top_ref[...]
+    out_ref[half:] = bottom_ref[...]
 
 
 def stack(top, bottom):
-    hbm = pl.BlockSpec(memory_space=pltpu.HBM)
+    vmem = pl.BlockSpec(memory_space=pltpu.VMEM)
     return pl.pallas_call(
         stack_kernel,
         out_shape=jax.ShapeDtypeStruct((2 * top.shape[0], top.shape[1]), top.dtype),
-        in_specs=[hbm] * 2,
-        out_specs=hbm,
-        scratch_shapes=[pltpu.SemaphoreType.DMA((2,))],
+        in_specs=[vmem] * 2,
+        out_specs=vmem,
         cost_estimate=SHORT,
         name="stack",
     )(top, bottom)
@@ -349,11 +359,6 @@
     return lax.index_in_dim(array, 0, axis, keepdims=False), lax.index_in_dim(array, 1, axis, keepdims=False)
 
 
-def meet(values, owners):
-    for owner, value in zip(owners, lax.optimization_barrier(tuple(values))):
-        owner.part = value
-
-
 def nearest_pair(count, by):
     return [(i, i + by) for i in range(0, count - by, 2)] + [(i, i - by) for i in range(by + 1, count, 2)]
 
@@ -365,12 +370,12 @@
 
     def start(self):
         bit = self.order.pop(0)
-        self.kept, sent = parts(self.part, self.left.index(bit))
+        self.kept, self.sent = parts(self.part, self.left.index(bit))
         self.left.remove(bit)
-        self.came = flipped(sent, self.count, 1 << bit)
-
-    def finish(self):
-        self.part = added(self.kept, self.came)
+        self.came = flipped(self.sent, self.count, 1 << bit)
+
+    def finish(self, *done):
+        self.part = added(after(self.kept, *done), self.came)
         return self.part
 
     def start_last(self):
@@ -439,7 +444,7 @@
     else:
         order = (order[:, None] * (rows // BLOCK) + jnp.arange(rows // BLOCK, dtype=jnp.int32)).reshape(-1)
 
-    feats = jnp.concatenate([feats_img, feats_cap], axis=0)
+    feats = after(jnp.concatenate([feats_img, feats_cap], axis=0), pair)
     across = (((1,), (1,)), ((), ()))
     preact = lax.dot_general(w_in, feats, across, preferred_element_type=F32) + b_in[:, None]
     gelu_value, gelu_slope = gelu_parts(preact)
@@ -447,7 +452,7 @@
 
     bases = jnp.where(even, jnp.array([3, 1]), jnp.array([1, 3])).astype(jnp.int32) * tiles
     mid_places = (places - tiles)[tiles : 6 * tiles].reshape(-1)
-    logit = propagate(mid_places, bases, cot_img, cot_cap, low, high, mate, far, pats, tiles, slots)
+    logit = propagate(mid_places, bases, block, low, high, mate, far, pats, tiles, slots)
 
     width = cot_img.shape[1]
     nodes = 2 * local_rows
@@ -481,7 +486,7 @@
     in_came = flipped(in_sent, count, core)
     in_kept, grad_kept = in_half(order[:half], after(logit, grad_sent))
     g_in = added(in_kept, in_came)
-    cut = f_in // 3
+    cut = f_in // 2
     r_a = Reduction(g_in[..., :cut], count, rest, img_bits + cap_bits)
     r_b = Reduction(g_in[..., cut:], count, rest, cap_bits + img_bits)
     r_a.start()
@@ -492,14 +497,14 @@
         (whole((local_rows, f_in)),) * 2, (jax.ShapeDtypeStruct((local_rows, f_in), BF16),) * 2,
         [pltpu.VMEM((nodes, f_in), F32)], [w_in] * GROUP + [grad_kept, grad_sent],
     )
-    chunks = (r_out, r_a, r_b)
-    for _ in range(m - 4):
-        meet([r.finish() for r in chunks], chunks)
-        for r in chunks:
-            r.start()
-    meet([r.finish() for r in chunks], chunks)
-    for r in chunks:
-        r.start_last()
+    done = (r_a.sent, r_b.sent)
+    for k in range(m - 3):
+        for r in (r_out, r_b, r_a):
+            done = (r.finish(*done),)
+            if k < m - 4:
+                r.start()
+            else:
+                r.start_last()
     grad_scale = 1.0 / math.sqrt(nodes * count)
     g_out, g_b, g_a = [r.result() * grad_scale for r in (r_out, r_b, r_a)]
     g_in = jnp.concatenate([g_a, g_b[:, : f_in - cut]], axis=1)

time: 163 us -> 135 us (0.83)
  Pallas kernels: 61 us -> 37.5 us
  local copies, waits for them, and re-layouts: 21.5 us -> 15.3 us
  waiting for transfers between devices: 22.4 us -> 26.8 us
  other arithmetic: 8.49 us -> 6.41 us
    pallas_call x1, Pallas kernels: 24.9 us -> 2.08 us  [stack(): pl.pallas_call(stack_kernel, out_shape=jax.ShapeDtypeStruct((2 * top.shap...]
    ppermute x19, waiting for transfers between devices: 22.4 us -> 26.8 us  [flipped(): return lax.ppermute(array, AXES, [(i, i ^ mask) for i in range(count)])]
    pallas_call x5, Pallas kernels: 20.4 us -> 17.8 us  [over_hidden(): pl.pallas_call(kernel, out_shape=out_shape, grid_spec=pltpu.PrefetchScala...]
    concatenate x0 -> x1, other arithmetic: none -> 2.34 us  [per_device(): feats = after(jnp.concatenate([feats_img, feats_cap], axis=0), pair)]
    unnamed x37 -> x38, local copies, waits for them, and re-layouts: 15.2 us -> 13 us
  transfers between devices with their start and end apart: 25 -> 25, of which waited for: 9 -> 12; matrix products, arithmetic and copies ran while one was open for 14% -> 11% of each run, Pallas kernels for 12% -> 14%
where the time goes in v4:
time: 135 us
  starting transfers between devices  40.1 us (30%)
  Pallas kernels  37.5 us (28%)
  waiting for transfers between devices  26.8 us (20%)
  local copies, waits for them, and re-layouts  15.3 us (11%)
  matrix products  7.7 us (6%)
  other arithmetic  6.41 us (5%)
    ppermute x19, waiting for transfers between devices, flipped(): return lax.ppermute(array, AXES, [(i, i ^ mask) for i in range(count)])  26.8 us
    ppermute x19, starting transfers between devices, flipped(): return lax.ppermute(array, AXES, [(i, i ^ mask) for i in range(count)])  22.9 us
    pallas_call x5, Pallas kernels, over_hidden(): pl.pallas_call(kernel, out_shape=out_shape, grid_spec=pltpu.PrefetchScala...  17.8 us
    unnamed x38, local copies, waits for them, and re-layouts  13 us
    pallas_call x1, Pallas kernels, propagate(): pl.pallas_call(lambda *r: hops_kernel(*r, tiles=tiles, slots=slots, width...  10.3 us
    ppermute x4, starting transfers between devices, moved(): lax.ppermute(array, AXES, [(i, i + by) for i in range(count) if 0 <= i +...  8.61 us
    dot_general x1, matrix products, per_device(): lax.dot_general(w_in, feats, across, preferred_element_type=F32)  7.7 us
    pallas_call x1, Pallas kernels, make_tiles(): pl.pallas_call(lambda *r: tiles_kernel(*r, tiles=tiles, slots=slots), out...  7.24 us
  transfers between devices with their start and end apart: 25, of which 12 were waited for; matrix products, arithmetic and copies ran while one was open for 11% of the time, Pallas kernels for 14%

profile of v4, /device:TPU:0, one launch (start us, length us, event | category | flops | bytes accessed | tf_op | source)
XLA Modules:
  0.0 134.8 jit_solution(6560930433671373965)
XLA Ops:
  0.7 2.1 %stack.1.r_2_ = bf16[768,512]{1,0:T(8,128)(2,1)} custom-call(bf16[384,512]{1,0:T(8,128)(2,1)} %top_ref.1, bf16[384,512]{1,0:T(8,128)(2,1)} %bottom_ref.1), custom_call_target="tpu_custom_call" | custom-call | flops 1 | bytes 1 | tf_op jit(solution)/shard_map/stack/pallas_call | solution.py:332
  2.8 2.9 %collective-permute-start.6 = (bf16[768,512]{1,0:T(8,128)(2,1)}, bf16[768,512]{1,0:T(8,128)(2,1)}, u32[]{:S(2)}, u32[]{:S(2)}) collective-permute-start(bf16[768,512]{1,0:T(8,128)(2,1)} %stack.1.r_2_), channel_id=1, source_target_pairs={{0,1},{1,0},{2,3},{3,2},{4,5},{5,4},{6,7},{7,6},{8,9},{9,8},{10,11... | collective-permute-start | bytes 2359304 | tf_op jit(solution)/shard_map/ppermute | solution.py:351
  7.0 3.9 %collective-permute-start.4 = (bf16[768,512]{1,0:T(8,128)(2,1)}, bf16[768,512]{1,0:T(8,128)(2,1)}, u32[]{:S(2)}, u32[]{:S(2)}) collective-permute-start(bf16[768,512]{1,0:T(8,128)(2,1)} %stack.1.r_2_), channel_id=1, source_target_pairs={{0,2},{1,3},{2,4},{3,5},{4,6},{5,7},{6,8},{7,9},{8,10},{9,11},{10,... | collective-permute-start | bytes 2359304 | tf_op jit(solution)/shard_map/ppermute | solution.py:347
  12.6 2.3 %pad_maximum_fusion.refs_9_ = bf16[768,768]{1,0:T(8,128)(2,1)} fusion(bf16[384,768]{1,0:T(8,128)(2,1)} %param.13, bf16[384,768]{1,0:T(8,128)(2,1)} %param.12), kind=kLoop, calls=%fused_computation.15 | loop fusion | flops 2359296 | bytes 2359296 | tf_op jit(solution)/shard_map/concatenate | solution.py:447
  14.9 8.7 %collective-permute-done = s32[3,9]{1,0:T(4,128)S(1)} collective-permute-done((s32[3,9]{1,0:T(4,128)S(1)}, s32[3,9]{1,0:T(4,128)S(1)}, u32[]{:S(2)}, u32[]{:S(2)}) %collective-permute-start) | collective-permute-done | bytes 140 | tf_op jit(solution)/shard_map/ppermute | solution.py:351
  25.0 4.3 %collective-permute-start.1 = (s32[6,9]{1,0:T(8,128)S(1)}, s32[6,9]{1,0:T(8,128)S(1)}, u32[]{:S(2)}, u32[]{:S(2)}) collective-permute-start(s32[6,9]{1,0:T(8,128)S(1)} %add_select_fusion.1), channel_id=1, source_target_pairs={{0,4},{2,6},{4,8},{6,10},{8,12},{10,14},{12,16},{14,18},{16,20},{1... | collective-permute-start | bytes 656 | tf_op jit(solution)/shard_map/ppermute | solution.py:416
  29.3 7.7 %fusion.3 = (f32[2048,768]{1,0:T(8,128)}, bf16[2048,768]{1,0:T(8,128)(2,1)S(1)}) fusion(f32[2048]{0:T(1024)S(1)} %copy-done.16, bf16[768,768]{1,0:T(8,128)(2,1)} %pad_maximum_fusion.refs_9_, bf16[2048,768]{1,0:T(8,128)(2,1)} %refs_3_.1), kind=kOutput, calls=%fused_computation.4 | convolution fusion | flops 2433220608 | bytes 13770752 | tf_op jit(solution)/shard_map/dot_general | solution.py:449
  37.0 2.1 %collective-permute-start.2 = (s32[6,9]{1,0:T(8,128)S(1)}, s32[6,9]{1,0:T(8,128)S(1)}, u32[]{:S(2)}, u32[]{:S(2)}) collective-permute-start(s32[6,9]{1,0:T(8,128)S(1)} %add_select_fusion.1), channel_id=1, source_target_pairs={{0,2},{1,3},{2,4},{3,5},{4,6},{5,7},{6,8},{7,9},{8,10},{9,11},{10,... | collective-permute-start | bytes 656 | tf_op jit(solution)/shard_map/ppermute | solution.py:347
  39.1 4.2 %collective-permute-start.7 = (bf16[768,512]{1,0:T(8,128)(2,1)}, bf16[768,512]{1,0:T(8,128)(2,1)}, u32[]{:S(2)}, u32[]{:S(2)}) collective-permute-start(bf16[768,512]{1,0:T(8,128)(2,1)} %collective-permute-done.6.r_5_), channel_id=1, source_target_pairs={{0,2},{2,4},{4,6},{6,8},{8,10},{10,12},{12,14},{14,16},{16,18},{18... | collective-permute-start | bytes 2359304 | tf_op jit(solution)/shard_map/ppermute | solution.py:412
  44.0 7.2 %tiles.1 = (bf16[15,128,512]{2,1,0:T(8,128)(2,1)S(1)}, bf16[15,512,128]{2,1,0:T(8,128)(2,1)S(1)}, f32[15,128,128]{2,1,0:T(8,128)S(1)}, f32[15,128,128]{2,1,0:T(8,128)S(1)}) custom-call(s32[84]{0:T(128)S(1)} %reshape.48.r_0_, s32[84]{0:T(128)S(1)} %reshape.49.r_1_, s32[21]{0:T(128)S(1)} %slice_reduce_fusion.1.r_2_), custom_call_target="tpu_custom_call" | custom-call | flops 1 | bytes 1 | tf_op jit(solution)/shard_map/tiles/pallas_call | solution.py:103
  51.3 1.3 copy-done.4
  57.1 1.5 %copy-done.5 = bf16[15,128,512]{2,1,0:T(8,128)(2,1)S(1)} copy-done((bf16[15,128,512]{2,1,0:T(8,128)(2,1)S(1)}, bf16[15,128,512]{2,1,0:T(8,128)(2,1)}, u32[]{:S(2)}) %copy-start.5) | copy-done | bytes 1966104
  58.7 1.5 %copy-done.7 = bf16[15,512,128]{2,1,0:T(8,128)(2,1)S(1)} copy-done((bf16[15,512,128]{2,1,0:T(8,128)(2,1)S(1)}, bf16[15,512,128]{2,1,0:T(8,128)(2,1)}, u32[]{:S(2)}) %copy-start.7) | copy-done | bytes 1966104
  62.6 10.3 %hops.1.refs_4_.refs_8_ = bf16[768,512]{1,0:T(8,128)(2,1)S(1)} custom-call(s32[60]{0:T(128)S(1)} %reshape.47.r_0_, s32[2]{0:T(128)S(1)} %fusion.20.r_1_, bf16[768,512]{1,0:T(8,128)(2,1)S(1)} %copy-done.3, bf16[768,512]{1,0:T(8,128)(2,1)} %collective-permute-done.4.r_3_, bf16[768,512]{1,0:T(8,128)(2,1)} %collective-permute-done.5.r_4_, ...), custom_call_target="tpu_custom_call" | custom-call | flops 1 | bytes 1 | tf_op jit(solution)/shard_map/hops/pallas_call | solution.py:211
  72.9 2.0 %part_out.2 = bf16[1024,512]{1,0:T(8,128)(2,1)S(1)} custom-call(s32[16]{0:T(128)S(1)} %get-tuple-element.79.order_ref, bf16[2048,768]{1,0:T(8,128)(2,1)S(1)} %get-tuple-element.34.refs_0_.refs_1_.refs_2_.refs_3_, bf16[2048,768]{1,0:T(8,128)(2,1)S(1)} %get-tuple-element.34.refs_0_.refs_1_.refs_2_.refs_3_, ...), custom_call_target="tpu_custom_call" | custom-call | flops 1 | bytes 1 | tf_op jit(solution)/shard_map/part_out/pallas_call | solution.py:295
  75.1 2.0 %part_out.3 = bf16[1024,512]{1,0:T(8,128)(2,1)S(1)} custom-call(s32[16]{0:T(128)S(1)} %get-tuple-element.80.order_ref, bf16[2048,768]{1,0:T(8,128)(2,1)S(1)} %get-tuple-element.34.refs_0_.refs_1_.refs_2_.refs_3_, bf16[2048,768]{1,0:T(8,128)(2,1)S(1)} %get-tuple-element.34.refs_0_.refs_1_.refs_2_.refs_3_, ...), custom_call_target="tpu_custom_call" | custom-call | flops 1 | bytes 1 | tf_op jit(solution)/shard_map/part_out/pallas_call | solution.py:295
  79.1 3.7 %part_in.2 = (bf16[1024,896]{1,0:T(8,128)(2,1)S(1)}, bf16[1024,768]{1,0:T(8,128)(2,1)S(1)}) custom-call(s32[16]{0:T(128)S(1)} %get-tuple-element.79.order_ref, f32[2048,768]{1,0:T(8,128)S(1)} %bitcast.90, f32[2048,768]{1,0:T(8,128)S(1)} %bitcast.90, f32[2048,768]{1,0:T(8,128)S(1)} %bitcast.90, f32[2048,768]{1,0:T(8,128)S(1)} %bitcast.90, ...), custom_call_target="tpu_custom_call" | custom-call | flops 1 | bytes 1 | tf_op jit(solution)/shard_map/part_in/pallas_call | solution.py:295
  84.4 3.7 %part_in.3 = (bf16[1024,896]{1,0:T(8,128)(2,1)S(1)}, bf16[1024,768]{1,0:T(8,128)(2,1)S(1)}) custom-call(s32[16]{0:T(128)S(1)} %get-tuple-element.80.order_ref, f32[2048,768]{1,0:T(8,128)S(1)} %bitcast.90, f32[2048,768]{1,0:T(8,128)S(1)} %bitcast.90, f32[2048,768]{1,0:T(8,128)S(1)} %bitcast.90, f32[2048,768]{1,0:T(8,128)S(1)} %bitcast.90, ...), custom_call_target="tpu_custom_call" | custom-call | flops 1 | bytes 1 | tf_op jit(solution)/shard_map/part_in/pallas_call | solution.py:295
  90.6 6.2 %feat_grad.1 = (bf16[384,768]{1,0:T(8,128)(2,1)}, bf16[384,768]{1,0:T(8,128)(2,1)}) custom-call(s32[32]{0:T(128)S(1)} %fusion.33.order_ref, bf16[2048,768]{1,0:T(8,128)(2,1)S(1)} %copy-done.1, bf16[2048,768]{1,0:T(8,128)(2,1)S(1)} %copy-done.1, bf16[2048,768]{1,0:T(8,128)(2,1)S(1)} %copy-done.1, bf16[2048,768]{1,0:T(8,128)(2,1)S(1)} %copy-done.1, ...), custom_call_target="tpu_custom_call" | custom-call | flops 1 | bytes 1 | tf_op jit(solution)/shard_map/feat_grad/pallas_call | solution.py:295
  98.8 5.0 %collective-permute-done.11 = bf16[2,2,2,64,512]{4,3,2,1,0:T(8,128)(2,1)S(1)} collective-permute-done((bf16[2,2,2,64,512]{4,3,2,1,0:T(8,128)(2,1)S(1)}, bf16[2,2,2,64,512]{4,3,2,1,0:T(8,128)(2,1)S(1)}, u32[]{:S(2)}, u32[]{:S(2)}) %collective-permute-start.11) | collective-permute-done | bytes 524320 | tf_op jit(solution)/shard_map/ppermute | solution.py:351
  103.9 3.9 %collective-permute-done.12 = bf16[2,2,2,64,384]{4,3,2,1,0:T(8,128)(2,1)S(1)} collective-permute-done((bf16[2,2,2,64,384]{4,3,2,1,0:T(8,128)(2,1)S(1)}, bf16[2,2,2,64,384]{4,3,2,1,0:T(8,128)(2,1)S(1)}, u32[]{:S(2)}, u32[]{:S(2)}) %collective-permute-start.12) | collective-permute-done | bytes 393248 | tf_op jit(solution)/shard_map/ppermute | solution.py:351
  108.4 1.6 %collective-permute-start.22 = (bf16[64,512]{1,0:T(8,128)(2,1)S(1)}, bf16[64,512]{1,0:T(8,128)(2,1)S(1)}, u32[]{:S(2)}, u32[]{:S(2)}) collective-permute-start(bf16[64,512]{1,0:T(8,128)(2,1)S(1)} %get-tuple-element.67), channel_id=1, source_target_pairs={{0,8},{1,9},{2,10},{3,11},{4,12},{5,13},{6,14},{7,15},{8,0},{9,1},... | collective-permute-start | bytes 196616 | tf_op jit(solution)/shard_map/ppermute | solution.py:351
  110.0 2.5 %collective-permute-start.24 = (bf16[64,512]{1,0:T(8,128)(2,1)S(1)}, bf16[64,512]{1,0:T(8,128)(2,1)S(1)}, u32[]{:S(2)}, u32[]{:S(2)}) collective-permute-start(bf16[64,512]{1,0:T(8,128)(2,1)S(1)} %get-tuple-element.68), channel_id=1, source_target_pairs={{0,24},{1,25},{2,26},{3,27},{4,28},{5,29},{6,30},{7,31},{8,16},{9,... | collective-permute-start | bytes 196616 | tf_op jit(solution)/shard_map/ppermute | solution.py:351
  113.6 1.8 %collective-permute-start.15 = (bf16[2,2,64,384]{3,2,1,0:T(8,128)(2,1)S(1)}, bf16[2,2,64,384]{3,2,1,0:T(8,128)(2,1)S(1)}, u32[]{:S(2)}, u32[]{:S(2)}) collective-permute-start(bf16[2,2,64,384]{3,2,1,0:T(8,128)(2,1)S(1)} %get-tuple-element.66), channel_id=1, source_target_pairs={{0,1},{1,0},{2,3},{3,2},{4,5},{5,4},{6,7},{7,6},{8,9},{9,8},{10,11... | collective-permute-start | bytes 589832 | tf_op jit(solution)/shard_map/ppermute | solution.py:351
  116.2 2.0 %collective-permute-done.23 = bf16[64,512]{1,0:T(8,128)(2,1)S(1)} collective-permute-done((bf16[64,512]{1,0:T(8,128)(2,1)S(1)}, bf16[64,512]{1,0:T(8,128)(2,1)S(1)}, u32[]{:S(2)}, u32[]{:S(2)}) %collective-permute-start.23) | collective-permute-done | bytes 65568 | tf_op jit(solution)/shard_map/ppermute | solution.py:351
  119.5 1.9 %collective-permute-start.16 = (bf16[64,384]{1,0:T(8,128)(2,1)S(1)}, bf16[64,384]{1,0:T(8,128)(2,1)S(1)}, u32[]{:S(2)}, u32[]{:S(2)}) collective-permute-start(bf16[64,384]{1,0:T(8,128)(2,1)S(1)} %get-tuple-element.73), channel_id=1, source_target_pairs={{0,8},{1,9},{2,10},{3,11},{4,12},{5,13},{6,14},{7,15},{8,0},{9,1},... | collective-permute-start | bytes 147464 | tf_op jit(solution)/shard_map/ppermute | solution.py:351
  121.3 2.5 %collective-permute-start.18 = (bf16[64,384]{1,0:T(8,128)(2,1)S(1)}, bf16[64,384]{1,0:T(8,128)(2,1)S(1)}, u32[]{:S(2)}, u32[]{:S(2)}) collective-permute-start(bf16[64,384]{1,0:T(8,128)(2,1)S(1)} %get-tuple-element.74), channel_id=1, source_target_pairs={{0,24},{1,25},{2,26},{3,27},{4,28},{5,29},{6,30},{7,31},{8,16},{9,... | collective-permute-start | bytes 147464 | tf_op jit(solution)/shard_map/ppermute | solution.py:351
  123.8 2.0 %collective-permute-start.19 = (bf16[64,512]{1,0:T(8,128)(2,1)S(1)}, bf16[64,512]{1,0:T(8,128)(2,1)S(1)}, u32[]{:S(2)}, u32[]{:S(2)}) collective-permute-start(bf16[64,512]{1,0:T(8,128)(2,1)S(1)} %get-tuple-element.70), channel_id=1, source_target_pairs={{0,8},{1,9},{2,10},{3,11},{4,12},{5,13},{6,14},{7,15},{8,0},{9,1},... | collective-permute-start | bytes 196616 | tf_op jit(solution)/shard_map/ppermute | solution.py:351
  125.8 2.5 %collective-permute-start.21 = (bf16[64,512]{1,0:T(8,128)(2,1)S(1)}, bf16[64,512]{1,0:T(8,128)(2,1)S(1)}, u32[]{:S(2)}, u32[]{:S(2)}) collective-permute-start(bf16[64,512]{1,0:T(8,128)(2,1)S(1)} %get-tuple-element.71), channel_id=1, source_target_pairs={{0,24},{1,25},{2,26},{3,27},{4,28},{5,29},{6,30},{7,31},{8,16},{9,... | collective-permute-start | bytes 196616 | tf_op jit(solution)/shard_map/ppermute | solution.py:351
  128.3 2.0 %collective-permute-done.17 = bf16[64,384]{1,0:T(8,128)(2,1)S(1)} collective-permute-done((bf16[64,384]{1,0:T(8,128)(2,1)S(1)}, bf16[64,384]{1,0:T(8,128)(2,1)S(1)}, u32[]{:S(2)}, u32[]{:S(2)}) %collective-permute-start.17) | collective-permute-done | bytes 49184 | tf_op jit(solution)/shard_map/ppermute | solution.py:351
  130.3 1.6 %collective-permute-done.21 = bf16[64,512]{1,0:T(8,128)(2,1)S(1)} collective-permute-done((bf16[64,512]{1,0:T(8,128)(2,1)S(1)}, bf16[64,512]{1,0:T(8,128)(2,1)S(1)}, u32[]{:S(2)}, u32[]{:S(2)}) %collective-permute-start.21) | collective-permute-done | bytes 65568 | tf_op jit(solution)/shard_map/ppermute | solution.py:351
  131.8 1.6 %collective-permute-done.20 = bf16[64,512]{1,0:T(8,128)(2,1)S(1)} collective-permute-done((bf16[64,512]{1,0:T(8,128)(2,1)S(1)}, bf16[64,512]{1,0:T(8,128)(2,1)S(1)}, u32[]{:S(2)}, u32[]{:S(2)}) %collective-permute-start.20) | collective-permute-done | bytes 65568 | tf_op jit(solution)/shard_map/ppermute | solution.py:351
  (105 shorter events, 24.9 us)
Async XLA Ops:
  0.6 14.3 %copy-start.14 = (s32[2]{0:T(128)S(1)}, s32[2]{0:T(128)}, u32[]{:S(2)}) copy-start(s32[2]{0:T(128)} %constant.14.clone) | copy-start | bytes 28
  0.6 14.3 %copy-start.15 = (s32[2]{0:T(128)S(1)}, s32[2]{0:T(128)}, u32[]{:S(2)}) copy-start(s32[2]{0:T(128)} %constant.13.clone) | copy-start | bytes 28
  0.7 22.9 %copy-start.12 = (s32[3,4]{1,0:T(4,128)S(1)}, s32[3,4]{1,0:T(4,128)}, u32[]{:S(2)}) copy-start(s32[3,4]{1,0:T(4,128)} %param.20) | copy-start | bytes 148
  0.7 22.9 %copy-start.13 = (s32[3,4]{1,0:T(4,128)S(1)}, s32[3,4]{1,0:T(4,128)}, u32[]{:S(2)}) copy-start(s32[3,4]{1,0:T(4,128)} %param.19) | copy-start | bytes 148
  0.7 28.6 %copy-start.16 = (f32[2048]{0:T(1024)S(1)}, f32[2048]{0:T(1024)}, u32[]{:S(2)}) copy-start(f32[2048]{0:T(1024)} %param.17) | copy-start | bytes 24580
  2.8 36.4 %collective-permute-start.6 = (bf16[768,512]{1,0:T(8,128)(2,1)}, bf16[768,512]{1,0:T(8,128)(2,1)}, u32[]{:S(2)}, u32[]{:S(2)}) collective-permute-start(bf16[768,512]{1,0:T(8,128)(2,1)} %stack.1.r_2_), channel_id=1, source_target_pairs={{0,1},{1,0},{2,3},{3,2},{4,5},{5,4},{6,7},{7,6},{8,9},{9,8},{10,11... | collective-permute-start | bytes 2359304 | tf_op jit(solution)/shard_map/ppermute | solution.py:351
  5.7 50.2 %collective-permute-start.5 = (bf16[768,512]{1,0:T(8,128)(2,1)}, bf16[768,512]{1,0:T(8,128)(2,1)}, u32[]{:S(2)}, u32[]{:S(2)}) collective-permute-start(bf16[768,512]{1,0:T(8,128)(2,1)} %stack.1.r_2_), channel_id=1, source_target_pairs={{2,0},{3,1},{4,2},{5,3},{6,4},{7,5},{8,6},{9,7},{10,8},{11,9},{12,... | collective-permute-start | bytes 2359304 | tf_op jit(solution)/shard_map/ppermute | solution.py:347
  7.0 49.0 %collective-permute-start.4 = (bf16[768,512]{1,0:T(8,128)(2,1)}, bf16[768,512]{1,0:T(8,128)(2,1)}, u32[]{:S(2)}, u32[]{:S(2)}) collective-permute-start(bf16[768,512]{1,0:T(8,128)(2,1)} %stack.1.r_2_), channel_id=1, source_target_pairs={{0,2},{1,3},{2,4},{3,5},{4,6},{5,7},{6,8},{7,9},{8,10},{9,11},{10,... | collective-permute-start | bytes 2359304 | tf_op jit(solution)/shard_map/ppermute | solution.py:347
  12.5 11.1 %collective-permute-start = (s32[3,9]{1,0:T(4,128)S(1)}, s32[3,9]{1,0:T(4,128)S(1)}, u32[]{:S(2)}, u32[]{:S(2)}) collective-permute-start(s32[3,9]{1,0:T(4,128)S(1)} %pad_add_fusion), channel_id=1, source_target_pairs={{0,1},{1,0},{2,3},{3,2},{4,5},{5,4},{6,7},{7,6},{8,9},{9,8},{10,11... | collective-permute-start | bytes 332 | tf_op jit(solution)/shard_map/ppermute | solution.py:351
  23.7 19.7 %collective-permute-start.3 = (s32[6,9]{1,0:T(8,128)S(1)}, s32[6,9]{1,0:T(8,128)S(1)}, u32[]{:S(2)}, u32[]{:S(2)}) collective-permute-start(s32[6,9]{1,0:T(8,128)S(1)} %add_select_fusion.1), channel_id=1, source_target_pairs={{2,0},{3,1},{4,2},{5,3},{6,4},{7,5},{8,6},{9,7},{10,8},{11,9},{12,... | collective-permute-start | bytes 656 | tf_op jit(solution)/shard_map/ppermute | solution.py:347
  25.0 12.0 %collective-permute-start.1 = (s32[6,9]{1,0:T(8,128)S(1)}, s32[6,9]{1,0:T(8,128)S(1)}, u32[]{:S(2)}, u32[]{:S(2)}) collective-permute-start(s32[6,9]{1,0:T(8,128)S(1)} %add_select_fusion.1), channel_id=1, source_target_pairs={{0,4},{2,6},{4,8},{6,10},{8,12},{10,14},{12,16},{14,18},{16,20},{1... | collective-permute-start | bytes 656 | tf_op jit(solution)/shard_map/ppermute | solution.py:416
  37.0 6.4 %collective-permute-start.2 = (s32[6,9]{1,0:T(8,128)S(1)}, s32[6,9]{1,0:T(8,128)S(1)}, u32[]{:S(2)}, u32[]{:S(2)}) collective-permute-start(s32[6,9]{1,0:T(8,128)S(1)} %add_select_fusion.1), channel_id=1, source_target_pairs={{0,2},{1,3},{2,4},{3,5},{4,6},{5,7},{6,8},{7,9},{8,10},{9,11},{10,... | collective-permute-start | bytes 656 | tf_op jit(solution)/shard_map/ppermute | solution.py:347
  39.1 16.8 %collective-permute-start.7 = (bf16[768,512]{1,0:T(8,128)(2,1)}, bf16[768,512]{1,0:T(8,128)(2,1)}, u32[]{:S(2)}, u32[]{:S(2)}) collective-permute-start(bf16[768,512]{1,0:T(8,128)(2,1)} %collective-permute-done.6.r_5_), channel_id=1, source_target_pairs={{0,2},{2,4},{4,6},{6,8},{8,10},{10,12},{12,14},{14,16},{16,18},{18... | collective-permute-start | bytes 2359304 | tf_op jit(solution)/shard_map/ppermute | solution.py:412
  75.0 2.7 %collective-permute-start.8 = (bf16[2,2,2,2,64,512]{5,4,3,2,1,0:T(8,128)(2,1)S(1)}, bf16[2,2,2,2,64,512]{5,4,3,2,1,0:T(8,128)(2,1)S(1)}, u32[]{:S(2)}, u32[]{:S(2)}) collective-permute-start(bf16[2,2,2,2,64,512]{5,4,3,2,1,0:T(8,128)(2,1)S(1)} %bitcast.93), channel_id=1, source_target_pairs={{0,2},{1,3},{2,0},{3,1},{4,6},{5,7},{6,4},{7,5},{8,10},{9,11},{10,... | collective-permute-start | bytes 3145736 | tf_op jit(solution)/shard_map/ppermute | solution.py:351
  75.1 3.0 %slice-start = ((s8[6291456]{0:T(1024)(128)(4,1)}), s8[4194304]{0:T(1024)(128)(4,1)S(1)}, s32[]{:S(2)}) async-start(s8[6291456]{0:T(1024)(128)(4,1)} %bitcast.89), calls=%async_computation | async-start | bytes 8388608
  75.1 3.1 %copy-start.2 = (bf16[768,768]{1,0:T(8,128)(2,1)S(1)}, bf16[768,768]{1,0:T(8,128)(2,1)}, u32[]{:S(2)}) copy-start(bf16[768,768]{1,0:T(8,128)(2,1)} %pad_maximum_fusion.refs_9_) | copy-start | bytes 3538948
  82.8 5.3 %collective-permute-start.9 = (bf16[2,2,2,2,64,896]{5,4,3,2,1,0:T(8,128)(2,1)S(1)}, bf16[2,2,2,2,64,896]{5,4,3,2,1,0:T(8,128)(2,1)S(1)}, u32[]{:S(2)}, u32[]{:S(2)}) collective-permute-start(bf16[2,2,2,2,64,896]{5,4,3,2,1,0:T(8,128)(2,1)S(1)} %bitcast.94), channel_id=1, source_target_pairs={{0,2},{1,3},{2,0},{3,1},{4,6},{5,7},{6,4},{7,5},{8,10},{9,11},{10,... | collective-permute-start | bytes 5505032 | tf_op jit(solution)/shard_map/ppermute | solution.py:351
  83.5 14.6 %collective-permute-start.10 = (bf16[2,2,2,64,512]{4,3,2,1,0:T(8,128)(2,1)S(1)}, bf16[2,2,2,64,512]{4,3,2,1,0:T(8,128)(2,1)S(1)}, u32[]{:S(2)}, u32[]{:S(2)}) collective-permute-start(bf16[2,2,2,64,512]{4,3,2,1,0:T(8,128)(2,1)S(1)} %get-tuple-element.60), channel_id=1, source_target_pairs={{0,4},{1,5},{2,6},{3,7},{4,0},{5,1},{6,2},{7,3},{8,12},{9,13},{10,... | collective-permute-start | bytes 1572872 | tf_op jit(solution)/shard_map/ppermute | solution.py:351
  88.9 14.9 %collective-permute-start.11 = (bf16[2,2,2,64,512]{4,3,2,1,0:T(8,128)(2,1)S(1)}, bf16[2,2,2,64,512]{4,3,2,1,0:T(8,128)(2,1)S(1)}, u32[]{:S(2)}, u32[]{:S(2)}) collective-permute-start(bf16[2,2,2,64,512]{4,3,2,1,0:T(8,128)(2,1)S(1)} %get-tuple-element.58), channel_id=1, source_target_pairs={{0,1},{1,0},{2,3},{3,2},{4,5},{5,4},{6,7},{7,6},{8,9},{9,8},{10,11... | collective-permute-start | bytes 1572872 | tf_op jit(solution)/shard_map/ppermute | solution.py:351
  96.9 11.0 %collective-permute-start.12 = (bf16[2,2,2,64,384]{4,3,2,1,0:T(8,128)(2,1)S(1)}, bf16[2,2,2,64,384]{4,3,2,1,0:T(8,128)(2,1)S(1)}, u32[]{:S(2)}, u32[]{:S(2)}) collective-permute-start(bf16[2,2,2,64,384]{4,3,2,1,0:T(8,128)(2,1)S(1)} %get-tuple-element.56), channel_id=1, source_target_pairs={{0,4},{1,5},{2,6},{3,7},{4,0},{5,1},{6,2},{7,3},{8,12},{9,13},{10,... | collective-permute-start | bytes 1179656 | tf_op jit(solution)/shard_map/ppermute | solution.py:351
  98.2 10.1 %collective-permute-start.13 = (bf16[2,2,64,512]{3,2,1,0:T(8,128)(2,1)S(1)}, bf16[2,2,64,512]{3,2,1,0:T(8,128)(2,1)S(1)}, u32[]{:S(2)}, u32[]{:S(2)}) collective-permute-start(bf16[2,2,64,512]{3,2,1,0:T(8,128)(2,1)S(1)} %get-tuple-element.62), channel_id=1, source_target_pairs={{0,1},{1,0},{2,3},{3,2},{4,5},{5,4},{6,7},{7,6},{8,9},{9,8},{10,11... | collective-permute-start | bytes 786440 | tf_op jit(solution)/shard_map/ppermute | solution.py:351
  108.4 7.0 %collective-permute-start.22 = (bf16[64,512]{1,0:T(8,128)(2,1)S(1)}, bf16[64,512]{1,0:T(8,128)(2,1)S(1)}, u32[]{:S(2)}, u32[]{:S(2)}) collective-permute-start(bf16[64,512]{1,0:T(8,128)(2,1)S(1)} %get-tuple-element.67), channel_id=1, source_target_pairs={{0,8},{1,9},{2,10},{3,11},{4,12},{5,13},{6,14},{7,15},{8,0},{9,1},... | collective-permute-start | bytes 196616 | tf_op jit(solution)/shard_map/ppermute | solution.py:351
  110.0 6.1 %collective-permute-start.24 = (bf16[64,512]{1,0:T(8,128)(2,1)S(1)}, bf16[64,512]{1,0:T(8,128)(2,1)S(1)}, u32[]{:S(2)}, u32[]{:S(2)}) collective-permute-start(bf16[64,512]{1,0:T(8,128)(2,1)S(1)} %get-tuple-element.68), channel_id=1, source_target_pairs={{0,24},{1,25},{2,26},{3,27},{4,28},{5,29},{6,30},{7,31},{8,16},{9,... | collective-permute-start | bytes 196616 | tf_op jit(solution)/shard_map/ppermute | solution.py:351
  112.5 5.6 %collective-permute-start.23 = (bf16[64,512]{1,0:T(8,128)(2,1)S(1)}, bf16[64,512]{1,0:T(8,128)(2,1)S(1)}, u32[]{:S(2)}, u32[]{:S(2)}) collective-permute-start(bf16[64,512]{1,0:T(8,128)(2,1)S(1)} %get-tuple-element.69), channel_id=1, source_target_pairs={{0,16},{1,17},{2,18},{3,19},{4,20},{5,21},{6,22},{7,23},{8,24},{9,... | collective-permute-start | bytes 196616 | tf_op jit(solution)/shard_map/ppermute | solution.py:351
  112.5 6.7 %collective-permute-start.14 = (bf16[2,2,64,512]{3,2,1,0:T(8,128)(2,1)S(1)}, bf16[2,2,64,512]{3,2,1,0:T(8,128)(2,1)S(1)}, u32[]{:S(2)}, u32[]{:S(2)}) collective-permute-start(bf16[2,2,64,512]{3,2,1,0:T(8,128)(2,1)S(1)} %get-tuple-element.64), channel_id=1, source_target_pairs={{0,4},{1,5},{2,6},{3,7},{4,0},{5,1},{6,2},{7,3},{8,12},{9,13},{10,... | collective-permute-start | bytes 786440 | tf_op jit(solution)/shard_map/ppermute | solution.py:351
  113.6 5.7 %collective-permute-start.15 = (bf16[2,2,64,384]{3,2,1,0:T(8,128)(2,1)S(1)}, bf16[2,2,64,384]{3,2,1,0:T(8,128)(2,1)S(1)}, u32[]{:S(2)}, u32[]{:S(2)}) collective-permute-start(bf16[2,2,64,384]{3,2,1,0:T(8,128)(2,1)S(1)} %get-tuple-element.66), channel_id=1, source_target_pairs={{0,1},{1,0},{2,3},{3,2},{4,5},{5,4},{6,7},{7,6},{8,9},{9,8},{10,11... | collective-permute-start | bytes 589832 | tf_op jit(solution)/shard_map/ppermute | solution.py:351
  119.5 8.8 %collective-permute-start.16 = (bf16[64,384]{1,0:T(8,128)(2,1)S(1)}, bf16[64,384]{1,0:T(8,128)(2,1)S(1)}, u32[]{:S(2)}, u32[]{:S(2)}) collective-permute-start(bf16[64,384]{1,0:T(8,128)(2,1)S(1)} %get-tuple-element.73), channel_id=1, source_target_pairs={{0,8},{1,9},{2,10},{3,11},{4,12},{5,13},{6,14},{7,15},{8,0},{9,1},... | collective-permute-start | bytes 147464 | tf_op jit(solution)/shard_map/ppermute | solution.py:351
  121.3 7.0 %collective-permute-start.18 = (bf16[64,384]{1,0:T(8,128)(2,1)S(1)}, bf16[64,384]{1,0:T(8,128)(2,1)S(1)}, u32[]{:S(2)}, u32[]{:S(2)}) collective-permute-start(bf16[64,384]{1,0:T(8,128)(2,1)S(1)} %get-tuple-element.74), channel_id=1, source_target_pairs={{0,24},{1,25},{2,26},{3,27},{4,28},{5,29},{6,30},{7,31},{8,16},{9,... | collective-permute-start | bytes 147464 | tf_op jit(solution)/shard_map/ppermute | solution.py:351
  123.8 6.5 %collective-permute-start.17 = (bf16[64,384]{1,0:T(8,128)(2,1)S(1)}, bf16[64,384]{1,0:T(8,128)(2,1)S(1)}, u32[]{:S(2)}, u32[]{:S(2)}) collective-permute-start(bf16[64,384]{1,0:T(8,128)(2,1)S(1)} %get-tuple-element.75), channel_id=1, source_target_pairs={{0,16},{1,17},{2,18},{3,19},{4,20},{5,21},{6,22},{7,23},{8,24},{9,... | collective-permute-start | bytes 147464 | tf_op jit(solution)/shard_map/ppermute | solution.py:351
  123.8 6.5 %collective-permute-start.19 = (bf16[64,512]{1,0:T(8,128)(2,1)S(1)}, bf16[64,512]{1,0:T(8,128)(2,1)S(1)}, u32[]{:S(2)}, u32[]{:S(2)}) collective-permute-start(bf16[64,512]{1,0:T(8,128)(2,1)S(1)} %get-tuple-element.70), channel_id=1, source_target_pairs={{0,8},{1,9},{2,10},{3,11},{4,12},{5,13},{6,14},{7,15},{8,0},{9,1},... | collective-permute-start | bytes 196616 | tf_op jit(solution)/shard_map/ppermute | solution.py:351
  125.8 6.1 %collective-permute-start.21 = (bf16[64,512]{1,0:T(8,128)(2,1)S(1)}, bf16[64,512]{1,0:T(8,128)(2,1)S(1)}, u32[]{:S(2)}, u32[]{:S(2)}) collective-permute-start(bf16[64,512]{1,0:T(8,128)(2,1)S(1)} %get-tuple-element.71), channel_id=1, source_target_pairs={{0,24},{1,25},{2,26},{3,27},{4,28},{5,29},{6,30},{7,31},{8,16},{9,... | collective-permute-start | bytes 196616 | tf_op jit(solution)/shard_map/ppermute | solution.py:351
  128.3 5.2 %collective-permute-start.20 = (bf16[64,512]{1,0:T(8,128)(2,1)S(1)}, bf16[64,512]{1,0:T(8,128)(2,1)S(1)}, u32[]{:S(2)}, u32[]{:S(2)}) collective-permute-start(bf16[64,512]{1,0:T(8,128)(2,1)S(1)} %get-tuple-element.72), channel_id=1, source_target_pairs={{0,16},{1,17},{2,18},{3,19},{4,20},{5,21},{6,22},{7,23},{8,24},{9,... | collective-permute-start | bytes 196616 | tf_op jit(solution)/shard_map/ppermute | solution.py:351
  (12 other events, 18.1 us)

commit v5 on v4

--- a/solution.py
+++ b/solution.py
@@ -102,7 +102,7 @@
     tables = table_shapes(tiles, slots)
     return pl.pallas_call(
         lambda *r: tiles_kernel(*r, tiles=tiles, slots=slots),
-        out_shape=tuple(jax.ShapeDtypeStruct(*t) for t in tables),
+        out_shape=tuple(pltpu.HBM(*t) for t in tables),
         in_specs=[smem] * 3,
         out_specs=(hbm,) * 4,
         scratch_shapes=[pltpu.VMEM(*t) for t in tables]
@@ -229,7 +229,7 @@
         compiler_params=pltpu.CompilerParams(vmem_limit_bytes=34 << 20),
         cost_estimate=SHORT,
         name="hops",
-    )(places, bases, own, low, high, mate, far, *tables)
+    )(places, bases, *[pltpu.with_memory_space_constraint(v, pltpu.HBM) for v in (own, low, high, mate, far, *tables)])
 
 
 BLOCK = 64
@@ -321,22 +321,32 @@
     return pl.BlockSpec((GROUP * BLOCK, width), lambda i, order: (i, 0))
 
 
-def stack_kernel(top_ref, bottom_ref, out_ref):
+def stack_kernel(count_ref, top_ref, bottom_ref, seed_ref, cols_ref, out_ref, meta_ref):
     half = top_ref.shape[0]
     out_ref[:half] = top_ref[...]
     out_ref[half:] = bottom_ref[...]
-
-
-def stack(top, bottom):
+    tiles, slots = seed_ref.shape
+    meta_ref[:, :slots] = seed_ref[...]
+    meta_ref[:, slots : 2 * slots] = cols_ref[...]
+    row = lax.broadcasted_iota(jnp.int32, (tiles, slots), 0)
+    live = jnp.zeros((tiles, slots), jnp.int32)
+    for t in range(tiles):
+        live = jnp.where(row == t, count_ref[t], live)
+    meta_ref[:, 2 * slots :] = live
+
+
+def stack(top, bottom, seed, cols, counts):
     vmem = pl.BlockSpec(memory_space=pltpu.VMEM)
+    shape = (2 * top.shape[0], top.shape[1])
+    codes = (seed.shape[0], 3 * seed.shape[1])
     return pl.pallas_call(
         stack_kernel,
-        out_shape=jax.ShapeDtypeStruct((2 * top.shape[0], top.shape[1]), top.dtype),
-        in_specs=[vmem] * 2,
-        out_specs=vmem,
+        out_shape=(pltpu.HBM(shape, top.dtype), jax.ShapeDtypeStruct(codes, jnp.int32)),
+        in_specs=[pl.BlockSpec(memory_space=pltpu.SMEM)] + [vmem] * 4,
+        out_specs=(pl.BlockSpec(shape, lambda: (0, 0)), pl.BlockSpec(codes, lambda: (0, 0))),
         cost_estimate=SHORT,
         name="stack",
-    )(top, bottom)
+    )(counts, top, bottom, seed, cols)
 
 
 def after(value, *done):
@@ -403,14 +413,16 @@
     me = lax.axis_index(AXES)
 
     even = (me & 1) == 0
-    meta = jnp.concatenate([tile_seed, tile_cols, tile_count[:, None]], axis=1)
+    block, meta = stack(cot_img, cot_cap, tile_seed, tile_cols, tile_count)
     other = flipped(meta, count, 1)
-    block = stack(cot_img, cot_cap)
+    block = after(block, other)
     mate = flipped(block, count, 1)
     low = moved(block, count, 2)
     high = moved(block, count, -2)
     far = lax.ppermute(mate, AXES, nearest_pair(count, 2))
     pair = jnp.where(even, jnp.concatenate([meta, other]), jnp.concatenate([other, meta]))
+    feats = jnp.concatenate([feats_img, feats_cap], axis=0)
+    pair, feats = lax.optimization_barrier((pair, after(feats, block)))
     pair_low = moved(pair, count, 2)
     pair_high = moved(pair, count, -2)
     pair_far = lax.ppermute(pair, AXES, nearest_pair(count, 4))
@@ -444,7 +456,6 @@
     else:
         order = (order[:, None] * (rows // BLOCK) + jnp.arange(rows // BLOCK, dtype=jnp.int32)).reshape(-1)
 
-    feats = after(jnp.concatenate([feats_img, feats_cap], axis=0), pair)
     across = (((1,), (1,)), ((), ()))
     preact = lax.dot_general(w_in, feats, across, preferred_element_type=F32) + b_in[:, None]
     gelu_value, gelu_slope = gelu_parts(preact)

time: 135 us -> 123 us (0.911)
  local copies, waits for them, and re-layouts: 15.3 us -> 3 us
  waiting for transfers between devices: 26.8 us -> 19.2 us
  starting transfers between devices: 40.1 us -> 46.5 us
  Pallas kernels: 37.5 us -> 39.4 us
    unnamed x38 -> x16, local copies, waits for them, and re-layouts: 13 us -> 1.43 us
    ppermute x19, waiting for transfers between devices: 26.8 us -> 19.2 us  [flipped(): return lax.ppermute(array, AXES, [(i, i ^ mask) for i in range(count)])]
    ppermute x19, starting transfers between devices: 22.9 us -> 28.3 us  [flipped(): return lax.ppermute(array, AXES, [(i, i ^ mask) for i in range(count)])]
    ppermute x4, starting transfers between devices: 8.61 us -> 10.3 us  [moved(): lax.ppermute(array, AXES, [(i, i + by) for i in range(count) if 0 <= i +...]
    concatenate x2 -> x1, other arithmetic: 3.11 us -> 2.34 us  [per_device(): feats = jnp.concatenate([feats_img, feats_cap], axis=0)]
  transfers between devices with their start and end apart: 25 -> 25, of which waited for: 12 -> 10; matrix products, arithmetic and copies ran while one was open for 11% -> 11% of each run, Pallas kernels for 14% -> 16%
where the time goes in v5:
time: 123 us
  starting transfers between devices  46.5 us (38%)
  Pallas kernels  39.4 us (32%)
  waiting for transfers between devices  19.2 us (16%)
  matrix products  7.74 us (6%)
  other arithmetic  6.34 us (5%)
  local copies, waits for them, and re-layouts  3 us (2%)
    ppermute x19, starting transfers between devices, flipped(): return lax.ppermute(array, AXES, [(i, i ^ mask) for i in range(count)])  28.3 us
    ppermute x19, waiting for transfers between devices, flipped(): return lax.ppermute(array, AXES, [(i, i ^ mask) for i in range(count)])  19.2 us
    pallas_call x5, Pallas kernels, over_hidden(): pl.pallas_call(kernel, out_shape=out_shape, grid_spec=pltpu.PrefetchScala...  17.9 us
    pallas_call x1, Pallas kernels, propagate(): pl.pallas_call(lambda *r: hops_kernel(*r, tiles=tiles, slots=slots, width...  11.6 us
    ppermute x4, starting transfers between devices, moved(): lax.ppermute(array, AXES, [(i, i + by) for i in range(count) if 0 <= i +...  10.3 us
    pallas_call x1, Pallas kernels, make_tiles(): pl.pallas_call(lambda *r: tiles_kernel(*r, tiles=tiles, slots=slots), out...  7.8 us
    dot_general x1, matrix products, per_device(): lax.dot_general(w_in, feats, across, preferred_element_type=F32)  7.74 us
    ppermute x1, starting transfers between devices, per_device(): pair_far = lax.ppermute(pair, AXES, nearest_pair(count, 4))  4.4 us
  transfers between devices with their start and end apart: 25, of which 10 were waited for; matrix products, arithmetic and copies ran while one was open for 11% of the time, Pallas kernels for 16%

profile of v5, /device:TPU:0, one launch (start us, length us, event | category | flops | bytes accessed | tf_op | source)
XLA Modules:
  0.0 123.1 jit_solution(15697869717643948223)
XLA Ops:
  0.7 2.1 %stack.1 = (bf16[768,512]{1,0:T(8,128)(2,1)}, s32[3,12]{1,0:T(4,128)}) custom-call(s32[3]{0:T(128)} %count_ref.1, bf16[384,512]{1,0:T(8,128)(2,1)} %top_ref.1, bf16[384,512]{1,0:T(8,128)(2,1)} %bottom_ref.1, s32[3,4]{1,0:T(4,128)} %seed_ref.1, s32[3,4]{1,0:T(4,128)} %cols_ref.1), custom_call_target="tpu_custom_call" | custom-call | flops 1 | bytes 1 | tf_op jit(solution)/shard_map/stack/pallas_call | solution.py:342
  2.7 2.9 %collective-permute-start = (s32[3,12]{1,0:T(4,128)}, s32[3,12]{1,0:T(4,128)S(1)}, u32[]{:S(2)}, u32[]{:S(2)}) collective-permute-start(s32[3,12]{1,0:T(4,128)} %get-tuple-element.33), channel_id=1, source_target_pairs={{0,1},{1,0},{2,3},{3,2},{4,5},{5,4},{6,7},{7,6},{8,9},{9,8},{10,11... | collective-permute-start | bytes 440 | tf_op jit(solution)/shard_map/ppermute | solution.py:361
  5.8 2.3 %pad_maximum_fusion.refs_9_ = bf16[768,768]{1,0:T(8,128)(2,1)} fusion(bf16[384,768]{1,0:T(8,128)(2,1)} %param.13, bf16[384,768]{1,0:T(8,128)(2,1)} %param.12), kind=kLoop, calls=%fused_computation.15 | loop fusion | flops 2359296 | bytes 2359296 | tf_op jit(solution)/shard_map/concatenate | solution.py:424
  10.7 3.9 %collective-permute-start.4 = (bf16[768,512]{1,0:T(8,128)(2,1)}, bf16[768,512]{1,0:T(8,128)(2,1)}, u32[]{:S(2)}, u32[]{:S(2)}) collective-permute-start(bf16[768,512]{1,0:T(8,128)(2,1)} %get-tuple-element.35.r_2_), channel_id=1, source_target_pairs={{0,2},{1,3},{2,4},{3,5},{4,6},{5,7},{6,8},{7,9},{8,10},{9,11},{10,... | collective-permute-start | bytes 2359304 | tf_op jit(solution)/shard_map/ppermute | solution.py:357
  16.7 4.4 %collective-permute-start.1 = (s32[6,12]{1,0:T(8,128)S(1)}, s32[6,12]{1,0:T(8,128)S(1)}, u32[]{:S(2)}, u32[]{:S(2)}) collective-permute-start(s32[6,12]{1,0:T(8,128)S(1)} %add_select_fusion.1), channel_id=1, source_target_pairs={{0,4},{2,6},{4,8},{6,10},{8,12},{10,14},{12,16},{14,18},{16,20},{1... | collective-permute-start | bytes 872 | tf_op jit(solution)/shard_map/ppermute | solution.py:428
  21.2 7.7 %fusion.3 = (f32[2048,768]{1,0:T(8,128)}, bf16[2048,768]{1,0:T(8,128)(2,1)S(1)}) fusion(f32[2048]{0:T(1024)S(1)} %copy-done.5, bf16[768,768]{1,0:T(8,128)(2,1)} %pad_maximum_fusion.refs_9_, bf16[2048,768]{1,0:T(8,128)(2,1)} %refs_3_.1), kind=kOutput, calls=%fused_computation.4 | convolution fusion | flops 2433220608 | bytes 13770752 | tf_op jit(solution)/shard_map/dot_general | solution.py:460
  28.9 3.8 %collective-permute-start.2 = (s32[6,12]{1,0:T(8,128)S(1)}, s32[6,12]{1,0:T(8,128)S(1)}, u32[]{:S(2)}, u32[]{:S(2)}) collective-permute-start(s32[6,12]{1,0:T(8,128)S(1)} %add_select_fusion.1), channel_id=1, source_target_pairs={{0,2},{1,3},{2,4},{3,5},{4,6},{5,7},{6,8},{7,9},{8,10},{9,11},{10,... | collective-permute-start | bytes 872 | tf_op jit(solution)/shard_map/ppermute | solution.py:357
  32.7 3.4 %collective-permute-start.7 = (bf16[768,512]{1,0:T(8,128)(2,1)}, bf16[768,512]{1,0:T(8,128)(2,1)}, u32[]{:S(2)}, u32[]{:S(2)}) collective-permute-start(bf16[768,512]{1,0:T(8,128)(2,1)} %collective-permute-done.6.r_5_), channel_id=1, source_target_pairs={{0,2},{2,4},{4,6},{6,8},{8,10},{10,12},{12,14},{14,16},{16,18},{18... | collective-permute-start | bytes 2359304 | tf_op jit(solution)/shard_map/ppermute | solution.py:422
  36.8 7.8 %tiles.1 = (bf16[15,128,512]{2,1,0:T(8,128)(2,1)}, bf16[15,512,128]{2,1,0:T(8,128)(2,1)}, f32[15,128,128]{2,1,0:T(8,128)}, f32[15,128,128]{2,1,0:T(8,128)}) custom-call(s32[84]{0:T(128)S(1)} %reshape.48.r_0_, s32[84]{0:T(128)S(1)} %reshape.49.r_1_, s32[21]{0:T(128)S(1)} %slice_reduce_fusion.1.r_2_), custom_call_target="tpu_custom_call" | custom-call | flops 1 | bytes 1 | tf_op jit(solution)/shard_map/tiles/pallas_call | solution.py:103
  44.8 11.6 %hops.1.refs_4_.refs_8_ = bf16[768,512]{1,0:T(8,128)(2,1)S(1)} custom-call(s32[60]{0:T(128)S(1)} %reshape.47.r_0_, s32[2]{0:T(128)S(1)} %fusion.20.r_1_, bf16[768,512]{1,0:T(8,128)(2,1)} %get-tuple-element.35.r_2_, bf16[768,512]{1,0:T(8,128)(2,1)} %collective-permute-done.4.r_3_, bf16[768,512]{1,0:T(8,128)(2,1)} %collective-permute-done.5.r_4_, ...), custom_call_target="tpu_custom_call" | custom-call | flops 1 | bytes 1 | tf_op jit(solution)/shard_map/hops/pallas_call | solution.py:211
  56.4 2.0 %part_out.2 = bf16[1024,512]{1,0:T(8,128)(2,1)S(1)} custom-call(s32[16]{0:T(128)S(1)} %get-tuple-element.89.order_ref, bf16[2048,768]{1,0:T(8,128)(2,1)S(1)} %get-tuple-element.44.refs_0_.refs_1_.refs_2_.refs_3_, bf16[2048,768]{1,0:T(8,128)(2,1)S(1)} %get-tuple-element.44.refs_0_.refs_1_.refs_2_.refs_3_, ...), custom_call_target="tpu_custom_call" | custom-call | flops 1 | bytes 1 | tf_op jit(solution)/shard_map/part_out/pallas_call | solution.py:295
  58.4 1.8 %collective-permute-start.8 = (bf16[2,2,2,2,64,512]{5,4,3,2,1,0:T(8,128)(2,1)S(1)}, bf16[2,2,2,2,64,512]{5,4,3,2,1,0:T(8,128)(2,1)S(1)}, u32[]{:S(2)}, u32[]{:S(2)}) collective-permute-start(bf16[2,2,2,2,64,512]{5,4,3,2,1,0:T(8,128)(2,1)S(1)} %bitcast.92), channel_id=1, source_target_pairs={{0,2},{1,3},{2,0},{3,1},{4,6},{5,7},{6,4},{7,5},{8,10},{9,11},{10,... | collective-permute-start | bytes 3145736 | tf_op jit(solution)/shard_map/ppermute | solution.py:361
  60.2 2.0 %part_out.3 = bf16[1024,512]{1,0:T(8,128)(2,1)S(1)} custom-call(s32[16]{0:T(128)S(1)} %get-tuple-element.90.order_ref, bf16[2048,768]{1,0:T(8,128)(2,1)S(1)} %get-tuple-element.44.refs_0_.refs_1_.refs_2_.refs_3_, bf16[2048,768]{1,0:T(8,128)(2,1)S(1)} %get-tuple-element.44.refs_0_.refs_1_.refs_2_.refs_3_, ...), custom_call_target="tpu_custom_call" | custom-call | flops 1 | bytes 1 | tf_op jit(solution)/shard_map/part_out/pallas_call | solution.py:295
  64.2 3.8 %part_in.2 = (bf16[1024,896]{1,0:T(8,128)(2,1)S(1)}, bf16[1024,768]{1,0:T(8,128)(2,1)S(1)}) custom-call(s32[16]{0:T(128)S(1)} %get-tuple-element.89.order_ref, f32[2048,768]{1,0:T(8,128)S(1)} %bitcast.89, f32[2048,768]{1,0:T(8,128)S(1)} %bitcast.89, f32[2048,768]{1,0:T(8,128)S(1)} %bitcast.89, f32[2048,768]{1,0:T(8,128)S(1)} %bitcast.89, ...), custom_call_target="tpu_custom_call" | custom-call | flops 1 | bytes 1 | tf_op jit(solution)/shard_map/part_in/pallas_call | solution.py:295
  68.2 2.9 %collective-permute-start.10 = (bf16[2,2,2,64,512]{4,3,2,1,0:T(8,128)(2,1)S(1)}, bf16[2,2,2,64,512]{4,3,2,1,0:T(8,128)(2,1)S(1)}, u32[]{:S(2)}, u32[]{:S(2)}) collective-permute-start(bf16[2,2,2,64,512]{4,3,2,1,0:T(8,128)(2,1)S(1)} %get-tuple-element.70), channel_id=1, source_target_pairs={{0,4},{1,5},{2,6},{3,7},{4,0},{5,1},{6,2},{7,3},{8,12},{9,13},{10,... | collective-permute-start | bytes 1572872 | tf_op jit(solution)/shard_map/ppermute | solution.py:361
  71.1 3.8 %part_in.3 = (bf16[1024,896]{1,0:T(8,128)(2,1)S(1)}, bf16[1024,768]{1,0:T(8,128)(2,1)S(1)}) custom-call(s32[16]{0:T(128)S(1)} %get-tuple-element.90.order_ref, f32[2048,768]{1,0:T(8,128)S(1)} %bitcast.89, f32[2048,768]{1,0:T(8,128)S(1)} %bitcast.89, f32[2048,768]{1,0:T(8,128)S(1)} %bitcast.89, f32[2048,768]{1,0:T(8,128)S(1)} %bitcast.89, ...), custom_call_target="tpu_custom_call" | custom-call | flops 1 | bytes 1 | tf_op jit(solution)/shard_map/part_in/pallas_call | solution.py:295
  75.6 2.7 %collective-permute-start.11 = (bf16[2,2,2,64,512]{4,3,2,1,0:T(8,128)(2,1)S(1)}, bf16[2,2,2,64,512]{4,3,2,1,0:T(8,128)(2,1)S(1)}, u32[]{:S(2)}, u32[]{:S(2)}) collective-permute-start(bf16[2,2,2,64,512]{4,3,2,1,0:T(8,128)(2,1)S(1)} %get-tuple-element.68), channel_id=1, source_target_pairs={{0,1},{1,0},{2,3},{3,2},{4,5},{5,4},{6,7},{7,6},{8,9},{9,8},{10,11... | collective-permute-start | bytes 1572872 | tf_op jit(solution)/shard_map/ppermute | solution.py:361
  78.4 6.3 %feat_grad.1 = (bf16[384,768]{1,0:T(8,128)(2,1)}, bf16[384,768]{1,0:T(8,128)(2,1)}) custom-call(s32[32]{0:T(128)S(1)} %fusion.33.order_ref, bf16[2048,768]{1,0:T(8,128)(2,1)S(1)} %copy-done.1, bf16[2048,768]{1,0:T(8,128)(2,1)S(1)} %copy-done.1, bf16[2048,768]{1,0:T(8,128)(2,1)S(1)} %copy-done.1, bf16[2048,768]{1,0:T(8,128)(2,1)S(1)} %copy-done.1, ...), custom_call_target="tpu_custom_call" | custom-call | flops 1 | bytes 1 | tf_op jit(solution)/shard_map/feat_grad/pallas_call | solution.py:295
  84.9 1.7 %collective-permute-start.13 = (bf16[2,2,64,512]{3,2,1,0:T(8,128)(2,1)S(1)}, bf16[2,2,64,512]{3,2,1,0:T(8,128)(2,1)S(1)}, u32[]{:S(2)}, u32[]{:S(2)}) collective-permute-start(bf16[2,2,64,512]{3,2,1,0:T(8,128)(2,1)S(1)} %get-tuple-element.72), channel_id=1, source_target_pairs={{0,1},{1,0},{2,3},{3,2},{4,5},{5,4},{6,7},{7,6},{8,9},{9,8},{10,11... | collective-permute-start | bytes 786440 | tf_op jit(solution)/shard_map/ppermute | solution.py:361
  86.6 4.4 %collective-permute-done.11 = bf16[2,2,2,64,512]{4,3,2,1,0:T(8,128)(2,1)S(1)} collective-permute-done((bf16[2,2,2,64,512]{4,3,2,1,0:T(8,128)(2,1)S(1)}, bf16[2,2,2,64,512]{4,3,2,1,0:T(8,128)(2,1)S(1)}, u32[]{:S(2)}, u32[]{:S(2)}) %collective-permute-start.11) | collective-permute-done | bytes 524320 | tf_op jit(solution)/shard_map/ppermute | solution.py:361
  91.1 4.5 %collective-permute-done.12 = bf16[2,2,2,64,384]{4,3,2,1,0:T(8,128)(2,1)S(1)} collective-permute-done((bf16[2,2,2,64,384]{4,3,2,1,0:T(8,128)(2,1)S(1)}, bf16[2,2,2,64,384]{4,3,2,1,0:T(8,128)(2,1)S(1)}, u32[]{:S(2)}, u32[]{:S(2)}) %collective-permute-start.12) | collective-permute-done | bytes 393248 | tf_op jit(solution)/shard_map/ppermute | solution.py:361
  96.3 1.6 %collective-permute-start.22 = (bf16[64,512]{1,0:T(8,128)(2,1)S(1)}, bf16[64,512]{1,0:T(8,128)(2,1)S(1)}, u32[]{:S(2)}, u32[]{:S(2)}) collective-permute-start(bf16[64,512]{1,0:T(8,128)(2,1)S(1)} %get-tuple-element.77), channel_id=1, source_target_pairs={{0,8},{1,9},{2,10},{3,11},{4,12},{5,13},{6,14},{7,15},{8,0},{9,1},... | collective-permute-start | bytes 196616 | tf_op jit(solution)/shard_map/ppermute | solution.py:361
  97.9 2.5 %collective-permute-start.24 = (bf16[64,512]{1,0:T(8,128)(2,1)S(1)}, bf16[64,512]{1,0:T(8,128)(2,1)S(1)}, u32[]{:S(2)}, u32[]{:S(2)}) collective-permute-start(bf16[64,512]{1,0:T(8,128)(2,1)S(1)} %get-tuple-element.78), channel_id=1, source_target_pairs={{0,24},{1,25},{2,26},{3,27},{4,28},{5,29},{6,30},{7,31},{8,16},{9,... | collective-permute-start | bytes 196616 | tf_op jit(solution)/shard_map/ppermute | solution.py:361
  100.8 1.8 %collective-permute-start.15 = (bf16[2,2,64,384]{3,2,1,0:T(8,128)(2,1)S(1)}, bf16[2,2,64,384]{3,2,1,0:T(8,128)(2,1)S(1)}, u32[]{:S(2)}, u32[]{:S(2)}) collective-permute-start(bf16[2,2,64,384]{3,2,1,0:T(8,128)(2,1)S(1)} %get-tuple-element.76), channel_id=1, source_target_pairs={{0,1},{1,0},{2,3},{3,2},{4,5},{5,4},{6,7},{7,6},{8,9},{9,8},{10,11... | collective-permute-start | bytes 589832 | tf_op jit(solution)/shard_map/ppermute | solution.py:361
  102.6 2.0 %collective-permute-done.24 = bf16[64,512]{1,0:T(8,128)(2,1)S(1)} collective-permute-done((bf16[64,512]{1,0:T(8,128)(2,1)S(1)}, bf16[64,512]{1,0:T(8,128)(2,1)S(1)}, u32[]{:S(2)}, u32[]{:S(2)}) %collective-permute-start.24) | collective-permute-done | bytes 65568 | tf_op jit(solution)/shard_map/ppermute | solution.py:361
  104.6 2.0 %collective-permute-done.23 = bf16[64,512]{1,0:T(8,128)(2,1)S(1)} collective-permute-done((bf16[64,512]{1,0:T(8,128)(2,1)S(1)}, bf16[64,512]{1,0:T(8,128)(2,1)S(1)}, u32[]{:S(2)}, u32[]{:S(2)}) %collective-permute-start.23) | collective-permute-done | bytes 65568 | tf_op jit(solution)/shard_map/ppermute | solution.py:361
  107.9 1.7 %collective-permute-start.16 = (bf16[64,384]{1,0:T(8,128)(2,1)S(1)}, bf16[64,384]{1,0:T(8,128)(2,1)S(1)}, u32[]{:S(2)}, u32[]{:S(2)}) collective-permute-start(bf16[64,384]{1,0:T(8,128)(2,1)S(1)} %get-tuple-element.83), channel_id=1, source_target_pairs={{0,8},{1,9},{2,10},{3,11},{4,12},{5,13},{6,14},{7,15},{8,0},{9,1},... | collective-permute-start | bytes 147464 | tf_op jit(solution)/shard_map/ppermute | solution.py:361
  109.6 2.5 %collective-permute-start.18 = (bf16[64,384]{1,0:T(8,128)(2,1)S(1)}, bf16[64,384]{1,0:T(8,128)(2,1)S(1)}, u32[]{:S(2)}, u32[]{:S(2)}) collective-permute-start(bf16[64,384]{1,0:T(8,128)(2,1)S(1)} %get-tuple-element.84), channel_id=1, source_target_pairs={{0,24},{1,25},{2,26},{3,27},{4,28},{5,29},{6,30},{7,31},{8,16},{9,... | collective-permute-start | bytes 147464 | tf_op jit(solution)/shard_map/ppermute | solution.py:361
  112.1 2.0 %collective-permute-start.19 = (bf16[64,512]{1,0:T(8,128)(2,1)S(1)}, bf16[64,512]{1,0:T(8,128)(2,1)S(1)}, u32[]{:S(2)}, u32[]{:S(2)}) collective-permute-start(bf16[64,512]{1,0:T(8,128)(2,1)S(1)} %get-tuple-element.80), channel_id=1, source_target_pairs={{0,8},{1,9},{2,10},{3,11},{4,12},{5,13},{6,14},{7,15},{8,0},{9,1},... | collective-permute-start | bytes 196616 | tf_op jit(solution)/shard_map/ppermute | solution.py:361
  114.1 2.5 %collective-permute-start.21 = (bf16[64,512]{1,0:T(8,128)(2,1)S(1)}, bf16[64,512]{1,0:T(8,128)(2,1)S(1)}, u32[]{:S(2)}, u32[]{:S(2)}) collective-permute-start(bf16[64,512]{1,0:T(8,128)(2,1)S(1)} %get-tuple-element.81), channel_id=1, source_target_pairs={{0,24},{1,25},{2,26},{3,27},{4,28},{5,29},{6,30},{7,31},{8,16},{9,... | collective-permute-start | bytes 196616 | tf_op jit(solution)/shard_map/ppermute | solution.py:361
  116.6 2.1 %collective-permute-done.17 = bf16[64,384]{1,0:T(8,128)(2,1)S(1)} collective-permute-done((bf16[64,384]{1,0:T(8,128)(2,1)S(1)}, bf16[64,384]{1,0:T(8,128)(2,1)S(1)}, u32[]{:S(2)}, u32[]{:S(2)}) %collective-permute-start.17) | collective-permute-done | bytes 49184 | tf_op jit(solution)/shard_map/ppermute | solution.py:361
  120.2 1.5 %collective-permute-done.20 = bf16[64,512]{1,0:T(8,128)(2,1)S(1)} collective-permute-done((bf16[64,512]{1,0:T(8,128)(2,1)S(1)}, bf16[64,512]{1,0:T(8,128)(2,1)S(1)}, u32[]{:S(2)}, u32[]{:S(2)}) %collective-permute-start.20) | collective-permute-done | bytes 65568 | tf_op jit(solution)/shard_map/ppermute | solution.py:361
  (81 shorter events, 14.1 us)
Async XLA Ops:
  0.6 7.5 %copy-start.3 = (s32[2]{0:T(128)S(1)}, s32[2]{0:T(128)}, u32[]{:S(2)}) copy-start(s32[2]{0:T(128)} %constant.14.clone) | copy-start | bytes 28
  0.6 7.5 %copy-start.4 = (s32[2]{0:T(128)S(1)}, s32[2]{0:T(128)}, u32[]{:S(2)}) copy-start(s32[2]{0:T(128)} %constant.13.clone) | copy-start | bytes 28
  0.7 20.5 %copy-start.5 = (f32[2048]{0:T(1024)S(1)}, f32[2048]{0:T(1024)}, u32[]{:S(2)}) copy-start(f32[2048]{0:T(1024)} %param.17) | copy-start | bytes 24580
  2.7 5.4 %collective-permute-start = (s32[3,12]{1,0:T(4,128)}, s32[3,12]{1,0:T(4,128)S(1)}, u32[]{:S(2)}, u32[]{:S(2)}) collective-permute-start(s32[3,12]{1,0:T(4,128)} %get-tuple-element.33), channel_id=1, source_target_pairs={{0,1},{1,0},{2,3},{3,2},{4,5},{5,4},{6,7},{7,6},{8,9},{9,8},{10,11... | collective-permute-start | bytes 440 | tf_op jit(solution)/shard_map/ppermute | solution.py:361
  8.1 24.6 %collective-permute-start.6 = (bf16[768,512]{1,0:T(8,128)(2,1)}, bf16[768,512]{1,0:T(8,128)(2,1)}, u32[]{:S(2)}, u32[]{:S(2)}) collective-permute-start(bf16[768,512]{1,0:T(8,128)(2,1)} %get-tuple-element.35.r_2_), channel_id=1, source_target_pairs={{0,1},{1,0},{2,3},{3,2},{4,5},{5,4},{6,7},{7,6},{8,9},{9,8},{10,11... | collective-permute-start | bytes 2359304 | tf_op jit(solution)/shard_map/ppermute | solution.py:361
  9.5 35.3 %collective-permute-start.5 = (bf16[768,512]{1,0:T(8,128)(2,1)}, bf16[768,512]{1,0:T(8,128)(2,1)}, u32[]{:S(2)}, u32[]{:S(2)}) collective-permute-start(bf16[768,512]{1,0:T(8,128)(2,1)} %get-tuple-element.35.r_2_), channel_id=1, source_target_pairs={{2,0},{3,1},{4,2},{5,3},{6,4},{7,5},{8,6},{9,7},{10,8},{11,9},{12,... | collective-permute-start | bytes 2359304 | tf_op jit(solution)/shard_map/ppermute | solution.py:357
  10.7 34.0 %collective-permute-start.4 = (bf16[768,512]{1,0:T(8,128)(2,1)}, bf16[768,512]{1,0:T(8,128)(2,1)}, u32[]{:S(2)}, u32[]{:S(2)}) collective-permute-start(bf16[768,512]{1,0:T(8,128)(2,1)} %get-tuple-element.35.r_2_), channel_id=1, source_target_pairs={{0,2},{1,3},{2,4},{3,5},{4,6},{5,7},{6,8},{7,9},{8,10},{9,11},{10,... | collective-permute-start | bytes 2359304 | tf_op jit(solution)/shard_map/ppermute | solution.py:357
  15.5 20.7 %collective-permute-start.3 = (s32[6,12]{1,0:T(8,128)S(1)}, s32[6,12]{1,0:T(8,128)S(1)}, u32[]{:S(2)}, u32[]{:S(2)}) collective-permute-start(s32[6,12]{1,0:T(8,128)S(1)} %add_select_fusion.1), channel_id=1, source_target_pairs={{2,0},{3,1},{4,2},{5,3},{6,4},{7,5},{8,6},{9,7},{10,8},{11,9},{12,... | collective-permute-start | bytes 872 | tf_op jit(solution)/shard_map/ppermute | solution.py:357
  16.7 12.2 %collective-permute-start.1 = (s32[6,12]{1,0:T(8,128)S(1)}, s32[6,12]{1,0:T(8,128)S(1)}, u32[]{:S(2)}, u32[]{:S(2)}) collective-permute-start(s32[6,12]{1,0:T(8,128)S(1)} %add_select_fusion.1), channel_id=1, source_target_pairs={{0,4},{2,6},{4,8},{6,10},{8,12},{10,14},{12,16},{14,18},{16,20},{1... | collective-permute-start | bytes 872 | tf_op jit(solution)/shard_map/ppermute | solution.py:428
  28.9 7.3 %collective-permute-start.2 = (s32[6,12]{1,0:T(8,128)S(1)}, s32[6,12]{1,0:T(8,128)S(1)}, u32[]{:S(2)}, u32[]{:S(2)}) collective-permute-start(s32[6,12]{1,0:T(8,128)S(1)} %add_select_fusion.1), channel_id=1, source_target_pairs={{0,2},{1,3},{2,4},{3,5},{4,6},{5,7},{6,8},{7,9},{8,10},{9,11},{10,... | collective-permute-start | bytes 872 | tf_op jit(solution)/shard_map/ppermute | solution.py:357
  32.7 12.0 %collective-permute-start.7 = (bf16[768,512]{1,0:T(8,128)(2,1)}, bf16[768,512]{1,0:T(8,128)(2,1)}, u32[]{:S(2)}, u32[]{:S(2)}) collective-permute-start(bf16[768,512]{1,0:T(8,128)(2,1)} %collective-permute-done.6.r_5_), channel_id=1, source_target_pairs={{0,2},{2,4},{4,6},{6,8},{8,10},{10,12},{12,14},{14,16},{16,18},{18... | collective-permute-start | bytes 2359304 | tf_op jit(solution)/shard_map/ppermute | solution.py:422
  58.4 4.1 %collective-permute-start.8 = (bf16[2,2,2,2,64,512]{5,4,3,2,1,0:T(8,128)(2,1)S(1)}, bf16[2,2,2,2,64,512]{5,4,3,2,1,0:T(8,128)(2,1)S(1)}, u32[]{:S(2)}, u32[]{:S(2)}) collective-permute-start(bf16[2,2,2,2,64,512]{5,4,3,2,1,0:T(8,128)(2,1)S(1)} %bitcast.92), channel_id=1, source_target_pairs={{0,2},{1,3},{2,0},{3,1},{4,6},{5,7},{6,4},{7,5},{8,10},{9,11},{10,... | collective-permute-start | bytes 3145736 | tf_op jit(solution)/shard_map/ppermute | solution.py:361
  60.2 2.6 %slice-start = ((s8[6291456]{0:T(1024)(128)(4,1)}), s8[4194304]{0:T(1024)(128)(4,1)S(1)}, s32[]{:S(2)}) async-start(s8[6291456]{0:T(1024)(128)(4,1)} %bitcast.88), calls=%async_computation | async-start | bytes 8388608
  60.2 2.9 %slice-start.1 = ((s8[6291456]{0:T(1024)(128)(4,1)}), s8[2097152]{0:T(1024)(128)(4,1)S(1)}, s32[]{:S(2)}) async-start(s8[6291456]{0:T(1024)(128)(4,1)} %bitcast.88), calls=%async_computation.1 | async-start | bytes 4194304
  60.2 3.1 %copy-start.2 = (bf16[768,768]{1,0:T(8,128)(2,1)S(1)}, bf16[768,768]{1,0:T(8,128)(2,1)}, u32[]{:S(2)}) copy-start(bf16[768,768]{1,0:T(8,128)(2,1)} %pad_maximum_fusion.refs_9_) | copy-start | bytes 3538948
  68.0 6.9 %collective-permute-start.9 = (bf16[2,2,2,2,64,896]{5,4,3,2,1,0:T(8,128)(2,1)S(1)}, bf16[2,2,2,2,64,896]{5,4,3,2,1,0:T(8,128)(2,1)S(1)}, u32[]{:S(2)}, u32[]{:S(2)}) collective-permute-start(bf16[2,2,2,2,64,896]{5,4,3,2,1,0:T(8,128)(2,1)S(1)} %bitcast.93), channel_id=1, source_target_pairs={{0,2},{1,3},{2,0},{3,1},{4,6},{5,7},{6,4},{7,5},{8,10},{9,11},{10,... | collective-permute-start | bytes 5505032 | tf_op jit(solution)/shard_map/ppermute | solution.py:361
  68.2 16.5 %collective-permute-start.10 = (bf16[2,2,2,64,512]{4,3,2,1,0:T(8,128)(2,1)S(1)}, bf16[2,2,2,64,512]{4,3,2,1,0:T(8,128)(2,1)S(1)}, u32[]{:S(2)}, u32[]{:S(2)}) collective-permute-start(bf16[2,2,2,64,512]{4,3,2,1,0:T(8,128)(2,1)S(1)} %get-tuple-element.70), channel_id=1, source_target_pairs={{0,4},{1,5},{2,6},{3,7},{4,0},{5,1},{6,2},{7,3},{8,12},{9,13},{10,... | collective-permute-start | bytes 1572872 | tf_op jit(solution)/shard_map/ppermute | solution.py:361
  75.5 2.9 %copy-start.1 = (bf16[2048,768]{1,0:T(8,128)(2,1)S(1)}, bf16[2048,768]{1,0:T(8,128)(2,1)}, u32[]{:S(2)}) copy-start(bf16[2048,768]{1,0:T(8,128)(2,1)} %refs_3_.1) | copy-start | bytes 9437188
  75.6 15.4 %collective-permute-start.11 = (bf16[2,2,2,64,512]{4,3,2,1,0:T(8,128)(2,1)S(1)}, bf16[2,2,2,64,512]{4,3,2,1,0:T(8,128)(2,1)S(1)}, u32[]{:S(2)}, u32[]{:S(2)}) collective-permute-start(bf16[2,2,2,64,512]{4,3,2,1,0:T(8,128)(2,1)S(1)} %get-tuple-element.68), channel_id=1, source_target_pairs={{0,1},{1,0},{2,3},{3,2},{4,5},{5,4},{6,7},{7,6},{8,9},{9,8},{10,11... | collective-permute-start | bytes 1572872 | tf_op jit(solution)/shard_map/ppermute | solution.py:361
  84.6 10.9 %collective-permute-start.12 = (bf16[2,2,2,64,384]{4,3,2,1,0:T(8,128)(2,1)S(1)}, bf16[2,2,2,64,384]{4,3,2,1,0:T(8,128)(2,1)S(1)}, u32[]{:S(2)}, u32[]{:S(2)}) collective-permute-start(bf16[2,2,2,64,384]{4,3,2,1,0:T(8,128)(2,1)S(1)} %get-tuple-element.66), channel_id=1, source_target_pairs={{0,4},{1,5},{2,6},{3,7},{4,0},{5,1},{6,2},{7,3},{8,12},{9,13},{10,... | collective-permute-start | bytes 1179656 | tf_op jit(solution)/shard_map/ppermute | solution.py:361
  84.9 11.3 %collective-permute-start.13 = (bf16[2,2,64,512]{3,2,1,0:T(8,128)(2,1)S(1)}, bf16[2,2,64,512]{3,2,1,0:T(8,128)(2,1)S(1)}, u32[]{:S(2)}, u32[]{:S(2)}) collective-permute-start(bf16[2,2,64,512]{3,2,1,0:T(8,128)(2,1)S(1)} %get-tuple-element.72), channel_id=1, source_target_pairs={{0,1},{1,0},{2,3},{3,2},{4,5},{5,4},{6,7},{7,6},{8,9},{9,8},{10,11... | collective-permute-start | bytes 786440 | tf_op jit(solution)/shard_map/ppermute | solution.py:361
  96.3 6.3 %collective-permute-start.22 = (bf16[64,512]{1,0:T(8,128)(2,1)S(1)}, bf16[64,512]{1,0:T(8,128)(2,1)S(1)}, u32[]{:S(2)}, u32[]{:S(2)}) collective-permute-start(bf16[64,512]{1,0:T(8,128)(2,1)S(1)} %get-tuple-element.77), channel_id=1, source_target_pairs={{0,8},{1,9},{2,10},{3,11},{4,12},{5,13},{6,14},{7,15},{8,0},{9,1},... | collective-permute-start | bytes 196616 | tf_op jit(solution)/shard_map/ppermute | solution.py:361
  97.9 6.6 %collective-permute-start.24 = (bf16[64,512]{1,0:T(8,128)(2,1)S(1)}, bf16[64,512]{1,0:T(8,128)(2,1)S(1)}, u32[]{:S(2)}, u32[]{:S(2)}) collective-permute-start(bf16[64,512]{1,0:T(8,128)(2,1)S(1)} %get-tuple-element.78), channel_id=1, source_target_pairs={{0,24},{1,25},{2,26},{3,27},{4,28},{5,29},{6,30},{7,31},{8,16},{9,... | collective-permute-start | bytes 196616 | tf_op jit(solution)/shard_map/ppermute | solution.py:361
  100.4 6.1 %collective-permute-start.23 = (bf16[64,512]{1,0:T(8,128)(2,1)S(1)}, bf16[64,512]{1,0:T(8,128)(2,1)S(1)}, u32[]{:S(2)}, u32[]{:S(2)}) collective-permute-start(bf16[64,512]{1,0:T(8,128)(2,1)S(1)} %get-tuple-element.79), channel_id=1, source_target_pairs={{0,16},{1,17},{2,18},{3,19},{4,20},{5,21},{6,22},{7,23},{8,24},{9,... | collective-permute-start | bytes 196616 | tf_op jit(solution)/shard_map/ppermute | solution.py:361
  100.4 7.4 %collective-permute-start.14 = (bf16[2,2,64,512]{3,2,1,0:T(8,128)(2,1)S(1)}, bf16[2,2,64,512]{3,2,1,0:T(8,128)(2,1)S(1)}, u32[]{:S(2)}, u32[]{:S(2)}) collective-permute-start(bf16[2,2,64,512]{3,2,1,0:T(8,128)(2,1)S(1)} %get-tuple-element.74), channel_id=1, source_target_pairs={{0,4},{1,5},{2,6},{3,7},{4,0},{5,1},{6,2},{7,3},{8,12},{9,13},{10,... | collective-permute-start | bytes 786440 | tf_op jit(solution)/shard_map/ppermute | solution.py:361
  100.8 7.1 %collective-permute-start.15 = (bf16[2,2,64,384]{3,2,1,0:T(8,128)(2,1)S(1)}, bf16[2,2,64,384]{3,2,1,0:T(8,128)(2,1)S(1)}, u32[]{:S(2)}, u32[]{:S(2)}) collective-permute-start(bf16[2,2,64,384]{3,2,1,0:T(8,128)(2,1)S(1)} %get-tuple-element.76), channel_id=1, source_target_pairs={{0,1},{1,0},{2,3},{3,2},{4,5},{5,4},{6,7},{7,6},{8,9},{9,8},{10,11... | collective-permute-start | bytes 589832 | tf_op jit(solution)/shard_map/ppermute | solution.py:361
  107.9 8.6 %collective-permute-start.16 = (bf16[64,384]{1,0:T(8,128)(2,1)S(1)}, bf16[64,384]{1,0:T(8,128)(2,1)S(1)}, u32[]{:S(2)}, u32[]{:S(2)}) collective-permute-start(bf16[64,384]{1,0:T(8,128)(2,1)S(1)} %get-tuple-element.83), channel_id=1, source_target_pairs={{0,8},{1,9},{2,10},{3,11},{4,12},{5,13},{6,14},{7,15},{8,0},{9,1},... | collective-permute-start | bytes 147464 | tf_op jit(solution)/shard_map/ppermute | solution.py:361
  109.6 7.0 %collective-permute-start.18 = (bf16[64,384]{1,0:T(8,128)(2,1)S(1)}, bf16[64,384]{1,0:T(8,128)(2,1)S(1)}, u32[]{:S(2)}, u32[]{:S(2)}) collective-permute-start(bf16[64,384]{1,0:T(8,128)(2,1)S(1)} %get-tuple-element.84), channel_id=1, source_target_pairs={{0,24},{1,25},{2,26},{3,27},{4,28},{5,29},{6,30},{7,31},{8,16},{9,... | collective-permute-start | bytes 147464 | tf_op jit(solution)/shard_map/ppermute | solution.py:361
  112.1 6.6 %collective-permute-start.17 = (bf16[64,384]{1,0:T(8,128)(2,1)S(1)}, bf16[64,384]{1,0:T(8,128)(2,1)S(1)}, u32[]{:S(2)}, u32[]{:S(2)}) collective-permute-start(bf16[64,384]{1,0:T(8,128)(2,1)S(1)} %get-tuple-element.85), channel_id=1, source_target_pairs={{0,16},{1,17},{2,18},{3,19},{4,20},{5,21},{6,22},{7,23},{8,24},{9,... | collective-permute-start | bytes 147464 | tf_op jit(solution)/shard_map/ppermute | solution.py:361
  112.1 6.6 %collective-permute-start.19 = (bf16[64,512]{1,0:T(8,128)(2,1)S(1)}, bf16[64,512]{1,0:T(8,128)(2,1)S(1)}, u32[]{:S(2)}, u32[]{:S(2)}) collective-permute-start(bf16[64,512]{1,0:T(8,128)(2,1)S(1)} %get-tuple-element.80), channel_id=1, source_target_pairs={{0,8},{1,9},{2,10},{3,11},{4,12},{5,13},{6,14},{7,15},{8,0},{9,1},... | collective-permute-start | bytes 196616 | tf_op jit(solution)/shard_map/ppermute | solution.py:361
  114.1 6.1 %collective-permute-start.21 = (bf16[64,512]{1,0:T(8,128)(2,1)S(1)}, bf16[64,512]{1,0:T(8,128)(2,1)S(1)}, u32[]{:S(2)}, u32[]{:S(2)}) collective-permute-start(bf16[64,512]{1,0:T(8,128)(2,1)S(1)} %get-tuple-element.81), channel_id=1, source_target_pairs={{0,24},{1,25},{2,26},{3,27},{4,28},{5,29},{6,30},{7,31},{8,16},{9,... | collective-permute-start | bytes 196616 | tf_op jit(solution)/shard_map/ppermute | solution.py:361
  116.6 5.2 %collective-permute-start.20 = (bf16[64,512]{1,0:T(8,128)(2,1)S(1)}, bf16[64,512]{1,0:T(8,128)(2,1)S(1)}, u32[]{:S(2)}, u32[]{:S(2)}) collective-permute-start(bf16[64,512]{1,0:T(8,128)(2,1)S(1)} %get-tuple-element.82), channel_id=1, source_target_pairs={{0,16},{1,17},{2,18},{3,19},{4,20},{5,21},{6,22},{7,23},{8,24},{9,... | collective-permute-start | bytes 196616 | tf_op jit(solution)/shard_map/ppermute | solution.py:361
  (1 other events, 2.0 us)

commit v6 on v5

--- a/solution.py
+++ b/solution.py
@@ -375,22 +375,32 @@
 
 class Reduction:
 
-    def __init__(self, part, count, bits, order):
-        self.part, self.count, self.left, self.order = part, count, list(bits), list(order)
+    def __init__(self, part, count, bits, orders):
+        lanes = part.shape[-1]
+        cut = lanes // 2 // TILE * TILE
+        self.count, self.last = count, bits[-2:]
+        self.parts = [part[..., :cut], part[..., cut:]]
+        self.left = [list(bits), list(bits)]
+        self.orders = [list(order) for order in orders]
 
     def start(self):
-        bit = self.order.pop(0)
-        self.kept, self.sent = parts(self.part, self.left.index(bit))
-        self.left.remove(bit)
-        self.came = flipped(self.sent, self.count, 1 << bit)
+        self.kept, self.sent, self.came = [], [], []
+        for part, left, order in zip(self.parts, self.left, self.orders):
+            bit = order.pop(0)
+            kept, sent = parts(part, left.index(bit))
+            left.remove(bit)
+            self.kept.append(kept)
+            self.sent.append(sent)
+            self.came.append(flipped(sent, self.count, 1 << bit))
 
     def finish(self, *done):
-        self.part = added(after(self.kept, *done), self.came)
-        return self.part
+        self.parts = [added(after(k, *done), c) for k, c in zip(self.kept, self.came)]
+        return tuple(self.parts)
 
     def start_last(self):
-        part = self.part.reshape((4,) + self.part.shape[-2:])
-        hi, lo = self.left
+        part = jnp.concatenate(self.parts, axis=-1)
+        part = part.reshape((4,) + part.shape[-2:])
+        hi, lo = self.last
         self.own = part[0]
         self.got = [flipped(part[k], self.count, ((k >> 1) << hi) | ((k & 1) << lo)) for k in range(1, 4)]
 
@@ -491,35 +501,42 @@
     out_sent = out_half(order[half:], logit)
     out_came = flipped(out_sent, count, core)
     out_kept = out_half(order[:half], after(logit, out_sent))
-    r_out = Reduction(added(out_kept, out_came), count, rest, img_bits + cap_bits)
+    orders = (cap_bits + img_bits, img_bits + cap_bits)
+    out_core = added(out_kept, out_came)
+    r_out = Reduction(out_core, count, rest, orders)
     r_out.start()
-    in_sent, grad_sent = in_half(order[half:], after(logit, r_out.part))
+    in_sent, grad_sent = in_half(order[half:], after(logit, out_core))
     in_came = flipped(in_sent, count, core)
     in_kept, grad_kept = in_half(order[:half], after(logit, grad_sent))
-    g_in = added(in_kept, in_came)
-    cut = f_in // 2
-    r_a = Reduction(g_in[..., :cut], count, rest, img_bits + cap_bits)
-    r_b = Reduction(g_in[..., cut:], count, rest, cap_bits + img_bits)
-    r_a.start()
-    r_b.start()
-    grad_kept = after(grad_kept, g_in)
+    r_in = Reduction(added(in_kept, in_came), count, rest, orders)
+    r_in.start()
+    done = r_out.finish(*r_in.sent)
+    steps = m - 3
+    if steps > 1:
+        r_out.start()
+    else:
+        r_out.start_last()
     grad_img, grad_cap = over_hidden(
         feat_kernel, "feat_grad", order, grouped(f_in) + [rows_of_half(nodes, half, 0), rows_of_half(nodes, half, 1)],
         (whole((local_rows, f_in)),) * 2, (jax.ShapeDtypeStruct((local_rows, f_in), BF16),) * 2,
-        [pltpu.VMEM((nodes, f_in), F32)], [w_in] * GROUP + [grad_kept, grad_sent],
+        [pltpu.VMEM((nodes, f_in), F32)], [w_in] * GROUP + [after(grad_kept, *done), grad_sent],
     )
-    done = (r_a.sent, r_b.sent)
-    for k in range(m - 3):
-        for r in (r_out, r_b, r_a):
-            done = (r.finish(*done),)
-            if k < m - 4:
-                r.start()
-            else:
-                r.start_last()
+    done = (grad_img,)
+    for k in range(1, steps):
+        done = r_out.finish(*done)
+        if k + 1 < steps:
+            r_out.start()
+        else:
+            r_out.start_last()
+    for k in range(steps):
+        done = r_in.finish(*done)
+        if k + 1 < steps:
+            r_in.start()
+        else:
+            r_in.start_last()
     grad_scale = 1.0 / math.sqrt(nodes * count)
-    g_out, g_b, g_a = [r.result() * grad_scale for r in (r_out, r_b, r_a)]
-    g_in = jnp.concatenate([g_a, g_b[:, : f_in - cut]], axis=1)
-    return (grad_img, grad_cap, g_in, g_out, g_b[:, f_in - cut])
+    g_out, g_in = [r.result() * grad_scale for r in (r_out, r_in)]
+    return (grad_img, grad_cap, g_in[:, :f_in], g_out, g_in[:, f_in])
 
 
 def solution(mesh):

time: 123 us -> 118 us (0.959)
  starting transfers between devices: 46.5 us -> 43 us
  waiting for transfers between devices: 19.2 us -> 17.7 us
    ppermute x19 -> x18, starting transfers between devices: 28.3 us -> 24.8 us  [flipped(): return lax.ppermute(array, AXES, [(i, i ^ mask) for i in range(count)])]
    ppermute x19 -> x18, waiting for transfers between devices: 19.2 us -> 17.7 us  [flipped(): return lax.ppermute(array, AXES, [(i, i ^ mask) for i in range(count)])]
  transfers between devices with their start and end apart: 25 -> 24, of which waited for: 10 -> 7; matrix products, arithmetic and copies ran while one was open for 11% -> 12% of each run, Pallas kernels for 16% -> 17%
where the time goes in v6:
time: 118 us
  starting transfers between devices  43 us (36%)
  Pallas kernels  39.4 us (33%)
  waiting for transfers between devices  17.7 us (15%)
  matrix products  7.74 us (7%)
  other arithmetic  5.69 us (5%)
  local copies, waits for them, and re-layouts  3.68 us (3%)
    ppermute x18, starting transfers between devices, flipped(): return lax.ppermute(array, AXES, [(i, i ^ mask) for i in range(count)])  24.8 us
    pallas_call x5, Pallas kernels, over_hidden(): pl.pallas_call(kernel, out_shape=out_shape, grid_spec=pltpu.PrefetchScala...  17.9 us
    ppermute x18, waiting for transfers between devices, flipped(): return lax.ppermute(array, AXES, [(i, i ^ mask) for i in range(count)])  17.7 us
    pallas_call x1, Pallas kernels, propagate(): pl.pallas_call(lambda *r: hops_kernel(*r, tiles=tiles, slots=slots, width...  11.6 us
    ppermute x4, starting transfers between devices, moved(): lax.ppermute(array, AXES, [(i, i + by) for i in range(count) if 0 <= i +...  10.3 us
    pallas_call x1, Pallas kernels, make_tiles(): pl.pallas_call(lambda *r: tiles_kernel(*r, tiles=tiles, slots=slots), out...  7.8 us
    dot_general x1, matrix products, per_device(): lax.dot_general(w_in, feats, across, preferred_element_type=F32)  7.74 us
    ppermute x1, starting transfers between devices, per_device(): pair_far = lax.ppermute(pair, AXES, nearest_pair(count, 4))  4.4 us
  transfers between devices with their start and end apart: 24, of which 7 were waited for; matrix products, arithmetic and copies ran while one was open for 12% of the time, Pallas kernels for 17%

profile of v6, /device:TPU:0, one launch (start us, length us, event | category | flops | bytes accessed | tf_op | source)
XLA Modules:
  0.0 118.2 jit_solution(17900377118042855518)
XLA Ops:
  0.7 2.1 %stack.1 = (bf16[768,512]{1,0:T(8,128)(2,1)}, s32[3,12]{1,0:T(4,128)}) custom-call(s32[3]{0:T(128)} %count_ref.1, bf16[384,512]{1,0:T(8,128)(2,1)} %top_ref.1, bf16[384,512]{1,0:T(8,128)(2,1)} %bottom_ref.1, s32[3,4]{1,0:T(4,128)} %seed_ref.1, s32[3,4]{1,0:T(4,128)} %cols_ref.1), custom_call_target="tpu_custom_call" | custom-call | flops 1 | bytes 1 | tf_op jit(solution)/shard_map/stack/pallas_call | solution.py:342
  2.7 2.9 %collective-permute-start = (s32[3,12]{1,0:T(4,128)}, s32[3,12]{1,0:T(4,128)S(1)}, u32[]{:S(2)}, u32[]{:S(2)}) collective-permute-start(s32[3,12]{1,0:T(4,128)} %get-tuple-element.35), channel_id=1, source_target_pairs={{0,1},{1,0},{2,3},{3,2},{4,5},{5,4},{6,7},{7,6},{8,9},{9,8},{10,11... | collective-permute-start | bytes 440 | tf_op jit(solution)/shard_map/ppermute | solution.py:361
  5.8 2.3 %pad_maximum_fusion.refs_9_ = bf16[768,768]{1,0:T(8,128)(2,1)} fusion(bf16[384,768]{1,0:T(8,128)(2,1)} %param.13, bf16[384,768]{1,0:T(8,128)(2,1)} %param.12), kind=kLoop, calls=%fused_computation.15 | loop fusion | flops 2359296 | bytes 2359296 | tf_op jit(solution)/shard_map/concatenate | solution.py:434
  8.1 1.3 %collective-permute-start.6 = (bf16[768,512]{1,0:T(8,128)(2,1)}, bf16[768,512]{1,0:T(8,128)(2,1)}, u32[]{:S(2)}, u32[]{:S(2)}) collective-permute-start(bf16[768,512]{1,0:T(8,128)(2,1)} %get-tuple-element.37.r_2_), channel_id=1, source_target_pairs={{0,1},{1,0},{2,3},{3,2},{4,5},{5,4},{6,7},{7,6},{8,9},{9,8},{10,11... | collective-permute-start | bytes 2359304 | tf_op jit(solution)/shard_map/ppermute | solution.py:361
  9.5 1.3 %collective-permute-start.5 = (bf16[768,512]{1,0:T(8,128)(2,1)}, bf16[768,512]{1,0:T(8,128)(2,1)}, u32[]{:S(2)}, u32[]{:S(2)}) collective-permute-start(bf16[768,512]{1,0:T(8,128)(2,1)} %get-tuple-element.37.r_2_), channel_id=1, source_target_pairs={{2,0},{3,1},{4,2},{5,3},{6,4},{7,5},{8,6},{9,7},{10,8},{11,9},{12,... | collective-permute-start | bytes 2359304 | tf_op jit(solution)/shard_map/ppermute | solution.py:357
  10.7 3.9 %collective-permute-start.4 = (bf16[768,512]{1,0:T(8,128)(2,1)}, bf16[768,512]{1,0:T(8,128)(2,1)}, u32[]{:S(2)}, u32[]{:S(2)}) collective-permute-start(bf16[768,512]{1,0:T(8,128)(2,1)} %get-tuple-element.37.r_2_), channel_id=1, source_target_pairs={{0,2},{1,3},{2,4},{3,5},{4,6},{5,7},{6,8},{7,9},{8,10},{9,11},{10,... | collective-permute-start | bytes 2359304 | tf_op jit(solution)/shard_map/ppermute | solution.py:357
  16.7 4.4 %collective-permute-start.1 = (s32[6,12]{1,0:T(8,128)S(1)}, s32[6,12]{1,0:T(8,128)S(1)}, u32[]{:S(2)}, u32[]{:S(2)}) collective-permute-start(s32[6,12]{1,0:T(8,128)S(1)} %add_select_fusion.1), channel_id=1, source_target_pairs={{0,4},{2,6},{4,8},{6,10},{8,12},{10,14},{12,16},{14,18},{16,20},{1... | collective-permute-start | bytes 872 | tf_op jit(solution)/shard_map/ppermute | solution.py:438
  21.2 7.7 %fusion.3 = (f32[2048,768]{1,0:T(8,128)}, bf16[2048,768]{1,0:T(8,128)(2,1)S(1)}) fusion(f32[2048]{0:T(1024)S(1)} %copy-done.5, bf16[768,768]{1,0:T(8,128)(2,1)} %pad_maximum_fusion.refs_9_, bf16[2048,768]{1,0:T(8,128)(2,1)} %refs_3_.1), kind=kOutput, calls=%fused_computation.4 | convolution fusion | flops 2433220608 | bytes 13770752 | tf_op jit(solution)/shard_map/dot_general | solution.py:470
  28.9 3.8 %collective-permute-start.2 = (s32[6,12]{1,0:T(8,128)S(1)}, s32[6,12]{1,0:T(8,128)S(1)}, u32[]{:S(2)}, u32[]{:S(2)}) collective-permute-start(s32[6,12]{1,0:T(8,128)S(1)} %add_select_fusion.1), channel_id=1, source_target_pairs={{0,2},{1,3},{2,4},{3,5},{4,6},{5,7},{6,8},{7,9},{8,10},{9,11},{10,... | collective-permute-start | bytes 872 | tf_op jit(solution)/shard_map/ppermute | solution.py:357
  32.7 3.4 %collective-permute-start.7 = (bf16[768,512]{1,0:T(8,128)(2,1)}, bf16[768,512]{1,0:T(8,128)(2,1)}, u32[]{:S(2)}, u32[]{:S(2)}) collective-permute-start(bf16[768,512]{1,0:T(8,128)(2,1)} %collective-permute-done.6.r_5_), channel_id=1, source_target_pairs={{0,2},{2,4},{4,6},{6,8},{8,10},{10,12},{12,14},{14,16},{16,18},{18... | collective-permute-start | bytes 2359304 | tf_op jit(solution)/shard_map/ppermute | solution.py:432
  36.8 7.8 %tiles.1 = (bf16[15,128,512]{2,1,0:T(8,128)(2,1)}, bf16[15,512,128]{2,1,0:T(8,128)(2,1)}, f32[15,128,128]{2,1,0:T(8,128)}, f32[15,128,128]{2,1,0:T(8,128)}) custom-call(s32[84]{0:T(128)S(1)} %reshape.43.r_0_, s32[84]{0:T(128)S(1)} %reshape.44.r_1_, s32[21]{0:T(128)S(1)} %slice_reduce_fusion.1.r_2_), custom_call_target="tpu_custom_call" | custom-call | flops 1 | bytes 1 | tf_op jit(solution)/shard_map/tiles/pallas_call | solution.py:103
  44.8 11.6 %hops.1.refs_4_.refs_8_ = bf16[768,512]{1,0:T(8,128)(2,1)S(1)} custom-call(s32[60]{0:T(128)S(1)} %reshape.42.r_0_, s32[2]{0:T(128)S(1)} %fusion.17.r_1_, bf16[768,512]{1,0:T(8,128)(2,1)} %get-tuple-element.37.r_2_, bf16[768,512]{1,0:T(8,128)(2,1)} %collective-permute-done.4.r_3_, bf16[768,512]{1,0:T(8,128)(2,1)} %collective-permute-done.5.r_4_, ...), custom_call_target="tpu_custom_call" | custom-call | flops 1 | bytes 1 | tf_op jit(solution)/shard_map/hops/pallas_call | solution.py:211
  56.4 2.0 %part_out.2 = bf16[1024,512]{1,0:T(8,128)(2,1)S(1)} custom-call(s32[16]{0:T(128)S(1)} %get-tuple-element.94.order_ref, bf16[2048,768]{1,0:T(8,128)(2,1)S(1)} %get-tuple-element.46.refs_0_.refs_1_.refs_2_.refs_3_, bf16[2048,768]{1,0:T(8,128)(2,1)S(1)} %get-tuple-element.46.refs_0_.refs_1_.refs_2_.refs_3_, ...), custom_call_target="tpu_custom_call" | custom-call | flops 1 | bytes 1 | tf_op jit(solution)/shard_map/part_out/pallas_call | solution.py:295
  58.4 1.8 %collective-permute-start.8 = (bf16[2,2,2,2,64,512]{5,4,3,2,1,0:T(8,128)(2,1)S(1)}, bf16[2,2,2,2,64,512]{5,4,3,2,1,0:T(8,128)(2,1)S(1)}, u32[]{:S(2)}, u32[]{:S(2)}) collective-permute-start(bf16[2,2,2,2,64,512]{5,4,3,2,1,0:T(8,128)(2,1)S(1)} %bitcast.88), channel_id=1, source_target_pairs={{0,2},{1,3},{2,0},{3,1},{4,6},{5,7},{6,4},{7,5},{8,10},{9,11},{10,... | collective-permute-start | bytes 3145736 | tf_op jit(solution)/shard_map/ppermute | solution.py:361
  60.2 2.0 %part_out.3 = bf16[1024,512]{1,0:T(8,128)(2,1)S(1)} custom-call(s32[16]{0:T(128)S(1)} %get-tuple-element.95.order_ref, bf16[2048,768]{1,0:T(8,128)(2,1)S(1)} %get-tuple-element.46.refs_0_.refs_1_.refs_2_.refs_3_, bf16[2048,768]{1,0:T(8,128)(2,1)S(1)} %get-tuple-element.46.refs_0_.refs_1_.refs_2_.refs_3_, ...), custom_call_target="tpu_custom_call" | custom-call | flops 1 | bytes 1 | tf_op jit(solution)/shard_map/part_out/pallas_call | solution.py:295
  64.2 3.8 %part_in.2 = (bf16[1024,896]{1,0:T(8,128)(2,1)S(1)}, bf16[1024,768]{1,0:T(8,128)(2,1)S(1)}) custom-call(s32[16]{0:T(128)S(1)} %get-tuple-element.94.order_ref, f32[2048,768]{1,0:T(8,128)S(1)} %bitcast.85, f32[2048,768]{1,0:T(8,128)S(1)} %bitcast.85, f32[2048,768]{1,0:T(8,128)S(1)} %bitcast.85, f32[2048,768]{1,0:T(8,128)S(1)} %bitcast.85, ...), custom_call_target="tpu_custom_call" | custom-call | flops 1 | bytes 1 | tf_op jit(solution)/shard_map/part_in/pallas_call | solution.py:295
  68.2 2.9 %collective-permute-start.11 = (bf16[2,2,2,64,256]{4,3,2,1,0:T(8,128)(2,1)S(1)}, bf16[2,2,2,64,256]{4,3,2,1,0:T(8,128)(2,1)S(1)}, u32[]{:S(2)}, u32[]{:S(2)}) collective-permute-start(bf16[2,2,2,64,256]{4,3,2,1,0:T(8,128)(2,1)S(1)} %get-tuple-element.74), channel_id=1, source_target_pairs={{0,4},{1,5},{2,6},{3,7},{4,0},{5,1},{6,2},{7,3},{8,12},{9,13},{10,... | collective-permute-start | bytes 786440 | tf_op jit(solution)/shard_map/ppermute | solution.py:361
  71.1 2.7 %collective-permute-start.10 = (bf16[2,2,2,64,256]{4,3,2,1,0:T(8,128)(2,1)S(1)}, bf16[2,2,2,64,256]{4,3,2,1,0:T(8,128)(2,1)S(1)}, u32[]{:S(2)}, u32[]{:S(2)}) collective-permute-start(bf16[2,2,2,64,256]{4,3,2,1,0:T(8,128)(2,1)S(1)} %get-tuple-element.76), channel_id=1, source_target_pairs={{0,1},{1,0},{2,3},{3,2},{4,5},{5,4},{6,7},{7,6},{8,9},{9,8},{10,11... | collective-permute-start | bytes 786440 | tf_op jit(solution)/shard_map/ppermute | solution.py:361
  73.8 3.8 %part_in.3 = (bf16[1024,896]{1,0:T(8,128)(2,1)S(1)}, bf16[1024,768]{1,0:T(8,128)(2,1)S(1)}) custom-call(s32[16]{0:T(128)S(1)} %get-tuple-element.95.order_ref, f32[2048,768]{1,0:T(8,128)S(1)} %bitcast.85, f32[2048,768]{1,0:T(8,128)S(1)} %bitcast.85, f32[2048,768]{1,0:T(8,128)S(1)} %bitcast.85, f32[2048,768]{1,0:T(8,128)S(1)} %bitcast.85, ...), custom_call_target="tpu_custom_call" | custom-call | flops 1 | bytes 1 | tf_op jit(solution)/shard_map/part_in/pallas_call | solution.py:295
  78.5 1.9 %collective-permute-done.10 = bf16[2,2,2,64,256]{4,3,2,1,0:T(8,128)(2,1)S(1)} collective-permute-done((bf16[2,2,2,64,256]{4,3,2,1,0:T(8,128)(2,1)S(1)}, bf16[2,2,2,64,256]{4,3,2,1,0:T(8,128)(2,1)S(1)}, u32[]{:S(2)}, u32[]{:S(2)}) %collective-permute-start.10) | collective-permute-done | bytes 262176 | tf_op jit(solution)/shard_map/ppermute | solution.py:361
  80.7 6.3 %feat_grad.1 = (bf16[384,768]{1,0:T(8,128)(2,1)}, bf16[384,768]{1,0:T(8,128)(2,1)}) custom-call(s32[32]{0:T(128)S(1)} %fusion.30.order_ref, bf16[2048,768]{1,0:T(8,128)(2,1)S(1)} %copy-done.1, bf16[2048,768]{1,0:T(8,128)(2,1)S(1)} %copy-done.1, bf16[2048,768]{1,0:T(8,128)(2,1)S(1)} %copy-done.1, bf16[2048,768]{1,0:T(8,128)(2,1)S(1)} %copy-done.1, ...), custom_call_target="tpu_custom_call" | custom-call | flops 1 | bytes 1 | tf_op jit(solution)/shard_map/feat_grad/pallas_call | solution.py:295
  87.3 2.2 %collective-permute-start.13 = (bf16[2,2,64,256]{3,2,1,0:T(8,128)(2,1)S(1)}, bf16[2,2,64,256]{3,2,1,0:T(8,128)(2,1)S(1)}, u32[]{:S(2)}, u32[]{:S(2)}) collective-permute-start(bf16[2,2,64,256]{3,2,1,0:T(8,128)(2,1)S(1)} %get-tuple-element.88), channel_id=1, source_target_pairs={{0,1},{1,0},{2,3},{3,2},{4,5},{5,4},{6,7},{7,6},{8,9},{9,8},{10,11... | collective-permute-start | bytes 393224 | tf_op jit(solution)/shard_map/ppermute | solution.py:361
  89.5 5.6 %collective-permute-done.12 = bf16[2,2,64,256]{3,2,1,0:T(8,128)(2,1)S(1)} collective-permute-done((bf16[2,2,64,256]{3,2,1,0:T(8,128)(2,1)S(1)}, bf16[2,2,64,256]{3,2,1,0:T(8,128)(2,1)S(1)}, u32[]{:S(2)}, u32[]{:S(2)}) %collective-permute-start.12) | collective-permute-done | bytes 131104 | tf_op jit(solution)/shard_map/ppermute | solution.py:361
  95.9 1.8 %collective-permute-start.17 = (bf16[2,2,64,512]{3,2,1,0:T(8,128)(2,1)S(1)}, bf16[2,2,64,512]{3,2,1,0:T(8,128)(2,1)S(1)}, u32[]{:S(2)}, u32[]{:S(2)}) collective-permute-start(bf16[2,2,64,512]{3,2,1,0:T(8,128)(2,1)S(1)} %get-tuple-element.78), channel_id=1, source_target_pairs={{0,1},{1,0},{2,3},{3,2},{4,5},{5,4},{6,7},{7,6},{8,9},{9,8},{10,11... | collective-permute-start | bytes 786440 | tf_op jit(solution)/shard_map/ppermute | solution.py:361
  97.8 1.6 %collective-permute-start.21 = (bf16[64,512]{1,0:T(8,128)(2,1)S(1)}, bf16[64,512]{1,0:T(8,128)(2,1)S(1)}, u32[]{:S(2)}, u32[]{:S(2)}) collective-permute-start(bf16[64,512]{1,0:T(8,128)(2,1)S(1)} %get-tuple-element.84), channel_id=1, source_target_pairs={{0,8},{1,9},{2,10},{3,11},{4,12},{5,13},{6,14},{7,15},{8,0},{9,1},... | collective-permute-start | bytes 196616 | tf_op jit(solution)/shard_map/ppermute | solution.py:361
  99.4 2.5 %collective-permute-start.23 = (bf16[64,512]{1,0:T(8,128)(2,1)S(1)}, bf16[64,512]{1,0:T(8,128)(2,1)S(1)}, u32[]{:S(2)}, u32[]{:S(2)}) collective-permute-start(bf16[64,512]{1,0:T(8,128)(2,1)S(1)} %get-tuple-element.85), channel_id=1, source_target_pairs={{0,24},{1,25},{2,26},{3,27},{4,28},{5,29},{6,30},{7,31},{8,16},{9,... | collective-permute-start | bytes 196616 | tf_op jit(solution)/shard_map/ppermute | solution.py:361
  101.9 1.4 %collective-permute-done.17 = bf16[2,2,64,512]{3,2,1,0:T(8,128)(2,1)S(1)} collective-permute-done((bf16[2,2,64,512]{3,2,1,0:T(8,128)(2,1)S(1)}, bf16[2,2,64,512]{3,2,1,0:T(8,128)(2,1)S(1)}, u32[]{:S(2)}, u32[]{:S(2)}) %collective-permute-start.17) | collective-permute-done | bytes 262176 | tf_op jit(solution)/shard_map/ppermute | solution.py:361
  103.5 1.6 %collective-permute-start.18 = (bf16[64,896]{1,0:T(8,128)(2,1)S(1)}, bf16[64,896]{1,0:T(8,128)(2,1)S(1)}, u32[]{:S(2)}, u32[]{:S(2)}) collective-permute-start(bf16[64,896]{1,0:T(8,128)(2,1)S(1)} %get-tuple-element.79), channel_id=1, source_target_pairs={{0,8},{1,9},{2,10},{3,11},{4,12},{5,13},{6,14},{7,15},{8,0},{9,1},... | collective-permute-start | bytes 344072 | tf_op jit(solution)/shard_map/ppermute | solution.py:361
  105.1 2.5 %collective-permute-start.20 = (bf16[64,896]{1,0:T(8,128)(2,1)S(1)}, bf16[64,896]{1,0:T(8,128)(2,1)S(1)}, u32[]{:S(2)}, u32[]{:S(2)}) collective-permute-start(bf16[64,896]{1,0:T(8,128)(2,1)S(1)} %get-tuple-element.80), channel_id=1, source_target_pairs={{0,24},{1,25},{2,26},{3,27},{4,28},{5,29},{6,30},{7,31},{8,16},{9,... | collective-permute-start | bytes 344072 | tf_op jit(solution)/shard_map/ppermute | solution.py:361
  107.6 1.7 %collective-permute-done.22 = bf16[64,512]{1,0:T(8,128)(2,1)S(1)} collective-permute-done((bf16[64,512]{1,0:T(8,128)(2,1)S(1)}, bf16[64,512]{1,0:T(8,128)(2,1)S(1)}, u32[]{:S(2)}, u32[]{:S(2)}) %collective-permute-start.22) | collective-permute-done | bytes 65568 | tf_op jit(solution)/shard_map/ppermute | solution.py:361
  110.1 2.5 %collective-permute-done.20 = bf16[64,896]{1,0:T(8,128)(2,1)S(1)} collective-permute-done((bf16[64,896]{1,0:T(8,128)(2,1)S(1)}, bf16[64,896]{1,0:T(8,128)(2,1)S(1)}, u32[]{:S(2)}, u32[]{:S(2)}) %collective-permute-start.20) | collective-permute-done | bytes 114720 | tf_op jit(solution)/shard_map/ppermute | solution.py:361
  112.6 4.2 %collective-permute-done.19 = bf16[64,896]{1,0:T(8,128)(2,1)S(1)} collective-permute-done((bf16[64,896]{1,0:T(8,128)(2,1)S(1)}, bf16[64,896]{1,0:T(8,128)(2,1)S(1)}, u32[]{:S(2)}, u32[]{:S(2)}) %collective-permute-start.19) | collective-permute-done | bytes 114720 | tf_op jit(solution)/shard_map/ppermute | solution.py:361
  (82 shorter events, 9.5 us)
Async XLA Ops:
  0.6 7.5 %copy-start.3 = (s32[2]{0:T(128)S(1)}, s32[2]{0:T(128)}, u32[]{:S(2)}) copy-start(s32[2]{0:T(128)} %constant.14.clone) | copy-start | bytes 28
  0.6 7.5 %copy-start.4 = (s32[2]{0:T(128)S(1)}, s32[2]{0:T(128)}, u32[]{:S(2)}) copy-start(s32[2]{0:T(128)} %constant.13.clone) | copy-start | bytes 28
  0.7 20.5 %copy-start.5 = (f32[2048]{0:T(1024)S(1)}, f32[2048]{0:T(1024)}, u32[]{:S(2)}) copy-start(f32[2048]{0:T(1024)} %param.17) | copy-start | bytes 24580
  2.7 5.4 %collective-permute-start = (s32[3,12]{1,0:T(4,128)}, s32[3,12]{1,0:T(4,128)S(1)}, u32[]{:S(2)}, u32[]{:S(2)}) collective-permute-start(s32[3,12]{1,0:T(4,128)} %get-tuple-element.35), channel_id=1, source_target_pairs={{0,1},{1,0},{2,3},{3,2},{4,5},{5,4},{6,7},{7,6},{8,9},{9,8},{10,11... | collective-permute-start | bytes 440 | tf_op jit(solution)/shard_map/ppermute | solution.py:361
  8.1 24.6 %collective-permute-start.6 = (bf16[768,512]{1,0:T(8,128)(2,1)}, bf16[768,512]{1,0:T(8,128)(2,1)}, u32[]{:S(2)}, u32[]{:S(2)}) collective-permute-start(bf16[768,512]{1,0:T(8,128)(2,1)} %get-tuple-element.37.r_2_), channel_id=1, source_target_pairs={{0,1},{1,0},{2,3},{3,2},{4,5},{5,4},{6,7},{7,6},{8,9},{9,8},{10,11... | collective-permute-start | bytes 2359304 | tf_op jit(solution)/shard_map/ppermute | solution.py:361
  9.5 35.3 %collective-permute-start.5 = (bf16[768,512]{1,0:T(8,128)(2,1)}, bf16[768,512]{1,0:T(8,128)(2,1)}, u32[]{:S(2)}, u32[]{:S(2)}) collective-permute-start(bf16[768,512]{1,0:T(8,128)(2,1)} %get-tuple-element.37.r_2_), channel_id=1, source_target_pairs={{2,0},{3,1},{4,2},{5,3},{6,4},{7,5},{8,6},{9,7},{10,8},{11,9},{12,... | collective-permute-start | bytes 2359304 | tf_op jit(solution)/shard_map/ppermute | solution.py:357
  10.7 34.0 %collective-permute-start.4 = (bf16[768,512]{1,0:T(8,128)(2,1)}, bf16[768,512]{1,0:T(8,128)(2,1)}, u32[]{:S(2)}, u32[]{:S(2)}) collective-permute-start(bf16[768,512]{1,0:T(8,128)(2,1)} %get-tuple-element.37.r_2_), channel_id=1, source_target_pairs={{0,2},{1,3},{2,4},{3,5},{4,6},{5,7},{6,8},{7,9},{8,10},{9,11},{10,... | collective-permute-start | bytes 2359304 | tf_op jit(solution)/shard_map/ppermute | solution.py:357
  15.5 20.7 %collective-permute-start.3 = (s32[6,12]{1,0:T(8,128)S(1)}, s32[6,12]{1,0:T(8,128)S(1)}, u32[]{:S(2)}, u32[]{:S(2)}) collective-permute-start(s32[6,12]{1,0:T(8,128)S(1)} %add_select_fusion.1), channel_id=1, source_target_pairs={{2,0},{3,1},{4,2},{5,3},{6,4},{7,5},{8,6},{9,7},{10,8},{11,9},{12,... | collective-permute-start | bytes 872 | tf_op jit(solution)/shard_map/ppermute | solution.py:357
  16.7 12.2 %collective-permute-start.1 = (s32[6,12]{1,0:T(8,128)S(1)}, s32[6,12]{1,0:T(8,128)S(1)}, u32[]{:S(2)}, u32[]{:S(2)}) collective-permute-start(s32[6,12]{1,0:T(8,128)S(1)} %add_select_fusion.1), channel_id=1, source_target_pairs={{0,4},{2,6},{4,8},{6,10},{8,12},{10,14},{12,16},{14,18},{16,20},{1... | collective-permute-start | bytes 872 | tf_op jit(solution)/shard_map/ppermute | solution.py:438
  28.9 7.3 %collective-permute-start.2 = (s32[6,12]{1,0:T(8,128)S(1)}, s32[6,12]{1,0:T(8,128)S(1)}, u32[]{:S(2)}, u32[]{:S(2)}) collective-permute-start(s32[6,12]{1,0:T(8,128)S(1)} %add_select_fusion.1), channel_id=1, source_target_pairs={{0,2},{1,3},{2,4},{3,5},{4,6},{5,7},{6,8},{7,9},{8,10},{9,11},{10,... | collective-permute-start | bytes 872 | tf_op jit(solution)/shard_map/ppermute | solution.py:357
  32.7 12.0 %collective-permute-start.7 = (bf16[768,512]{1,0:T(8,128)(2,1)}, bf16[768,512]{1,0:T(8,128)(2,1)}, u32[]{:S(2)}, u32[]{:S(2)}) collective-permute-start(bf16[768,512]{1,0:T(8,128)(2,1)} %collective-permute-done.6.r_5_), channel_id=1, source_target_pairs={{0,2},{2,4},{4,6},{6,8},{8,10},{10,12},{12,14},{14,16},{16,18},{18... | collective-permute-start | bytes 2359304 | tf_op jit(solution)/shard_map/ppermute | solution.py:432
  58.4 4.1 %collective-permute-start.8 = (bf16[2,2,2,2,64,512]{5,4,3,2,1,0:T(8,128)(2,1)S(1)}, bf16[2,2,2,2,64,512]{5,4,3,2,1,0:T(8,128)(2,1)S(1)}, u32[]{:S(2)}, u32[]{:S(2)}) collective-permute-start(bf16[2,2,2,2,64,512]{5,4,3,2,1,0:T(8,128)(2,1)S(1)} %bitcast.88), channel_id=1, source_target_pairs={{0,2},{1,3},{2,0},{3,1},{4,6},{5,7},{6,4},{7,5},{8,10},{9,11},{10,... | collective-permute-start | bytes 3145736 | tf_op jit(solution)/shard_map/ppermute | solution.py:361
  60.2 2.6 %slice-start = ((s8[6291456]{0:T(1024)(128)(4,1)}), s8[4194304]{0:T(1024)(128)(4,1)S(1)}, s32[]{:S(2)}) async-start(s8[6291456]{0:T(1024)(128)(4,1)} %bitcast.84), calls=%async_computation | async-start | bytes 8388608
  60.2 2.9 %slice-start.1 = ((s8[6291456]{0:T(1024)(128)(4,1)}), s8[2097152]{0:T(1024)(128)(4,1)S(1)}, s32[]{:S(2)}) async-start(s8[6291456]{0:T(1024)(128)(4,1)} %bitcast.84), calls=%async_computation.1 | async-start | bytes 4194304
  60.2 3.1 %copy-start.2 = (bf16[768,768]{1,0:T(8,128)(2,1)S(1)}, bf16[768,768]{1,0:T(8,128)(2,1)}, u32[]{:S(2)}) copy-start(bf16[768,768]{1,0:T(8,128)(2,1)} %pad_maximum_fusion.refs_9_) | copy-start | bytes 3538948
  62.2 2.0 %copy-start = (bf16[2048,512]{1,0:T(8,128)(2,1)S(1)}, bf16[2048,512]{1,0:T(8,128)(2,1)}, u32[]{:S(2)}) copy-start(bf16[2048,512]{1,0:T(8,128)(2,1)} %refs_7_.3) | copy-start | bytes 6291460
  68.0 9.6 %collective-permute-start.9 = (bf16[2,2,2,2,64,896]{5,4,3,2,1,0:T(8,128)(2,1)S(1)}, bf16[2,2,2,2,64,896]{5,4,3,2,1,0:T(8,128)(2,1)S(1)}, u32[]{:S(2)}, u32[]{:S(2)}) collective-permute-start(bf16[2,2,2,2,64,896]{5,4,3,2,1,0:T(8,128)(2,1)S(1)} %bitcast.89), channel_id=1, source_target_pairs={{0,2},{1,3},{2,0},{3,1},{4,6},{5,7},{6,4},{7,5},{8,10},{9,11},{10,... | collective-permute-start | bytes 5505032 | tf_op jit(solution)/shard_map/ppermute | solution.py:361
  68.2 12.4 %collective-permute-start.11 = (bf16[2,2,2,64,256]{4,3,2,1,0:T(8,128)(2,1)S(1)}, bf16[2,2,2,64,256]{4,3,2,1,0:T(8,128)(2,1)S(1)}, u32[]{:S(2)}, u32[]{:S(2)}) collective-permute-start(bf16[2,2,2,64,256]{4,3,2,1,0:T(8,128)(2,1)S(1)} %get-tuple-element.74), channel_id=1, source_target_pairs={{0,4},{1,5},{2,6},{3,7},{4,0},{5,1},{6,2},{7,3},{8,12},{9,13},{10,... | collective-permute-start | bytes 786440 | tf_op jit(solution)/shard_map/ppermute | solution.py:361
  71.1 9.4 %collective-permute-start.10 = (bf16[2,2,2,64,256]{4,3,2,1,0:T(8,128)(2,1)S(1)}, bf16[2,2,2,64,256]{4,3,2,1,0:T(8,128)(2,1)S(1)}, u32[]{:S(2)}, u32[]{:S(2)}) collective-permute-start(bf16[2,2,2,64,256]{4,3,2,1,0:T(8,128)(2,1)S(1)} %get-tuple-element.76), channel_id=1, source_target_pairs={{0,1},{1,0},{2,3},{3,2},{4,5},{5,4},{6,7},{7,6},{8,9},{9,8},{10,11... | collective-permute-start | bytes 786440 | tf_op jit(solution)/shard_map/ppermute | solution.py:361
  78.2 2.5 %copy-start.1 = (bf16[2048,768]{1,0:T(8,128)(2,1)S(1)}, bf16[2048,768]{1,0:T(8,128)(2,1)}, u32[]{:S(2)}) copy-start(bf16[2048,768]{1,0:T(8,128)(2,1)} %refs_3_.1) | copy-start | bytes 9437188
  78.3 16.9 %collective-permute-start.14 = (bf16[2,2,2,64,384]{4,3,2,1,0:T(8,128)(2,1)S(1)}, bf16[2,2,2,64,384]{4,3,2,1,0:T(8,128)(2,1)S(1)}, u32[]{:S(2)}, u32[]{:S(2)}) collective-permute-start(bf16[2,2,2,64,384]{4,3,2,1,0:T(8,128)(2,1)S(1)} %get-tuple-element.70), channel_id=1, source_target_pairs={{0,1},{1,0},{2,3},{3,2},{4,5},{5,4},{6,7},{7,6},{8,9},{9,8},{10,11... | collective-permute-start | bytes 1179656 | tf_op jit(solution)/shard_map/ppermute | solution.py:361
  78.5 17.3 %collective-permute-start.15 = (bf16[2,2,2,64,512]{4,3,2,1,0:T(8,128)(2,1)S(1)}, bf16[2,2,2,64,512]{4,3,2,1,0:T(8,128)(2,1)S(1)}, u32[]{:S(2)}, u32[]{:S(2)}) collective-permute-start(bf16[2,2,2,64,512]{4,3,2,1,0:T(8,128)(2,1)S(1)} %get-tuple-element.72), channel_id=1, source_target_pairs={{0,4},{1,5},{2,6},{3,7},{4,0},{5,1},{6,2},{7,3},{8,12},{9,13},{10,... | collective-permute-start | bytes 1572872 | tf_op jit(solution)/shard_map/ppermute | solution.py:361
  86.9 8.2 %collective-permute-start.12 = (bf16[2,2,64,256]{3,2,1,0:T(8,128)(2,1)S(1)}, bf16[2,2,64,256]{3,2,1,0:T(8,128)(2,1)S(1)}, u32[]{:S(2)}, u32[]{:S(2)}) collective-permute-start(bf16[2,2,64,256]{3,2,1,0:T(8,128)(2,1)S(1)} %get-tuple-element.90), channel_id=1, source_target_pairs={{0,4},{1,5},{2,6},{3,7},{4,0},{5,1},{6,2},{7,3},{8,12},{9,13},{10,... | collective-permute-start | bytes 393224 | tf_op jit(solution)/shard_map/ppermute | solution.py:361
  87.3 7.9 %collective-permute-start.13 = (bf16[2,2,64,256]{3,2,1,0:T(8,128)(2,1)S(1)}, bf16[2,2,64,256]{3,2,1,0:T(8,128)(2,1)S(1)}, u32[]{:S(2)}, u32[]{:S(2)}) collective-permute-start(bf16[2,2,64,256]{3,2,1,0:T(8,128)(2,1)S(1)} %get-tuple-element.88), channel_id=1, source_target_pairs={{0,1},{1,0},{2,3},{3,2},{4,5},{5,4},{6,7},{7,6},{8,9},{9,8},{10,11... | collective-permute-start | bytes 393224 | tf_op jit(solution)/shard_map/ppermute | solution.py:361
  95.4 6.5 %collective-permute-start.16 = (bf16[2,2,64,384]{3,2,1,0:T(8,128)(2,1)S(1)}, bf16[2,2,64,384]{3,2,1,0:T(8,128)(2,1)S(1)}, u32[]{:S(2)}, u32[]{:S(2)}) collective-permute-start(bf16[2,2,64,384]{3,2,1,0:T(8,128)(2,1)S(1)} %get-tuple-element.83), channel_id=1, source_target_pairs={{0,4},{1,5},{2,6},{3,7},{4,0},{5,1},{6,2},{7,3},{8,12},{9,13},{10,... | collective-permute-start | bytes 589832 | tf_op jit(solution)/shard_map/ppermute | solution.py:361
  95.9 7.4 %collective-permute-start.17 = (bf16[2,2,64,512]{3,2,1,0:T(8,128)(2,1)S(1)}, bf16[2,2,64,512]{3,2,1,0:T(8,128)(2,1)S(1)}, u32[]{:S(2)}, u32[]{:S(2)}) collective-permute-start(bf16[2,2,64,512]{3,2,1,0:T(8,128)(2,1)S(1)} %get-tuple-element.78), channel_id=1, source_target_pairs={{0,1},{1,0},{2,3},{3,2},{4,5},{5,4},{6,7},{7,6},{8,9},{9,8},{10,11... | collective-permute-start | bytes 786440 | tf_op jit(solution)/shard_map/ppermute | solution.py:361
  97.8 9.9 %collective-permute-start.21 = (bf16[64,512]{1,0:T(8,128)(2,1)S(1)}, bf16[64,512]{1,0:T(8,128)(2,1)S(1)}, u32[]{:S(2)}, u32[]{:S(2)}) collective-permute-start(bf16[64,512]{1,0:T(8,128)(2,1)S(1)} %get-tuple-element.84), channel_id=1, source_target_pairs={{0,8},{1,9},{2,10},{3,11},{4,12},{5,13},{6,14},{7,15},{8,0},{9,1},... | collective-permute-start | bytes 196616 | tf_op jit(solution)/shard_map/ppermute | solution.py:361
  99.4 8.2 %collective-permute-start.23 = (bf16[64,512]{1,0:T(8,128)(2,1)S(1)}, bf16[64,512]{1,0:T(8,128)(2,1)S(1)}, u32[]{:S(2)}, u32[]{:S(2)}) collective-permute-start(bf16[64,512]{1,0:T(8,128)(2,1)S(1)} %get-tuple-element.85), channel_id=1, source_target_pairs={{0,24},{1,25},{2,26},{3,27},{4,28},{5,29},{6,30},{7,31},{8,16},{9,... | collective-permute-start | bytes 196616 | tf_op jit(solution)/shard_map/ppermute | solution.py:361
  101.9 7.5 %collective-permute-start.22 = (bf16[64,512]{1,0:T(8,128)(2,1)S(1)}, bf16[64,512]{1,0:T(8,128)(2,1)S(1)}, u32[]{:S(2)}, u32[]{:S(2)}) collective-permute-start(bf16[64,512]{1,0:T(8,128)(2,1)S(1)} %get-tuple-element.86), channel_id=1, source_target_pairs={{0,16},{1,17},{2,18},{3,19},{4,20},{5,21},{6,22},{7,23},{8,24},{9,... | collective-permute-start | bytes 196616 | tf_op jit(solution)/shard_map/ppermute | solution.py:361
  103.5 6.6 %collective-permute-start.18 = (bf16[64,896]{1,0:T(8,128)(2,1)S(1)}, bf16[64,896]{1,0:T(8,128)(2,1)S(1)}, u32[]{:S(2)}, u32[]{:S(2)}) collective-permute-start(bf16[64,896]{1,0:T(8,128)(2,1)S(1)} %get-tuple-element.79), channel_id=1, source_target_pairs={{0,8},{1,9},{2,10},{3,11},{4,12},{5,13},{6,14},{7,15},{8,0},{9,1},... | collective-permute-start | bytes 344072 | tf_op jit(solution)/shard_map/ppermute | solution.py:361
  105.1 7.4 %collective-permute-start.20 = (bf16[64,896]{1,0:T(8,128)(2,1)S(1)}, bf16[64,896]{1,0:T(8,128)(2,1)S(1)}, u32[]{:S(2)}, u32[]{:S(2)}) collective-permute-start(bf16[64,896]{1,0:T(8,128)(2,1)S(1)} %get-tuple-element.80), channel_id=1, source_target_pairs={{0,24},{1,25},{2,26},{3,27},{4,28},{5,29},{6,30},{7,31},{8,16},{9,... | collective-permute-start | bytes 344072 | tf_op jit(solution)/shard_map/ppermute | solution.py:361
  107.6 9.1 %collective-permute-start.19 = (bf16[64,896]{1,0:T(8,128)(2,1)S(1)}, bf16[64,896]{1,0:T(8,128)(2,1)S(1)}, u32[]{:S(2)}, u32[]{:S(2)}) collective-permute-start(bf16[64,896]{1,0:T(8,128)(2,1)S(1)} %get-tuple-element.81), channel_id=1, source_target_pairs={{0,16},{1,17},{2,18},{3,19},{4,20},{5,21},{6,22},{7,23},{8,24},{9,... | collective-permute-start | bytes 344072 | tf_op jit(solution)/shard_map/ppermute | solution.py:361

commit v7 on v6

--- a/solution.py
+++ b/solution.py
@@ -373,13 +373,19 @@
     return [(i, i + by) for i in range(0, count - by, 2)] + [(i, i - by) for i in range(by + 1, count, 2)]
 
 
+def advance(reduction, step, steps):
+    if step < steps:
+        reduction.start()
+    else:
+        reduction.start_last()
+
+
 class Reduction:
 
     def __init__(self, part, count, bits, orders):
-        lanes = part.shape[-1]
-        cut = lanes // 2 // TILE * TILE
+        cut = part.shape[-2] // 2
         self.count, self.last = count, bits[-2:]
-        self.parts = [part[..., :cut], part[..., cut:]]
+        self.parts = [part[..., :cut, :], part[..., cut:, :]]
         self.left = [list(bits), list(bits)]
         self.orders = [list(order) for order in orders]
 
@@ -398,8 +404,9 @@
         return tuple(self.parts)
 
     def start_last(self):
-        part = jnp.concatenate(self.parts, axis=-1)
+        part = jnp.concatenate(self.parts, axis=-2)
         part = part.reshape((4,) + part.shape[-2:])
+        self.sent = [part]
         hi, lo = self.last
         self.own = part[0]
         self.got = [flipped(part[k], self.count, ((k >> 1) << hi) | ((k & 1) << lo)) for k in range(1, 4)]
@@ -425,21 +432,22 @@
     even = (me & 1) == 0
     block, meta = stack(cot_img, cot_cap, tile_seed, tile_cols, tile_count)
     other = flipped(meta, count, 1)
-    block = after(block, other)
-    mate = flipped(block, count, 1)
+    third = lax.ppermute(
+        meta, AXES, [(i, i + 3) for i in range(1, count - 3, 2)] + [(i, i - 3) for i in range(4, count, 2)]
+    )
+    mate = flipped(after(block, other), count, 1)
     low = moved(block, count, 2)
     high = moved(block, count, -2)
     far = lax.ppermute(mate, AXES, nearest_pair(count, 2))
     pair = jnp.where(even, jnp.concatenate([meta, other]), jnp.concatenate([other, meta]))
     feats = jnp.concatenate([feats_img, feats_cap], axis=0)
-    pair, feats = lax.optimization_barrier((pair, after(feats, block)))
+    pair, feats, third = lax.optimization_barrier((pair, after(feats, block), third))
     pair_low = moved(pair, count, 2)
     pair_high = moved(pair, count, -2)
-    pair_far = lax.ppermute(pair, AXES, nearest_pair(count, 4))
     wide = jnp.where(
         even,
-        jnp.concatenate([pair_far[tiles:], pair_low, pair, pair_high]),
-        jnp.concatenate([pair_low, pair, pair_high, pair_far[:tiles]]),
+        jnp.concatenate([third, pair_low, pair, pair_high]),
+        jnp.concatenate([pair_low, pair, pair_high, third]),
     )
     frame = jnp.arange(7 * tiles, dtype=jnp.int32)[:, None]
     counts = wide[:, 2 * slots]
@@ -498,42 +506,31 @@
 
     core = 1 << a
     rest = bits[1:]
-    out_sent = out_half(order[half:], logit)
-    out_came = flipped(out_sent, count, core)
-    out_kept = out_half(order[:half], after(logit, out_sent))
     orders = (cap_bits + img_bits, img_bits + cap_bits)
-    out_core = added(out_kept, out_came)
-    r_out = Reduction(out_core, count, rest, orders)
-    r_out.start()
-    in_sent, grad_sent = in_half(order[half:], after(logit, out_core))
+    steps = m - 3
+    in_sent, grad_sent = in_half(order[half:], logit)
     in_came = flipped(in_sent, count, core)
     in_kept, grad_kept = in_half(order[:half], after(logit, grad_sent))
     r_in = Reduction(added(in_kept, in_came), count, rest, orders)
     r_in.start()
-    done = r_out.finish(*r_in.sent)
-    steps = m - 3
-    if steps > 1:
-        r_out.start()
-    else:
-        r_out.start_last()
+    out_sent = out_half(order[half:], after(logit, *r_in.sent))
+    out_came = flipped(out_sent, count, core)
+    out_kept = out_half(order[:half], after(logit, out_sent))
+    r_out = Reduction(added(out_kept, out_came), count, rest, orders)
+    r_out.start()
+    for k in range(steps):
+        r_in.finish(*r_out.sent)
+        advance(r_in, k + 1, steps)
+        r_out.finish(*r_in.sent)
+        if k + 1 < steps:
+            r_out.start()
     grad_img, grad_cap = over_hidden(
         feat_kernel, "feat_grad", order, grouped(f_in) + [rows_of_half(nodes, half, 0), rows_of_half(nodes, half, 1)],
         (whole((local_rows, f_in)),) * 2, (jax.ShapeDtypeStruct((local_rows, f_in), BF16),) * 2,
-        [pltpu.VMEM((nodes, f_in), F32)], [w_in] * GROUP + [after(grad_kept, *done), grad_sent],
-    )
-    done = (grad_img,)
-    for k in range(1, steps):
-        done = r_out.finish(*done)
-        if k + 1 < steps:
-            r_out.start()
-        else:
-            r_out.start_last()
-    for k in range(steps):
-        done = r_in.finish(*done)
-        if k + 1 < steps:
-            r_in.start()
-        else:
-            r_in.start_last()
+        [pltpu.VMEM((nodes, f_in), F32)], [w_in] * GROUP + [after(grad_kept, *r_out.parts), grad_sent],
+    )
+    r_out.start_last()
+    r_in.own = after(r_in.own, *r_out.sent)
     grad_scale = 1.0 / math.sqrt(nodes * count)
     g_out, g_in = [r.result() * grad_scale for r in (r_out, r_in)]
     return (grad_img, grad_cap, g_in[:, :f_in], g_out, g_in[:, f_in])

time: 118 us -> 126 us (1.068)
  waiting for transfers between devices: 17.7 us -> 28 us
  starting transfers between devices: 43 us -> 41.5 us
  local copies, waits for them, and re-layouts: 3.68 us -> 2.29 us
    ppermute x18, waiting for transfers between devices: 17.7 us -> 28 us  [flipped(): return lax.ppermute(array, AXES, [(i, i ^ mask) for i in range(count)])]
    ppermute x1, starting transfers between devices: 4.4 us -> 0.65 us  [per_device(): lax.ppermute(meta, AXES, [(i, i + 3) for i in range(1, count - 3, 2)] + [...]
    ppermute x18, starting transfers between devices: 24.8 us -> 28.2 us  [flipped(): return lax.ppermute(array, AXES, [(i, i ^ mask) for i in range(count)])]
    unnamed x16 -> x14, local copies, waits for them, and re-layouts: 1.43 us -> 0.04 us
  transfers between devices with their start and end apart: 24 -> 24, of which waited for: 7 -> 6; matrix products, arithmetic and copies ran while one was open for 12% -> 11% of each run, Pallas kernels for 17% -> 16%
where the time goes in v7:
time: 126 us
  starting transfers between devices  41.5 us (33%)
  Pallas kernels  39.7 us (32%)
  waiting for transfers between devices  28 us (22%)
  matrix products  7.72 us (6%)
  other arithmetic  5.66 us (4%)
  local copies, waits for them, and re-layouts  2.29 us (2%)
    ppermute x18, starting transfers between devices, flipped(): return lax.ppermute(array, AXES, [(i, i ^ mask) for i in range(count)])  28.2 us
    ppermute x18, waiting for transfers between devices, flipped(): return lax.ppermute(array, AXES, [(i, i ^ mask) for i in range(count)])  28 us
    pallas_call x5, Pallas kernels, over_hidden(): pl.pallas_call(kernel, out_shape=out_shape, grid_spec=pltpu.PrefetchScala...  18 us
    pallas_call x1, Pallas kernels, propagate(): pl.pallas_call(lambda *r: hops_kernel(*r, tiles=tiles, slots=slots, width...  11.8 us
    ppermute x4, starting transfers between devices, moved(): lax.ppermute(array, AXES, [(i, i + by) for i in range(count) if 0 <= i +...  9.52 us
    pallas_call x1, Pallas kernels, make_tiles(): pl.pallas_call(lambda *r: tiles_kernel(*r, tiles=tiles, slots=slots), out...  7.8 us
    dot_general x1, matrix products, per_device(): lax.dot_general(w_in, feats, across, preferred_element_type=F32)  7.72 us
    ppermute x1, starting transfers between devices, per_device(): far = lax.ppermute(mate, AXES, nearest_pair(count, 2))  3.09 us
  transfers between devices with their start and end apart: 24, of which 6 were waited for; matrix products, arithmetic and copies ran while one was open for 11% of the time, Pallas kernels for 16%

profile of v7, /device:TPU:0, one launch (start us, length us, event | category | flops | bytes accessed | tf_op | source)
XLA Modules:
  0.0 126.0 jit_solution(10779070947947491284)
XLA Ops:
  0.7 2.1 %stack.1 = (bf16[768,512]{1,0:T(8,128)(2,1)}, s32[3,12]{1,0:T(4,128)}) custom-call(s32[3]{0:T(128)} %count_ref.1, bf16[384,512]{1,0:T(8,128)(2,1)} %top_ref.1, bf16[384,512]{1,0:T(8,128)(2,1)} %bottom_ref.1, s32[3,4]{1,0:T(4,128)} %seed_ref.1, s32[3,4]{1,0:T(4,128)} %cols_ref.1), custom_call_target="tpu_custom_call" | custom-call | flops 1 | bytes 1 | tf_op jit(solution)/shard_map/stack/pallas_call | solution.py:342
  3.4 5.7 %collective-permute-start = (s32[3,12]{1,0:T(4,128)}, s32[3,12]{1,0:T(4,128)S(1)}, u32[]{:S(2)}, u32[]{:S(2)}) collective-permute-start(s32[3,12]{1,0:T(4,128)} %get-tuple-element.37), channel_id=1, source_target_pairs={{0,1},{1,0},{2,3},{3,2},{4,5},{5,4},{6,7},{7,6},{8,9},{9,8},{10,11... | collective-permute-start | bytes 440 | tf_op jit(solution)/shard_map/ppermute | solution.py:361
  9.2 1.3 %collective-permute-start.5 = (bf16[768,512]{1,0:T(8,128)(2,1)}, bf16[768,512]{1,0:T(8,128)(2,1)}, u32[]{:S(2)}, u32[]{:S(2)}) collective-permute-start(bf16[768,512]{1,0:T(8,128)(2,1)} %get-tuple-element.44.r_2_), channel_id=1, source_target_pairs={{2,0},{3,1},{4,2},{5,3},{6,4},{7,5},{8,6},{9,7},{10,8},{11,9},{12,... | collective-permute-start | bytes 2359304 | tf_op jit(solution)/shard_map/ppermute | solution.py:357
  10.4 3.9 %collective-permute-start.4 = (bf16[768,512]{1,0:T(8,128)(2,1)}, bf16[768,512]{1,0:T(8,128)(2,1)}, u32[]{:S(2)}, u32[]{:S(2)}) collective-permute-start(bf16[768,512]{1,0:T(8,128)(2,1)} %get-tuple-element.44.r_2_), channel_id=1, source_target_pairs={{0,2},{1,3},{2,4},{3,5},{4,6},{5,7},{6,8},{7,9},{8,10},{9,11},{10,... | collective-permute-start | bytes 2359304 | tf_op jit(solution)/shard_map/ppermute | solution.py:357
  14.5 2.3 %pad_maximum_fusion.refs_9_ = bf16[768,768]{1,0:T(8,128)(2,1)} fusion(bf16[384,768]{1,0:T(8,128)(2,1)} %param.13, bf16[384,768]{1,0:T(8,128)(2,1)} %param.12), kind=kLoop, calls=%fused_computation.15 | loop fusion | flops 2359296 | bytes 2359296 | tf_op jit(solution)/shard_map/concatenate | solution.py:443
  16.8 0.8 add_select_fusion.1
  17.6 1.3 %collective-permute-start.3 = (s32[6,12]{1,0:T(8,128)S(1)}, s32[6,12]{1,0:T(8,128)S(1)}, u32[]{:S(2)}, u32[]{:S(2)}) collective-permute-start(s32[6,12]{1,0:T(8,128)S(1)} %add_select_fusion.1), channel_id=1, source_target_pairs={{2,0},{3,1},{4,2},{5,3},{6,4},{7,5},{8,6},{9,7},{10,8},{11,9},{12,... | collective-permute-start | bytes 872 | tf_op jit(solution)/shard_map/ppermute | solution.py:357
  18.9 3.0 %collective-permute-start.2 = (s32[6,12]{1,0:T(8,128)S(1)}, s32[6,12]{1,0:T(8,128)S(1)}, u32[]{:S(2)}, u32[]{:S(2)}) collective-permute-start(s32[6,12]{1,0:T(8,128)S(1)} %add_select_fusion.1), channel_id=1, source_target_pairs={{0,2},{1,3},{2,4},{3,5},{4,6},{5,7},{6,8},{7,9},{8,10},{9,11},{10,... | collective-permute-start | bytes 872 | tf_op jit(solution)/shard_map/ppermute | solution.py:357
  22.3 7.7 %fusion.3 = (f32[2048,768]{1,0:T(8,128)}, bf16[2048,768]{1,0:T(8,128)(2,1)S(1)}) fusion(f32[2048]{0:T(1024)S(1)} %copy-done.6, bf16[768,768]{1,0:T(8,128)(2,1)} %pad_maximum_fusion.refs_9_, bf16[2048,768]{1,0:T(8,128)(2,1)} %refs_3_.1), kind=kOutput, calls=%fused_computation.4 | convolution fusion | flops 2433220608 | bytes 13770752 | tf_op jit(solution)/shard_map/dot_general | solution.py:478
  30.0 12.3 %collective-permute-done.6.r_5_ = bf16[768,512]{1,0:T(8,128)(2,1)} collective-permute-done((bf16[768,512]{1,0:T(8,128)(2,1)}, bf16[768,512]{1,0:T(8,128)(2,1)}, u32[]{:S(2)}, u32[]{:S(2)}) %collective-permute-start.6) | collective-permute-done | bytes 786464 | tf_op jit(solution)/shard_map/ppermute | solution.py:361
  42.3 3.1 %collective-permute-start.7 = (bf16[768,512]{1,0:T(8,128)(2,1)}, bf16[768,512]{1,0:T(8,128)(2,1)}, u32[]{:S(2)}, u32[]{:S(2)}) collective-permute-start(bf16[768,512]{1,0:T(8,128)(2,1)} %collective-permute-done.6.r_5_), channel_id=1, source_target_pairs={{0,2},{2,4},{4,6},{6,8},{8,10},{10,12},{12,14},{14,16},{16,18},{18... | collective-permute-start | bytes 2359304 | tf_op jit(solution)/shard_map/ppermute | solution.py:441
  46.0 7.8 %tiles.1 = (bf16[15,128,512]{2,1,0:T(8,128)(2,1)}, bf16[15,512,128]{2,1,0:T(8,128)(2,1)}, f32[15,128,128]{2,1,0:T(8,128)}, f32[15,128,128]{2,1,0:T(8,128)}) custom-call(s32[84]{0:T(128)S(1)} %reshape.41.r_0_, s32[84]{0:T(128)S(1)} %reshape.42.r_1_, s32[21]{0:T(128)S(1)} %slice_reduce_fusion.1.r_2_), custom_call_target="tpu_custom_call" | custom-call | flops 1 | bytes 1 | tf_op jit(solution)/shard_map/tiles/pallas_call | solution.py:103
  54.0 11.8 %hops.1.refs_8_.refs_4_ = bf16[768,512]{1,0:T(8,128)(2,1)S(1)} custom-call(s32[60]{0:T(128)S(1)} %reshape.40.r_0_, s32[2]{0:T(128)S(1)} %fusion.14.r_1_, bf16[768,512]{1,0:T(8,128)(2,1)} %get-tuple-element.44.r_2_, bf16[768,512]{1,0:T(8,128)(2,1)} %collective-permute-done.4.r_3_, bf16[768,512]{1,0:T(8,128)(2,1)} %collective-permute-done.5.r_4_, ...), custom_call_target="tpu_custom_call" | custom-call | flops 1 | bytes 1 | tf_op jit(solution)/shard_map/hops/pallas_call | solution.py:211
  65.8 3.8 %part_in.2 = (bf16[1024,896]{1,0:T(8,128)(2,1)S(1)}, bf16[1024,768]{1,0:T(8,128)(2,1)S(1)}) custom-call(s32[16]{0:T(128)S(1)} %get-tuple-element.97.order_ref, f32[2048,768]{1,0:T(8,128)S(1)} %copy-done, f32[2048,768]{1,0:T(8,128)S(1)} %copy-done, f32[2048,768]{1,0:T(8,128)S(1)} %copy-done, f32[2048,768]{1,0:T(8,128)S(1)} %copy-done, ...), custom_call_target="tpu_custom_call" | custom-call | flops 1 | bytes 1 | tf_op jit(solution)/shard_map/part_in/pallas_call | solution.py:295
  69.7 3.8 %part_in.3 = (bf16[1024,896]{1,0:T(8,128)(2,1)S(1)}, bf16[1024,768]{1,0:T(8,128)(2,1)S(1)}) custom-call(s32[16]{0:T(128)S(1)} %get-tuple-element.98.order_ref, f32[2048,768]{1,0:T(8,128)S(1)} %copy-done, f32[2048,768]{1,0:T(8,128)S(1)} %copy-done, f32[2048,768]{1,0:T(8,128)S(1)} %copy-done, f32[2048,768]{1,0:T(8,128)S(1)} %copy-done, ...), custom_call_target="tpu_custom_call" | custom-call | flops 1 | bytes 1 | tf_op jit(solution)/shard_map/part_in/pallas_call | solution.py:295
  74.3 2.0 %part_out.2 = bf16[1024,512]{1,0:T(8,128)(2,1)S(1)} custom-call(s32[16]{0:T(128)S(1)} %get-tuple-element.97.order_ref, bf16[2048,768]{1,0:T(8,128)(2,1)S(1)} %get-tuple-element.52.refs_0_.refs_1_.refs_2_.refs_3_, bf16[2048,768]{1,0:T(8,128)(2,1)S(1)} %get-tuple-element.52.refs_0_.refs_1_.refs_2_.refs_3_, ...), custom_call_target="tpu_custom_call" | custom-call | flops 1 | bytes 1 | tf_op jit(solution)/shard_map/part_out/pallas_call | solution.py:295
  76.9 3.2 %collective-permute-start.11 = (bf16[2,2,2,32,896]{4,3,2,1,0:T(8,128)(2,1)S(1)}, bf16[2,2,2,32,896]{4,3,2,1,0:T(8,128)(2,1)S(1)}, u32[]{:S(2)}, u32[]{:S(2)}) collective-permute-start(bf16[2,2,2,32,896]{4,3,2,1,0:T(8,128)(2,1)S(1)} %get-tuple-element.74), channel_id=1, source_target_pairs={{0,4},{1,5},{2,6},{3,7},{4,0},{5,1},{6,2},{7,3},{8,12},{9,13},{10,... | collective-permute-start | bytes 1376264 | tf_op jit(solution)/shard_map/ppermute | solution.py:361
  80.1 2.2 %collective-permute-start.10 = (bf16[2,2,2,32,896]{4,3,2,1,0:T(8,128)(2,1)S(1)}, bf16[2,2,2,32,896]{4,3,2,1,0:T(8,128)(2,1)S(1)}, u32[]{:S(2)}, u32[]{:S(2)}) collective-permute-start(bf16[2,2,2,32,896]{4,3,2,1,0:T(8,128)(2,1)S(1)} %get-tuple-element.76), channel_id=1, source_target_pairs={{0,1},{1,0},{2,3},{3,2},{4,5},{5,4},{6,7},{7,6},{8,9},{9,8},{10,11... | collective-permute-start | bytes 1376264 | tf_op jit(solution)/shard_map/ppermute | solution.py:361
  82.3 2.0 %part_out.3 = bf16[1024,512]{1,0:T(8,128)(2,1)S(1)} custom-call(s32[16]{0:T(128)S(1)} %get-tuple-element.98.order_ref, bf16[2048,768]{1,0:T(8,128)(2,1)S(1)} %get-tuple-element.52.refs_0_.refs_1_.refs_2_.refs_3_, bf16[2048,768]{1,0:T(8,128)(2,1)S(1)} %get-tuple-element.52.refs_0_.refs_1_.refs_2_.refs_3_, ...), custom_call_target="tpu_custom_call" | custom-call | flops 1 | bytes 1 | tf_op jit(solution)/shard_map/part_out/pallas_call | solution.py:295
  85.4 8.2 %collective-permute-done.10 = bf16[2,2,2,32,896]{4,3,2,1,0:T(8,128)(2,1)S(1)} collective-permute-done((bf16[2,2,2,32,896]{4,3,2,1,0:T(8,128)(2,1)S(1)}, bf16[2,2,2,32,896]{4,3,2,1,0:T(8,128)(2,1)S(1)}, u32[]{:S(2)}, u32[]{:S(2)}) %collective-permute-start.10) | collective-permute-done | bytes 458784 | tf_op jit(solution)/shard_map/ppermute | solution.py:361
  94.1 2.0 %collective-permute-start.15 = (bf16[2,2,32,896]{3,2,1,0:T(8,128)(2,1)S(1)}, bf16[2,2,32,896]{3,2,1,0:T(8,128)(2,1)S(1)}, u32[]{:S(2)}, u32[]{:S(2)}) collective-permute-start(bf16[2,2,32,896]{3,2,1,0:T(8,128)(2,1)S(1)} %get-tuple-element.88), channel_id=1, source_target_pairs={{0,1},{1,0},{2,3},{3,2},{4,5},{5,4},{6,7},{7,6},{8,9},{9,8},{10,11... | collective-permute-start | bytes 688136 | tf_op jit(solution)/shard_map/ppermute | solution.py:361
  96.1 0.9 collective-permute-done.13
  97.2 2.2 %collective-permute-start.17 = (bf16[2,2,32,512]{3,2,1,0:T(8,128)(2,1)S(1)}, bf16[2,2,32,512]{3,2,1,0:T(8,128)(2,1)S(1)}, u32[]{:S(2)}, u32[]{:S(2)}) collective-permute-start(bf16[2,2,32,512]{3,2,1,0:T(8,128)(2,1)S(1)} %get-tuple-element.93), channel_id=1, source_target_pairs={{0,1},{1,0},{2,3},{3,2},{4,5},{5,4},{6,7},{7,6},{8,9},{9,8},{10,11... | collective-permute-start | bytes 393224 | tf_op jit(solution)/shard_map/ppermute | solution.py:361
  99.5 2.0 %collective-permute-start.16 = (bf16[2,2,32,512]{3,2,1,0:T(8,128)(2,1)S(1)}, bf16[2,2,32,512]{3,2,1,0:T(8,128)(2,1)S(1)}, u32[]{:S(2)}, u32[]{:S(2)}) collective-permute-start(bf16[2,2,32,512]{3,2,1,0:T(8,128)(2,1)S(1)} %get-tuple-element.95), channel_id=1, source_target_pairs={{0,4},{1,5},{2,6},{3,7},{4,0},{5,1},{6,2},{7,3},{8,12},{9,13},{10,... | collective-permute-start | bytes 393224 | tf_op jit(solution)/shard_map/ppermute | solution.py:361
  101.5 2.5 %collective-permute-done.15 = bf16[2,2,32,896]{3,2,1,0:T(8,128)(2,1)S(1)} collective-permute-done((bf16[2,2,32,896]{3,2,1,0:T(8,128)(2,1)S(1)}, bf16[2,2,32,896]{3,2,1,0:T(8,128)(2,1)S(1)}, u32[]{:S(2)}, u32[]{:S(2)}) %collective-permute-start.15) | collective-permute-done | bytes 229408 | tf_op jit(solution)/shard_map/ppermute | solution.py:361
  104.3 4.1 %collective-permute-start.20 = (bf16[64,896]{1,0:T(8,128)(2,1)S(1)}, bf16[64,896]{1,0:T(8,128)(2,1)S(1)}, u32[]{:S(2)}, u32[]{:S(2)}) collective-permute-start(bf16[64,896]{1,0:T(8,128)(2,1)S(1)} %get-tuple-element.82), channel_id=1, source_target_pairs={{0,24},{1,25},{2,26},{3,27},{4,28},{5,29},{6,30},{7,31},{8,16},{9,... | collective-permute-start | bytes 344072 | tf_op jit(solution)/shard_map/ppermute | solution.py:361
  109.2 6.3 %feat_grad.1 = (bf16[384,768]{1,0:T(8,128)(2,1)}, bf16[384,768]{1,0:T(8,128)(2,1)}) custom-call(s32[32]{0:T(128)S(1)} %fusion.27.order_ref, bf16[2048,768]{1,0:T(8,128)(2,1)S(1)} %copy-done.2, bf16[2048,768]{1,0:T(8,128)(2,1)S(1)} %copy-done.2, bf16[2048,768]{1,0:T(8,128)(2,1)S(1)} %copy-done.2, bf16[2048,768]{1,0:T(8,128)(2,1)S(1)} %copy-done.2, ...), custom_call_target="tpu_custom_call" | custom-call | flops 1 | bytes 1 | tf_op jit(solution)/shard_map/feat_grad/pallas_call | solution.py:295
  115.5 1.4 %collective-permute-start.21 = (bf16[64,512]{1,0:T(8,128)(2,1)S(1)}, bf16[64,512]{1,0:T(8,128)(2,1)S(1)}, u32[]{:S(2)}, u32[]{:S(2)}) collective-permute-start(bf16[64,512]{1,0:T(8,128)(2,1)S(1)} %get-tuple-element.89), channel_id=1, source_target_pairs={{0,8},{1,9},{2,10},{3,11},{4,12},{5,13},{6,14},{7,15},{8,0},{9,1},... | collective-permute-start | bytes 196616 | tf_op jit(solution)/shard_map/ppermute | solution.py:361
  117.0 2.5 %collective-permute-start.23 = (bf16[64,512]{1,0:T(8,128)(2,1)S(1)}, bf16[64,512]{1,0:T(8,128)(2,1)S(1)}, u32[]{:S(2)}, u32[]{:S(2)}) collective-permute-start(bf16[64,512]{1,0:T(8,128)(2,1)S(1)} %get-tuple-element.90), channel_id=1, source_target_pairs={{0,24},{1,25},{2,26},{3,27},{4,28},{5,29},{6,30},{7,31},{8,16},{9,... | collective-permute-start | bytes 196616 | tf_op jit(solution)/shard_map/ppermute | solution.py:361
  121.2 1.8 %collective-permute-done.23 = bf16[64,512]{1,0:T(8,128)(2,1)S(1)} collective-permute-done((bf16[64,512]{1,0:T(8,128)(2,1)S(1)}, bf16[64,512]{1,0:T(8,128)(2,1)S(1)}, u32[]{:S(2)}, u32[]{:S(2)}) %collective-permute-start.23) | collective-permute-done | bytes 65568 | tf_op jit(solution)/shard_map/ppermute | solution.py:361
  123.0 2.3 %collective-permute-done.22 = bf16[64,512]{1,0:T(8,128)(2,1)S(1)} collective-permute-done((bf16[64,512]{1,0:T(8,128)(2,1)S(1)}, bf16[64,512]{1,0:T(8,128)(2,1)S(1)}, u32[]{:S(2)}, u32[]{:S(2)}) %collective-permute-start.22) | collective-permute-done | bytes 65568 | tf_op jit(solution)/shard_map/ppermute | solution.py:361
  125.3 0.7 fusion.12
  (78 shorter events, 7.7 us)
Async XLA Ops:
  0.6 16.2 %copy-start.4 = (s32[2]{0:T(128)S(1)}, s32[2]{0:T(128)}, u32[]{:S(2)}) copy-start(s32[2]{0:T(128)} %constant.14.clone) | copy-start | bytes 28
  0.6 16.2 %copy-start.5 = (s32[2]{0:T(128)S(1)}, s32[2]{0:T(128)}, u32[]{:S(2)}) copy-start(s32[2]{0:T(128)} %constant.13.clone) | copy-start | bytes 28
  0.7 21.6 %copy-start.6 = (f32[2048]{0:T(1024)S(1)}, f32[2048]{0:T(1024)}, u32[]{:S(2)}) copy-start(f32[2048]{0:T(1024)} %param.17) | copy-start | bytes 24580
  2.8 14.8 %collective-permute-start.1 = (s32[3,12]{1,0:T(4,128)}, s32[3,12]{1,0:T(4,128)S(1)}, u32[]{:S(2)}, u32[]{:S(2)}) collective-permute-start(s32[3,12]{1,0:T(4,128)} %get-tuple-element.37), channel_id=1, source_target_pairs={{1,4},{3,6},{5,8},{7,10},{9,12},{11,14},{13,16},{15,18},{17,20},{1... | collective-permute-start | bytes 440 | tf_op jit(solution)/shard_map/ppermute | solution.py:435
  3.4 13.4 %collective-permute-start = (s32[3,12]{1,0:T(4,128)}, s32[3,12]{1,0:T(4,128)S(1)}, u32[]{:S(2)}, u32[]{:S(2)}) collective-permute-start(s32[3,12]{1,0:T(4,128)} %get-tuple-element.37), channel_id=1, source_target_pairs={{0,1},{1,0},{2,3},{3,2},{4,5},{5,4},{6,7},{7,6},{8,9},{9,8},{10,11... | collective-permute-start | bytes 440 | tf_op jit(solution)/shard_map/ppermute | solution.py:361
  9.2 44.8 %collective-permute-start.5 = (bf16[768,512]{1,0:T(8,128)(2,1)}, bf16[768,512]{1,0:T(8,128)(2,1)}, u32[]{:S(2)}, u32[]{:S(2)}) collective-permute-start(bf16[768,512]{1,0:T(8,128)(2,1)} %get-tuple-element.44.r_2_), channel_id=1, source_target_pairs={{2,0},{3,1},{4,2},{5,3},{6,4},{7,5},{8,6},{9,7},{10,8},{11,9},{12,... | collective-permute-start | bytes 2359304 | tf_op jit(solution)/shard_map/ppermute | solution.py:357
  10.4 43.5 %collective-permute-start.4 = (bf16[768,512]{1,0:T(8,128)(2,1)}, bf16[768,512]{1,0:T(8,128)(2,1)}, u32[]{:S(2)}, u32[]{:S(2)}) collective-permute-start(bf16[768,512]{1,0:T(8,128)(2,1)} %get-tuple-element.44.r_2_), channel_id=1, source_target_pairs={{0,2},{1,3},{2,4},{3,5},{4,6},{5,7},{6,8},{7,9},{8,10},{9,11},{10,... | collective-permute-start | bytes 2359304 | tf_op jit(solution)/shard_map/ppermute | solution.py:357
  17.6 27.8 %collective-permute-start.3 = (s32[6,12]{1,0:T(8,128)S(1)}, s32[6,12]{1,0:T(8,128)S(1)}, u32[]{:S(2)}, u32[]{:S(2)}) collective-permute-start(s32[6,12]{1,0:T(8,128)S(1)} %add_select_fusion.1), channel_id=1, source_target_pairs={{2,0},{3,1},{4,2},{5,3},{6,4},{7,5},{8,6},{9,7},{10,8},{11,9},{12,... | collective-permute-start | bytes 872 | tf_op jit(solution)/shard_map/ppermute | solution.py:357
  18.9 26.5 %collective-permute-start.2 = (s32[6,12]{1,0:T(8,128)S(1)}, s32[6,12]{1,0:T(8,128)S(1)}, u32[]{:S(2)}, u32[]{:S(2)}) collective-permute-start(s32[6,12]{1,0:T(8,128)S(1)} %add_select_fusion.1), channel_id=1, source_target_pairs={{0,2},{1,3},{2,4},{3,5},{4,6},{5,7},{6,8},{7,9},{8,10},{9,11},{10,... | collective-permute-start | bytes 872 | tf_op jit(solution)/shard_map/ppermute | solution.py:357
  21.9 20.3 %collective-permute-start.6 = (bf16[768,512]{1,0:T(8,128)(2,1)}, bf16[768,512]{1,0:T(8,128)(2,1)}, u32[]{:S(2)}, u32[]{:S(2)}) collective-permute-start(bf16[768,512]{1,0:T(8,128)(2,1)} %get-tuple-element.44.r_2_), channel_id=1, source_target_pairs={{0,1},{1,0},{2,3},{3,2},{4,5},{5,4},{6,7},{7,6},{8,9},{9,8},{10,11... | collective-permute-start | bytes 2359304 | tf_op jit(solution)/shard_map/ppermute | solution.py:361
  42.3 11.7 %collective-permute-start.7 = (bf16[768,512]{1,0:T(8,128)(2,1)}, bf16[768,512]{1,0:T(8,128)(2,1)}, u32[]{:S(2)}, u32[]{:S(2)}) collective-permute-start(bf16[768,512]{1,0:T(8,128)(2,1)} %collective-permute-done.6.r_5_), channel_id=1, source_target_pairs={{0,2},{2,4},{4,6},{6,8},{8,10},{10,12},{12,14},{14,16},{16,18},{18... | collective-permute-start | bytes 2359304 | tf_op jit(solution)/shard_map/ppermute | solution.py:441
  53.9 11.8 %copy-start = (f32[2048,768]{1,0:T(8,128)S(1)}, f32[2048,768]{1,0:T(8,128)}, u32[]{:S(2)}) copy-start(f32[2048,768]{1,0:T(8,128)} %get-tuple-element.41.refs_0_.refs_1_.refs_2_.refs_3_) | copy-start | bytes 18874372
  54.0 11.8 %copy-start.1 = (bf16[2048,512]{1,0:T(8,128)(2,1)S(1)}, bf16[2048,512]{1,0:T(8,128)(2,1)}, u32[]{:S(2)}) copy-start(bf16[2048,512]{1,0:T(8,128)(2,1)} %refs_7_.3) | copy-start | bytes 6291460
  54.0 11.8 %copy-start.3 = (bf16[768,768]{1,0:T(8,128)(2,1)S(1)}, bf16[768,768]{1,0:T(8,128)(2,1)}, u32[]{:S(2)}) copy-start(bf16[768,768]{1,0:T(8,128)(2,1)} %pad_maximum_fusion.refs_9_) | copy-start | bytes 3538948
  69.6 3.9 %collective-permute-start.8 = (bf16[2,2,2,2,64,896]{5,4,3,2,1,0:T(8,128)(2,1)S(1)}, bf16[2,2,2,2,64,896]{5,4,3,2,1,0:T(8,128)(2,1)S(1)}, u32[]{:S(2)}, u32[]{:S(2)}) collective-permute-start(bf16[2,2,2,2,64,896]{5,4,3,2,1,0:T(8,128)(2,1)S(1)} %bitcast.84), channel_id=1, source_target_pairs={{0,2},{1,3},{2,0},{3,1},{4,6},{5,7},{6,4},{7,5},{8,10},{9,11},{10,... | collective-permute-start | bytes 5505032 | tf_op jit(solution)/shard_map/ppermute | solution.py:361
  76.4 7.9 %collective-permute-start.9 = (bf16[2,2,2,2,64,512]{5,4,3,2,1,0:T(8,128)(2,1)S(1)}, bf16[2,2,2,2,64,512]{5,4,3,2,1,0:T(8,128)(2,1)S(1)}, u32[]{:S(2)}, u32[]{:S(2)}) collective-permute-start(bf16[2,2,2,2,64,512]{5,4,3,2,1,0:T(8,128)(2,1)S(1)} %bitcast.83), channel_id=1, source_target_pairs={{0,2},{1,3},{2,0},{3,1},{4,6},{5,7},{6,4},{7,5},{8,10},{9,11},{10,... | collective-permute-start | bytes 3145736 | tf_op jit(solution)/shard_map/ppermute | solution.py:361
  76.9 17.0 %collective-permute-start.11 = (bf16[2,2,2,32,896]{4,3,2,1,0:T(8,128)(2,1)S(1)}, bf16[2,2,2,32,896]{4,3,2,1,0:T(8,128)(2,1)S(1)}, u32[]{:S(2)}, u32[]{:S(2)}) collective-permute-start(bf16[2,2,2,32,896]{4,3,2,1,0:T(8,128)(2,1)S(1)} %get-tuple-element.74), channel_id=1, source_target_pairs={{0,4},{1,5},{2,6},{3,7},{4,0},{5,1},{6,2},{7,3},{8,12},{9,13},{10,... | collective-permute-start | bytes 1376264 | tf_op jit(solution)/shard_map/ppermute | solution.py:361
  80.1 13.5 %collective-permute-start.10 = (bf16[2,2,2,32,896]{4,3,2,1,0:T(8,128)(2,1)S(1)}, bf16[2,2,2,32,896]{4,3,2,1,0:T(8,128)(2,1)S(1)}, u32[]{:S(2)}, u32[]{:S(2)}) collective-permute-start(bf16[2,2,2,32,896]{4,3,2,1,0:T(8,128)(2,1)S(1)} %get-tuple-element.76), channel_id=1, source_target_pairs={{0,1},{1,0},{2,3},{3,2},{4,5},{5,4},{6,7},{7,6},{8,9},{9,8},{10,11... | collective-permute-start | bytes 1376264 | tf_op jit(solution)/shard_map/ppermute | solution.py:361
  84.7 12.4 %collective-permute-start.13 = (bf16[2,2,2,32,512]{4,3,2,1,0:T(8,128)(2,1)S(1)}, bf16[2,2,2,32,512]{4,3,2,1,0:T(8,128)(2,1)S(1)}, u32[]{:S(2)}, u32[]{:S(2)}) collective-permute-start(bf16[2,2,2,32,512]{4,3,2,1,0:T(8,128)(2,1)S(1)} %get-tuple-element.78), channel_id=1, source_target_pairs={{0,4},{1,5},{2,6},{3,7},{4,0},{5,1},{6,2},{7,3},{8,12},{9,13},{10,... | collective-permute-start | bytes 786440 | tf_op jit(solution)/shard_map/ppermute | solution.py:361
  84.9 14.5 %collective-permute-start.12 = (bf16[2,2,2,32,512]{4,3,2,1,0:T(8,128)(2,1)S(1)}, bf16[2,2,2,32,512]{4,3,2,1,0:T(8,128)(2,1)S(1)}, u32[]{:S(2)}, u32[]{:S(2)}) collective-permute-start(bf16[2,2,2,32,512]{4,3,2,1,0:T(8,128)(2,1)S(1)} %get-tuple-element.80), channel_id=1, source_target_pairs={{0,1},{1,0},{2,3},{3,2},{4,5},{5,4},{6,7},{7,6},{8,9},{9,8},{10,11... | collective-permute-start | bytes 786440 | tf_op jit(solution)/shard_map/ppermute | solution.py:361
  93.7 10.4 %collective-permute-start.14 = (bf16[2,2,32,896]{3,2,1,0:T(8,128)(2,1)S(1)}, bf16[2,2,32,896]{3,2,1,0:T(8,128)(2,1)S(1)}, u32[]{:S(2)}, u32[]{:S(2)}) collective-permute-start(bf16[2,2,32,896]{3,2,1,0:T(8,128)(2,1)S(1)} %get-tuple-element.86), channel_id=1, source_target_pairs={{0,4},{1,5},{2,6},{3,7},{4,0},{5,1},{6,2},{7,3},{8,12},{9,13},{10,... | collective-permute-start | bytes 688136 | tf_op jit(solution)/shard_map/ppermute | solution.py:361
  94.1 10.0 %collective-permute-start.15 = (bf16[2,2,32,896]{3,2,1,0:T(8,128)(2,1)S(1)}, bf16[2,2,32,896]{3,2,1,0:T(8,128)(2,1)S(1)}, u32[]{:S(2)}, u32[]{:S(2)}) collective-permute-start(bf16[2,2,32,896]{3,2,1,0:T(8,128)(2,1)S(1)} %get-tuple-element.88), channel_id=1, source_target_pairs={{0,1},{1,0},{2,3},{3,2},{4,5},{5,4},{6,7},{7,6},{8,9},{9,8},{10,11... | collective-permute-start | bytes 688136 | tf_op jit(solution)/shard_map/ppermute | solution.py:361
  97.2 12.1 %copy-start.2 = (bf16[2048,768]{1,0:T(8,128)(2,1)S(1)}, bf16[2048,768]{1,0:T(8,128)(2,1)}, u32[]{:S(2)}) copy-start(bf16[2048,768]{1,0:T(8,128)(2,1)} %refs_3_.1) | copy-start | bytes 9437188
  97.2 11.9 %collective-permute-start.17 = (bf16[2,2,32,512]{3,2,1,0:T(8,128)(2,1)S(1)}, bf16[2,2,32,512]{3,2,1,0:T(8,128)(2,1)S(1)}, u32[]{:S(2)}, u32[]{:S(2)}) collective-permute-start(bf16[2,2,32,512]{3,2,1,0:T(8,128)(2,1)S(1)} %get-tuple-element.93), channel_id=1, source_target_pairs={{0,1},{1,0},{2,3},{3,2},{4,5},{5,4},{6,7},{7,6},{8,9},{9,8},{10,11... | collective-permute-start | bytes 393224 | tf_op jit(solution)/shard_map/ppermute | solution.py:361
  99.5 9.6 %collective-permute-start.16 = (bf16[2,2,32,512]{3,2,1,0:T(8,128)(2,1)S(1)}, bf16[2,2,32,512]{3,2,1,0:T(8,128)(2,1)S(1)}, u32[]{:S(2)}, u32[]{:S(2)}) collective-permute-start(bf16[2,2,32,512]{3,2,1,0:T(8,128)(2,1)S(1)} %get-tuple-element.95), channel_id=1, source_target_pairs={{0,4},{1,5},{2,6},{3,7},{4,0},{5,1},{6,2},{7,3},{8,12},{9,13},{10,... | collective-permute-start | bytes 393224 | tf_op jit(solution)/shard_map/ppermute | solution.py:361
  104.3 15.1 %collective-permute-start.20 = (bf16[64,896]{1,0:T(8,128)(2,1)S(1)}, bf16[64,896]{1,0:T(8,128)(2,1)S(1)}, u32[]{:S(2)}, u32[]{:S(2)}) collective-permute-start(bf16[64,896]{1,0:T(8,128)(2,1)S(1)} %get-tuple-element.82), channel_id=1, source_target_pairs={{0,24},{1,25},{2,26},{3,27},{4,28},{5,29},{6,30},{7,31},{8,16},{9,... | collective-permute-start | bytes 344072 | tf_op jit(solution)/shard_map/ppermute | solution.py:361
  108.4 11.4 %collective-permute-start.19 = (bf16[64,896]{1,0:T(8,128)(2,1)S(1)}, bf16[64,896]{1,0:T(8,128)(2,1)S(1)}, u32[]{:S(2)}, u32[]{:S(2)}) collective-permute-start(bf16[64,896]{1,0:T(8,128)(2,1)S(1)} %get-tuple-element.83), channel_id=1, source_target_pairs={{0,16},{1,17},{2,18},{3,19},{4,20},{5,21},{6,22},{7,23},{8,24},{9,... | collective-permute-start | bytes 344072 | tf_op jit(solution)/shard_map/ppermute | solution.py:361
  108.5 11.3 %collective-permute-start.18 = (bf16[64,896]{1,0:T(8,128)(2,1)S(1)}, bf16[64,896]{1,0:T(8,128)(2,1)S(1)}, u32[]{:S(2)}, u32[]{:S(2)}) collective-permute-start(bf16[64,896]{1,0:T(8,128)(2,1)S(1)} %get-tuple-element.84), channel_id=1, source_target_pairs={{0,8},{1,9},{2,10},{3,11},{4,12},{5,13},{6,14},{7,15},{8,0},{9,1},... | collective-permute-start | bytes 344072 | tf_op jit(solution)/shard_map/ppermute | solution.py:361
  115.5 5.7 %collective-permute-start.21 = (bf16[64,512]{1,0:T(8,128)(2,1)S(1)}, bf16[64,512]{1,0:T(8,128)(2,1)S(1)}, u32[]{:S(2)}, u32[]{:S(2)}) collective-permute-start(bf16[64,512]{1,0:T(8,128)(2,1)S(1)} %get-tuple-element.89), channel_id=1, source_target_pairs={{0,8},{1,9},{2,10},{3,11},{4,12},{5,13},{6,14},{7,15},{8,0},{9,1},... | collective-permute-start | bytes 196616 | tf_op jit(solution)/shard_map/ppermute | solution.py:361
  117.0 6.1 %collective-permute-start.23 = (bf16[64,512]{1,0:T(8,128)(2,1)S(1)}, bf16[64,512]{1,0:T(8,128)(2,1)S(1)}, u32[]{:S(2)}, u32[]{:S(2)}) collective-permute-start(bf16[64,512]{1,0:T(8,128)(2,1)S(1)} %get-tuple-element.90), channel_id=1, source_target_pairs={{0,24},{1,25},{2,26},{3,27},{4,28},{5,29},{6,30},{7,31},{8,16},{9,... | collective-permute-start | bytes 196616 | tf_op jit(solution)/shard_map/ppermute | solution.py:361
  119.5 5.9 %collective-permute-start.22 = (bf16[64,512]{1,0:T(8,128)(2,1)S(1)}, bf16[64,512]{1,0:T(8,128)(2,1)S(1)}, u32[]{:S(2)}, u32[]{:S(2)}) collective-permute-start(bf16[64,512]{1,0:T(8,128)(2,1)S(1)} %get-tuple-element.91), channel_id=1, source_target_pairs={{0,16},{1,17},{2,18},{3,19},{4,20},{5,21},{6,22},{7,23},{8,24},{9,... | collective-permute-start | bytes 196616 | tf_op jit(solution)/shard_map/ppermute | solution.py:361

commit v8 on v7

--- a/solution.py
+++ b/solution.py
@@ -373,23 +373,20 @@
     return [(i, i + by) for i in range(0, count - by, 2)] + [(i, i - by) for i in range(by + 1, count, 2)]
 
 
-def advance(reduction, step, steps):
-    if step < steps:
-        reduction.start()
-    else:
-        reduction.start_last()
-
-
 class Reduction:
 
-    def __init__(self, part, count, bits, orders):
+    def __init__(self, part, count, bits, orders, ends):
         cut = part.shape[-2] // 2
-        self.count, self.last = count, bits[-2:]
+        self.count = count
         self.parts = [part[..., :cut, :], part[..., cut:, :]]
         self.left = [list(bits), list(bits)]
-        self.orders = [list(order) for order in orders]
+        self.orders = [list(order) + list(ends) for order in orders]
+        self.split = len(orders[0])
 
     def start(self):
+        if not self.split:
+            self.parts = [jnp.concatenate(self.parts, axis=-2)]
+        self.split -= 1
         self.kept, self.sent, self.came = [], [], []
         for part, left, order in zip(self.parts, self.left, self.orders):
             bit = order.pop(0)
@@ -401,21 +398,9 @@
 
     def finish(self, *done):
         self.parts = [added(after(k, *done), c) for k, c in zip(self.kept, self.came)]
-        return tuple(self.parts)
-
-    def start_last(self):
-        part = jnp.concatenate(self.parts, axis=-2)
-        part = part.reshape((4,) + part.shape[-2:])
-        self.sent = [part]
-        hi, lo = self.last
-        self.own = part[0]
-        self.got = [flipped(part[k], self.count, ((k >> 1) << hi) | ((k & 1) << lo)) for k in range(1, 4)]
 
     def result(self):
-        total = self.own.astype(F32)
-        for piece in self.got:
-            total = total + piece.astype(F32)
-        return total
+        return self.kept[0].astype(F32) + self.came[0].astype(F32)
 
 
 def per_device(
@@ -435,7 +420,8 @@
     third = lax.ppermute(
         meta, AXES, [(i, i + 3) for i in range(1, count - 3, 2)] + [(i, i - 3) for i in range(4, count, 2)]
     )
-    mate = flipped(after(block, other), count, 1)
+    block = after(block, other)
+    mate = flipped(block, count, 1)
     low = moved(block, count, 2)
     high = moved(block, count, -2)
     far = lax.ppermute(mate, AXES, nearest_pair(count, 2))
@@ -459,7 +445,7 @@
     a = n_cap.bit_length() - 1
     cap_bits = list(range(a))
     img_bits = list(range(a + 1, m - 2))
-    bits = [a] + cap_bits + img_bits + [m - 1, m - 2]
+    bits = [a] + cap_bits + img_bits + [m - 2, m - 1]
     pos = jnp.arange(count, dtype=jnp.int32)
     order = jnp.zeros_like(pos)
     for k, bit in enumerate(bits):
@@ -507,30 +493,29 @@
     core = 1 << a
     rest = bits[1:]
     orders = (cap_bits + img_bits, img_bits + cap_bits)
-    steps = m - 3
+    ends = (m - 2, m - 1)
     in_sent, grad_sent = in_half(order[half:], logit)
     in_came = flipped(in_sent, count, core)
     in_kept, grad_kept = in_half(order[:half], after(logit, grad_sent))
-    r_in = Reduction(added(in_kept, in_came), count, rest, orders)
+    r_in = Reduction(added(in_kept, in_came), count, rest, orders, ends)
     r_in.start()
     out_sent = out_half(order[half:], after(logit, *r_in.sent))
     out_came = flipped(out_sent, count, core)
     out_kept = out_half(order[:half], after(logit, out_sent))
-    r_out = Reduction(added(out_kept, out_came), count, rest, orders)
+    r_out = Reduction(added(out_kept, out_came), count, rest, orders, ends)
     r_out.start()
-    for k in range(steps):
+    for k in range(m - 2):
         r_in.finish(*r_out.sent)
-        advance(r_in, k + 1, steps)
+        r_in.start()
         r_out.finish(*r_in.sent)
-        if k + 1 < steps:
+        if k < m - 3:
             r_out.start()
     grad_img, grad_cap = over_hidden(
         feat_kernel, "feat_grad", order, grouped(f_in) + [rows_of_half(nodes, half, 0), rows_of_half(nodes, half, 1)],
         (whole((local_rows, f_in)),) * 2, (jax.ShapeDtypeStruct((local_rows, f_in), BF16),) * 2,
         [pltpu.VMEM((nodes, f_in), F32)], [w_in] * GROUP + [after(grad_kept, *r_out.parts), grad_sent],
     )
-    r_out.start_last()
-    r_in.own = after(r_in.own, *r_out.sent)
+    r_out.start()
     grad_scale = 1.0 / math.sqrt(nodes * count)
     g_out, g_in = [r.result() * grad_scale for r in (r_out, r_in)]
     return (grad_img, grad_cap, g_in[:, :f_in], g_out, g_in[:, f_in])

time: 126 us -> 117 us (0.929)
  waiting for transfers between devices: 28 us -> 17.2 us
  starting transfers between devices: 41.5 us -> 43 us
    ppermute x18 -> x16, waiting for transfers between devices: 28 us -> 17.2 us  [flipped(): return lax.ppermute(array, AXES, [(i, i ^ mask) for i in range(count)])]
    ppermute x18 -> x16, starting transfers between devices: 28.2 us -> 28.5 us  [flipped(): return lax.ppermute(array, AXES, [(i, i ^ mask) for i in range(count)])]
  transfers between devices with their start and end apart: 24 -> 22, of which waited for: 6 -> 6; matrix products, arithmetic and copies ran while one was open for 11% -> 12% of each run, Pallas kernels for 16% -> 17%
where the time goes in v8:
time: 117 us
  starting transfers between devices  43 us (37%)
  Pallas kernels  39.7 us (34%)
  waiting for transfers between devices  17.2 us (15%)
  matrix products  7.73 us (7%)
  other arithmetic  5.69 us (5%)
  local copies, waits for them, and re-layouts  2.53 us (2%)
    ppermute x16, starting transfers between devices, flipped(): return lax.ppermute(array, AXES, [(i, i ^ mask) for i in range(count)])  28.5 us
    pallas_call x5, Pallas kernels, over_hidden(): pl.pallas_call(kernel, out_shape=out_shape, grid_spec=pltpu.PrefetchScala...  18 us
    ppermute x16, waiting for transfers between devices, flipped(): return lax.ppermute(array, AXES, [(i, i ^ mask) for i in range(count)])  17.2 us
    pallas_call x1, Pallas kernels, propagate(): pl.pallas_call(lambda *r: hops_kernel(*r, tiles=tiles, slots=slots, width...  11.8 us
    ppermute x4, starting transfers between devices, moved(): lax.ppermute(array, AXES, [(i, i + by) for i in range(count) if 0 <= i +...  9.53 us
    pallas_call x1, Pallas kernels, make_tiles(): pl.pallas_call(lambda *r: tiles_kernel(*r, tiles=tiles, slots=slots), out...  7.82 us
    dot_general x1, matrix products, per_device(): lax.dot_general(w_in, feats, across, preferred_element_type=F32)  7.73 us
    ppermute x1, starting transfers between devices, per_device(): far = lax.ppermute(mate, AXES, nearest_pair(count, 2))  4.3 us
  transfers between devices with their start and end apart: 22, of which 6 were waited for; matrix products, arithmetic and copies ran while one was open for 12% of the time, Pallas kernels for 17%

profile of v8, /device:TPU:0, one launch (start us, length us, event | category | flops | bytes accessed | tf_op | source)
XLA Modules:
  0.0 116.9 jit_solution(10626304967004755676)
XLA Ops:
  0.7 2.1 %stack.1 = (bf16[768,512]{1,0:T(8,128)(2,1)}, s32[3,12]{1,0:T(4,128)}) custom-call(s32[3]{0:T(128)} %count_ref.1, bf16[384,512]{1,0:T(8,128)(2,1)} %top_ref.1, bf16[384,512]{1,0:T(8,128)(2,1)} %bottom_ref.1, s32[3,4]{1,0:T(4,128)} %seed_ref.1, s32[3,4]{1,0:T(4,128)} %cols_ref.1), custom_call_target="tpu_custom_call" | custom-call | flops 1 | bytes 1 | tf_op jit(solution)/shard_map/stack/pallas_call | solution.py:342
  3.4 5.7 %collective-permute-start = (s32[3,12]{1,0:T(4,128)}, s32[3,12]{1,0:T(4,128)S(1)}, u32[]{:S(2)}, u32[]{:S(2)}) collective-permute-start(s32[3,12]{1,0:T(4,128)} %get-tuple-element.38), channel_id=1, source_target_pairs={{0,1},{1,0},{2,3},{3,2},{4,5},{5,4},{6,7},{7,6},{8,9},{9,8},{10,11... | collective-permute-start | bytes 440 | tf_op jit(solution)/shard_map/ppermute | solution.py:361
  9.2 2.3 %pad_maximum_fusion.refs_9_ = bf16[768,768]{1,0:T(8,128)(2,1)} fusion(bf16[384,768]{1,0:T(8,128)(2,1)} %param.13, bf16[384,768]{1,0:T(8,128)(2,1)} %param.12), kind=kLoop, calls=%fused_computation.15 | loop fusion | flops 2359296 | bytes 2359296 | tf_op jit(solution)/shard_map/concatenate | solution.py:429
  11.6 1.3 %collective-permute-start.6 = (bf16[768,512]{1,0:T(8,128)(2,1)}, bf16[768,512]{1,0:T(8,128)(2,1)}, u32[]{:S(2)}, u32[]{:S(2)}) collective-permute-start(bf16[768,512]{1,0:T(8,128)(2,1)} %get-tuple-element.40.r_2_), channel_id=1, source_target_pairs={{0,1},{1,0},{2,3},{3,2},{4,5},{5,4},{6,7},{7,6},{8,9},{9,8},{10,11... | collective-permute-start | bytes 2359304 | tf_op jit(solution)/shard_map/ppermute | solution.py:361
  12.9 1.3 %collective-permute-start.5 = (bf16[768,512]{1,0:T(8,128)(2,1)}, bf16[768,512]{1,0:T(8,128)(2,1)}, u32[]{:S(2)}, u32[]{:S(2)}) collective-permute-start(bf16[768,512]{1,0:T(8,128)(2,1)} %get-tuple-element.40.r_2_), channel_id=1, source_target_pairs={{2,0},{3,1},{4,2},{5,3},{6,4},{7,5},{8,6},{9,7},{10,8},{11,9},{12,... | collective-permute-start | bytes 2359304 | tf_op jit(solution)/shard_map/ppermute | solution.py:357
  14.2 3.9 %collective-permute-start.4 = (bf16[768,512]{1,0:T(8,128)(2,1)}, bf16[768,512]{1,0:T(8,128)(2,1)}, u32[]{:S(2)}, u32[]{:S(2)}) collective-permute-start(bf16[768,512]{1,0:T(8,128)(2,1)} %get-tuple-element.40.r_2_), channel_id=1, source_target_pairs={{0,2},{1,3},{2,4},{3,5},{4,6},{5,7},{6,8},{7,9},{8,10},{9,11},{10,... | collective-permute-start | bytes 2359304 | tf_op jit(solution)/shard_map/ppermute | solution.py:357
  18.2 0.8 add_select_fusion.1
  18.9 1.3 %collective-permute-start.3 = (s32[6,12]{1,0:T(8,128)S(1)}, s32[6,12]{1,0:T(8,128)S(1)}, u32[]{:S(2)}, u32[]{:S(2)}) collective-permute-start(s32[6,12]{1,0:T(8,128)S(1)} %add_select_fusion.1), channel_id=1, source_target_pairs={{2,0},{3,1},{4,2},{5,3},{6,4},{7,5},{8,6},{9,7},{10,8},{11,9},{12,... | collective-permute-start | bytes 872 | tf_op jit(solution)/shard_map/ppermute | solution.py:357
  20.2 3.0 %collective-permute-start.2 = (s32[6,12]{1,0:T(8,128)S(1)}, s32[6,12]{1,0:T(8,128)S(1)}, u32[]{:S(2)}, u32[]{:S(2)}) collective-permute-start(s32[6,12]{1,0:T(8,128)S(1)} %add_select_fusion.1), channel_id=1, source_target_pairs={{0,2},{1,3},{2,4},{3,5},{4,6},{5,7},{6,8},{7,9},{8,10},{9,11},{10,... | collective-permute-start | bytes 872 | tf_op jit(solution)/shard_map/ppermute | solution.py:357
  23.3 7.7 %fusion.3 = (f32[2048,768]{1,0:T(8,128)}, bf16[2048,768]{1,0:T(8,128)(2,1)S(1)}) fusion(f32[2048]{0:T(1024)S(1)} %copy-done.6, bf16[768,768]{1,0:T(8,128)(2,1)} %pad_maximum_fusion.refs_9_, bf16[2048,768]{1,0:T(8,128)(2,1)} %refs_3_.1), kind=kOutput, calls=%fused_computation.4 | convolution fusion | flops 2433220608 | bytes 13770752 | tf_op jit(solution)/shard_map/dot_general | solution.py:464
  31.0 4.3 %collective-permute-start.7 = (bf16[768,512]{1,0:T(8,128)(2,1)}, bf16[768,512]{1,0:T(8,128)(2,1)}, u32[]{:S(2)}, u32[]{:S(2)}) collective-permute-start(bf16[768,512]{1,0:T(8,128)(2,1)} %collective-permute-done.6.r_5_), channel_id=1, source_target_pairs={{0,2},{2,4},{4,6},{6,8},{8,10},{10,12},{12,14},{14,16},{16,18},{18... | collective-permute-start | bytes 2359304 | tf_op jit(solution)/shard_map/ppermute | solution.py:427
  36.0 7.8 %tiles.1 = (bf16[15,128,512]{2,1,0:T(8,128)(2,1)}, bf16[15,512,128]{2,1,0:T(8,128)(2,1)}, f32[15,128,128]{2,1,0:T(8,128)}, f32[15,128,128]{2,1,0:T(8,128)}) custom-call(s32[84]{0:T(128)S(1)} %reshape.37.r_0_, s32[84]{0:T(128)S(1)} %reshape.38.r_1_, s32[21]{0:T(128)S(1)} %slice_reduce_fusion.1.r_2_), custom_call_target="tpu_custom_call" | custom-call | flops 1 | bytes 1 | tf_op jit(solution)/shard_map/tiles/pallas_call | solution.py:103
  44.0 11.8 %hops.1.refs_8_.refs_4_ = bf16[768,512]{1,0:T(8,128)(2,1)S(1)} custom-call(s32[60]{0:T(128)S(1)} %reshape.36.r_0_, s32[2]{0:T(128)S(1)} %fusion.19.r_1_, bf16[768,512]{1,0:T(8,128)(2,1)} %get-tuple-element.40.r_2_, bf16[768,512]{1,0:T(8,128)(2,1)} %collective-permute-done.4.r_3_, bf16[768,512]{1,0:T(8,128)(2,1)} %collective-permute-done.5.r_4_, ...), custom_call_target="tpu_custom_call" | custom-call | flops 1 | bytes 1 | tf_op jit(solution)/shard_map/hops/pallas_call | solution.py:211
  55.8 3.8 %part_in.2 = (bf16[1024,896]{1,0:T(8,128)(2,1)S(1)}, bf16[1024,768]{1,0:T(8,128)(2,1)S(1)}) custom-call(s32[16]{0:T(128)S(1)} %get-tuple-element.96.order_ref, f32[2048,768]{1,0:T(8,128)S(1)} %copy-done, f32[2048,768]{1,0:T(8,128)S(1)} %copy-done, f32[2048,768]{1,0:T(8,128)S(1)} %copy-done, f32[2048,768]{1,0:T(8,128)S(1)} %copy-done, ...), custom_call_target="tpu_custom_call" | custom-call | flops 1 | bytes 1 | tf_op jit(solution)/shard_map/part_in/pallas_call | solution.py:295
  59.9 3.8 %part_in.3 = (bf16[1024,896]{1,0:T(8,128)(2,1)S(1)}, bf16[1024,768]{1,0:T(8,128)(2,1)S(1)}) custom-call(s32[16]{0:T(128)S(1)} %get-tuple-element.97.order_ref, f32[2048,768]{1,0:T(8,128)S(1)} %copy-done, f32[2048,768]{1,0:T(8,128)S(1)} %copy-done, f32[2048,768]{1,0:T(8,128)S(1)} %copy-done, f32[2048,768]{1,0:T(8,128)S(1)} %copy-done, ...), custom_call_target="tpu_custom_call" | custom-call | flops 1 | bytes 1 | tf_op jit(solution)/shard_map/part_in/pallas_call | solution.py:295
  64.5 2.0 %part_out.2 = bf16[1024,512]{1,0:T(8,128)(2,1)S(1)} custom-call(s32[16]{0:T(128)S(1)} %get-tuple-element.96.order_ref, bf16[2048,768]{1,0:T(8,128)(2,1)S(1)} %get-tuple-element.53.refs_0_.refs_1_.refs_2_.refs_3_, bf16[2048,768]{1,0:T(8,128)(2,1)S(1)} %get-tuple-element.53.refs_0_.refs_1_.refs_2_.refs_3_, ...), custom_call_target="tpu_custom_call" | custom-call | flops 1 | bytes 1 | tf_op jit(solution)/shard_map/part_out/pallas_call | solution.py:295
  67.2 2.1 %collective-permute-start.11 = (bf16[2,2,2,32,896]{4,3,2,1,0:T(8,128)(2,1)S(1)}, bf16[2,2,2,32,896]{4,3,2,1,0:T(8,128)(2,1)S(1)}, u32[]{:S(2)}, u32[]{:S(2)}) collective-permute-start(bf16[2,2,2,32,896]{4,3,2,1,0:T(8,128)(2,1)S(1)} %get-tuple-element.76), channel_id=1, source_target_pairs={{0,4},{1,5},{2,6},{3,7},{4,0},{5,1},{6,2},{7,3},{8,12},{9,13},{10,... | collective-permute-start | bytes 1376264 | tf_op jit(solution)/shard_map/ppermute | solution.py:361
  69.2 4.4 %collective-permute-start.10 = (bf16[2,2,2,32,896]{4,3,2,1,0:T(8,128)(2,1)S(1)}, bf16[2,2,2,32,896]{4,3,2,1,0:T(8,128)(2,1)S(1)}, u32[]{:S(2)}, u32[]{:S(2)}) collective-permute-start(bf16[2,2,2,32,896]{4,3,2,1,0:T(8,128)(2,1)S(1)} %get-tuple-element.78), channel_id=1, source_target_pairs={{0,1},{1,0},{2,3},{3,2},{4,5},{5,4},{6,7},{7,6},{8,9},{9,8},{10,11... | collective-permute-start | bytes 1376264 | tf_op jit(solution)/shard_map/ppermute | solution.py:361
  73.6 2.0 %part_out.3 = bf16[1024,512]{1,0:T(8,128)(2,1)S(1)} custom-call(s32[16]{0:T(128)S(1)} %get-tuple-element.97.order_ref, bf16[2048,768]{1,0:T(8,128)(2,1)S(1)} %get-tuple-element.53.refs_0_.refs_1_.refs_2_.refs_3_, bf16[2048,768]{1,0:T(8,128)(2,1)S(1)} %get-tuple-element.53.refs_0_.refs_1_.refs_2_.refs_3_, ...), custom_call_target="tpu_custom_call" | custom-call | flops 1 | bytes 1 | tf_op jit(solution)/shard_map/part_out/pallas_call | solution.py:295
  76.8 8.1 %collective-permute-done.10 = bf16[2,2,2,32,896]{4,3,2,1,0:T(8,128)(2,1)S(1)} collective-permute-done((bf16[2,2,2,32,896]{4,3,2,1,0:T(8,128)(2,1)S(1)}, bf16[2,2,2,32,896]{4,3,2,1,0:T(8,128)(2,1)S(1)}, u32[]{:S(2)}, u32[]{:S(2)}) %collective-permute-start.10) | collective-permute-done | bytes 458784 | tf_op jit(solution)/shard_map/ppermute | solution.py:361
  85.5 2.0 %collective-permute-start.15 = (bf16[2,2,32,896]{3,2,1,0:T(8,128)(2,1)S(1)}, bf16[2,2,32,896]{3,2,1,0:T(8,128)(2,1)S(1)}, u32[]{:S(2)}, u32[]{:S(2)}) collective-permute-start(bf16[2,2,32,896]{3,2,1,0:T(8,128)(2,1)S(1)} %get-tuple-element.86), channel_id=1, source_target_pairs={{0,1},{1,0},{2,3},{3,2},{4,5},{5,4},{6,7},{7,6},{8,9},{9,8},{10,11... | collective-permute-start | bytes 688136 | tf_op jit(solution)/shard_map/ppermute | solution.py:361
  87.6 3.2 %collective-permute-start.17 = (bf16[2,2,32,512]{3,2,1,0:T(8,128)(2,1)S(1)}, bf16[2,2,32,512]{3,2,1,0:T(8,128)(2,1)S(1)}, u32[]{:S(2)}, u32[]{:S(2)}) collective-permute-start(bf16[2,2,32,512]{3,2,1,0:T(8,128)(2,1)S(1)} %get-tuple-element.94), channel_id=1, source_target_pairs={{0,1},{1,0},{2,3},{3,2},{4,5},{5,4},{6,7},{7,6},{8,9},{9,8},{10,11... | collective-permute-start | bytes 393224 | tf_op jit(solution)/shard_map/ppermute | solution.py:361
  90.9 2.0 %collective-permute-start.16 = (bf16[2,2,32,512]{3,2,1,0:T(8,128)(2,1)S(1)}, bf16[2,2,32,512]{3,2,1,0:T(8,128)(2,1)S(1)}, u32[]{:S(2)}, u32[]{:S(2)}) collective-permute-start(bf16[2,2,32,512]{3,2,1,0:T(8,128)(2,1)S(1)} %get-tuple-element.92), channel_id=1, source_target_pairs={{0,4},{1,5},{2,6},{3,7},{4,0},{5,1},{6,2},{7,3},{8,12},{9,13},{10,... | collective-permute-start | bytes 393224 | tf_op jit(solution)/shard_map/ppermute | solution.py:361
  92.9 2.5 %collective-permute-done.15 = bf16[2,2,32,896]{3,2,1,0:T(8,128)(2,1)S(1)} collective-permute-done((bf16[2,2,32,896]{3,2,1,0:T(8,128)(2,1)S(1)}, bf16[2,2,32,896]{3,2,1,0:T(8,128)(2,1)S(1)}, u32[]{:S(2)}, u32[]{:S(2)}) %collective-permute-start.15) | collective-permute-done | bytes 229408 | tf_op jit(solution)/shard_map/ppermute | solution.py:361
  95.6 1.6 %collective-permute-start.18 = (bf16[2,64,896]{2,1,0:T(8,128)(2,1)S(1)}, bf16[2,64,896]{2,1,0:T(8,128)(2,1)S(1)}, u32[]{:S(2)}, u32[]{:S(2)}) collective-permute-start(bf16[2,64,896]{2,1,0:T(8,128)(2,1)S(1)} %get-tuple-element.84), channel_id=1, source_target_pairs={{0,8},{1,9},{2,10},{3,11},{4,12},{5,13},{6,14},{7,15},{8,0},{9,1},... | collective-permute-start | bytes 688136 | tf_op jit(solution)/shard_map/ppermute | solution.py:361
  97.9 1.6 %collective-permute-start.19 = (bf16[2,64,512]{2,1,0:T(8,128)(2,1)S(1)}, bf16[2,64,512]{2,1,0:T(8,128)(2,1)S(1)}, u32[]{:S(2)}, u32[]{:S(2)}) collective-permute-start(bf16[2,64,512]{2,1,0:T(8,128)(2,1)S(1)} %get-tuple-element.90), channel_id=1, source_target_pairs={{0,8},{1,9},{2,10},{3,11},{4,12},{5,13},{6,14},{7,15},{8,0},{9,1},... | collective-permute-start | bytes 393224 | tf_op jit(solution)/shard_map/ppermute | solution.py:361
  99.6 4.3 %collective-permute-done.18 = bf16[2,64,896]{2,1,0:T(8,128)(2,1)S(1)} collective-permute-done((bf16[2,64,896]{2,1,0:T(8,128)(2,1)S(1)}, bf16[2,64,896]{2,1,0:T(8,128)(2,1)S(1)}, u32[]{:S(2)}, u32[]{:S(2)}) %collective-permute-start.18) | collective-permute-done | bytes 229408 | tf_op jit(solution)/shard_map/ppermute | solution.py:361
  103.9 1.3 %collective-permute-done.19 = bf16[2,64,512]{2,1,0:T(8,128)(2,1)S(1)} collective-permute-done((bf16[2,64,512]{2,1,0:T(8,128)(2,1)S(1)}, bf16[2,64,512]{2,1,0:T(8,128)(2,1)S(1)}, u32[]{:S(2)}, u32[]{:S(2)}) %collective-permute-start.19) | collective-permute-done | bytes 131104 | tf_op jit(solution)/shard_map/ppermute | solution.py:361
  105.3 2.6 %collective-permute-start.21 = (bf16[64,512]{1,0:T(8,128)(2,1)S(1)}, bf16[64,512]{1,0:T(8,128)(2,1)S(1)}, u32[]{:S(2)}, u32[]{:S(2)}) collective-permute-start(bf16[64,512]{1,0:T(8,128)(2,1)S(1)} %slice_bitcast_fusion.18), channel_id=1, source_target_pairs={{0,16},{1,17},{2,18},{3,19},{4,20},{5,21},{6,22},{7,23},{8,24},{9,... | collective-permute-start | bytes 196616 | tf_op jit(solution)/shard_map/ppermute | solution.py:361
  108.3 6.3 %feat_grad.1 = (bf16[384,768]{1,0:T(8,128)(2,1)}, bf16[384,768]{1,0:T(8,128)(2,1)}) custom-call(s32[32]{0:T(128)S(1)} %fusion.32.order_ref, bf16[2048,768]{1,0:T(8,128)(2,1)S(1)} %copy-done.2, bf16[2048,768]{1,0:T(8,128)(2,1)S(1)} %copy-done.2, bf16[2048,768]{1,0:T(8,128)(2,1)S(1)} %copy-done.2, bf16[2048,768]{1,0:T(8,128)(2,1)S(1)} %copy-done.2, ...), custom_call_target="tpu_custom_call" | custom-call | flops 1 | bytes 1 | tf_op jit(solution)/shard_map/feat_grad/pallas_call | solution.py:295
  114.6 0.7 fusion.17
  116.2 0.7 slice.168
  (78 shorter events, 7.1 us)
Async XLA Ops:
  0.6 10.9 %copy-start.4 = (s32[2]{0:T(128)S(1)}, s32[2]{0:T(128)}, u32[]{:S(2)}) copy-start(s32[2]{0:T(128)} %constant.14.clone) | copy-start | bytes 28
  0.6 10.9 %copy-start.5 = (s32[2]{0:T(128)S(1)}, s32[2]{0:T(128)}, u32[]{:S(2)}) copy-start(s32[2]{0:T(128)} %constant.13.clone) | copy-start | bytes 28
  0.7 22.6 %copy-start.6 = (f32[2048]{0:T(1024)S(1)}, f32[2048]{0:T(1024)}, u32[]{:S(2)}) copy-start(f32[2048]{0:T(1024)} %param.17) | copy-start | bytes 24580
  2.7 16.2 %collective-permute-start.1 = (s32[3,12]{1,0:T(4,128)}, s32[3,12]{1,0:T(4,128)S(1)}, u32[]{:S(2)}, u32[]{:S(2)}) collective-permute-start(s32[3,12]{1,0:T(4,128)} %get-tuple-element.38), channel_id=1, source_target_pairs={{1,4},{3,6},{5,8},{7,10},{9,12},{11,14},{13,16},{15,18},{17,20},{1... | collective-permute-start | bytes 440 | tf_op jit(solution)/shard_map/ppermute | solution.py:420
  3.4 8.2 %collective-permute-start = (s32[3,12]{1,0:T(4,128)}, s32[3,12]{1,0:T(4,128)S(1)}, u32[]{:S(2)}, u32[]{:S(2)}) collective-permute-start(s32[3,12]{1,0:T(4,128)} %get-tuple-element.38), channel_id=1, source_target_pairs={{0,1},{1,0},{2,3},{3,2},{4,5},{5,4},{6,7},{7,6},{8,9},{9,8},{10,11... | collective-permute-start | bytes 440 | tf_op jit(solution)/shard_map/ppermute | solution.py:361
  11.6 19.4 %collective-permute-start.6 = (bf16[768,512]{1,0:T(8,128)(2,1)}, bf16[768,512]{1,0:T(8,128)(2,1)}, u32[]{:S(2)}, u32[]{:S(2)}) collective-permute-start(bf16[768,512]{1,0:T(8,128)(2,1)} %get-tuple-element.40.r_2_), channel_id=1, source_target_pairs={{0,1},{1,0},{2,3},{3,2},{4,5},{5,4},{6,7},{7,6},{8,9},{9,8},{10,11... | collective-permute-start | bytes 2359304 | tf_op jit(solution)/shard_map/ppermute | solution.py:361
  12.9 31.0 %collective-permute-start.5 = (bf16[768,512]{1,0:T(8,128)(2,1)}, bf16[768,512]{1,0:T(8,128)(2,1)}, u32[]{:S(2)}, u32[]{:S(2)}) collective-permute-start(bf16[768,512]{1,0:T(8,128)(2,1)} %get-tuple-element.40.r_2_), channel_id=1, source_target_pairs={{2,0},{3,1},{4,2},{5,3},{6,4},{7,5},{8,6},{9,7},{10,8},{11,9},{12,... | collective-permute-start | bytes 2359304 | tf_op jit(solution)/shard_map/ppermute | solution.py:357
  14.2 29.7 %collective-permute-start.4 = (bf16[768,512]{1,0:T(8,128)(2,1)}, bf16[768,512]{1,0:T(8,128)(2,1)}, u32[]{:S(2)}, u32[]{:S(2)}) collective-permute-start(bf16[768,512]{1,0:T(8,128)(2,1)} %get-tuple-element.40.r_2_), channel_id=1, source_target_pairs={{0,2},{1,3},{2,4},{3,5},{4,6},{5,7},{6,8},{7,9},{8,10},{9,11},{10,... | collective-permute-start | bytes 2359304 | tf_op jit(solution)/shard_map/ppermute | solution.py:357
  18.9 16.4 %collective-permute-start.3 = (s32[6,12]{1,0:T(8,128)S(1)}, s32[6,12]{1,0:T(8,128)S(1)}, u32[]{:S(2)}, u32[]{:S(2)}) collective-permute-start(s32[6,12]{1,0:T(8,128)S(1)} %add_select_fusion.1), channel_id=1, source_target_pairs={{2,0},{3,1},{4,2},{5,3},{6,4},{7,5},{8,6},{9,7},{10,8},{11,9},{12,... | collective-permute-start | bytes 872 | tf_op jit(solution)/shard_map/ppermute | solution.py:357
  20.2 15.1 %collective-permute-start.2 = (s32[6,12]{1,0:T(8,128)S(1)}, s32[6,12]{1,0:T(8,128)S(1)}, u32[]{:S(2)}, u32[]{:S(2)}) collective-permute-start(s32[6,12]{1,0:T(8,128)S(1)} %add_select_fusion.1), channel_id=1, source_target_pairs={{0,2},{1,3},{2,4},{3,5},{4,6},{5,7},{6,8},{7,9},{8,10},{9,11},{10,... | collective-permute-start | bytes 872 | tf_op jit(solution)/shard_map/ppermute | solution.py:357
  31.0 12.9 %collective-permute-start.7 = (bf16[768,512]{1,0:T(8,128)(2,1)}, bf16[768,512]{1,0:T(8,128)(2,1)}, u32[]{:S(2)}, u32[]{:S(2)}) collective-permute-start(bf16[768,512]{1,0:T(8,128)(2,1)} %collective-permute-done.6.r_5_), channel_id=1, source_target_pairs={{0,2},{2,4},{4,6},{6,8},{8,10},{10,12},{12,14},{14,16},{16,18},{18... | collective-permute-start | bytes 2359304 | tf_op jit(solution)/shard_map/ppermute | solution.py:427
  43.9 11.8 %copy-start = (f32[2048,768]{1,0:T(8,128)S(1)}, f32[2048,768]{1,0:T(8,128)}, u32[]{:S(2)}) copy-start(f32[2048,768]{1,0:T(8,128)} %get-tuple-element.43.refs_0_.refs_1_.refs_2_.refs_3_) | copy-start | bytes 18874372
  43.9 11.8 %copy-start.1 = (bf16[2048,512]{1,0:T(8,128)(2,1)S(1)}, bf16[2048,512]{1,0:T(8,128)(2,1)}, u32[]{:S(2)}) copy-start(bf16[2048,512]{1,0:T(8,128)(2,1)} %refs_7_.3) | copy-start | bytes 6291460
  43.9 11.8 %copy-start.3 = (bf16[768,768]{1,0:T(8,128)(2,1)S(1)}, bf16[768,768]{1,0:T(8,128)(2,1)}, u32[]{:S(2)}) copy-start(bf16[768,768]{1,0:T(8,128)(2,1)} %pad_maximum_fusion.refs_9_) | copy-start | bytes 3538948
  59.8 3.9 %collective-permute-start.8 = (bf16[2,2,2,2,64,896]{5,4,3,2,0,1:T(8,128)(2,1)S(1)}, bf16[2,2,2,2,64,896]{5,4,3,2,0,1:T(8,128)(2,1)S(1)}, u32[]{:S(2)}, u32[]{:S(2)}) collective-permute-start(bf16[2,2,2,2,64,896]{5,4,3,2,0,1:T(8,128)(2,1)S(1)} %copy.25), channel_id=1, source_target_pairs={{0,2},{1,3},{2,0},{3,1},{4,6},{5,7},{6,4},{7,5},{8,10},{9,11},{10,... | collective-permute-start | bytes 5505032 | tf_op jit(solution)/shard_map/ppermute | solution.py:361
  66.6 9.0 %collective-permute-start.9 = (bf16[2,2,2,2,64,512]{5,4,3,2,0,1:T(8,128)(2,1)S(1)}, bf16[2,2,2,2,64,512]{5,4,3,2,0,1:T(8,128)(2,1)S(1)}, u32[]{:S(2)}, u32[]{:S(2)}) collective-permute-start(bf16[2,2,2,2,64,512]{5,4,3,2,0,1:T(8,128)(2,1)S(1)} %copy.28), channel_id=1, source_target_pairs={{0,2},{1,3},{2,0},{3,1},{4,6},{5,7},{6,4},{7,5},{8,10},{9,11},{10,... | collective-permute-start | bytes 3145736 | tf_op jit(solution)/shard_map/ppermute | solution.py:361
  67.2 18.1 %collective-permute-start.11 = (bf16[2,2,2,32,896]{4,3,2,1,0:T(8,128)(2,1)S(1)}, bf16[2,2,2,32,896]{4,3,2,1,0:T(8,128)(2,1)S(1)}, u32[]{:S(2)}, u32[]{:S(2)}) collective-permute-start(bf16[2,2,2,32,896]{4,3,2,1,0:T(8,128)(2,1)S(1)} %get-tuple-element.76), channel_id=1, source_target_pairs={{0,4},{1,5},{2,6},{3,7},{4,0},{5,1},{6,2},{7,3},{8,12},{9,13},{10,... | collective-permute-start | bytes 1376264 | tf_op jit(solution)/shard_map/ppermute | solution.py:361
  69.2 15.7 %collective-permute-start.10 = (bf16[2,2,2,32,896]{4,3,2,1,0:T(8,128)(2,1)S(1)}, bf16[2,2,2,32,896]{4,3,2,1,0:T(8,128)(2,1)S(1)}, u32[]{:S(2)}, u32[]{:S(2)}) collective-permute-start(bf16[2,2,2,32,896]{4,3,2,1,0:T(8,128)(2,1)S(1)} %get-tuple-element.78), channel_id=1, source_target_pairs={{0,1},{1,0},{2,3},{3,2},{4,5},{5,4},{6,7},{7,6},{8,9},{9,8},{10,11... | collective-permute-start | bytes 1376264 | tf_op jit(solution)/shard_map/ppermute | solution.py:361
  76.1 11.4 %collective-permute-start.13 = (bf16[2,2,2,32,512]{4,3,2,1,0:T(8,128)(2,1)S(1)}, bf16[2,2,2,32,512]{4,3,2,1,0:T(8,128)(2,1)S(1)}, u32[]{:S(2)}, u32[]{:S(2)}) collective-permute-start(bf16[2,2,2,32,512]{4,3,2,1,0:T(8,128)(2,1)S(1)} %get-tuple-element.82), channel_id=1, source_target_pairs={{0,4},{1,5},{2,6},{3,7},{4,0},{5,1},{6,2},{7,3},{8,12},{9,13},{10,... | collective-permute-start | bytes 786440 | tf_op jit(solution)/shard_map/ppermute | solution.py:361
  76.3 14.5 %collective-permute-start.12 = (bf16[2,2,2,32,512]{4,3,2,1,0:T(8,128)(2,1)S(1)}, bf16[2,2,2,32,512]{4,3,2,1,0:T(8,128)(2,1)S(1)}, u32[]{:S(2)}, u32[]{:S(2)}) collective-permute-start(bf16[2,2,2,32,512]{4,3,2,1,0:T(8,128)(2,1)S(1)} %get-tuple-element.80), channel_id=1, source_target_pairs={{0,1},{1,0},{2,3},{3,2},{4,5},{5,4},{6,7},{7,6},{8,9},{9,8},{10,11... | collective-permute-start | bytes 786440 | tf_op jit(solution)/shard_map/ppermute | solution.py:361
  85.1 10.4 %collective-permute-start.14 = (bf16[2,2,32,896]{3,2,1,0:T(8,128)(2,1)S(1)}, bf16[2,2,32,896]{3,2,1,0:T(8,128)(2,1)S(1)}, u32[]{:S(2)}, u32[]{:S(2)}) collective-permute-start(bf16[2,2,32,896]{3,2,1,0:T(8,128)(2,1)S(1)} %get-tuple-element.88), channel_id=1, source_target_pairs={{0,4},{1,5},{2,6},{3,7},{4,0},{5,1},{6,2},{7,3},{8,12},{9,13},{10,... | collective-permute-start | bytes 688136 | tf_op jit(solution)/shard_map/ppermute | solution.py:361
  85.5 10.0 %collective-permute-start.15 = (bf16[2,2,32,896]{3,2,1,0:T(8,128)(2,1)S(1)}, bf16[2,2,32,896]{3,2,1,0:T(8,128)(2,1)S(1)}, u32[]{:S(2)}, u32[]{:S(2)}) collective-permute-start(bf16[2,2,32,896]{3,2,1,0:T(8,128)(2,1)S(1)} %get-tuple-element.86), channel_id=1, source_target_pairs={{0,1},{1,0},{2,3},{3,2},{4,5},{5,4},{6,7},{7,6},{8,9},{9,8},{10,11... | collective-permute-start | bytes 688136 | tf_op jit(solution)/shard_map/ppermute | solution.py:361
  87.6 20.7 %copy-start.2 = (bf16[2048,768]{1,0:T(8,128)(2,1)S(1)}, bf16[2048,768]{1,0:T(8,128)(2,1)}, u32[]{:S(2)}) copy-start(bf16[2048,768]{1,0:T(8,128)(2,1)} %refs_3_.1) | copy-start | bytes 9437188
  87.6 10.2 %collective-permute-start.17 = (bf16[2,2,32,512]{3,2,1,0:T(8,128)(2,1)S(1)}, bf16[2,2,32,512]{3,2,1,0:T(8,128)(2,1)S(1)}, u32[]{:S(2)}, u32[]{:S(2)}) collective-permute-start(bf16[2,2,32,512]{3,2,1,0:T(8,128)(2,1)S(1)} %get-tuple-element.94), channel_id=1, source_target_pairs={{0,1},{1,0},{2,3},{3,2},{4,5},{5,4},{6,7},{7,6},{8,9},{9,8},{10,11... | collective-permute-start | bytes 393224 | tf_op jit(solution)/shard_map/ppermute | solution.py:361
  90.9 7.0 %collective-permute-start.16 = (bf16[2,2,32,512]{3,2,1,0:T(8,128)(2,1)S(1)}, bf16[2,2,32,512]{3,2,1,0:T(8,128)(2,1)S(1)}, u32[]{:S(2)}, u32[]{:S(2)}) collective-permute-start(bf16[2,2,32,512]{3,2,1,0:T(8,128)(2,1)S(1)} %get-tuple-element.92), channel_id=1, source_target_pairs={{0,4},{1,5},{2,6},{3,7},{4,0},{5,1},{6,2},{7,3},{8,12},{9,13},{10,... | collective-permute-start | bytes 393224 | tf_op jit(solution)/shard_map/ppermute | solution.py:361
  95.6 8.2 %collective-permute-start.18 = (bf16[2,64,896]{2,1,0:T(8,128)(2,1)S(1)}, bf16[2,64,896]{2,1,0:T(8,128)(2,1)S(1)}, u32[]{:S(2)}, u32[]{:S(2)}) collective-permute-start(bf16[2,64,896]{2,1,0:T(8,128)(2,1)S(1)} %get-tuple-element.84), channel_id=1, source_target_pairs={{0,8},{1,9},{2,10},{3,11},{4,12},{5,13},{6,14},{7,15},{8,0},{9,1},... | collective-permute-start | bytes 688136 | tf_op jit(solution)/shard_map/ppermute | solution.py:361
  97.9 7.3 %collective-permute-start.19 = (bf16[2,64,512]{2,1,0:T(8,128)(2,1)S(1)}, bf16[2,64,512]{2,1,0:T(8,128)(2,1)S(1)}, u32[]{:S(2)}, u32[]{:S(2)}) collective-permute-start(bf16[2,64,512]{2,1,0:T(8,128)(2,1)S(1)} %get-tuple-element.90), channel_id=1, source_target_pairs={{0,8},{1,9},{2,10},{3,11},{4,12},{5,13},{6,14},{7,15},{8,0},{9,1},... | collective-permute-start | bytes 393224 | tf_op jit(solution)/shard_map/ppermute | solution.py:361
  105.3 9.3 %collective-permute-start.21 = (bf16[64,512]{1,0:T(8,128)(2,1)S(1)}, bf16[64,512]{1,0:T(8,128)(2,1)S(1)}, u32[]{:S(2)}, u32[]{:S(2)}) collective-permute-start(bf16[64,512]{1,0:T(8,128)(2,1)S(1)} %slice_bitcast_fusion.18), channel_id=1, source_target_pairs={{0,16},{1,17},{2,18},{3,19},{4,20},{5,21},{6,22},{7,23},{8,24},{9,... | collective-permute-start | bytes 196616 | tf_op jit(solution)/shard_map/ppermute | solution.py:361
  107.9 7.6 %collective-permute-start.20 = (bf16[64,896]{1,0:T(8,128)(2,1)S(1)}, bf16[64,896]{1,0:T(8,128)(2,1)S(1)}, u32[]{:S(2)}, u32[]{:S(2)}) collective-permute-start(bf16[64,896]{1,0:T(8,128)(2,1)S(1)} %slice_bitcast_fusion.17), channel_id=1, source_target_pairs={{0,16},{1,17},{2,18},{3,19},{4,20},{5,21},{6,22},{7,23},{8,24},{9,... | collective-permute-start | bytes 344072 | tf_op jit(solution)/shard_map/ppermute | solution.py:361

commit v9 on v8

--- a/solution.py
+++ b/solution.py
@@ -375,21 +375,21 @@
 
 class Reduction:
 
-    def __init__(self, part, count, bits, orders, ends):
-        cut = part.shape[-2] // 2
-        self.count = count
-        self.parts = [part[..., :cut, :], part[..., cut:, :]]
-        self.left = [list(bits), list(bits)]
-        self.orders = [list(order) + list(ends) for order in orders]
-        self.split = len(orders[0])
+    def __init__(self, part, count, bits, first, orders, ends):
+        self.count, self.parts, self.left = count, [part], [list(bits)]
+        self.steps = [(bit,) for bit in first] + list(zip(*orders)) + [(bit,) for bit in ends]
 
     def start(self):
-        if not self.split:
+        step = self.steps.pop(0)
+        if len(step) > len(self.parts):
+            part = self.parts[0]
+            cut = part.shape[-2] // 2
+            self.parts = [part[..., :cut, :], part[..., cut:, :]]
+            self.left = [list(self.left[0]), list(self.left[0])]
+        elif len(step) < len(self.parts):
             self.parts = [jnp.concatenate(self.parts, axis=-2)]
-        self.split -= 1
         self.kept, self.sent, self.came = [], [], []
-        for part, left, order in zip(self.parts, self.left, self.orders):
-            bit = order.pop(0)
+        for part, left, bit in zip(self.parts, self.left, step):
             kept, sent = parts(part, left.index(bit))
             left.remove(bit)
             self.kept.append(kept)
@@ -493,29 +493,29 @@
     core = 1 << a
     rest = bits[1:]
     orders = (cap_bits + img_bits, img_bits + cap_bits)
-    ends = (m - 2, m - 1)
+    near, last = m - 2, m - 1
     in_sent, grad_sent = in_half(order[half:], logit)
     in_came = flipped(in_sent, count, core)
     in_kept, grad_kept = in_half(order[:half], after(logit, grad_sent))
-    r_in = Reduction(added(in_kept, in_came), count, rest, orders, ends)
+    r_in = Reduction(added(in_kept, in_came), count, rest, (), orders, (near, last))
     r_in.start()
     out_sent = out_half(order[half:], after(logit, *r_in.sent))
     out_came = flipped(out_sent, count, core)
     out_kept = out_half(order[:half], after(logit, out_sent))
-    r_out = Reduction(added(out_kept, out_came), count, rest, orders, ends)
+    r_out = Reduction(added(out_kept, out_came), count, rest, (near,), orders, (last,))
     r_out.start()
-    for k in range(m - 2):
-        r_in.finish(*r_out.sent)
-        r_in.start()
-        r_out.finish(*r_in.sent)
-        if k < m - 3:
-            r_out.start()
     grad_img, grad_cap = over_hidden(
         feat_kernel, "feat_grad", order, grouped(f_in) + [rows_of_half(nodes, half, 0), rows_of_half(nodes, half, 1)],
         (whole((local_rows, f_in)),) * 2, (jax.ShapeDtypeStruct((local_rows, f_in), BF16),) * 2,
-        [pltpu.VMEM((nodes, f_in), F32)], [w_in] * GROUP + [after(grad_kept, *r_out.parts), grad_sent],
-    )
-    r_out.start()
+        [pltpu.VMEM((nodes, f_in), F32)], [w_in] * GROUP + [after(grad_kept, *r_out.sent), grad_sent],
+    )
+    done = (grad_img,)
+    for _ in range(m - 2):
+        r_in.finish(*done)
+        r_in.start()
+        r_out.finish(*r_in.sent)
+        r_out.start()
+        done = r_out.sent
     grad_scale = 1.0 / math.sqrt(nodes * count)
     g_out, g_in = [r.result() * grad_scale for r in (r_out, r_in)]
     return (grad_img, grad_cap, g_in[:, :f_in], g_out, g_in[:, f_in])

time: 117 us -> 110 us (0.940)
  waiting for transfers between devices: 17.2 us -> 12.1 us
  starting transfers between devices: 43 us -> 40.9 us
    ppermute x16, waiting for transfers between devices: 17.2 us -> 12.1 us  [flipped(): return lax.ppermute(array, AXES, [(i, i ^ mask) for i in range(count)])]
    ppermute x16, starting transfers between devices: 28.5 us -> 26.5 us  [flipped(): return lax.ppermute(array, AXES, [(i, i ^ mask) for i in range(count)])]
  transfers between devices with their start and end apart: 22 -> 22, of which waited for: 6 -> 8; matrix products, arithmetic and copies ran while one was open for 12% -> 12% of each run, Pallas kernels for 17% -> 18%
where the time goes in v9:
time: 110 us
  starting transfers between devices  40.9 us (37%)
  Pallas kernels  39.7 us (36%)
  waiting for transfers between devices  12.1 us (11%)
  matrix products  7.73 us (7%)
  other arithmetic  5.68 us (5%)
  local copies, waits for them, and re-layouts  2.53 us (2%)
    ppermute x16, starting transfers between devices, flipped(): return lax.ppermute(array, AXES, [(i, i ^ mask) for i in range(count)])  26.5 us
    pallas_call x5, Pallas kernels, over_hidden(): pl.pallas_call(kernel, out_shape=out_shape, grid_spec=pltpu.PrefetchScala...  18 us
    ppermute x16, waiting for transfers between devices, flipped(): return lax.ppermute(array, AXES, [(i, i ^ mask) for i in range(count)])  12.1 us
    pallas_call x1, Pallas kernels, propagate(): pl.pallas_call(lambda *r: hops_kernel(*r, tiles=tiles, slots=slots, width...  11.8 us
    ppermute x4, starting transfers between devices, moved(): lax.ppermute(array, AXES, [(i, i + by) for i in range(count) if 0 <= i +...  9.53 us
    pallas_call x1, Pallas kernels, make_tiles(): pl.pallas_call(lambda *r: tiles_kernel(*r, tiles=tiles, slots=slots), out...  7.82 us
    dot_general x1, matrix products, per_device(): lax.dot_general(w_in, feats, across, preferred_element_type=F32)  7.73 us
    ppermute x1, starting transfers between devices, per_device(): far = lax.ppermute(mate, AXES, nearest_pair(count, 2))  4.3 us
  transfers between devices with their start and end apart: 22, of which 8 were waited for; matrix products, arithmetic and copies ran while one was open for 12% of the time, Pallas kernels for 18%

profile of v9, /device:TPU:0, one launch (start us, length us, event | category | flops | bytes accessed | tf_op | source)
XLA Modules:
  0.0 109.8 jit_solution(13063037284866917676)
XLA Ops:
  0.7 2.1 %stack.1 = (bf16[768,512]{1,0:T(8,128)(2,1)}, s32[3,12]{1,0:T(4,128)}) custom-call(s32[3]{0:T(128)} %count_ref.1, bf16[384,512]{1,0:T(8,128)(2,1)} %top_ref.1, bf16[384,512]{1,0:T(8,128)(2,1)} %bottom_ref.1, s32[3,4]{1,0:T(4,128)} %seed_ref.1, s32[3,4]{1,0:T(4,128)} %cols_ref.1), custom_call_target="tpu_custom_call" | custom-call | flops 1 | bytes 1 | tf_op jit(solution)/shard_map/stack/pallas_call | solution.py:342
  3.4 5.7 %collective-permute-start = (s32[3,12]{1,0:T(4,128)}, s32[3,12]{1,0:T(4,128)S(1)}, u32[]{:S(2)}, u32[]{:S(2)}) collective-permute-start(s32[3,12]{1,0:T(4,128)} %get-tuple-element.38), channel_id=1, source_target_pairs={{0,1},{1,0},{2,3},{3,2},{4,5},{5,4},{6,7},{7,6},{8,9},{9,8},{10,11... | collective-permute-start | bytes 440 | tf_op jit(solution)/shard_map/ppermute | solution.py:361
  9.2 2.3 %pad_maximum_fusion.refs_9_ = bf16[768,768]{1,0:T(8,128)(2,1)} fusion(bf16[384,768]{1,0:T(8,128)(2,1)} %param.13, bf16[384,768]{1,0:T(8,128)(2,1)} %param.12), kind=kLoop, calls=%fused_computation.15 | loop fusion | flops 2359296 | bytes 2359296 | tf_op jit(solution)/shard_map/concatenate | solution.py:429
  11.6 1.3 %collective-permute-start.6 = (bf16[768,512]{1,0:T(8,128)(2,1)}, bf16[768,512]{1,0:T(8,128)(2,1)}, u32[]{:S(2)}, u32[]{:S(2)}) collective-permute-start(bf16[768,512]{1,0:T(8,128)(2,1)} %get-tuple-element.40.r_2_), channel_id=1, source_target_pairs={{0,1},{1,0},{2,3},{3,2},{4,5},{5,4},{6,7},{7,6},{8,9},{9,8},{10,11... | collective-permute-start | bytes 2359304 | tf_op jit(solution)/shard_map/ppermute | solution.py:361
  12.9 1.3 %collective-permute-start.5 = (bf16[768,512]{1,0:T(8,128)(2,1)}, bf16[768,512]{1,0:T(8,128)(2,1)}, u32[]{:S(2)}, u32[]{:S(2)}) collective-permute-start(bf16[768,512]{1,0:T(8,128)(2,1)} %get-tuple-element.40.r_2_), channel_id=1, source_target_pairs={{2,0},{3,1},{4,2},{5,3},{6,4},{7,5},{8,6},{9,7},{10,8},{11,9},{12,... | collective-permute-start | bytes 2359304 | tf_op jit(solution)/shard_map/ppermute | solution.py:357
  14.2 3.9 %collective-permute-start.4 = (bf16[768,512]{1,0:T(8,128)(2,1)}, bf16[768,512]{1,0:T(8,128)(2,1)}, u32[]{:S(2)}, u32[]{:S(2)}) collective-permute-start(bf16[768,512]{1,0:T(8,128)(2,1)} %get-tuple-element.40.r_2_), channel_id=1, source_target_pairs={{0,2},{1,3},{2,4},{3,5},{4,6},{5,7},{6,8},{7,9},{8,10},{9,11},{10,... | collective-permute-start | bytes 2359304 | tf_op jit(solution)/shard_map/ppermute | solution.py:357
  18.2 0.8 add_select_fusion.1
  18.9 1.3 %collective-permute-start.3 = (s32[6,12]{1,0:T(8,128)S(1)}, s32[6,12]{1,0:T(8,128)S(1)}, u32[]{:S(2)}, u32[]{:S(2)}) collective-permute-start(s32[6,12]{1,0:T(8,128)S(1)} %add_select_fusion.1), channel_id=1, source_target_pairs={{2,0},{3,1},{4,2},{5,3},{6,4},{7,5},{8,6},{9,7},{10,8},{11,9},{12,... | collective-permute-start | bytes 872 | tf_op jit(solution)/shard_map/ppermute | solution.py:357
  20.2 3.0 %collective-permute-start.2 = (s32[6,12]{1,0:T(8,128)S(1)}, s32[6,12]{1,0:T(8,128)S(1)}, u32[]{:S(2)}, u32[]{:S(2)}) collective-permute-start(s32[6,12]{1,0:T(8,128)S(1)} %add_select_fusion.1), channel_id=1, source_target_pairs={{0,2},{1,3},{2,4},{3,5},{4,6},{5,7},{6,8},{7,9},{8,10},{9,11},{10,... | collective-permute-start | bytes 872 | tf_op jit(solution)/shard_map/ppermute | solution.py:357
  23.3 7.7 %fusion.3 = (f32[2048,768]{1,0:T(8,128)}, bf16[2048,768]{1,0:T(8,128)(2,1)S(1)}) fusion(f32[2048]{0:T(1024)S(1)} %copy-done.6, bf16[768,768]{1,0:T(8,128)(2,1)} %pad_maximum_fusion.refs_9_, bf16[2048,768]{1,0:T(8,128)(2,1)} %refs_3_.1), kind=kOutput, calls=%fused_computation.4 | convolution fusion | flops 2433220608 | bytes 13770752 | tf_op jit(solution)/shard_map/dot_general | solution.py:464
  31.0 4.3 %collective-permute-start.7 = (bf16[768,512]{1,0:T(8,128)(2,1)}, bf16[768,512]{1,0:T(8,128)(2,1)}, u32[]{:S(2)}, u32[]{:S(2)}) collective-permute-start(bf16[768,512]{1,0:T(8,128)(2,1)} %collective-permute-done.6.r_5_), channel_id=1, source_target_pairs={{0,2},{2,4},{4,6},{6,8},{8,10},{10,12},{12,14},{14,16},{16,18},{18... | collective-permute-start | bytes 2359304 | tf_op jit(solution)/shard_map/ppermute | solution.py:427
  36.0 7.8 %tiles.1 = (bf16[15,128,512]{2,1,0:T(8,128)(2,1)}, bf16[15,512,128]{2,1,0:T(8,128)(2,1)}, f32[15,128,128]{2,1,0:T(8,128)}, f32[15,128,128]{2,1,0:T(8,128)}) custom-call(s32[84]{0:T(128)S(1)} %reshape.37.r_0_, s32[84]{0:T(128)S(1)} %reshape.38.r_1_, s32[21]{0:T(128)S(1)} %slice_reduce_fusion.1.r_2_), custom_call_target="tpu_custom_call" | custom-call | flops 1 | bytes 1 | tf_op jit(solution)/shard_map/tiles/pallas_call | solution.py:103
  44.0 11.8 %hops.1.refs_8_.refs_4_ = bf16[768,512]{1,0:T(8,128)(2,1)S(1)} custom-call(s32[60]{0:T(128)S(1)} %reshape.36.r_0_, s32[2]{0:T(128)S(1)} %fusion.19.r_1_, bf16[768,512]{1,0:T(8,128)(2,1)} %get-tuple-element.40.r_2_, bf16[768,512]{1,0:T(8,128)(2,1)} %collective-permute-done.4.r_3_, bf16[768,512]{1,0:T(8,128)(2,1)} %collective-permute-done.5.r_4_, ...), custom_call_target="tpu_custom_call" | custom-call | flops 1 | bytes 1 | tf_op jit(solution)/shard_map/hops/pallas_call | solution.py:211
  55.8 3.8 %part_in.2 = (bf16[1024,896]{1,0:T(8,128)(2,1)S(1)}, bf16[1024,768]{1,0:T(8,128)(2,1)S(1)}) custom-call(s32[16]{0:T(128)S(1)} %get-tuple-element.96.order_ref, f32[2048,768]{1,0:T(8,128)S(1)} %copy-done, f32[2048,768]{1,0:T(8,128)S(1)} %copy-done, f32[2048,768]{1,0:T(8,128)S(1)} %copy-done, f32[2048,768]{1,0:T(8,128)S(1)} %copy-done, ...), custom_call_target="tpu_custom_call" | custom-call | flops 1 | bytes 1 | tf_op jit(solution)/shard_map/part_in/pallas_call | solution.py:295
  59.9 3.8 %part_in.3 = (bf16[1024,896]{1,0:T(8,128)(2,1)S(1)}, bf16[1024,768]{1,0:T(8,128)(2,1)S(1)}) custom-call(s32[16]{0:T(128)S(1)} %get-tuple-element.97.order_ref, f32[2048,768]{1,0:T(8,128)S(1)} %copy-done, f32[2048,768]{1,0:T(8,128)S(1)} %copy-done, f32[2048,768]{1,0:T(8,128)S(1)} %copy-done, f32[2048,768]{1,0:T(8,128)S(1)} %copy-done, ...), custom_call_target="tpu_custom_call" | custom-call | flops 1 | bytes 1 | tf_op jit(solution)/shard_map/part_in/pallas_call | solution.py:295
  64.5 2.0 %part_out.2 = bf16[1024,512]{1,0:T(8,128)(2,1)S(1)} custom-call(s32[16]{0:T(128)S(1)} %get-tuple-element.96.order_ref, bf16[2048,768]{1,0:T(8,128)(2,1)S(1)} %get-tuple-element.53.refs_0_.refs_1_.refs_2_.refs_3_, bf16[2048,768]{1,0:T(8,128)(2,1)S(1)} %get-tuple-element.53.refs_0_.refs_1_.refs_2_.refs_3_, ...), custom_call_target="tpu_custom_call" | custom-call | flops 1 | bytes 1 | tf_op jit(solution)/shard_map/part_out/pallas_call | solution.py:295
  67.2 2.5 %collective-permute-start.10 = (bf16[2,2,2,32,896]{4,3,2,1,0:T(8,128)(2,1)S(1)}, bf16[2,2,2,32,896]{4,3,2,1,0:T(8,128)(2,1)S(1)}, u32[]{:S(2)}, u32[]{:S(2)}) collective-permute-start(bf16[2,2,2,32,896]{4,3,2,1,0:T(8,128)(2,1)S(1)} %get-tuple-element.76), channel_id=1, source_target_pairs={{0,1},{1,0},{2,3},{3,2},{4,5},{5,4},{6,7},{7,6},{8,9},{9,8},{10,11... | collective-permute-start | bytes 1376264 | tf_op jit(solution)/shard_map/ppermute | solution.py:361
  69.7 3.9 %collective-permute-start.11 = (bf16[2,2,2,32,896]{4,3,2,1,0:T(8,128)(2,1)S(1)}, bf16[2,2,2,32,896]{4,3,2,1,0:T(8,128)(2,1)S(1)}, u32[]{:S(2)}, u32[]{:S(2)}) collective-permute-start(bf16[2,2,2,32,896]{4,3,2,1,0:T(8,128)(2,1)S(1)} %get-tuple-element.78), channel_id=1, source_target_pairs={{0,4},{1,5},{2,6},{3,7},{4,0},{5,1},{6,2},{7,3},{8,12},{9,13},{10,... | collective-permute-start | bytes 1376264 | tf_op jit(solution)/shard_map/ppermute | solution.py:361
  73.6 2.0 %part_out.3 = bf16[1024,512]{1,0:T(8,128)(2,1)S(1)} custom-call(s32[16]{0:T(128)S(1)} %get-tuple-element.97.order_ref, bf16[2048,768]{1,0:T(8,128)(2,1)S(1)} %get-tuple-element.53.refs_0_.refs_1_.refs_2_.refs_3_, bf16[2048,768]{1,0:T(8,128)(2,1)S(1)} %get-tuple-element.53.refs_0_.refs_1_.refs_2_.refs_3_, ...), custom_call_target="tpu_custom_call" | custom-call | flops 1 | bytes 1 | tf_op jit(solution)/shard_map/part_out/pallas_call | solution.py:295
  76.1 1.6 %collective-permute-start.12 = (bf16[2,2,2,64,512]{4,3,2,0,1:T(8,128)(2,1)S(1)}, bf16[2,2,2,64,512]{4,3,2,0,1:T(8,128)(2,1)S(1)}, u32[]{:S(2)}, u32[]{:S(2)}) collective-permute-start(bf16[2,2,2,64,512]{4,3,2,0,1:T(8,128)(2,1)S(1)} %get-tuple-element.80), channel_id=1, source_target_pairs={{0,8},{1,9},{2,10},{3,11},{4,12},{5,13},{6,14},{7,15},{8,0},{9,1},... | collective-permute-start | bytes 1572872 | tf_op jit(solution)/shard_map/ppermute | solution.py:361
  77.7 6.3 %feat_grad.1 = (bf16[384,768]{1,0:T(8,128)(2,1)}, bf16[384,768]{1,0:T(8,128)(2,1)}) custom-call(s32[32]{0:T(128)S(1)} %fusion.32.order_ref, bf16[2048,768]{1,0:T(8,128)(2,1)S(1)} %copy-done.2, bf16[2048,768]{1,0:T(8,128)(2,1)S(1)} %copy-done.2, bf16[2048,768]{1,0:T(8,128)(2,1)S(1)} %copy-done.2, bf16[2048,768]{1,0:T(8,128)(2,1)S(1)} %copy-done.2, ...), custom_call_target="tpu_custom_call" | custom-call | flops 1 | bytes 1 | tf_op jit(solution)/shard_map/feat_grad/pallas_call | solution.py:295
  84.2 0.8 collective-permute-start.13
  85.1 1.8 %collective-permute-start.14 = (bf16[2,2,32,896]{3,2,1,0:T(8,128)(2,1)S(1)}, bf16[2,2,32,896]{3,2,1,0:T(8,128)(2,1)S(1)}, u32[]{:S(2)}, u32[]{:S(2)}) collective-permute-start(bf16[2,2,32,896]{3,2,1,0:T(8,128)(2,1)S(1)} %get-tuple-element.90), channel_id=1, source_target_pairs={{0,1},{1,0},{2,3},{3,2},{4,5},{5,4},{6,7},{7,6},{8,9},{9,8},{10,11... | collective-permute-start | bytes 688136 | tf_op jit(solution)/shard_map/ppermute | solution.py:361
  87.0 2.9 %collective-permute-done.12 = bf16[2,2,2,64,512]{4,3,2,0,1:T(8,128)(2,1)S(1)} collective-permute-done((bf16[2,2,2,64,512]{4,3,2,0,1:T(8,128)(2,1)S(1)}, bf16[2,2,2,64,512]{4,3,2,0,1:T(8,128)(2,1)S(1)}, u32[]{:S(2)}, u32[]{:S(2)}) %collective-permute-start.12) | collective-permute-done | bytes 524320 | tf_op jit(solution)/shard_map/ppermute | solution.py:361
  91.0 1.6 %collective-permute-done.14 = bf16[2,2,32,896]{3,2,1,0:T(8,128)(2,1)S(1)} collective-permute-done((bf16[2,2,32,896]{3,2,1,0:T(8,128)(2,1)S(1)}, bf16[2,2,32,896]{3,2,1,0:T(8,128)(2,1)S(1)}, u32[]{:S(2)}, u32[]{:S(2)}) %collective-permute-start.14) | collective-permute-done | bytes 229408 | tf_op jit(solution)/shard_map/ppermute | solution.py:361
  92.7 1.6 %collective-permute-start.17 = (bf16[2,64,896]{2,1,0:T(8,128)(2,1)S(1)}, bf16[2,64,896]{2,1,0:T(8,128)(2,1)S(1)}, u32[]{:S(2)}, u32[]{:S(2)}) collective-permute-start(bf16[2,64,896]{2,1,0:T(8,128)(2,1)S(1)} %get-tuple-element.86), channel_id=1, source_target_pairs={{0,8},{1,9},{2,10},{3,11},{4,12},{5,13},{6,14},{7,15},{8,0},{9,1},... | collective-permute-start | bytes 688136 | tf_op jit(solution)/shard_map/ppermute | solution.py:361
  95.1 1.8 %collective-permute-start.20 = (bf16[2,32,512]{2,1,0:T(8,128)(2,1)S(1)}, bf16[2,32,512]{2,1,0:T(8,128)(2,1)S(1)}, u32[]{:S(2)}, u32[]{:S(2)}) collective-permute-start(bf16[2,32,512]{2,1,0:T(8,128)(2,1)S(1)} %get-tuple-element.94), channel_id=1, source_target_pairs={{0,1},{1,0},{2,3},{3,2},{4,5},{5,4},{6,7},{7,6},{8,9},{9,8},{10,11... | collective-permute-start | bytes 196616 | tf_op jit(solution)/shard_map/ppermute | solution.py:361
  97.8 1.0 collective-permute-done.17
  99.5 1.9 %collective-permute-done.19 = bf16[2,32,512]{2,1,0:T(8,128)(2,1)S(1)} collective-permute-done((bf16[2,32,512]{2,1,0:T(8,128)(2,1)S(1)}, bf16[2,32,512]{2,1,0:T(8,128)(2,1)S(1)}, u32[]{:S(2)}, u32[]{:S(2)}) %collective-permute-start.19) | collective-permute-done | bytes 65568 | tf_op jit(solution)/shard_map/ppermute | solution.py:361
  101.4 1.3 %collective-permute-start.21 = (bf16[64,512]{1,0:T(8,128)(2,1)S(1)}, bf16[64,512]{1,0:T(8,128)(2,1)S(1)}, u32[]{:S(2)}, u32[]{:S(2)}) collective-permute-start(bf16[64,512]{1,0:T(8,128)(2,1)S(1)} %fusion.17), channel_id=1, source_target_pairs={{0,16},{1,17},{2,18},{3,19},{4,20},{5,21},{6,22},{7,23},{8,24},{9,... | collective-permute-start | bytes 196616 | tf_op jit(solution)/shard_map/ppermute | solution.py:361
  102.7 1.7 %collective-permute-start.18 = (bf16[64,896]{1,0:T(8,128)(2,1)S(1)}, bf16[64,896]{1,0:T(8,128)(2,1)S(1)}, u32[]{:S(2)}, u32[]{:S(2)}) collective-permute-start(bf16[64,896]{1,0:T(8,128)(2,1)S(1)} %slice_bitcast_fusion.14), channel_id=1, source_target_pairs={{0,16},{1,17},{2,18},{3,19},{4,20},{5,21},{6,22},{7,23},{8,24},{9,... | collective-permute-start | bytes 344072 | tf_op jit(solution)/shard_map/ppermute | solution.py:361
  104.4 2.8 %collective-permute-done.21 = bf16[64,512]{1,0:T(8,128)(2,1)S(1)} collective-permute-done((bf16[64,512]{1,0:T(8,128)(2,1)S(1)}, bf16[64,512]{1,0:T(8,128)(2,1)S(1)}, u32[]{:S(2)}, u32[]{:S(2)}) %collective-permute-start.21) | collective-permute-done | bytes 65568 | tf_op jit(solution)/shard_map/ppermute | solution.py:361
  (78 shorter events, 9.9 us)
Async XLA Ops:
  0.6 10.9 %copy-start.4 = (s32[2]{0:T(128)S(1)}, s32[2]{0:T(128)}, u32[]{:S(2)}) copy-start(s32[2]{0:T(128)} %constant.14.clone) | copy-start | bytes 28
  0.6 10.9 %copy-start.5 = (s32[2]{0:T(128)S(1)}, s32[2]{0:T(128)}, u32[]{:S(2)}) copy-start(s32[2]{0:T(128)} %constant.13.clone) | copy-start | bytes 28
  0.7 22.6 %copy-start.6 = (f32[2048]{0:T(1024)S(1)}, f32[2048]{0:T(1024)}, u32[]{:S(2)}) copy-start(f32[2048]{0:T(1024)} %param.17) | copy-start | bytes 24580
  2.7 16.2 %collective-permute-start.1 = (s32[3,12]{1,0:T(4,128)}, s32[3,12]{1,0:T(4,128)S(1)}, u32[]{:S(2)}, u32[]{:S(2)}) collective-permute-start(s32[3,12]{1,0:T(4,128)} %get-tuple-element.38), channel_id=1, source_target_pairs={{1,4},{3,6},{5,8},{7,10},{9,12},{11,14},{13,16},{15,18},{17,20},{1... | collective-permute-start | bytes 440 | tf_op jit(solution)/shard_map/ppermute | solution.py:420
  3.4 8.2 %collective-permute-start = (s32[3,12]{1,0:T(4,128)}, s32[3,12]{1,0:T(4,128)S(1)}, u32[]{:S(2)}, u32[]{:S(2)}) collective-permute-start(s32[3,12]{1,0:T(4,128)} %get-tuple-element.38), channel_id=1, source_target_pairs={{0,1},{1,0},{2,3},{3,2},{4,5},{5,4},{6,7},{7,6},{8,9},{9,8},{10,11... | collective-permute-start | bytes 440 | tf_op jit(solution)/shard_map/ppermute | solution.py:361
  11.6 19.4 %collective-permute-start.6 = (bf16[768,512]{1,0:T(8,128)(2,1)}, bf16[768,512]{1,0:T(8,128)(2,1)}, u32[]{:S(2)}, u32[]{:S(2)}) collective-permute-start(bf16[768,512]{1,0:T(8,128)(2,1)} %get-tuple-element.40.r_2_), channel_id=1, source_target_pairs={{0,1},{1,0},{2,3},{3,2},{4,5},{5,4},{6,7},{7,6},{8,9},{9,8},{10,11... | collective-permute-start | bytes 2359304 | tf_op jit(solution)/shard_map/ppermute | solution.py:361
  12.9 31.0 %collective-permute-start.5 = (bf16[768,512]{1,0:T(8,128)(2,1)}, bf16[768,512]{1,0:T(8,128)(2,1)}, u32[]{:S(2)}, u32[]{:S(2)}) collective-permute-start(bf16[768,512]{1,0:T(8,128)(2,1)} %get-tuple-element.40.r_2_), channel_id=1, source_target_pairs={{2,0},{3,1},{4,2},{5,3},{6,4},{7,5},{8,6},{9,7},{10,8},{11,9},{12,... | collective-permute-start | bytes 2359304 | tf_op jit(solution)/shard_map/ppermute | solution.py:357
  14.2 29.7 %collective-permute-start.4 = (bf16[768,512]{1,0:T(8,128)(2,1)}, bf16[768,512]{1,0:T(8,128)(2,1)}, u32[]{:S(2)}, u32[]{:S(2)}) collective-permute-start(bf16[768,512]{1,0:T(8,128)(2,1)} %get-tuple-element.40.r_2_), channel_id=1, source_target_pairs={{0,2},{1,3},{2,4},{3,5},{4,6},{5,7},{6,8},{7,9},{8,10},{9,11},{10,... | collective-permute-start | bytes 2359304 | tf_op jit(solution)/shard_map/ppermute | solution.py:357
  18.9 16.4 %collective-permute-start.3 = (s32[6,12]{1,0:T(8,128)S(1)}, s32[6,12]{1,0:T(8,128)S(1)}, u32[]{:S(2)}, u32[]{:S(2)}) collective-permute-start(s32[6,12]{1,0:T(8,128)S(1)} %add_select_fusion.1), channel_id=1, source_target_pairs={{2,0},{3,1},{4,2},{5,3},{6,4},{7,5},{8,6},{9,7},{10,8},{11,9},{12,... | collective-permute-start | bytes 872 | tf_op jit(solution)/shard_map/ppermute | solution.py:357
  20.2 15.1 %collective-permute-start.2 = (s32[6,12]{1,0:T(8,128)S(1)}, s32[6,12]{1,0:T(8,128)S(1)}, u32[]{:S(2)}, u32[]{:S(2)}) collective-permute-start(s32[6,12]{1,0:T(8,128)S(1)} %add_select_fusion.1), channel_id=1, source_target_pairs={{0,2},{1,3},{2,4},{3,5},{4,6},{5,7},{6,8},{7,9},{8,10},{9,11},{10,... | collective-permute-start | bytes 872 | tf_op jit(solution)/shard_map/ppermute | solution.py:357
  31.0 12.9 %collective-permute-start.7 = (bf16[768,512]{1,0:T(8,128)(2,1)}, bf16[768,512]{1,0:T(8,128)(2,1)}, u32[]{:S(2)}, u32[]{:S(2)}) collective-permute-start(bf16[768,512]{1,0:T(8,128)(2,1)} %collective-permute-done.6.r_5_), channel_id=1, source_target_pairs={{0,2},{2,4},{4,6},{6,8},{8,10},{10,12},{12,14},{14,16},{16,18},{18... | collective-permute-start | bytes 2359304 | tf_op jit(solution)/shard_map/ppermute | solution.py:427
  43.9 11.8 %copy-start = (f32[2048,768]{1,0:T(8,128)S(1)}, f32[2048,768]{1,0:T(8,128)}, u32[]{:S(2)}) copy-start(f32[2048,768]{1,0:T(8,128)} %get-tuple-element.43.refs_0_.refs_1_.refs_2_.refs_3_) | copy-start | bytes 18874372
  43.9 11.8 %copy-start.1 = (bf16[2048,512]{1,0:T(8,128)(2,1)S(1)}, bf16[2048,512]{1,0:T(8,128)(2,1)}, u32[]{:S(2)}) copy-start(bf16[2048,512]{1,0:T(8,128)(2,1)} %refs_7_.3) | copy-start | bytes 6291460
  43.9 11.8 %copy-start.3 = (bf16[768,768]{1,0:T(8,128)(2,1)S(1)}, bf16[768,768]{1,0:T(8,128)(2,1)}, u32[]{:S(2)}) copy-start(bf16[768,768]{1,0:T(8,128)(2,1)} %pad_maximum_fusion.refs_9_) | copy-start | bytes 3538948
  59.8 3.9 %collective-permute-start.8 = (bf16[2,2,2,2,64,896]{5,4,3,2,0,1:T(8,128)(2,1)S(1)}, bf16[2,2,2,2,64,896]{5,4,3,2,0,1:T(8,128)(2,1)S(1)}, u32[]{:S(2)}, u32[]{:S(2)}) collective-permute-start(bf16[2,2,2,2,64,896]{5,4,3,2,0,1:T(8,128)(2,1)S(1)} %copy.25), channel_id=1, source_target_pairs={{0,2},{1,3},{2,0},{3,1},{4,6},{5,7},{6,4},{7,5},{8,10},{9,11},{10,... | collective-permute-start | bytes 5505032 | tf_op jit(solution)/shard_map/ppermute | solution.py:361
  66.6 9.0 %collective-permute-start.9 = (bf16[2,2,2,2,64,512]{5,4,3,0,1,2:T(8,128)(2,1)S(1)}, bf16[2,2,2,2,64,512]{5,4,3,0,1,2:T(8,128)(2,1)S(1)}, u32[]{:S(2)}, u32[]{:S(2)}) collective-permute-start(bf16[2,2,2,2,64,512]{5,4,3,0,1,2:T(8,128)(2,1)S(1)} %copy.28), channel_id=1, source_target_pairs={{0,2},{1,3},{2,0},{3,1},{4,6},{5,7},{6,4},{7,5},{8,10},{9,11},{10,... | collective-permute-start | bytes 3145736 | tf_op jit(solution)/shard_map/ppermute | solution.py:361
  67.2 16.8 %collective-permute-start.10 = (bf16[2,2,2,32,896]{4,3,2,1,0:T(8,128)(2,1)S(1)}, bf16[2,2,2,32,896]{4,3,2,1,0:T(8,128)(2,1)S(1)}, u32[]{:S(2)}, u32[]{:S(2)}) collective-permute-start(bf16[2,2,2,32,896]{4,3,2,1,0:T(8,128)(2,1)S(1)} %get-tuple-element.76), channel_id=1, source_target_pairs={{0,1},{1,0},{2,3},{3,2},{4,5},{5,4},{6,7},{7,6},{8,9},{9,8},{10,11... | collective-permute-start | bytes 1376264 | tf_op jit(solution)/shard_map/ppermute | solution.py:361
  69.7 15.3 %collective-permute-start.11 = (bf16[2,2,2,32,896]{4,3,2,1,0:T(8,128)(2,1)S(1)}, bf16[2,2,2,32,896]{4,3,2,1,0:T(8,128)(2,1)S(1)}, u32[]{:S(2)}, u32[]{:S(2)}) collective-permute-start(bf16[2,2,2,32,896]{4,3,2,1,0:T(8,128)(2,1)S(1)} %get-tuple-element.78), channel_id=1, source_target_pairs={{0,4},{1,5},{2,6},{3,7},{4,0},{5,1},{6,2},{7,3},{8,12},{9,13},{10,... | collective-permute-start | bytes 1376264 | tf_op jit(solution)/shard_map/ppermute | solution.py:361
  75.7 2.1 %copy-start.2 = (bf16[2048,768]{1,0:T(8,128)(2,1)S(1)}, bf16[2048,768]{1,0:T(8,128)(2,1)}, u32[]{:S(2)}) copy-start(bf16[2048,768]{1,0:T(8,128)(2,1)} %refs_3_.1) | copy-start | bytes 9437188
  76.1 13.8 %collective-permute-start.12 = (bf16[2,2,2,64,512]{4,3,2,0,1:T(8,128)(2,1)S(1)}, bf16[2,2,2,64,512]{4,3,2,0,1:T(8,128)(2,1)S(1)}, u32[]{:S(2)}, u32[]{:S(2)}) collective-permute-start(bf16[2,2,2,64,512]{4,3,2,0,1:T(8,128)(2,1)S(1)} %get-tuple-element.80), channel_id=1, source_target_pairs={{0,8},{1,9},{2,10},{3,11},{4,12},{5,13},{6,14},{7,15},{8,0},{9,1},... | collective-permute-start | bytes 1572872 | tf_op jit(solution)/shard_map/ppermute | solution.py:361
  84.2 8.4 %collective-permute-start.13 = (bf16[2,2,32,896]{3,2,1,0:T(8,128)(2,1)S(1)}, bf16[2,2,32,896]{3,2,1,0:T(8,128)(2,1)S(1)}, u32[]{:S(2)}, u32[]{:S(2)}) collective-permute-start(bf16[2,2,32,896]{3,2,1,0:T(8,128)(2,1)S(1)} %get-tuple-element.88), channel_id=1, source_target_pairs={{0,4},{1,5},{2,6},{3,7},{4,0},{5,1},{6,2},{7,3},{8,12},{9,13},{10,... | collective-permute-start | bytes 688136 | tf_op jit(solution)/shard_map/ppermute | solution.py:361
  85.1 7.4 %collective-permute-start.14 = (bf16[2,2,32,896]{3,2,1,0:T(8,128)(2,1)S(1)}, bf16[2,2,32,896]{3,2,1,0:T(8,128)(2,1)S(1)}, u32[]{:S(2)}, u32[]{:S(2)}) collective-permute-start(bf16[2,2,32,896]{3,2,1,0:T(8,128)(2,1)S(1)} %get-tuple-element.90), channel_id=1, source_target_pairs={{0,1},{1,0},{2,3},{3,2},{4,5},{5,4},{6,7},{7,6},{8,9},{9,8},{10,11... | collective-permute-start | bytes 688136 | tf_op jit(solution)/shard_map/ppermute | solution.py:361
  90.1 5.0 %collective-permute-start.16 = (bf16[2,2,32,512]{3,2,1,0:T(8,128)(2,1)S(1)}, bf16[2,2,32,512]{3,2,1,0:T(8,128)(2,1)S(1)}, u32[]{:S(2)}, u32[]{:S(2)}) collective-permute-start(bf16[2,2,32,512]{3,2,1,0:T(8,128)(2,1)S(1)} %get-tuple-element.82), channel_id=1, source_target_pairs={{0,4},{1,5},{2,6},{3,7},{4,0},{5,1},{6,2},{7,3},{8,12},{9,13},{10,... | collective-permute-start | bytes 393224 | tf_op jit(solution)/shard_map/ppermute | solution.py:361
  90.4 6.6 %collective-permute-start.15 = (bf16[2,2,32,512]{3,2,1,0:T(8,128)(2,1)S(1)}, bf16[2,2,32,512]{3,2,1,0:T(8,128)(2,1)S(1)}, u32[]{:S(2)}, u32[]{:S(2)}) collective-permute-start(bf16[2,2,32,512]{3,2,1,0:T(8,128)(2,1)S(1)} %get-tuple-element.84), channel_id=1, source_target_pairs={{0,1},{1,0},{2,3},{3,2},{4,5},{5,4},{6,7},{7,6},{8,9},{9,8},{10,11... | collective-permute-start | bytes 393224 | tf_op jit(solution)/shard_map/ppermute | solution.py:361
  92.7 6.1 %collective-permute-start.17 = (bf16[2,64,896]{2,1,0:T(8,128)(2,1)S(1)}, bf16[2,64,896]{2,1,0:T(8,128)(2,1)S(1)}, u32[]{:S(2)}, u32[]{:S(2)}) collective-permute-start(bf16[2,64,896]{2,1,0:T(8,128)(2,1)S(1)} %get-tuple-element.86), channel_id=1, source_target_pairs={{0,8},{1,9},{2,10},{3,11},{4,12},{5,13},{6,14},{7,15},{8,0},{9,1},... | collective-permute-start | bytes 688136 | tf_op jit(solution)/shard_map/ppermute | solution.py:361
  95.1 4.3 %collective-permute-start.20 = (bf16[2,32,512]{2,1,0:T(8,128)(2,1)S(1)}, bf16[2,32,512]{2,1,0:T(8,128)(2,1)S(1)}, u32[]{:S(2)}, u32[]{:S(2)}) collective-permute-start(bf16[2,32,512]{2,1,0:T(8,128)(2,1)S(1)} %get-tuple-element.94), channel_id=1, source_target_pairs={{0,1},{1,0},{2,3},{3,2},{4,5},{5,4},{6,7},{7,6},{8,9},{9,8},{10,11... | collective-permute-start | bytes 196616 | tf_op jit(solution)/shard_map/ppermute | solution.py:361
  97.0 4.3 %collective-permute-start.19 = (bf16[2,32,512]{2,1,0:T(8,128)(2,1)S(1)}, bf16[2,32,512]{2,1,0:T(8,128)(2,1)S(1)}, u32[]{:S(2)}, u32[]{:S(2)}) collective-permute-start(bf16[2,32,512]{2,1,0:T(8,128)(2,1)S(1)} %get-tuple-element.92), channel_id=1, source_target_pairs={{0,4},{1,5},{2,6},{3,7},{4,0},{5,1},{6,2},{7,3},{8,12},{9,13},{10,... | collective-permute-start | bytes 196616 | tf_op jit(solution)/shard_map/ppermute | solution.py:361
  101.4 5.8 %collective-permute-start.21 = (bf16[64,512]{1,0:T(8,128)(2,1)S(1)}, bf16[64,512]{1,0:T(8,128)(2,1)S(1)}, u32[]{:S(2)}, u32[]{:S(2)}) collective-permute-start(bf16[64,512]{1,0:T(8,128)(2,1)S(1)} %fusion.17), channel_id=1, source_target_pairs={{0,16},{1,17},{2,18},{3,19},{4,20},{5,21},{6,22},{7,23},{8,24},{9,... | collective-permute-start | bytes 196616 | tf_op jit(solution)/shard_map/ppermute | solution.py:361
  102.7 5.8 %collective-permute-start.18 = (bf16[64,896]{1,0:T(8,128)(2,1)S(1)}, bf16[64,896]{1,0:T(8,128)(2,1)S(1)}, u32[]{:S(2)}, u32[]{:S(2)}) collective-permute-start(bf16[64,896]{1,0:T(8,128)(2,1)S(1)} %slice_bitcast_fusion.14), channel_id=1, source_target_pairs={{0,16},{1,17},{2,18},{3,19},{4,20},{5,21},{6,22},{7,23},{8,24},{9,... | collective-permute-start | bytes 344072 | tf_op jit(solution)/shard_map/ppermute | solution.py:361

commit v10 on v9

--- a/solution.py
+++ b/solution.py
@@ -121,8 +121,8 @@
     mid = 5 * tiles
     near = 3 * tiles
     keep = 1.0 - ALPHA
-    sources = (own_hbm, nimg_hbm, ncap_hbm, low_hbm, high_hbm, mate_hbm, far_hbm, pat_t_hbm, pat_hbm)
-    targets = (bands.at[0], nimg_ref, ncap_ref) + tuple(bands.at[k] for k in range(1, 5)) + (pat_t_ref, pat_ref)
+    sources = (own_hbm, nimg_hbm, ncap_hbm, pat_t_hbm, low_hbm, high_hbm, mate_hbm, far_hbm, pat_hbm)
+    targets = (bands.at[0], nimg_ref, ncap_ref, pat_t_ref) + tuple(bands.at[k] for k in range(1, 5)) + (pat_ref,)
     copies = [pltpu.make_async_copy(s, t, sems.at[k]) for k, (s, t) in enumerate(zip(sources, targets))]
     for copy in copies:
         copy.start()
@@ -139,14 +139,6 @@
 
     acc[...] = jnp.zeros_like(acc)
     acc2[...] = jnp.zeros_like(acc2)
-    for copy in copies[:3]:
-        copy.wait()
-    for k, base in enumerate((2 * tiles, 0, 4 * tiles, base_ref[0], base_ref[1])):
-        if k:
-            copies[2 + k].wait()
-        scale(k, base)
-    for copy in copies[7:]:
-        copy.wait()
 
     def push(q, state, target, lo, count):
         r = jnp.dot(pat_t_ref[q], state, preferred_element_type=F32)
@@ -163,11 +155,15 @@
             total = r if total is None else total + r
         return total
 
-    def push1(q, c):
-        push(q, img0[q], acc, tiles, near)
-        return c
-
-    lax.fori_loop(0, mid, push1, 0, unroll=3)
+    for copy in copies[:4]:
+        copy.wait()
+    for k, base in enumerate((2 * tiles, 0, 4 * tiles, base_ref[0], base_ref[1])):
+        if k:
+            copies[3 + k].wait()
+        scale(k, base)
+        for t in range(tiles):
+            push(base + t, img0[base + t], acc, tiles, near)
+    copies[8].wait()
 
     def pull1(q, c):
         n = wide(nimg_ref, q)
@@ -176,7 +172,7 @@
         keep_img[q - tiles] = flow
         return c
 
-    lax.fori_loop(tiles, tiles + near, pull1, 0, unroll=3)
+    lax.fori_loop(tiles, tiles + near, pull1, 0, unroll=9)
 
     def finish1(m, c):
         n = wide(ncap_ref, m + tiles)
@@ -399,8 +395,8 @@
     def finish(self, *done):
         self.parts = [added(after(k, *done), c) for k, c in zip(self.kept, self.came)]
 
-    def result(self):
-        return self.kept[0].astype(F32) + self.came[0].astype(F32)
+    def result(self, lanes):
+        return self.kept[0][:, lanes].astype(F32) + self.came[0][:, lanes].astype(F32)
 
 
 def per_device(
@@ -426,8 +422,8 @@
     high = moved(block, count, -2)
     far = lax.ppermute(mate, AXES, nearest_pair(count, 2))
     pair = jnp.where(even, jnp.concatenate([meta, other]), jnp.concatenate([other, meta]))
-    feats = jnp.concatenate([feats_img, feats_cap], axis=0)
-    pair, feats, third = lax.optimization_barrier((pair, after(feats, block), third))
+    feats = jnp.concatenate([after(feats_img, block), feats_cap], axis=0)
+    pair, feats, third = lax.optimization_barrier((pair, feats, third))
     pair_low = moved(pair, count, 2)
     pair_high = moved(pair, count, -2)
     wide = jnp.where(
@@ -517,8 +513,10 @@
         r_out.start()
         done = r_out.sent
     grad_scale = 1.0 / math.sqrt(nodes * count)
-    g_out, g_in = [r.result() * grad_scale for r in (r_out, r_in)]
-    return (grad_img, grad_cap, g_in[:, :f_in], g_out, g_in[:, f_in])
+    g_out = r_out.result(slice(None)) * grad_scale
+    g_in = r_in.result(slice(0, f_in)) * grad_scale
+    g_bias = r_in.result(f_in) * grad_scale
+    return (grad_img, grad_cap, g_in, g_out, g_bias)
 
 
 def solution(mesh):

time: 110 us -> 110 us (level)
  Pallas kernels: 39.7 us -> 38.3 us
  local copies, waits for them, and re-layouts: 2.53 us -> 1.22 us
    pallas_call x1, Pallas kernels: 11.8 us -> 10.4 us  [propagate(): pl.pallas_call(lambda *r: hops_kernel(*r, tiles=tiles, slots=slots, width...]
    slice x2 -> x0, local copies, waits for them, and re-layouts: 1.32 us -> none  [per_device(): return (grad_img, grad_cap, g_in[:, :f_in], g_out, g_in[:, f_in])]
    mul x2 -> x3, other arithmetic: 0.71 us -> 2.01 us  [the longest x1 0.7 us: per_device(): g_in = r_in.result(slice(0, f_in)) * grad_scale]
  transfers between devices with their start and end apart: 22 -> 22, of which waited for: 8 -> 9; matrix products, arithmetic and copies ran while one was open for 12% -> 12% of each run, Pallas kernels for 18% -> 18%
where the time goes in v10:
time: 110 us; the launch traced here: 109 us
  starting transfers between devices  41.7 us (38%)
  Pallas kernels  38.3 us (35%)
  waiting for transfers between devices  13.1 us (12%)
  matrix products  7.41 us (7%)
  other arithmetic  6.62 us (6%)
  local copies, waits for them, and re-layouts  1.22 us (1%)
    ppermute x16, starting transfers between devices, flipped(): return lax.ppermute(array, AXES, [(i, i ^ mask) for i in range(count)])  27.2 us
    pallas_call x5, Pallas kernels, over_hidden(): pl.pallas_call(kernel, out_shape=out_shape, grid_spec=pltpu.PrefetchScala...  17.9 us
    ppermute x16, waiting for transfers between devices, flipped(): return lax.ppermute(array, AXES, [(i, i ^ mask) for i in range(count)])  13.1 us
    pallas_call x1, Pallas kernels, propagate(): pl.pallas_call(lambda *r: hops_kernel(*r, tiles=tiles, slots=slots, width...  10.4 us
    ppermute x4, starting transfers between devices, moved(): lax.ppermute(array, AXES, [(i, i + by) for i in range(count) if 0 <= i +...  9.53 us
    pallas_call x1, Pallas kernels, make_tiles(): pl.pallas_call(lambda *r: tiles_kernel(*r, tiles=tiles, slots=slots), out...  7.82 us
    dot_general x1, matrix products, per_device(): lax.dot_general(w_in, feats, across, preferred_element_type=F32)  7.41 us
    ppermute x1, starting transfers between devices, per_device(): far = lax.ppermute(mate, AXES, nearest_pair(count, 2))  4.29 us
  transfers between devices with their start and end apart: 22, of which 9 were waited for; matrix products, arithmetic and copies ran while one was open for 12% of the time, Pallas kernels for 18%

profile of v10, /device:TPU:0, one launch (start us, length us, event | category | flops | bytes accessed | tf_op | source)
XLA Modules:
  0.0 109.4 jit_solution(12112568725861046986)
XLA Ops:
  0.6 2.1 %stack.1 = (bf16[768,512]{1,0:T(8,128)(2,1)}, s32[3,12]{1,0:T(4,128)}) custom-call(s32[3]{0:T(128)} %count_ref.1, bf16[384,512]{1,0:T(8,128)(2,1)} %top_ref.1, bf16[384,512]{1,0:T(8,128)(2,1)} %bottom_ref.1, s32[3,4]{1,0:T(4,128)} %seed_ref.1, s32[3,4]{1,0:T(4,128)} %cols_ref.1), custom_call_target="tpu_custom_call" | custom-call | flops 1 | bytes 1 | tf_op jit(solution)/shard_map/stack/pallas_call | solution.py:338
  3.4 5.7 %collective-permute-start = (s32[3,12]{1,0:T(4,128)}, s32[3,12]{1,0:T(4,128)S(1)}, u32[]{:S(2)}, u32[]{:S(2)}) collective-permute-start(s32[3,12]{1,0:T(4,128)} %get-tuple-element.38), channel_id=1, source_target_pairs={{0,1},{1,0},{2,3},{3,2},{4,5},{5,4},{6,7},{7,6},{8,9},{9,8},{10,11... | collective-permute-start | bytes 440 | tf_op jit(solution)/shard_map/ppermute | solution.py:357
  9.9 1.0 collective-permute-done
  10.9 2.0 %collective-permute-start.6 = (bf16[768,512]{1,0:T(8,128)(2,1)}, bf16[768,512]{1,0:T(8,128)(2,1)}, u32[]{:S(2)}, u32[]{:S(2)}) collective-permute-start(bf16[768,512]{1,0:T(8,128)(2,1)} %get-tuple-element.40.r_2_), channel_id=1, source_target_pairs={{0,1},{1,0},{2,3},{3,2},{4,5},{5,4},{6,7},{7,6},{8,9},{9,8},{10,11... | collective-permute-start | bytes 2359304 | tf_op jit(solution)/shard_map/ppermute | solution.py:357
  12.9 1.3 %collective-permute-start.5 = (bf16[768,512]{1,0:T(8,128)(2,1)}, bf16[768,512]{1,0:T(8,128)(2,1)}, u32[]{:S(2)}, u32[]{:S(2)}) collective-permute-start(bf16[768,512]{1,0:T(8,128)(2,1)} %get-tuple-element.40.r_2_), channel_id=1, source_target_pairs={{2,0},{3,1},{4,2},{5,3},{6,4},{7,5},{8,6},{9,7},{10,8},{11,9},{12,... | collective-permute-start | bytes 2359304 | tf_op jit(solution)/shard_map/ppermute | solution.py:353
  14.2 3.9 %collective-permute-start.4 = (bf16[768,512]{1,0:T(8,128)(2,1)}, bf16[768,512]{1,0:T(8,128)(2,1)}, u32[]{:S(2)}, u32[]{:S(2)}) collective-permute-start(bf16[768,512]{1,0:T(8,128)(2,1)} %get-tuple-element.40.r_2_), channel_id=1, source_target_pairs={{0,2},{1,3},{2,4},{3,5},{4,6},{5,7},{6,8},{7,9},{8,10},{9,11},{10,... | collective-permute-start | bytes 2359304 | tf_op jit(solution)/shard_map/ppermute | solution.py:353
  18.1 1.3 %pad_maximum_fusion.refs_9_ = bf16[768,768]{1,0:T(8,128)(2,1)S(1)} fusion(bf16[384,768]{1,0:T(8,128)(2,1)} %param.13, bf16[384,768]{1,0:T(8,128)(2,1)} %param.12), kind=kLoop, calls=%fused_computation.15 | loop fusion | flops 2359296 | bytes 2359296 | tf_op jit(solution)/shard_map/concatenate | solution.py:425
  20.2 1.3 %collective-permute-start.3 = (s32[6,12]{1,0:T(8,128)S(1)}, s32[6,12]{1,0:T(8,128)S(1)}, u32[]{:S(2)}, u32[]{:S(2)}) collective-permute-start(s32[6,12]{1,0:T(8,128)S(1)} %add_select_fusion.1), channel_id=1, source_target_pairs={{2,0},{3,1},{4,2},{5,3},{6,4},{7,5},{8,6},{9,7},{10,8},{11,9},{12,... | collective-permute-start | bytes 872 | tf_op jit(solution)/shard_map/ppermute | solution.py:353
  21.5 3.0 %collective-permute-start.2 = (s32[6,12]{1,0:T(8,128)S(1)}, s32[6,12]{1,0:T(8,128)S(1)}, u32[]{:S(2)}, u32[]{:S(2)}) collective-permute-start(s32[6,12]{1,0:T(8,128)S(1)} %add_select_fusion.1), channel_id=1, source_target_pairs={{0,2},{1,3},{2,4},{3,5},{4,6},{5,7},{6,8},{7,9},{8,10},{9,11},{10,... | collective-permute-start | bytes 872 | tf_op jit(solution)/shard_map/ppermute | solution.py:353
  24.6 7.4 %fusion.3 = (f32[2048,768]{1,0:T(8,128)}, bf16[2048,768]{1,0:T(8,128)(2,1)S(1)}) fusion(f32[2048]{0:T(1024)S(1)} %copy-done.5, bf16[768,768]{1,0:T(8,128)(2,1)S(1)} %pad_maximum_fusion.refs_9_, bf16[2048,768]{1,0:T(8,128)(2,1)} %refs_3_.1), kind=kOutput, calls=%fused_computation.4 | convolution fusion | flops 2433220608 | bytes 13770752 | tf_op jit(solution)/shard_map/dot_general | solution.py:460
  32.0 4.3 %collective-permute-start.7 = (bf16[768,512]{1,0:T(8,128)(2,1)}, bf16[768,512]{1,0:T(8,128)(2,1)}, u32[]{:S(2)}, u32[]{:S(2)}) collective-permute-start(bf16[768,512]{1,0:T(8,128)(2,1)} %collective-permute-done.6.r_5_), channel_id=1, source_target_pairs={{0,2},{2,4},{4,6},{6,8},{8,10},{10,12},{12,14},{14,16},{16,18},{18... | collective-permute-start | bytes 2359304 | tf_op jit(solution)/shard_map/ppermute | solution.py:423
  37.0 7.8 %tiles.1 = (bf16[15,128,512]{2,1,0:T(8,128)(2,1)}, bf16[15,512,128]{2,1,0:T(8,128)(2,1)}, f32[15,128,128]{2,1,0:T(8,128)}, f32[15,128,128]{2,1,0:T(8,128)}) custom-call(s32[84]{0:T(128)S(1)} %reshape.40.r_0_, s32[84]{0:T(128)S(1)} %reshape.41.r_1_, s32[21]{0:T(128)S(1)} %slice_reduce_fusion.r_2_), custom_call_target="tpu_custom_call" | custom-call | flops 1 | bytes 1 | tf_op jit(solution)/shard_map/tiles/pallas_call | solution.py:103
  45.0 10.4 %hops.1.refs_8_.refs_4_ = bf16[768,512]{1,0:T(8,128)(2,1)S(1)} custom-call(s32[60]{0:T(128)S(1)} %reshape.39.r_0_, s32[2]{0:T(128)S(1)} %fusion.18.r_1_, bf16[768,512]{1,0:T(8,128)(2,1)} %get-tuple-element.40.r_2_, bf16[768,512]{1,0:T(8,128)(2,1)} %collective-permute-done.4.r_3_, bf16[768,512]{1,0:T(8,128)(2,1)} %collective-permute-done.5.r_4_, ...), custom_call_target="tpu_custom_call" | custom-call | flops 1 | bytes 1 | tf_op jit(solution)/shard_map/hops/pallas_call | solution.py:207
  55.4 3.8 %part_in.2 = (bf16[1024,896]{1,0:T(8,128)(2,1)S(1)}, bf16[1024,768]{1,0:T(8,128)(2,1)S(1)}) custom-call(s32[16]{0:T(128)S(1)} %get-tuple-element.98.order_ref, f32[2048,768]{1,0:T(8,128)S(1)} %copy-done, f32[2048,768]{1,0:T(8,128)S(1)} %copy-done, f32[2048,768]{1,0:T(8,128)S(1)} %copy-done, f32[2048,768]{1,0:T(8,128)S(1)} %copy-done, ...), custom_call_target="tpu_custom_call" | custom-call | flops 1 | bytes 1 | tf_op jit(solution)/shard_map/part_in/pallas_call | solution.py:291
  59.5 3.8 %part_in.3 = (bf16[1024,896]{1,0:T(8,128)(2,1)S(1)}, bf16[1024,768]{1,0:T(8,128)(2,1)S(1)}) custom-call(s32[16]{0:T(128)S(1)} %get-tuple-element.99.order_ref, f32[2048,768]{1,0:T(8,128)S(1)} %copy-done, f32[2048,768]{1,0:T(8,128)S(1)} %copy-done, f32[2048,768]{1,0:T(8,128)S(1)} %copy-done, f32[2048,768]{1,0:T(8,128)S(1)} %copy-done, ...), custom_call_target="tpu_custom_call" | custom-call | flops 1 | bytes 1 | tf_op jit(solution)/shard_map/part_in/pallas_call | solution.py:291
  64.1 2.0 %part_out.2 = bf16[1024,512]{1,0:T(8,128)(2,1)S(1)} custom-call(s32[16]{0:T(128)S(1)} %get-tuple-element.98.order_ref, bf16[2048,768]{1,0:T(8,128)(2,1)S(1)} %get-tuple-element.53.refs_0_.refs_1_.refs_2_.refs_3_, bf16[2048,768]{1,0:T(8,128)(2,1)S(1)} %get-tuple-element.53.refs_0_.refs_1_.refs_2_.refs_3_, ...), custom_call_target="tpu_custom_call" | custom-call | flops 1 | bytes 1 | tf_op jit(solution)/shard_map/part_out/pallas_call | solution.py:291
  66.8 2.2 %collective-permute-start.10 = (bf16[2,2,2,32,896]{4,3,2,1,0:T(8,128)(2,1)S(1)}, bf16[2,2,2,32,896]{4,3,2,1,0:T(8,128)(2,1)S(1)}, u32[]{:S(2)}, u32[]{:S(2)}) collective-permute-start(bf16[2,2,2,32,896]{4,3,2,1,0:T(8,128)(2,1)S(1)} %get-tuple-element.76), channel_id=1, source_target_pairs={{0,1},{1,0},{2,3},{3,2},{4,5},{5,4},{6,7},{7,6},{8,9},{9,8},{10,11... | collective-permute-start | bytes 1376264 | tf_op jit(solution)/shard_map/ppermute | solution.py:357
  69.0 4.2 %collective-permute-start.11 = (bf16[2,2,2,32,896]{4,3,2,1,0:T(8,128)(2,1)S(1)}, bf16[2,2,2,32,896]{4,3,2,1,0:T(8,128)(2,1)S(1)}, u32[]{:S(2)}, u32[]{:S(2)}) collective-permute-start(bf16[2,2,2,32,896]{4,3,2,1,0:T(8,128)(2,1)S(1)} %get-tuple-element.78), channel_id=1, source_target_pairs={{0,4},{1,5},{2,6},{3,7},{4,0},{5,1},{6,2},{7,3},{8,12},{9,13},{10,... | collective-permute-start | bytes 1376264 | tf_op jit(solution)/shard_map/ppermute | solution.py:357
  73.2 2.0 %part_out.3 = bf16[1024,512]{1,0:T(8,128)(2,1)S(1)} custom-call(s32[16]{0:T(128)S(1)} %get-tuple-element.99.order_ref, bf16[2048,768]{1,0:T(8,128)(2,1)S(1)} %get-tuple-element.53.refs_0_.refs_1_.refs_2_.refs_3_, bf16[2048,768]{1,0:T(8,128)(2,1)S(1)} %get-tuple-element.53.refs_0_.refs_1_.refs_2_.refs_3_, ...), custom_call_target="tpu_custom_call" | custom-call | flops 1 | bytes 1 | tf_op jit(solution)/shard_map/part_out/pallas_call | solution.py:291
  75.7 1.7 %collective-permute-start.12 = (bf16[2,2,2,64,512]{4,3,2,0,1:T(8,128)(2,1)S(1)}, bf16[2,2,2,64,512]{4,3,2,0,1:T(8,128)(2,1)S(1)}, u32[]{:S(2)}, u32[]{:S(2)}) collective-permute-start(bf16[2,2,2,64,512]{4,3,2,0,1:T(8,128)(2,1)S(1)} %get-tuple-element.80), channel_id=1, source_target_pairs={{0,8},{1,9},{2,10},{3,11},{4,12},{5,13},{6,14},{7,15},{8,0},{9,1},... | collective-permute-start | bytes 1572872 | tf_op jit(solution)/shard_map/ppermute | solution.py:357
  77.4 6.2 %feat_grad.1 = (bf16[384,768]{1,0:T(8,128)(2,1)}, bf16[384,768]{1,0:T(8,128)(2,1)}) custom-call(s32[32]{0:T(128)S(1)} %fusion.31.order_ref, bf16[2048,768]{1,0:T(8,128)(2,1)S(1)} %copy-done.2, bf16[2048,768]{1,0:T(8,128)(2,1)S(1)} %copy-done.2, bf16[2048,768]{1,0:T(8,128)(2,1)S(1)} %copy-done.2, bf16[2048,768]{1,0:T(8,128)(2,1)S(1)} %copy-done.2, ...), custom_call_target="tpu_custom_call" | custom-call | flops 1 | bytes 1 | tf_op jit(solution)/shard_map/feat_grad/pallas_call | solution.py:291
  83.7 0.8 collective-permute-start.13
  84.8 1.8 %collective-permute-start.14 = (bf16[2,2,32,896]{3,2,1,0:T(8,128)(2,1)S(1)}, bf16[2,2,32,896]{3,2,1,0:T(8,128)(2,1)S(1)}, u32[]{:S(2)}, u32[]{:S(2)}) collective-permute-start(bf16[2,2,32,896]{3,2,1,0:T(8,128)(2,1)S(1)} %get-tuple-element.90), channel_id=1, source_target_pairs={{0,1},{1,0},{2,3},{3,2},{4,5},{5,4},{6,7},{7,6},{8,9},{9,8},{10,11... | collective-permute-start | bytes 688136 | tf_op jit(solution)/shard_map/ppermute | solution.py:357
  86.6 2.9 %collective-permute-done.12 = bf16[2,2,2,64,512]{4,3,2,0,1:T(8,128)(2,1)S(1)} collective-permute-done((bf16[2,2,2,64,512]{4,3,2,0,1:T(8,128)(2,1)S(1)}, bf16[2,2,2,64,512]{4,3,2,0,1:T(8,128)(2,1)S(1)}, u32[]{:S(2)}, u32[]{:S(2)}) %collective-permute-start.12) | collective-permute-done | bytes 524320 | tf_op jit(solution)/shard_map/ppermute | solution.py:357
  90.6 1.6 %collective-permute-done.14 = bf16[2,2,32,896]{3,2,1,0:T(8,128)(2,1)S(1)} collective-permute-done((bf16[2,2,32,896]{3,2,1,0:T(8,128)(2,1)S(1)}, bf16[2,2,32,896]{3,2,1,0:T(8,128)(2,1)S(1)}, u32[]{:S(2)}, u32[]{:S(2)}) %collective-permute-start.14) | collective-permute-done | bytes 229408 | tf_op jit(solution)/shard_map/ppermute | solution.py:357
  92.4 1.7 %collective-permute-start.17 = (bf16[2,64,896]{2,1,0:T(8,128)(2,1)S(1)}, bf16[2,64,896]{2,1,0:T(8,128)(2,1)S(1)}, u32[]{:S(2)}, u32[]{:S(2)}) collective-permute-start(bf16[2,64,896]{2,1,0:T(8,128)(2,1)S(1)} %get-tuple-element.86), channel_id=1, source_target_pairs={{0,8},{1,9},{2,10},{3,11},{4,12},{5,13},{6,14},{7,15},{8,0},{9,1},... | collective-permute-start | bytes 688136 | tf_op jit(solution)/shard_map/ppermute | solution.py:357
  94.8 1.9 %collective-permute-start.20 = (bf16[2,32,512]{2,1,0:T(8,128)(2,1)S(1)}, bf16[2,32,512]{2,1,0:T(8,128)(2,1)S(1)}, u32[]{:S(2)}, u32[]{:S(2)}) collective-permute-start(bf16[2,32,512]{2,1,0:T(8,128)(2,1)S(1)} %get-tuple-element.96), channel_id=1, source_target_pairs={{0,1},{1,0},{2,3},{3,2},{4,5},{5,4},{6,7},{7,6},{8,9},{9,8},{10,11... | collective-permute-start | bytes 196616 | tf_op jit(solution)/shard_map/ppermute | solution.py:357
  97.4 1.0 collective-permute-done.17
  99.1 1.9 %collective-permute-done.19 = bf16[2,32,512]{2,1,0:T(8,128)(2,1)S(1)} collective-permute-done((bf16[2,32,512]{2,1,0:T(8,128)(2,1)S(1)}, bf16[2,32,512]{2,1,0:T(8,128)(2,1)S(1)}, u32[]{:S(2)}, u32[]{:S(2)}) %collective-permute-start.19) | collective-permute-done | bytes 65568 | tf_op jit(solution)/shard_map/ppermute | solution.py:357
  101.1 1.3 %collective-permute-start.21 = (bf16[64,512]{1,0:T(8,128)(2,1)S(1)}, bf16[64,512]{1,0:T(8,128)(2,1)S(1)}, u32[]{:S(2)}, u32[]{:S(2)}) collective-permute-start(bf16[64,512]{1,0:T(8,128)(2,1)S(1)} %fusion.16), channel_id=1, source_target_pairs={{0,16},{1,17},{2,18},{3,19},{4,20},{5,21},{6,22},{7,23},{8,24},{9,... | collective-permute-start | bytes 196616 | tf_op jit(solution)/shard_map/ppermute | solution.py:357
  102.4 1.7 %collective-permute-start.18 = (bf16[64,896]{1,0:T(8,128)(2,1)S(1)}, bf16[64,896]{1,0:T(8,128)(2,1)S(1)}, u32[]{:S(2)}, u32[]{:S(2)}) collective-permute-start(bf16[64,896]{1,0:T(8,128)(2,1)S(1)} %get-tuple-element.92), channel_id=1, source_target_pairs={{0,16},{1,17},{2,18},{3,19},{4,20},{5,21},{6,22},{7,23},{8,24},{9,... | collective-permute-start | bytes 344072 | tf_op jit(solution)/shard_map/ppermute | solution.py:357
  104.0 2.8 %collective-permute-done.21 = bf16[64,512]{1,0:T(8,128)(2,1)S(1)} collective-permute-done((bf16[64,512]{1,0:T(8,128)(2,1)S(1)}, bf16[64,512]{1,0:T(8,128)(2,1)S(1)}, u32[]{:S(2)}, u32[]{:S(2)}) %collective-permute-start.21) | collective-permute-done | bytes 65568 | tf_op jit(solution)/shard_map/ppermute | solution.py:357
  (75 shorter events, 11.3 us)
Async XLA Ops:
  0.6 23.9 %copy-start.5 = (f32[2048]{0:T(1024)S(1)}, f32[2048]{0:T(1024)}, u32[]{:S(2)}) copy-start(f32[2048]{0:T(1024)} %param.17) | copy-start | bytes 24580
  2.7 17.5 %collective-permute-start.1 = (s32[3,12]{1,0:T(4,128)}, s32[3,12]{1,0:T(4,128)S(1)}, u32[]{:S(2)}, u32[]{:S(2)}) collective-permute-start(s32[3,12]{1,0:T(4,128)} %get-tuple-element.38), channel_id=1, source_target_pairs={{1,4},{3,6},{5,8},{7,10},{9,12},{11,14},{13,16},{15,18},{17,20},{1... | collective-permute-start | bytes 440 | tf_op jit(solution)/shard_map/ppermute | solution.py:416
  3.4 7.5 %collective-permute-start = (s32[3,12]{1,0:T(4,128)}, s32[3,12]{1,0:T(4,128)S(1)}, u32[]{:S(2)}, u32[]{:S(2)}) collective-permute-start(s32[3,12]{1,0:T(4,128)} %get-tuple-element.38), channel_id=1, source_target_pairs={{0,1},{1,0},{2,3},{3,2},{4,5},{5,4},{6,7},{7,6},{8,9},{9,8},{10,11... | collective-permute-start | bytes 440 | tf_op jit(solution)/shard_map/ppermute | solution.py:357
  10.9 21.1 %collective-permute-start.6 = (bf16[768,512]{1,0:T(8,128)(2,1)}, bf16[768,512]{1,0:T(8,128)(2,1)}, u32[]{:S(2)}, u32[]{:S(2)}) collective-permute-start(bf16[768,512]{1,0:T(8,128)(2,1)} %get-tuple-element.40.r_2_), channel_id=1, source_target_pairs={{0,1},{1,0},{2,3},{3,2},{4,5},{5,4},{6,7},{7,6},{8,9},{9,8},{10,11... | collective-permute-start | bytes 2359304 | tf_op jit(solution)/shard_map/ppermute | solution.py:357
  12.9 32.0 %collective-permute-start.5 = (bf16[768,512]{1,0:T(8,128)(2,1)}, bf16[768,512]{1,0:T(8,128)(2,1)}, u32[]{:S(2)}, u32[]{:S(2)}) collective-permute-start(bf16[768,512]{1,0:T(8,128)(2,1)} %get-tuple-element.40.r_2_), channel_id=1, source_target_pairs={{2,0},{3,1},{4,2},{5,3},{6,4},{7,5},{8,6},{9,7},{10,8},{11,9},{12,... | collective-permute-start | bytes 2359304 | tf_op jit(solution)/shard_map/ppermute | solution.py:353
  14.2 30.7 %collective-permute-start.4 = (bf16[768,512]{1,0:T(8,128)(2,1)}, bf16[768,512]{1,0:T(8,128)(2,1)}, u32[]{:S(2)}, u32[]{:S(2)}) collective-permute-start(bf16[768,512]{1,0:T(8,128)(2,1)} %get-tuple-element.40.r_2_), channel_id=1, source_target_pairs={{0,2},{1,3},{2,4},{3,5},{4,6},{5,7},{6,8},{7,9},{8,10},{9,11},{10,... | collective-permute-start | bytes 2359304 | tf_op jit(solution)/shard_map/ppermute | solution.py:353
  19.4 12.6 %copy-start.3 = (bf16[768,768]{1,0:T(8,128)(2,1)}, bf16[768,768]{1,0:T(8,128)(2,1)S(1)}, u32[]{:S(2)}) copy-start(bf16[768,768]{1,0:T(8,128)(2,1)S(1)} %pad_maximum_fusion.refs_9_) | copy-start | bytes 3538948
  20.2 16.1 %collective-permute-start.3 = (s32[6,12]{1,0:T(8,128)S(1)}, s32[6,12]{1,0:T(8,128)S(1)}, u32[]{:S(2)}, u32[]{:S(2)}) collective-permute-start(s32[6,12]{1,0:T(8,128)S(1)} %add_select_fusion.1), channel_id=1, source_target_pairs={{2,0},{3,1},{4,2},{5,3},{6,4},{7,5},{8,6},{9,7},{10,8},{11,9},{12,... | collective-permute-start | bytes 872 | tf_op jit(solution)/shard_map/ppermute | solution.py:353
  21.5 14.8 %collective-permute-start.2 = (s32[6,12]{1,0:T(8,128)S(1)}, s32[6,12]{1,0:T(8,128)S(1)}, u32[]{:S(2)}, u32[]{:S(2)}) collective-permute-start(s32[6,12]{1,0:T(8,128)S(1)} %add_select_fusion.1), channel_id=1, source_target_pairs={{0,2},{1,3},{2,4},{3,5},{4,6},{5,7},{6,8},{7,9},{8,10},{9,11},{10,... | collective-permute-start | bytes 872 | tf_op jit(solution)/shard_map/ppermute | solution.py:353
  32.0 12.9 %collective-permute-start.7 = (bf16[768,512]{1,0:T(8,128)(2,1)}, bf16[768,512]{1,0:T(8,128)(2,1)}, u32[]{:S(2)}, u32[]{:S(2)}) collective-permute-start(bf16[768,512]{1,0:T(8,128)(2,1)} %collective-permute-done.6.r_5_), channel_id=1, source_target_pairs={{0,2},{2,4},{4,6},{6,8},{8,10},{10,12},{12,14},{14,16},{16,18},{18... | collective-permute-start | bytes 2359304 | tf_op jit(solution)/shard_map/ppermute | solution.py:423
  44.9 10.5 %copy-start = (f32[2048,768]{1,0:T(8,128)S(1)}, f32[2048,768]{1,0:T(8,128)}, u32[]{:S(2)}) copy-start(f32[2048,768]{1,0:T(8,128)} %get-tuple-element.43.refs_0_.refs_1_.refs_2_.refs_3_) | copy-start | bytes 18874372
  44.9 10.5 %copy-start.1 = (bf16[2048,512]{1,0:T(8,128)(2,1)S(1)}, bf16[2048,512]{1,0:T(8,128)(2,1)}, u32[]{:S(2)}) copy-start(bf16[2048,512]{1,0:T(8,128)(2,1)} %refs_7_.3) | copy-start | bytes 6291460
  44.9 10.5 %copy-start.4 = (bf16[768,768]{1,0:T(8,128)(2,1)S(1)}, bf16[768,768]{1,0:T(8,128)(2,1)}, u32[]{:S(2)}) copy-start(bf16[768,768]{1,0:T(8,128)(2,1)} %copy-done.3) | copy-start | bytes 3538948
  59.5 3.9 %collective-permute-start.8 = (bf16[2,2,2,2,64,896]{5,4,3,2,0,1:T(8,128)(2,1)S(1)}, bf16[2,2,2,2,64,896]{5,4,3,2,0,1:T(8,128)(2,1)S(1)}, u32[]{:S(2)}, u32[]{:S(2)}) collective-permute-start(bf16[2,2,2,2,64,896]{5,4,3,2,0,1:T(8,128)(2,1)S(1)} %copy.25), channel_id=1, source_target_pairs={{0,2},{1,3},{2,0},{3,1},{4,6},{5,7},{6,4},{7,5},{8,10},{9,11},{10,... | collective-permute-start | bytes 5505032 | tf_op jit(solution)/shard_map/ppermute | solution.py:357
  66.3 9.0 %collective-permute-start.9 = (bf16[2,2,2,2,64,512]{5,4,3,0,1,2:T(8,128)(2,1)S(1)}, bf16[2,2,2,2,64,512]{5,4,3,0,1,2:T(8,128)(2,1)S(1)}, u32[]{:S(2)}, u32[]{:S(2)}) collective-permute-start(bf16[2,2,2,2,64,512]{5,4,3,0,1,2:T(8,128)(2,1)S(1)} %copy.28), channel_id=1, source_target_pairs={{0,2},{1,3},{2,0},{3,1},{4,6},{5,7},{6,4},{7,5},{8,10},{9,11},{10,... | collective-permute-start | bytes 3145736 | tf_op jit(solution)/shard_map/ppermute | solution.py:357
  66.8 16.7 %collective-permute-start.10 = (bf16[2,2,2,32,896]{4,3,2,1,0:T(8,128)(2,1)S(1)}, bf16[2,2,2,32,896]{4,3,2,1,0:T(8,128)(2,1)S(1)}, u32[]{:S(2)}, u32[]{:S(2)}) collective-permute-start(bf16[2,2,2,32,896]{4,3,2,1,0:T(8,128)(2,1)S(1)} %get-tuple-element.76), channel_id=1, source_target_pairs={{0,1},{1,0},{2,3},{3,2},{4,5},{5,4},{6,7},{7,6},{8,9},{9,8},{10,11... | collective-permute-start | bytes 1376264 | tf_op jit(solution)/shard_map/ppermute | solution.py:357
  69.0 15.6 %collective-permute-start.11 = (bf16[2,2,2,32,896]{4,3,2,1,0:T(8,128)(2,1)S(1)}, bf16[2,2,2,32,896]{4,3,2,1,0:T(8,128)(2,1)S(1)}, u32[]{:S(2)}, u32[]{:S(2)}) collective-permute-start(bf16[2,2,2,32,896]{4,3,2,1,0:T(8,128)(2,1)S(1)} %get-tuple-element.78), channel_id=1, source_target_pairs={{0,4},{1,5},{2,6},{3,7},{4,0},{5,1},{6,2},{7,3},{8,12},{9,13},{10,... | collective-permute-start | bytes 1376264 | tf_op jit(solution)/shard_map/ppermute | solution.py:357
  75.3 2.1 %copy-start.2 = (bf16[2048,768]{1,0:T(8,128)(2,1)S(1)}, bf16[2048,768]{1,0:T(8,128)(2,1)}, u32[]{:S(2)}) copy-start(bf16[2048,768]{1,0:T(8,128)(2,1)} %refs_3_.1) | copy-start | bytes 9437188
  75.7 13.8 %collective-permute-start.12 = (bf16[2,2,2,64,512]{4,3,2,0,1:T(8,128)(2,1)S(1)}, bf16[2,2,2,64,512]{4,3,2,0,1:T(8,128)(2,1)S(1)}, u32[]{:S(2)}, u32[]{:S(2)}) collective-permute-start(bf16[2,2,2,64,512]{4,3,2,0,1:T(8,128)(2,1)S(1)} %get-tuple-element.80), channel_id=1, source_target_pairs={{0,8},{1,9},{2,10},{3,11},{4,12},{5,13},{6,14},{7,15},{8,0},{9,1},... | collective-permute-start | bytes 1572872 | tf_op jit(solution)/shard_map/ppermute | solution.py:357
  83.7 8.5 %collective-permute-start.13 = (bf16[2,2,32,896]{3,2,1,0:T(8,128)(2,1)S(1)}, bf16[2,2,32,896]{3,2,1,0:T(8,128)(2,1)S(1)}, u32[]{:S(2)}, u32[]{:S(2)}) collective-permute-start(bf16[2,2,32,896]{3,2,1,0:T(8,128)(2,1)S(1)} %get-tuple-element.88), channel_id=1, source_target_pairs={{0,4},{1,5},{2,6},{3,7},{4,0},{5,1},{6,2},{7,3},{8,12},{9,13},{10,... | collective-permute-start | bytes 688136 | tf_op jit(solution)/shard_map/ppermute | solution.py:357
  84.8 7.4 %collective-permute-start.14 = (bf16[2,2,32,896]{3,2,1,0:T(8,128)(2,1)S(1)}, bf16[2,2,32,896]{3,2,1,0:T(8,128)(2,1)S(1)}, u32[]{:S(2)}, u32[]{:S(2)}) collective-permute-start(bf16[2,2,32,896]{3,2,1,0:T(8,128)(2,1)S(1)} %get-tuple-element.90), channel_id=1, source_target_pairs={{0,1},{1,0},{2,3},{3,2},{4,5},{5,4},{6,7},{7,6},{8,9},{9,8},{10,11... | collective-permute-start | bytes 688136 | tf_op jit(solution)/shard_map/ppermute | solution.py:357
  89.7 5.0 %collective-permute-start.16 = (bf16[2,2,32,512]{3,2,1,0:T(8,128)(2,1)S(1)}, bf16[2,2,32,512]{3,2,1,0:T(8,128)(2,1)S(1)}, u32[]{:S(2)}, u32[]{:S(2)}) collective-permute-start(bf16[2,2,32,512]{3,2,1,0:T(8,128)(2,1)S(1)} %get-tuple-element.82), channel_id=1, source_target_pairs={{0,4},{1,5},{2,6},{3,7},{4,0},{5,1},{6,2},{7,3},{8,12},{9,13},{10,... | collective-permute-start | bytes 393224 | tf_op jit(solution)/shard_map/ppermute | solution.py:357
  90.0 6.6 %collective-permute-start.15 = (bf16[2,2,32,512]{3,2,1,0:T(8,128)(2,1)S(1)}, bf16[2,2,32,512]{3,2,1,0:T(8,128)(2,1)S(1)}, u32[]{:S(2)}, u32[]{:S(2)}) collective-permute-start(bf16[2,2,32,512]{3,2,1,0:T(8,128)(2,1)S(1)} %get-tuple-element.84), channel_id=1, source_target_pairs={{0,1},{1,0},{2,3},{3,2},{4,5},{5,4},{6,7},{7,6},{8,9},{9,8},{10,11... | collective-permute-start | bytes 393224 | tf_op jit(solution)/shard_map/ppermute | solution.py:357
  92.4 6.1 %collective-permute-start.17 = (bf16[2,64,896]{2,1,0:T(8,128)(2,1)S(1)}, bf16[2,64,896]{2,1,0:T(8,128)(2,1)S(1)}, u32[]{:S(2)}, u32[]{:S(2)}) collective-permute-start(bf16[2,64,896]{2,1,0:T(8,128)(2,1)S(1)} %get-tuple-element.86), channel_id=1, source_target_pairs={{0,8},{1,9},{2,10},{3,11},{4,12},{5,13},{6,14},{7,15},{8,0},{9,1},... | collective-permute-start | bytes 688136 | tf_op jit(solution)/shard_map/ppermute | solution.py:357
  94.8 4.3 %collective-permute-start.20 = (bf16[2,32,512]{2,1,0:T(8,128)(2,1)S(1)}, bf16[2,32,512]{2,1,0:T(8,128)(2,1)S(1)}, u32[]{:S(2)}, u32[]{:S(2)}) collective-permute-start(bf16[2,32,512]{2,1,0:T(8,128)(2,1)S(1)} %get-tuple-element.96), channel_id=1, source_target_pairs={{0,1},{1,0},{2,3},{3,2},{4,5},{5,4},{6,7},{7,6},{8,9},{9,8},{10,11... | collective-permute-start | bytes 196616 | tf_op jit(solution)/shard_map/ppermute | solution.py:357
  96.7 4.3 %collective-permute-start.19 = (bf16[2,32,512]{2,1,0:T(8,128)(2,1)S(1)}, bf16[2,32,512]{2,1,0:T(8,128)(2,1)S(1)}, u32[]{:S(2)}, u32[]{:S(2)}) collective-permute-start(bf16[2,32,512]{2,1,0:T(8,128)(2,1)S(1)} %get-tuple-element.94), channel_id=1, source_target_pairs={{0,4},{1,5},{2,6},{3,7},{4,0},{5,1},{6,2},{7,3},{8,12},{9,13},{10,... | collective-permute-start | bytes 196616 | tf_op jit(solution)/shard_map/ppermute | solution.py:357
  101.1 5.8 %collective-permute-start.21 = (bf16[64,512]{1,0:T(8,128)(2,1)S(1)}, bf16[64,512]{1,0:T(8,128)(2,1)S(1)}, u32[]{:S(2)}, u32[]{:S(2)}) collective-permute-start(bf16[64,512]{1,0:T(8,128)(2,1)S(1)} %fusion.16), channel_id=1, source_target_pairs={{0,16},{1,17},{2,18},{3,19},{4,20},{5,21},{6,22},{7,23},{8,24},{9,... | collective-permute-start | bytes 196616 | tf_op jit(solution)/shard_map/ppermute | solution.py:357
  102.4 5.7 %collective-permute-start.18 = (bf16[64,896]{1,0:T(8,128)(2,1)S(1)}, bf16[64,896]{1,0:T(8,128)(2,1)S(1)}, u32[]{:S(2)}, u32[]{:S(2)}) collective-permute-start(bf16[64,896]{1,0:T(8,128)(2,1)S(1)} %get-tuple-element.92), channel_id=1, source_target_pairs={{0,16},{1,17},{2,18},{3,19},{4,20},{5,21},{6,22},{7,23},{8,24},{9,... | collective-permute-start | bytes 344072 | tf_op jit(solution)/shard_map/ppermute | solution.py:357

commit v11 on v10

--- a/solution.py
+++ b/solution.py
@@ -114,16 +114,22 @@
 
 
 def hops_kernel(
-    place_ref, base_ref, own_hbm, low_hbm, high_hbm, mate_hbm, far_hbm, pat_hbm, pat_t_hbm, nimg_hbm, ncap_hbm,
+    place_ref, base_ref, own_hbm, low_hbm, high_hbm, mate_img, mate_cap, far_img, far_cap, pat_hbm, pat_t_hbm, nimg_hbm, ncap_hbm,
     out_ref, bands, pat_ref, pat_t_ref, nimg_ref, ncap_ref, img0, cap0, img1, cap1, acc, acc2, keep_img, keep_cap,
     sems, *, tiles, slots, width,
 ):
     mid = 5 * tiles
     near = 3 * tiles
     keep = 1.0 - ALPHA
-    sources = (own_hbm, nimg_hbm, ncap_hbm, pat_t_hbm, low_hbm, high_hbm, mate_hbm, far_hbm, pat_hbm)
-    targets = (bands.at[0], nimg_ref, ncap_ref, pat_t_ref) + tuple(bands.at[k] for k in range(1, 5)) + (pat_ref,)
-    copies = [pltpu.make_async_copy(s, t, sems.at[k]) for k, (s, t) in enumerate(zip(sources, targets))]
+    rows = tiles * TILE
+    upper, lower = pl.ds(0, rows), pl.ds(rows, rows)
+    pairs = (
+        (own_hbm, bands.at[0]), (nimg_hbm, nimg_ref), (ncap_hbm, ncap_ref), (pat_t_hbm, pat_t_ref),
+        (low_hbm, bands.at[1]), (high_hbm, bands.at[2]),
+        (mate_img, bands.at[3, upper]), (mate_cap, bands.at[3, lower]),
+        (far_img, bands.at[4, upper]), (far_cap, bands.at[4, lower]), (pat_hbm, pat_ref),
+    )
+    copies = [pltpu.make_async_copy(s, t, sems.at[k]) for k, (s, t) in enumerate(pairs)]
     for copy in copies:
         copy.start()
 
@@ -158,12 +164,12 @@
     for copy in copies[:4]:
         copy.wait()
     for k, base in enumerate((2 * tiles, 0, 4 * tiles, base_ref[0], base_ref[1])):
-        if k:
-            copies[3 + k].wait()
+        for copy in ((), copies[4:5], copies[5:6], copies[6:8], copies[8:10])[k]:
+            copy.wait()
         scale(k, base)
         for t in range(tiles):
             push(base + t, img0[base + t], acc, tiles, near)
-    copies[8].wait()
+    copies[10].wait()
 
     def pull1(q, c):
         n = wide(nimg_ref, q)
@@ -207,7 +213,7 @@
     return pl.pallas_call(
         lambda *r: hops_kernel(*r, tiles=tiles, slots=slots, width=width),
         out_shape=jax.ShapeDtypeStruct(own.shape, BF16),
-        in_specs=[smem] * 2 + [hbm] * 9,
+        in_specs=[smem] * 2 + [hbm] * 11,
         out_specs=vmem,
         scratch_shapes=[
             pltpu.VMEM((5,) + own.shape, BF16),
@@ -220,12 +226,12 @@
             pltpu.VMEM((tiles + 1, TILE, width), F32),
             pltpu.VMEM((near, TILE, width), F32),
             pltpu.VMEM((near, TILE, width), F32),
-            pltpu.SemaphoreType.DMA((9,)),
+            pltpu.SemaphoreType.DMA((11,)),
         ],
         compiler_params=pltpu.CompilerParams(vmem_limit_bytes=34 << 20),
         cost_estimate=SHORT,
         name="hops",
-    )(places, bases, *[pltpu.with_memory_space_constraint(v, pltpu.HBM) for v in (own, low, high, mate, far, *tables)])
+    )(places, bases, *[pltpu.with_memory_space_constraint(v, pltpu.HBM) for v in (own, low, high, *mate, *far, *tables)])
 
 
 BLOCK = 64
@@ -411,32 +417,17 @@
     me = lax.axis_index(AXES)
 
     even = (me & 1) == 0
+    mate = [flipped(cot_img, count, 1)]
     block, meta = stack(cot_img, cot_cap, tile_seed, tile_cols, tile_count)
+    low = moved(block, count, 2)
+    high = moved(block, count, -2)
     other = flipped(meta, count, 1)
+    cot_cap, meta = lax.optimization_barrier((cot_cap, meta, other))[:2]
+    mate.append(flipped(cot_cap, count, 1))
     third = lax.ppermute(
         meta, AXES, [(i, i + 3) for i in range(1, count - 3, 2)] + [(i, i - 3) for i in range(4, count, 2)]
     )
-    block = after(block, other)
-    mate = flipped(block, count, 1)
-    low = moved(block, count, 2)
-    high = moved(block, count, -2)
-    far = lax.ppermute(mate, AXES, nearest_pair(count, 2))
-    pair = jnp.where(even, jnp.concatenate([meta, other]), jnp.concatenate([other, meta]))
-    feats = jnp.concatenate([after(feats_img, block), feats_cap], axis=0)
-    pair, feats, third = lax.optimization_barrier((pair, feats, third))
-    pair_low = moved(pair, count, 2)
-    pair_high = moved(pair, count, -2)
-    wide = jnp.where(
-        even,
-        jnp.concatenate([third, pair_low, pair, pair_high]),
-        jnp.concatenate([pair_low, pair, pair_high, third]),
-    )
-    frame = jnp.arange(7 * tiles, dtype=jnp.int32)[:, None]
-    counts = wide[:, 2 * slots]
-    seeds = wide[:, :slots].reshape(-1)
-    places = jnp.where(counts[:, None] > 0, wide[:, slots : 2 * slots] - (me - 3) * tiles, frame)
-    pats = make_tiles(seeds, (places + tiles).reshape(-1), counts, tiles, slots)
-
+    far = [lax.ppermute(v, AXES, nearest_pair(count, 2)) for v in mate]
     m = count.bit_length() - 1
     a = n_cap.bit_length() - 1
     cap_bits = list(range(a))
@@ -456,10 +447,26 @@
     else:
         order = (order[:, None] * (rows // BLOCK) + jnp.arange(rows // BLOCK, dtype=jnp.int32)).reshape(-1)
 
+    feats = jnp.concatenate([after(feats_img, other), feats_cap], axis=0)
     across = (((1,), (1,)), ((), ()))
     preact = lax.dot_general(w_in, feats, across, preferred_element_type=F32) + b_in[:, None]
     gelu_value, gelu_slope = gelu_parts(preact)
     hidden_act, gelu_slope = lax.optimization_barrier((gelu_value.astype(BF16), gelu_slope))
+
+    pair = jnp.where(even, jnp.concatenate([meta, other]), jnp.concatenate([other, meta]))
+    pair, hidden_act, third, low, high = lax.optimization_barrier((pair, hidden_act, third, low, high))
+    pair_low = moved(pair, count, 2)
+    pair_high = moved(pair, count, -2)
+    wide = jnp.where(
+        even,
+        jnp.concatenate([third, pair_low, pair, pair_high]),
+        jnp.concatenate([pair_low, pair, pair_high, third]),
+    )
+    frame = jnp.arange(7 * tiles, dtype=jnp.int32)[:, None]
+    counts = wide[:, 2 * slots]
+    seeds = wide[:, :slots].reshape(-1)
+    places = jnp.where(counts[:, None] > 0, wide[:, slots : 2 * slots] - (me - 3) * tiles, frame)
+    pats = make_tiles(seeds, (places + tiles).reshape(-1), counts, tiles, slots)
 
     bases = jnp.where(even, jnp.array([3, 1]), jnp.array([1, 3])).astype(jnp.int32) * tiles
     mid_places = (places - tiles)[tiles : 6 * tiles].reshape(-1)

time: 110 us -> 120 us (1.091)
  waiting for transfers between devices: 13.1 us -> 22.3 us
  other arithmetic: 6.62 us -> 3.87 us
  local copies, waits for them, and re-layouts: 1.22 us -> 3.45 us
    ppermute x16 -> x17, waiting for transfers between devices: 13.1 us -> 22.2 us  [flipped(): return lax.ppermute(array, AXES, [(i, i ^ mask) for i in range(count)])]
    ppermute x1 -> x2, starting transfers between devices: 4.29 us -> 9.2 us  [per_device(): far = [lax.ppermute(v, AXES, nearest_pair(count, 2)) for v in mate]]
    ppermute x4, starting transfers between devices: 9.53 us -> 7.1 us  [moved(): lax.ppermute(array, AXES, [(i, i + by) for i in range(count) if 0 <= i +...]
    ppermute x16 -> x17, starting transfers between devices: 27.2 us -> 25.8 us  [flipped(): return lax.ppermute(array, AXES, [(i, i ^ mask) for i in range(count)])]
    concatenate x1 -> x0, other arithmetic: 1.32 us -> none  [per_device(): feats = jnp.concatenate([after(feats_img, block), feats_cap], axis=0)]
  transfers between devices with their start and end apart: 22 -> 24, of which waited for: 9 -> 9; matrix products, arithmetic and copies ran while one was open for 12% -> 11% of each run, Pallas kernels for 18% -> 17%
where the time goes in v11:
time: 120 us
  starting transfers between devices  42.8 us (36%)
  Pallas kernels  38.3 us (32%)
  waiting for transfers between devices  22.3 us (19%)
  matrix products  7.84 us (7%)
  other arithmetic  3.87 us (3%)
  local copies, waits for them, and re-layouts  3.45 us (3%)
    ppermute x17, starting transfers between devices, flipped(): return lax.ppermute(array, AXES, [(i, i ^ mask) for i in range(count)])  25.8 us
    ppermute x17, waiting for transfers between devices, flipped(): return lax.ppermute(array, AXES, [(i, i ^ mask) for i in range(count)])  22.2 us
    pallas_call x5, Pallas kernels, over_hidden(): pl.pallas_call(kernel, out_shape=out_shape, grid_spec=pltpu.PrefetchScala...  17.9 us
    pallas_call x1, Pallas kernels, propagate(): pl.pallas_call(lambda *r: hops_kernel(*r, tiles=tiles, slots=slots, width...  10.5 us
    ppermute x2, starting transfers between devices, per_device(): far = [lax.ppermute(v, AXES, nearest_pair(count, 2)) for v in mate]  9.2 us
    dot_general x1, matrix products, per_device(): lax.dot_general(w_in, feats, across, preferred_element_type=F32)  7.84 us
    pallas_call x1, Pallas kernels, make_tiles(): pl.pallas_call(lambda *r: tiles_kernel(*r, tiles=tiles, slots=slots), out...  7.8 us
    ppermute x4, starting transfers between devices, moved(): lax.ppermute(array, AXES, [(i, i + by) for i in range(count) if 0 <= i +...  7.1 us
  transfers between devices with their start and end apart: 24, of which 9 were waited for; matrix products, arithmetic and copies ran while one was open for 11% of the time, Pallas kernels for 17%

profile of v11, /device:TPU:0, one launch (start us, length us, event | category | flops | bytes accessed | tf_op | source)
XLA Modules:
  0.0 119.6 jit_solution(927385457845577894)
XLA Ops:
  0.6 2.1 %stack.1 = (bf16[768,512]{1,0:T(8,128)(2,1)}, s32[3,12]{1,0:T(4,128)}) custom-call(s32[3]{0:T(128)} %count_ref.1, bf16[384,512]{1,0:T(8,128)(2,1)} %top_ref.1, bf16[384,512]{1,0:T(8,128)(2,1)} %bottom_ref.1, s32[3,4]{1,0:T(4,128)} %seed_ref.1, s32[3,4]{1,0:T(4,128)} %cols_ref.1), custom_call_target="tpu_custom_call" | custom-call | flops 1 | bytes 1 | tf_op jit(solution)/shard_map/stack/pallas_call | solution.py:344
  2.7 3.2 %collective-permute-start.2 = (bf16[768,512]{1,0:T(8,128)(2,1)}, bf16[768,512]{1,0:T(8,128)(2,1)}, u32[]{:S(2)}, u32[]{:S(2)}) collective-permute-start(bf16[768,512]{1,0:T(8,128)(2,1)} %get-tuple-element.46.r_2_), channel_id=1, source_target_pairs={{0,2},{1,3},{2,4},{3,5},{4,6},{5,7},{6,8},{7,9},{8,10},{9,11},{10,... | collective-permute-start | bytes 2359304 | tf_op jit(solution)/shard_map/ppermute | solution.py:359
  5.9 1.3 %collective-permute-start.3 = (bf16[768,512]{1,0:T(8,128)(2,1)}, bf16[768,512]{1,0:T(8,128)(2,1)}, u32[]{:S(2)}, u32[]{:S(2)}) collective-permute-start(bf16[768,512]{1,0:T(8,128)(2,1)} %get-tuple-element.46.r_2_), channel_id=1, source_target_pairs={{2,0},{3,1},{4,2},{5,3},{6,4},{7,5},{8,6},{9,7},{10,8},{11,9},{12,... | collective-permute-start | bytes 2359304 | tf_op jit(solution)/shard_map/ppermute | solution.py:359
  7.2 2.4 %collective-permute-start.6 = (bf16[384,512]{1,0:T(8,128)(2,1)}, bf16[384,512]{1,0:T(8,128)(2,1)}, u32[]{:S(2)}, u32[]{:S(2)}) collective-permute-start(bf16[384,512]{1,0:T(8,128)(2,1)} %top_ref.1), channel_id=1, source_target_pairs={{0,1},{1,0},{2,3},{3,2},{4,5},{5,4},{6,7},{7,6},{8,9},{9,8},{10,11... | collective-permute-start | bytes 1179656 | tf_op jit(solution)/shard_map/ppermute | solution.py:363
  9.8 9.1 %collective-permute-done = s32[3,12]{1,0:T(4,128)S(1)} collective-permute-done((s32[3,12]{1,0:T(4,128)}, s32[3,12]{1,0:T(4,128)S(1)}, u32[]{:S(2)}, u32[]{:S(2)}) %collective-permute-start) | collective-permute-done | bytes 176 | tf_op jit(solution)/shard_map/ppermute | solution.py:363
  20.7 6.4 %collective-permute-start.7 = (bf16[384,512]{1,0:T(8,128)(2,1)}, bf16[384,512]{1,0:T(8,128)(2,1)}, u32[]{:S(2)}, u32[]{:S(2)}) collective-permute-start(bf16[384,512]{1,0:T(8,128)(2,1)} %bottom_ref.1), channel_id=1, source_target_pairs={{0,1},{1,0},{2,3},{3,2},{4,5},{5,4},{6,7},{7,6},{8,9},{9,8},{10,11... | collective-permute-start | bytes 1179656 | tf_op jit(solution)/shard_map/ppermute | solution.py:363
  28.3 7.8 %fusion.3 = (f32[2048,768]{1,0:T(8,128)}, bf16[2048,768]{1,0:T(8,128)(2,1)S(1)}) fusion(f32[2048]{0:T(1024)S(1)} %copy-done.8, bf16[768,768]{1,0:T(8,128)(2,1)S(1)} %constant_dynamic-update-slice_fusion.refs_9_, bf16[2048,768]{1,0:T(8,128)(2,1)} %refs_3_.1), kind=kOutput, calls=%fused_computation.4 | convolution fusion | flops 2433220608 | bytes 13770752 | tf_op jit(solution)/shard_map/dot_general | solution.py:452
  36.2 1.3 %collective-permute-start.4 = (s32[6,12]{1,0:T(8,128)S(1)}, s32[6,12]{1,0:T(8,128)S(1)}, u32[]{:S(2)}, u32[]{:S(2)}) collective-permute-start(s32[6,12]{1,0:T(8,128)S(1)} %add_select_fusion.1), channel_id=1, source_target_pairs={{0,2},{1,3},{2,4},{3,5},{4,6},{5,7},{6,8},{7,9},{8,10},{9,11},{10,... | collective-permute-start | bytes 872 | tf_op jit(solution)/shard_map/ppermute | solution.py:359
  37.5 1.3 %collective-permute-start.5 = (s32[6,12]{1,0:T(8,128)S(1)}, s32[6,12]{1,0:T(8,128)S(1)}, u32[]{:S(2)}, u32[]{:S(2)}) collective-permute-start(s32[6,12]{1,0:T(8,128)S(1)} %add_select_fusion.1), channel_id=1, source_target_pairs={{2,0},{3,1},{4,2},{5,3},{6,4},{7,5},{8,6},{9,7},{10,8},{11,9},{12,... | collective-permute-start | bytes 872 | tf_op jit(solution)/shard_map/ppermute | solution.py:359
  38.8 5.5 %collective-permute-start.8 = (bf16[384,512]{1,0:T(8,128)(2,1)}, bf16[384,512]{1,0:T(8,128)(2,1)}, u32[]{:S(2)}, u32[]{:S(2)}) collective-permute-start(bf16[384,512]{1,0:T(8,128)(2,1)} %collective-permute-done.6.r_5_), channel_id=1, source_target_pairs={{0,2},{2,4},{4,6},{6,8},{8,10},{10,12},{12,14},{14,16},{16,18},{18... | collective-permute-start | bytes 1179656 | tf_op jit(solution)/shard_map/ppermute | solution.py:430
  44.3 3.7 %collective-permute-start.9 = (bf16[384,512]{1,0:T(8,128)(2,1)}, bf16[384,512]{1,0:T(8,128)(2,1)}, u32[]{:S(2)}, u32[]{:S(2)}) collective-permute-start(bf16[384,512]{1,0:T(8,128)(2,1)} %collective-permute-done.7.r_6_), channel_id=1, source_target_pairs={{0,2},{2,4},{4,6},{6,8},{8,10},{10,12},{12,14},{14,16},{16,18},{18... | collective-permute-start | bytes 1179656 | tf_op jit(solution)/shard_map/ppermute | solution.py:430
  48.7 7.8 %tiles.1 = (bf16[15,128,512]{2,1,0:T(8,128)(2,1)}, bf16[15,512,128]{2,1,0:T(8,128)(2,1)}, f32[15,128,128]{2,1,0:T(8,128)}, f32[15,128,128]{2,1,0:T(8,128)}) custom-call(s32[84]{0:T(128)S(1)} %reshape.40.r_0_, s32[84]{0:T(128)S(1)} %reshape.41.r_1_, s32[21]{0:T(128)S(1)} %slice_reduce_fusion.r_2_), custom_call_target="tpu_custom_call" | custom-call | flops 1 | bytes 1 | tf_op jit(solution)/shard_map/tiles/pallas_call | solution.py:103
  56.6 10.5 %hops.1.refs_8_.refs_4_ = bf16[768,512]{1,0:T(8,128)(2,1)S(1)} custom-call(s32[60]{0:T(128)S(1)} %reshape.39.r_0_, s32[2]{0:T(128)S(1)} %fusion.18.r_1_, bf16[768,512]{1,0:T(8,128)(2,1)} %get-tuple-element.46.r_2_, bf16[768,512]{1,0:T(8,128)(2,1)} %collective-permute-done.2.r_3_, bf16[768,512]{1,0:T(8,128)(2,1)} %collective-permute-done.3.r_4_, ...), custom_call_target="tpu_custom_call" | custom-call | flops 1 | bytes 1 | tf_op jit(solution)/shard_map/hops/pallas_call | solution.py:213
  67.1 3.8 %part_in.2 = (bf16[1024,896]{1,0:T(8,128)(2,1)S(1)}, bf16[1024,768]{1,0:T(8,128)(2,1)S(1)}) custom-call(s32[16]{0:T(128)S(1)} %get-tuple-element.104.order_ref, f32[2048,768]{1,0:T(8,128)S(1)} %copy-done, f32[2048,768]{1,0:T(8,128)S(1)} %copy-done, f32[2048,768]{1,0:T(8,128)S(1)} %copy-done, f32[2048,768]{1,0:T(8,128)S(1)} %copy-done, ...), custom_call_target="tpu_custom_call" | custom-call | flops 1 | bytes 1 | tf_op jit(solution)/shard_map/part_in/pallas_call | solution.py:297
  71.2 3.8 %part_in.3 = (bf16[1024,896]{1,0:T(8,128)(2,1)S(1)}, bf16[1024,768]{1,0:T(8,128)(2,1)S(1)}) custom-call(s32[16]{0:T(128)S(1)} %get-tuple-element.105.order_ref, f32[2048,768]{1,0:T(8,128)S(1)} %copy-done, f32[2048,768]{1,0:T(8,128)S(1)} %copy-done, f32[2048,768]{1,0:T(8,128)S(1)} %copy-done, f32[2048,768]{1,0:T(8,128)S(1)} %copy-done, ...), custom_call_target="tpu_custom_call" | custom-call | flops 1 | bytes 1 | tf_op jit(solution)/shard_map/part_in/pallas_call | solution.py:297
  75.8 2.0 %part_out.2 = bf16[1024,512]{1,0:T(8,128)(2,1)S(1)} custom-call(s32[16]{0:T(128)S(1)} %get-tuple-element.104.order_ref, bf16[2048,768]{1,0:T(8,128)(2,1)S(1)} %get-tuple-element.59.refs_0_.refs_1_.refs_2_.refs_3_, bf16[2048,768]{1,0:T(8,128)(2,1)S(1)} %get-tuple-element.59.refs_0_.refs_1_.refs_2_.refs_3_, ...), custom_call_target="tpu_custom_call" | custom-call | flops 1 | bytes 1 | tf_op jit(solution)/shard_map/part_out/pallas_call | solution.py:297
  78.5 1.9 %collective-permute-start.13 = (bf16[2,2,2,32,896]{4,3,2,1,0:T(8,128)(2,1)S(1)}, bf16[2,2,2,32,896]{4,3,2,1,0:T(8,128)(2,1)S(1)}, u32[]{:S(2)}, u32[]{:S(2)}) collective-permute-start(bf16[2,2,2,32,896]{4,3,2,1,0:T(8,128)(2,1)S(1)} %get-tuple-element.84), channel_id=1, source_target_pairs={{0,4},{1,5},{2,6},{3,7},{4,0},{5,1},{6,2},{7,3},{8,12},{9,13},{10,... | collective-permute-start | bytes 1376264 | tf_op jit(solution)/shard_map/ppermute | solution.py:363
  80.5 2.0 %part_out.3 = bf16[1024,512]{1,0:T(8,128)(2,1)S(1)} custom-call(s32[16]{0:T(128)S(1)} %get-tuple-element.105.order_ref, bf16[2048,768]{1,0:T(8,128)(2,1)S(1)} %get-tuple-element.59.refs_0_.refs_1_.refs_2_.refs_3_, bf16[2048,768]{1,0:T(8,128)(2,1)S(1)} %get-tuple-element.59.refs_0_.refs_1_.refs_2_.refs_3_, ...), custom_call_target="tpu_custom_call" | custom-call | flops 1 | bytes 1 | tf_op jit(solution)/shard_map/part_out/pallas_call | solution.py:297
  83.0 1.9 %collective-permute-start.14 = (bf16[2,2,2,64,512]{4,3,2,0,1:T(8,128)(2,1)S(1)}, bf16[2,2,2,64,512]{4,3,2,0,1:T(8,128)(2,1)S(1)}, u32[]{:S(2)}, u32[]{:S(2)}) collective-permute-start(bf16[2,2,2,64,512]{4,3,2,0,1:T(8,128)(2,1)S(1)} %get-tuple-element.86), channel_id=1, source_target_pairs={{0,8},{1,9},{2,10},{3,11},{4,12},{5,13},{6,14},{7,15},{8,0},{9,1},... | collective-permute-start | bytes 1572872 | tf_op jit(solution)/shard_map/ppermute | solution.py:363
  84.9 6.2 %feat_grad.1 = (bf16[384,768]{1,0:T(8,128)(2,1)}, bf16[384,768]{1,0:T(8,128)(2,1)}) custom-call(s32[32]{0:T(128)S(1)} %fusion.31.order_ref, bf16[2048,768]{1,0:T(8,128)(2,1)S(1)} %copy-done.2, bf16[2048,768]{1,0:T(8,128)(2,1)S(1)} %copy-done.2, bf16[2048,768]{1,0:T(8,128)(2,1)S(1)} %copy-done.2, bf16[2048,768]{1,0:T(8,128)(2,1)S(1)} %copy-done.2, ...), custom_call_target="tpu_custom_call" | custom-call | flops 1 | bytes 1 | tf_op jit(solution)/shard_map/feat_grad/pallas_call | solution.py:297
  91.3 1.7 %collective-permute-start.16 = (bf16[2,2,32,896]{3,2,1,0:T(8,128)(2,1)S(1)}, bf16[2,2,32,896]{3,2,1,0:T(8,128)(2,1)S(1)}, u32[]{:S(2)}, u32[]{:S(2)}) collective-permute-start(bf16[2,2,32,896]{3,2,1,0:T(8,128)(2,1)S(1)} %get-tuple-element.96), channel_id=1, source_target_pairs={{0,1},{1,0},{2,3},{3,2},{4,5},{5,4},{6,7},{7,6},{8,9},{9,8},{10,11... | collective-permute-start | bytes 688136 | tf_op jit(solution)/shard_map/ppermute | solution.py:363
  93.9 2.9 %collective-permute-done.14 = bf16[2,2,2,64,512]{4,3,2,0,1:T(8,128)(2,1)S(1)} collective-permute-done((bf16[2,2,2,64,512]{4,3,2,0,1:T(8,128)(2,1)S(1)}, bf16[2,2,2,64,512]{4,3,2,0,1:T(8,128)(2,1)S(1)}, u32[]{:S(2)}, u32[]{:S(2)}) %collective-permute-start.14) | collective-permute-done | bytes 524320 | tf_op jit(solution)/shard_map/ppermute | solution.py:363
  97.6 1.5 %collective-permute-start.17 = (bf16[2,2,32,512]{3,2,1,0:T(8,128)(2,1)S(1)}, bf16[2,2,32,512]{3,2,1,0:T(8,128)(2,1)S(1)}, u32[]{:S(2)}, u32[]{:S(2)}) collective-permute-start(bf16[2,2,32,512]{3,2,1,0:T(8,128)(2,1)S(1)} %get-tuple-element.90), channel_id=1, source_target_pairs={{0,1},{1,0},{2,3},{3,2},{4,5},{5,4},{6,7},{7,6},{8,9},{9,8},{10,11... | collective-permute-start | bytes 393224 | tf_op jit(solution)/shard_map/ppermute | solution.py:363
  99.2 1.6 %collective-permute-done.15 = bf16[2,2,32,896]{3,2,1,0:T(8,128)(2,1)S(1)} collective-permute-done((bf16[2,2,32,896]{3,2,1,0:T(8,128)(2,1)S(1)}, bf16[2,2,32,896]{3,2,1,0:T(8,128)(2,1)S(1)}, u32[]{:S(2)}, u32[]{:S(2)}) %collective-permute-start.15) | collective-permute-done | bytes 229408 | tf_op jit(solution)/shard_map/ppermute | solution.py:363
  100.9 1.9 %collective-permute-start.19 = (bf16[2,64,896]{2,1,0:T(8,128)(2,1)S(1)}, bf16[2,64,896]{2,1,0:T(8,128)(2,1)S(1)}, u32[]{:S(2)}, u32[]{:S(2)}) collective-permute-start(bf16[2,64,896]{2,1,0:T(8,128)(2,1)S(1)} %get-tuple-element.92), channel_id=1, source_target_pairs={{0,8},{1,9},{2,10},{3,11},{4,12},{5,13},{6,14},{7,15},{8,0},{9,1},... | collective-permute-start | bytes 688136 | tf_op jit(solution)/shard_map/ppermute | solution.py:363
  102.9 1.3 %collective-permute-start.21 = (bf16[2,32,512]{2,1,0:T(8,128)(2,1)S(1)}, bf16[2,32,512]{2,1,0:T(8,128)(2,1)S(1)}, u32[]{:S(2)}, u32[]{:S(2)}) collective-permute-start(bf16[2,32,512]{2,1,0:T(8,128)(2,1)S(1)} %get-tuple-element.100), channel_id=1, source_target_pairs={{0,4},{1,5},{2,6},{3,7},{4,0},{5,1},{6,2},{7,3},{8,12},{9,13},{10,... | collective-permute-start | bytes 196616 | tf_op jit(solution)/shard_map/ppermute | solution.py:363
  104.3 1.6 %collective-permute-start.22 = (bf16[2,32,512]{2,1,0:T(8,128)(2,1)S(1)}, bf16[2,32,512]{2,1,0:T(8,128)(2,1)S(1)}, u32[]{:S(2)}, u32[]{:S(2)}) collective-permute-start(bf16[2,32,512]{2,1,0:T(8,128)(2,1)S(1)} %get-tuple-element.102), channel_id=1, source_target_pairs={{0,1},{1,0},{2,3},{3,2},{4,5},{5,4},{6,7},{7,6},{8,9},{9,8},{10,11... | collective-permute-start | bytes 196616 | tf_op jit(solution)/shard_map/ppermute | solution.py:363
  105.9 1.1 collective-permute-done.19
  107.3 1.3 %collective-permute-done.22 = bf16[2,32,512]{2,1,0:T(8,128)(2,1)S(1)} collective-permute-done((bf16[2,32,512]{2,1,0:T(8,128)(2,1)S(1)}, bf16[2,32,512]{2,1,0:T(8,128)(2,1)S(1)}, u32[]{:S(2)}, u32[]{:S(2)}) %collective-permute-start.22) | collective-permute-done | bytes 65568 | tf_op jit(solution)/shard_map/ppermute | solution.py:363
  108.7 2.6 %collective-permute-start.23 = (bf16[64,512]{1,0:T(8,128)(2,1)S(1)}, bf16[64,512]{1,0:T(8,128)(2,1)S(1)}, u32[]{:S(2)}, u32[]{:S(2)}) collective-permute-start(bf16[64,512]{1,0:T(8,128)(2,1)S(1)} %fusion.16), channel_id=1, source_target_pairs={{0,16},{1,17},{2,18},{3,19},{4,20},{5,21},{6,22},{7,23},{8,24},{9,... | collective-permute-start | bytes 196616 | tf_op jit(solution)/shard_map/ppermute | solution.py:363
  111.7 2.5 %collective-permute-done.23 = bf16[64,512]{1,0:T(8,128)(2,1)S(1)} collective-permute-done((bf16[64,512]{1,0:T(8,128)(2,1)S(1)}, bf16[64,512]{1,0:T(8,128)(2,1)S(1)}, u32[]{:S(2)}, u32[]{:S(2)}) %collective-permute-start.23) | collective-permute-done | bytes 65568 | tf_op jit(solution)/shard_map/ppermute | solution.py:363
  114.8 3.4 %collective-permute-done.20 = bf16[64,896]{1,0:T(8,128)(2,1)S(1)} collective-permute-done((bf16[64,896]{1,0:T(8,128)(2,1)S(1)}, bf16[64,896]{1,0:T(8,128)(2,1)S(1)}, u32[]{:S(2)}, u32[]{:S(2)}) %collective-permute-start.20) | collective-permute-done | bytes 114720 | tf_op jit(solution)/shard_map/ppermute | solution.py:363
  (86 shorter events, 10.8 us)
Async XLA Ops:
  0.6 27.6 %copy-start.8 = (f32[2048]{0:T(1024)S(1)}, f32[2048]{0:T(1024)}, u32[]{:S(2)}) copy-start(f32[2048]{0:T(1024)} %param.17) | copy-start | bytes 24580
  2.7 33.4 %collective-permute-start.2 = (bf16[768,512]{1,0:T(8,128)(2,1)}, bf16[768,512]{1,0:T(8,128)(2,1)}, u32[]{:S(2)}, u32[]{:S(2)}) collective-permute-start(bf16[768,512]{1,0:T(8,128)(2,1)} %get-tuple-element.46.r_2_), channel_id=1, source_target_pairs={{0,2},{1,3},{2,4},{3,5},{4,6},{5,7},{6,8},{7,9},{8,10},{9,11},{10,... | collective-permute-start | bytes 2359304 | tf_op jit(solution)/shard_map/ppermute | solution.py:359
  5.9 30.2 %collective-permute-start.3 = (bf16[768,512]{1,0:T(8,128)(2,1)}, bf16[768,512]{1,0:T(8,128)(2,1)}, u32[]{:S(2)}, u32[]{:S(2)}) collective-permute-start(bf16[768,512]{1,0:T(8,128)(2,1)} %get-tuple-element.46.r_2_), channel_id=1, source_target_pairs={{2,0},{3,1},{4,2},{5,3},{6,4},{7,5},{8,6},{9,7},{10,8},{11,9},{12,... | collective-permute-start | bytes 2359304 | tf_op jit(solution)/shard_map/ppermute | solution.py:359
  7.2 31.5 %collective-permute-start.6 = (bf16[384,512]{1,0:T(8,128)(2,1)}, bf16[384,512]{1,0:T(8,128)(2,1)}, u32[]{:S(2)}, u32[]{:S(2)}) collective-permute-start(bf16[384,512]{1,0:T(8,128)(2,1)} %top_ref.1), channel_id=1, source_target_pairs={{0,1},{1,0},{2,3},{3,2},{4,5},{5,4},{6,7},{7,6},{8,9},{9,8},{10,11... | collective-permute-start | bytes 1179656 | tf_op jit(solution)/shard_map/ppermute | solution.py:363
  9.6 9.3 %collective-permute-start = (s32[3,12]{1,0:T(4,128)}, s32[3,12]{1,0:T(4,128)S(1)}, u32[]{:S(2)}, u32[]{:S(2)}) collective-permute-start(s32[3,12]{1,0:T(4,128)} %get-tuple-element.44), channel_id=1, source_target_pairs={{0,1},{1,0},{2,3},{3,2},{4,5},{5,4},{6,7},{7,6},{8,9},{9,8},{10,11... | collective-permute-start | bytes 440 | tf_op jit(solution)/shard_map/ppermute | solution.py:363
  20.0 16.1 %collective-permute-start.1 = (s32[3,12]{1,0:T(4,128)}, s32[3,12]{1,0:T(4,128)S(1)}, u32[]{:S(2)}, u32[]{:S(2)}) collective-permute-start(s32[3,12]{1,0:T(4,128)} %get-tuple-element.44), channel_id=1, source_target_pairs={{1,4},{3,6},{5,8},{7,10},{9,12},{11,14},{13,16},{15,18},{17,20},{1... | collective-permute-start | bytes 440 | tf_op jit(solution)/shard_map/ppermute | solution.py:427
  20.7 23.6 %collective-permute-start.7 = (bf16[384,512]{1,0:T(8,128)(2,1)}, bf16[384,512]{1,0:T(8,128)(2,1)}, u32[]{:S(2)}, u32[]{:S(2)}) collective-permute-start(bf16[384,512]{1,0:T(8,128)(2,1)} %bottom_ref.1), channel_id=1, source_target_pairs={{0,1},{1,0},{2,3},{3,2},{4,5},{5,4},{6,7},{7,6},{8,9},{9,8},{10,11... | collective-permute-start | bytes 1179656 | tf_op jit(solution)/shard_map/ppermute | solution.py:363
  28.2 7.9 %copy-start.3 = (bf16[768,768]{1,0:T(8,128)(2,1)}, bf16[768,768]{1,0:T(8,128)(2,1)S(1)}, u32[]{:S(2)}) copy-start(bf16[768,768]{1,0:T(8,128)(2,1)S(1)} %constant_dynamic-update-slice_fusion.refs_9_) | copy-start | bytes 3538948
  28.2 7.9 %copy-start.5 = (s32[3,12]{1,0:T(4,128)S(1)}, s32[3,12]{1,0:T(4,128)}, u32[]{:S(2)}) copy-start(s32[3,12]{1,0:T(4,128)} %get-tuple-element.44) | copy-start | bytes 436
  28.2 20.4 %copy-start.6 = (s32[2]{0:T(128)S(1)}, s32[2]{0:T(128)}, u32[]{:S(2)}) copy-start(s32[2]{0:T(128)} %constant.12.clone) | copy-start | bytes 28
  28.3 20.4 %copy-start.7 = (s32[2]{0:T(128)S(1)}, s32[2]{0:T(128)}, u32[]{:S(2)}) copy-start(s32[2]{0:T(128)} %constant.13.clone) | copy-start | bytes 28
  36.2 11.8 %collective-permute-start.4 = (s32[6,12]{1,0:T(8,128)S(1)}, s32[6,12]{1,0:T(8,128)S(1)}, u32[]{:S(2)}, u32[]{:S(2)}) collective-permute-start(s32[6,12]{1,0:T(8,128)S(1)} %add_select_fusion.1), channel_id=1, source_target_pairs={{0,2},{1,3},{2,4},{3,5},{4,6},{5,7},{6,8},{7,9},{8,10},{9,11},{10,... | collective-permute-start | bytes 872 | tf_op jit(solution)/shard_map/ppermute | solution.py:359
  37.5 10.5 %collective-permute-start.5 = (s32[6,12]{1,0:T(8,128)S(1)}, s32[6,12]{1,0:T(8,128)S(1)}, u32[]{:S(2)}, u32[]{:S(2)}) collective-permute-start(s32[6,12]{1,0:T(8,128)S(1)} %add_select_fusion.1), channel_id=1, source_target_pairs={{2,0},{3,1},{4,2},{5,3},{6,4},{7,5},{8,6},{9,7},{10,8},{11,9},{12,... | collective-permute-start | bytes 872 | tf_op jit(solution)/shard_map/ppermute | solution.py:359
  38.8 17.8 %collective-permute-start.8 = (bf16[384,512]{1,0:T(8,128)(2,1)}, bf16[384,512]{1,0:T(8,128)(2,1)}, u32[]{:S(2)}, u32[]{:S(2)}) collective-permute-start(bf16[384,512]{1,0:T(8,128)(2,1)} %collective-permute-done.6.r_5_), channel_id=1, source_target_pairs={{0,2},{2,4},{4,6},{6,8},{8,10},{10,12},{12,14},{14,16},{16,18},{18... | collective-permute-start | bytes 1179656 | tf_op jit(solution)/shard_map/ppermute | solution.py:430
  44.3 12.3 %collective-permute-start.9 = (bf16[384,512]{1,0:T(8,128)(2,1)}, bf16[384,512]{1,0:T(8,128)(2,1)}, u32[]{:S(2)}, u32[]{:S(2)}) collective-permute-start(bf16[384,512]{1,0:T(8,128)(2,1)} %collective-permute-done.7.r_6_), channel_id=1, source_target_pairs={{0,2},{2,4},{4,6},{6,8},{8,10},{10,12},{12,14},{14,16},{16,18},{18... | collective-permute-start | bytes 1179656 | tf_op jit(solution)/shard_map/ppermute | solution.py:430
  56.6 10.5 %copy-start = (f32[2048,768]{1,0:T(8,128)S(1)}, f32[2048,768]{1,0:T(8,128)}, u32[]{:S(2)}) copy-start(f32[2048,768]{1,0:T(8,128)} %get-tuple-element.43.refs_0_.refs_1_.refs_2_.refs_3_) | copy-start | bytes 18874372
  56.6 10.5 %copy-start.1 = (bf16[2048,512]{1,0:T(8,128)(2,1)S(1)}, bf16[2048,512]{1,0:T(8,128)(2,1)}, u32[]{:S(2)}) copy-start(bf16[2048,512]{1,0:T(8,128)(2,1)} %refs_7_.3) | copy-start | bytes 6291460
  56.6 10.5 %copy-start.4 = (bf16[768,768]{1,0:T(8,128)(2,1)S(1)}, bf16[768,768]{1,0:T(8,128)(2,1)}, u32[]{:S(2)}) copy-start(bf16[768,768]{1,0:T(8,128)(2,1)} %copy-done.3) | copy-start | bytes 3538948
  71.2 3.9 %collective-permute-start.10 = (bf16[2,2,2,2,64,896]{5,4,3,2,0,1:T(8,128)(2,1)S(1)}, bf16[2,2,2,2,64,896]{5,4,3,2,0,1:T(8,128)(2,1)S(1)}, u32[]{:S(2)}, u32[]{:S(2)}) collective-permute-start(bf16[2,2,2,2,64,896]{5,4,3,2,0,1:T(8,128)(2,1)S(1)} %copy.25), channel_id=1, source_target_pairs={{0,2},{1,3},{2,0},{3,1},{4,6},{5,7},{6,4},{7,5},{8,10},{9,11},{10,... | collective-permute-start | bytes 5505032 | tf_op jit(solution)/shard_map/ppermute | solution.py:363
  78.0 4.6 %collective-permute-start.11 = (bf16[2,2,2,2,64,512]{5,4,3,0,1,2:T(8,128)(2,1)S(1)}, bf16[2,2,2,2,64,512]{5,4,3,0,1,2:T(8,128)(2,1)S(1)}, u32[]{:S(2)}, u32[]{:S(2)}) collective-permute-start(bf16[2,2,2,2,64,512]{5,4,3,0,1,2:T(8,128)(2,1)S(1)} %copy.28), channel_id=1, source_target_pairs={{0,2},{1,3},{2,0},{3,1},{4,6},{5,7},{6,4},{7,5},{8,10},{9,11},{10,... | collective-permute-start | bytes 3145736 | tf_op jit(solution)/shard_map/ppermute | solution.py:363
  78.5 12.6 %collective-permute-start.13 = (bf16[2,2,2,32,896]{4,3,2,1,0:T(8,128)(2,1)S(1)}, bf16[2,2,2,32,896]{4,3,2,1,0:T(8,128)(2,1)S(1)}, u32[]{:S(2)}, u32[]{:S(2)}) collective-permute-start(bf16[2,2,2,32,896]{4,3,2,1,0:T(8,128)(2,1)S(1)} %get-tuple-element.84), channel_id=1, source_target_pairs={{0,4},{1,5},{2,6},{3,7},{4,0},{5,1},{6,2},{7,3},{8,12},{9,13},{10,... | collective-permute-start | bytes 1376264 | tf_op jit(solution)/shard_map/ppermute | solution.py:363
  80.4 12.6 %collective-permute-start.12 = (bf16[2,2,2,32,896]{4,3,2,1,0:T(8,128)(2,1)S(1)}, bf16[2,2,2,32,896]{4,3,2,1,0:T(8,128)(2,1)S(1)}, u32[]{:S(2)}, u32[]{:S(2)}) collective-permute-start(bf16[2,2,2,32,896]{4,3,2,1,0:T(8,128)(2,1)S(1)} %get-tuple-element.82), channel_id=1, source_target_pairs={{0,1},{1,0},{2,3},{3,2},{4,5},{5,4},{6,7},{7,6},{8,9},{9,8},{10,11... | collective-permute-start | bytes 1376264 | tf_op jit(solution)/shard_map/ppermute | solution.py:363
  83.0 13.8 %collective-permute-start.14 = (bf16[2,2,2,64,512]{4,3,2,0,1:T(8,128)(2,1)S(1)}, bf16[2,2,2,64,512]{4,3,2,0,1:T(8,128)(2,1)S(1)}, u32[]{:S(2)}, u32[]{:S(2)}) collective-permute-start(bf16[2,2,2,64,512]{4,3,2,0,1:T(8,128)(2,1)S(1)} %get-tuple-element.86), channel_id=1, source_target_pairs={{0,8},{1,9},{2,10},{3,11},{4,12},{5,13},{6,14},{7,15},{8,0},{9,1},... | collective-permute-start | bytes 1572872 | tf_op jit(solution)/shard_map/ppermute | solution.py:363
  91.3 7.9 %collective-permute-start.16 = (bf16[2,2,32,896]{3,2,1,0:T(8,128)(2,1)S(1)}, bf16[2,2,32,896]{3,2,1,0:T(8,128)(2,1)S(1)}, u32[]{:S(2)}, u32[]{:S(2)}) collective-permute-start(bf16[2,2,32,896]{3,2,1,0:T(8,128)(2,1)S(1)} %get-tuple-element.96), channel_id=1, source_target_pairs={{0,1},{1,0},{2,3},{3,2},{4,5},{5,4},{6,7},{7,6},{8,9},{9,8},{10,11... | collective-permute-start | bytes 688136 | tf_op jit(solution)/shard_map/ppermute | solution.py:363
  93.2 7.7 %collective-permute-start.15 = (bf16[2,2,32,896]{3,2,1,0:T(8,128)(2,1)S(1)}, bf16[2,2,32,896]{3,2,1,0:T(8,128)(2,1)S(1)}, u32[]{:S(2)}, u32[]{:S(2)}) collective-permute-start(bf16[2,2,32,896]{3,2,1,0:T(8,128)(2,1)S(1)} %get-tuple-element.94), channel_id=1, source_target_pairs={{0,4},{1,5},{2,6},{3,7},{4,0},{5,1},{6,2},{7,3},{8,12},{9,13},{10,... | collective-permute-start | bytes 688136 | tf_op jit(solution)/shard_map/ppermute | solution.py:363
  97.0 7.3 %collective-permute-start.18 = (bf16[2,2,32,512]{3,2,1,0:T(8,128)(2,1)S(1)}, bf16[2,2,32,512]{3,2,1,0:T(8,128)(2,1)S(1)}, u32[]{:S(2)}, u32[]{:S(2)}) collective-permute-start(bf16[2,2,32,512]{3,2,1,0:T(8,128)(2,1)S(1)} %get-tuple-element.88), channel_id=1, source_target_pairs={{0,4},{1,5},{2,6},{3,7},{4,0},{5,1},{6,2},{7,3},{8,12},{9,13},{10,... | collective-permute-start | bytes 393224 | tf_op jit(solution)/shard_map/ppermute | solution.py:363
  97.6 5.3 %collective-permute-start.17 = (bf16[2,2,32,512]{3,2,1,0:T(8,128)(2,1)S(1)}, bf16[2,2,32,512]{3,2,1,0:T(8,128)(2,1)S(1)}, u32[]{:S(2)}, u32[]{:S(2)}) collective-permute-start(bf16[2,2,32,512]{3,2,1,0:T(8,128)(2,1)S(1)} %get-tuple-element.90), channel_id=1, source_target_pairs={{0,1},{1,0},{2,3},{3,2},{4,5},{5,4},{6,7},{7,6},{8,9},{9,8},{10,11... | collective-permute-start | bytes 393224 | tf_op jit(solution)/shard_map/ppermute | solution.py:363
  100.9 6.1 %collective-permute-start.19 = (bf16[2,64,896]{2,1,0:T(8,128)(2,1)S(1)}, bf16[2,64,896]{2,1,0:T(8,128)(2,1)S(1)}, u32[]{:S(2)}, u32[]{:S(2)}) collective-permute-start(bf16[2,64,896]{2,1,0:T(8,128)(2,1)S(1)} %get-tuple-element.92), channel_id=1, source_target_pairs={{0,8},{1,9},{2,10},{3,11},{4,12},{5,13},{6,14},{7,15},{8,0},{9,1},... | collective-permute-start | bytes 688136 | tf_op jit(solution)/shard_map/ppermute | solution.py:363
  102.9 4.3 %collective-permute-start.21 = (bf16[2,32,512]{2,1,0:T(8,128)(2,1)S(1)}, bf16[2,32,512]{2,1,0:T(8,128)(2,1)S(1)}, u32[]{:S(2)}, u32[]{:S(2)}) collective-permute-start(bf16[2,32,512]{2,1,0:T(8,128)(2,1)S(1)} %get-tuple-element.100), channel_id=1, source_target_pairs={{0,4},{1,5},{2,6},{3,7},{4,0},{5,1},{6,2},{7,3},{8,12},{9,13},{10,... | collective-permute-start | bytes 196616 | tf_op jit(solution)/shard_map/ppermute | solution.py:363
  104.3 4.3 %collective-permute-start.22 = (bf16[2,32,512]{2,1,0:T(8,128)(2,1)S(1)}, bf16[2,32,512]{2,1,0:T(8,128)(2,1)S(1)}, u32[]{:S(2)}, u32[]{:S(2)}) collective-permute-start(bf16[2,32,512]{2,1,0:T(8,128)(2,1)S(1)} %get-tuple-element.102), channel_id=1, source_target_pairs={{0,1},{1,0},{2,3},{3,2},{4,5},{5,4},{6,7},{7,6},{8,9},{9,8},{10,11... | collective-permute-start | bytes 196616 | tf_op jit(solution)/shard_map/ppermute | solution.py:363
  108.7 5.5 %collective-permute-start.23 = (bf16[64,512]{1,0:T(8,128)(2,1)S(1)}, bf16[64,512]{1,0:T(8,128)(2,1)S(1)}, u32[]{:S(2)}, u32[]{:S(2)}) collective-permute-start(bf16[64,512]{1,0:T(8,128)(2,1)S(1)} %fusion.16), channel_id=1, source_target_pairs={{0,16},{1,17},{2,18},{3,19},{4,20},{5,21},{6,22},{7,23},{8,24},{9,... | collective-permute-start | bytes 196616 | tf_op jit(solution)/shard_map/ppermute | solution.py:363
  111.3 6.9 %collective-permute-start.20 = (bf16[64,896]{1,0:T(8,128)(2,1)S(1)}, bf16[64,896]{1,0:T(8,128)(2,1)S(1)}, u32[]{:S(2)}, u32[]{:S(2)}) collective-permute-start(bf16[64,896]{1,0:T(8,128)(2,1)S(1)} %get-tuple-element.98), channel_id=1, source_target_pairs={{0,16},{1,17},{2,18},{3,19},{4,20},{5,21},{6,22},{7,23},{8,24},{9,... | collective-permute-start | bytes 344072 | tf_op jit(solution)/shard_map/ppermute | solution.py:363
  (1 other events, 2.3 us)

commit v12 on v10

--- a/solution.py
+++ b/solution.py
@@ -59,6 +59,8 @@
             d = jnp.sum(total, axis=1, keepdims=True)
             n = jnp.where(d > 0.0, lax.rsqrt(d), 0.0)
             nimg_ref[q - tiles] = jnp.broadcast_to(n, (TILE, TILE))
+            for k, (src, dst) in enumerate(zip((pat_ref, pat_t_ref, nimg_ref), outs)):
+                pltpu.make_async_copy(src.at[q - tiles], dst.at[q - tiles], sems.at[k]).start()
 
     def edge_body(q, c):
         one(q, False)
@@ -74,8 +76,6 @@
         pltpu.make_async_copy(src, dst, sems.at[k])
         for k, (src, dst) in enumerate(zip((pat_ref, pat_t_ref, nimg_ref, ncap_ref), outs))
     ]
-    for copy in copies[:3]:
-        copy.start()
     lax.fori_loop(tiles + mid, all_tiles, edge_body, 0)
     for m in range(mid):
         d = deg_ref[m + 2 * tiles]
@@ -247,22 +247,23 @@
 
 
 def out_kernel(order_ref, *refs):
-    act, (logit_ref, part_ref) = refs[:GROUP], refs[GROUP:]
-    part_ref[...] = jnp.dot(stacked(act), logit_ref[...], preferred_element_type=F32).astype(BF16)
+    act, (logit_ref, bias_ref, part_ref) = refs[:GROUP], refs[GROUP:]
+    width = logit_ref.shape[1]
+    part_ref[:, :width] = jnp.dot(stacked(act), logit_ref[...], preferred_element_type=F32).astype(BF16)
+    part_ref[:, width:] = bias_ref[...]
 
 
 def in_kernel(order_ref, *refs):
     slope, w_out = refs[:GROUP], refs[GROUP : 2 * GROUP]
-    logit_ref, feats_ref, part_ref, grad_ref = refs[2 * GROUP :]
+    logit_ref, feats_ref, part_ref, grad_ref, bias_ref = refs[2 * GROUP :]
     hidden = lax.dot_general(
         stacked(w_out), logit_ref[...], (((1,), (1,)), ((), ())), preferred_element_type=F32
     )
     grad = (hidden * stacked(slope)).astype(BF16)
     grad_ref[...] = grad
-    f_in = feats_ref.shape[1]
-    part_ref[:, :f_in] = jnp.dot(grad, feats_ref[...], preferred_element_type=F32).astype(BF16)
+    part_ref[...] = jnp.dot(grad, feats_ref[...], preferred_element_type=F32).astype(BF16)
     bias = jnp.sum(grad.astype(F32), axis=1, keepdims=True)
-    part_ref[:, f_in:] = jnp.broadcast_to(bias, (bias.shape[0], TILE)).astype(BF16)
+    bias_ref[...] = jnp.broadcast_to(bias, (bias.shape[0], TILE)).astype(BF16)
 
 
 def feat_kernel(order_ref, *refs):
@@ -470,34 +471,34 @@
     half = order.shape[0] // 2
     blocked = (2,) * (m - 1) + (rows,)
 
-    def out_half(order, logit):
+    def out_half(order, logit, bias):
         return over_hidden(
-            out_kernel, "part_out", order, grouped(nodes) + [whole(logit.shape)], rows_of(width),
-            jax.ShapeDtypeStruct((hid // 2, width), BF16), [], [hidden_act] * GROUP + [logit],
-        ).reshape(blocked + (width,))
+            out_kernel, "part_out", order, grouped(nodes) + [whole(logit.shape), rows_of(TILE)], rows_of(width + TILE),
+            jax.ShapeDtypeStruct((hid // 2, width + TILE), BF16), [], [hidden_act] * GROUP + [logit, bias],
+        ).reshape(blocked + (width + TILE,))
 
     def in_half(order, logit):
-        part, grad = over_hidden(
+        part, grad, bias = over_hidden(
             in_kernel, "part_in", order,
             grouped(nodes) + grouped(width) + [whole(logit.shape), whole(feats.shape)],
-            (rows_of(f_in + TILE), rows_of(nodes)),
-            (jax.ShapeDtypeStruct((hid // 2, f_in + TILE), BF16), jax.ShapeDtypeStruct((hid // 2, nodes), BF16)),
+            (rows_of(f_in), rows_of(nodes), rows_of(TILE)),
+            tuple(jax.ShapeDtypeStruct((hid // 2, lanes), BF16) for lanes in (f_in, nodes, TILE)),
             [], [gelu_slope] * GROUP + [w_out] * GROUP + [logit, feats],
         )
-        return part.reshape(blocked + (f_in + TILE,)), grad
+        return part.reshape(blocked + (f_in,)), grad, bias
 
     core = 1 << a
     rest = bits[1:]
     orders = (cap_bits + img_bits, img_bits + cap_bits)
     near, last = m - 2, m - 1
-    in_sent, grad_sent = in_half(order[half:], logit)
+    in_sent, grad_sent, bias_sent = in_half(order[half:], logit)
     in_came = flipped(in_sent, count, core)
-    in_kept, grad_kept = in_half(order[:half], after(logit, grad_sent))
+    in_kept, grad_kept, bias_kept = in_half(order[:half], after(logit, grad_sent))
     r_in = Reduction(added(in_kept, in_came), count, rest, (), orders, (near, last))
     r_in.start()
-    out_sent = out_half(order[half:], after(logit, *r_in.sent))
+    out_sent = out_half(order[half:], after(logit, *r_in.sent), bias_sent)
     out_came = flipped(out_sent, count, core)
-    out_kept = out_half(order[:half], after(logit, out_sent))
+    out_kept = out_half(order[:half], after(logit, out_sent), bias_kept)
     r_out = Reduction(added(out_kept, out_came), count, rest, (near,), orders, (last,))
     r_out.start()
     grad_img, grad_cap = over_hidden(
@@ -513,9 +514,9 @@
         r_out.start()
         done = r_out.sent
     grad_scale = 1.0 / math.sqrt(nodes * count)
-    g_out = r_out.result(slice(None)) * grad_scale
-    g_in = r_in.result(slice(0, f_in)) * grad_scale
-    g_bias = r_in.result(f_in) * grad_scale
+    g_out = r_out.result(slice(0, width)) * grad_scale
+    g_bias = r_out.result(width) * grad_scale
+    g_in = r_in.result(slice(None)) * grad_scale
     return (grad_img, grad_cap, g_in, g_out, g_bias)
 
 

time: 110 us -> 111 us (level)
  starting transfers between devices: 41.7 us -> 44.5 us
  Pallas kernels: 38.3 us -> 36.5 us
    ppermute x16, starting transfers between devices: 27.2 us -> 29.9 us  [flipped(): return lax.ppermute(array, AXES, [(i, i ^ mask) for i in range(count)])]
    pallas_call x1, Pallas kernels: 7.82 us -> 6.06 us  [make_tiles(): pl.pallas_call(lambda *r: tiles_kernel(*r, tiles=tiles, slots=slots), out...]
  transfers between devices with their start and end apart: 22 -> 22, of which waited for: 9 -> 5; matrix products, arithmetic and copies ran while one was open for 12% -> 11% of each run, Pallas kernels for 18% -> 16%
where the time goes in v12:
time: 111 us; the launch traced here: 110 us
  starting transfers between devices  44.5 us (40%)
  Pallas kernels  36.5 us (33%)
  waiting for transfers between devices  13.9 us (13%)
  matrix products  7.41 us (7%)
  other arithmetic  5.79 us (5%)
  local copies, waits for them, and re-layouts  1.21 us (1%)
    ppermute x16, starting transfers between devices, flipped(): return lax.ppermute(array, AXES, [(i, i ^ mask) for i in range(count)])  29.9 us
    pallas_call x5, Pallas kernels, over_hidden(): pl.pallas_call(kernel, out_shape=out_shape, grid_spec=pltpu.PrefetchScala...  17.9 us
    ppermute x16, waiting for transfers between devices, flipped(): return lax.ppermute(array, AXES, [(i, i ^ mask) for i in range(count)])  13.9 us
    pallas_call x1, Pallas kernels, propagate(): pl.pallas_call(lambda *r: hops_kernel(*r, tiles=tiles, slots=slots, width...  10.4 us
    ppermute x4, starting transfers between devices, moved(): lax.ppermute(array, AXES, [(i, i + by) for i in range(count) if 0 <= i +...  9.52 us
    dot_general x1, matrix products, per_device(): lax.dot_general(w_in, feats, across, preferred_element_type=F32)  7.41 us
    pallas_call x1, Pallas kernels, make_tiles(): pl.pallas_call(lambda *r: tiles_kernel(*r, tiles=tiles, slots=slots), out...  6.06 us
    ppermute x1, starting transfers between devices, per_device(): far = lax.ppermute(mate, AXES, nearest_pair(count, 2))  4.3 us
  transfers between devices with their start and end apart: 22, of which 5 were waited for; matrix products, arithmetic and copies ran while one was open for 11% of the time, Pallas kernels for 16%

profile of v12, /device:TPU:0, one launch (start us, length us, event | category | flops | bytes accessed | tf_op | source)
XLA Modules:
  0.0 110.5 jit_solution(12060860171872377204)
XLA Ops:
  0.6 2.1 %stack.1 = (bf16[768,512]{1,0:T(8,128)(2,1)}, s32[3,12]{1,0:T(4,128)}) custom-call(s32[3]{0:T(128)} %count_ref.1, bf16[384,512]{1,0:T(8,128)(2,1)} %top_ref.1, bf16[384,512]{1,0:T(8,128)(2,1)} %bottom_ref.1, s32[3,4]{1,0:T(4,128)} %seed_ref.1, s32[3,4]{1,0:T(4,128)} %cols_ref.1), custom_call_target="tpu_custom_call" | custom-call | flops 1 | bytes 1 | tf_op jit(solution)/shard_map/stack/pallas_call | solution.py:339
  3.5 5.7 %collective-permute-start = (s32[3,12]{1,0:T(4,128)}, s32[3,12]{1,0:T(4,128)S(1)}, u32[]{:S(2)}, u32[]{:S(2)}) collective-permute-start(s32[3,12]{1,0:T(4,128)} %get-tuple-element.40), channel_id=1, source_target_pairs={{0,1},{1,0},{2,3},{3,2},{4,5},{5,4},{6,7},{7,6},{8,9},{9,8},{10,11... | collective-permute-start | bytes 440 | tf_op jit(solution)/shard_map/ppermute | solution.py:358
  10.0 1.0 collective-permute-done
  11.0 2.0 %collective-permute-start.6 = (bf16[768,512]{1,0:T(8,128)(2,1)}, bf16[768,512]{1,0:T(8,128)(2,1)}, u32[]{:S(2)}, u32[]{:S(2)}) collective-permute-start(bf16[768,512]{1,0:T(8,128)(2,1)} %get-tuple-element.42.r_2_), channel_id=1, source_target_pairs={{0,1},{1,0},{2,3},{3,2},{4,5},{5,4},{6,7},{7,6},{8,9},{9,8},{10,11... | collective-permute-start | bytes 2359304 | tf_op jit(solution)/shard_map/ppermute | solution.py:358
  13.1 1.3 %collective-permute-start.5 = (bf16[768,512]{1,0:T(8,128)(2,1)}, bf16[768,512]{1,0:T(8,128)(2,1)}, u32[]{:S(2)}, u32[]{:S(2)}) collective-permute-start(bf16[768,512]{1,0:T(8,128)(2,1)} %get-tuple-element.42.r_2_), channel_id=1, source_target_pairs={{2,0},{3,1},{4,2},{5,3},{6,4},{7,5},{8,6},{9,7},{10,8},{11,9},{12,... | collective-permute-start | bytes 2359304 | tf_op jit(solution)/shard_map/ppermute | solution.py:354
  14.3 3.9 %collective-permute-start.4 = (bf16[768,512]{1,0:T(8,128)(2,1)}, bf16[768,512]{1,0:T(8,128)(2,1)}, u32[]{:S(2)}, u32[]{:S(2)}) collective-permute-start(bf16[768,512]{1,0:T(8,128)(2,1)} %get-tuple-element.42.r_2_), channel_id=1, source_target_pairs={{0,2},{1,3},{2,4},{3,5},{4,6},{5,7},{6,8},{7,9},{8,10},{9,11},{10,... | collective-permute-start | bytes 2359304 | tf_op jit(solution)/shard_map/ppermute | solution.py:354
  18.3 1.3 %pad_maximum_fusion.refs_9_ = bf16[768,768]{1,0:T(8,128)(2,1)S(1)} fusion(bf16[384,768]{1,0:T(8,128)(2,1)} %param.13, bf16[384,768]{1,0:T(8,128)(2,1)} %param.12), kind=kLoop, calls=%fused_computation.16 | loop fusion | flops 2359296 | bytes 2359296 | tf_op jit(solution)/shard_map/concatenate | solution.py:426
  19.6 1.3 %collective-permute-start.3 = (s32[6,12]{1,0:T(8,128)S(1)}, s32[6,12]{1,0:T(8,128)S(1)}, u32[]{:S(2)}, u32[]{:S(2)}) collective-permute-start(s32[6,12]{1,0:T(8,128)S(1)} %add_select_fusion.1), channel_id=1, source_target_pairs={{2,0},{3,1},{4,2},{5,3},{6,4},{7,5},{8,6},{9,7},{10,8},{11,9},{12,... | collective-permute-start | bytes 872 | tf_op jit(solution)/shard_map/ppermute | solution.py:354
  20.9 3.0 %collective-permute-start.2 = (s32[6,12]{1,0:T(8,128)S(1)}, s32[6,12]{1,0:T(8,128)S(1)}, u32[]{:S(2)}, u32[]{:S(2)}) collective-permute-start(s32[6,12]{1,0:T(8,128)S(1)} %add_select_fusion.1), channel_id=1, source_target_pairs={{0,2},{1,3},{2,4},{3,5},{4,6},{5,7},{6,8},{7,9},{8,10},{9,11},{10,... | collective-permute-start | bytes 872 | tf_op jit(solution)/shard_map/ppermute | solution.py:354
  24.0 7.4 %fusion.3 = (f32[2048,768]{1,0:T(8,128)}, bf16[2048,768]{1,0:T(8,128)(2,1)S(1)}) fusion(f32[2048]{0:T(1024)S(1)} %copy-done.6, bf16[768,768]{1,0:T(8,128)(2,1)S(1)} %pad_maximum_fusion.refs_9_, bf16[2048,768]{1,0:T(8,128)(2,1)} %refs_3_.1), kind=kOutput, calls=%fused_computation.4 | convolution fusion | flops 2433220608 | bytes 13770752 | tf_op jit(solution)/shard_map/dot_general | solution.py:461
  31.4 4.3 %collective-permute-start.7 = (bf16[768,512]{1,0:T(8,128)(2,1)}, bf16[768,512]{1,0:T(8,128)(2,1)}, u32[]{:S(2)}, u32[]{:S(2)}) collective-permute-start(bf16[768,512]{1,0:T(8,128)(2,1)} %collective-permute-done.6.r_5_), channel_id=1, source_target_pairs={{0,2},{2,4},{4,6},{6,8},{8,10},{10,12},{12,14},{14,16},{16,18},{18... | collective-permute-start | bytes 2359304 | tf_op jit(solution)/shard_map/ppermute | solution.py:424
  36.4 6.1 %tiles.1 = (bf16[15,128,512]{2,1,0:T(8,128)(2,1)}, bf16[15,512,128]{2,1,0:T(8,128)(2,1)}, f32[15,128,128]{2,1,0:T(8,128)}, f32[15,128,128]{2,1,0:T(8,128)}) custom-call(s32[84]{0:T(128)S(1)} %reshape.40.r_0_, s32[84]{0:T(128)S(1)} %reshape.41.r_1_, s32[21]{0:T(128)S(1)} %slice_reduce_fusion.r_2_), custom_call_target="tpu_custom_call" | custom-call | flops 1 | bytes 1 | tf_op jit(solution)/shard_map/tiles/pallas_call | solution.py:103
  42.6 10.4 %hops.1.refs_8_.refs_4_ = bf16[768,512]{1,0:T(8,128)(2,1)S(1)} custom-call(s32[60]{0:T(128)S(1)} %reshape.39.r_0_, s32[2]{0:T(128)S(1)} %fusion.18.r_1_, bf16[768,512]{1,0:T(8,128)(2,1)} %get-tuple-element.42.r_2_, bf16[768,512]{1,0:T(8,128)(2,1)} %collective-permute-done.4.r_3_, bf16[768,512]{1,0:T(8,128)(2,1)} %collective-permute-done.5.r_4_, ...), custom_call_target="tpu_custom_call" | custom-call | flops 1 | bytes 1 | tf_op jit(solution)/shard_map/hops/pallas_call | solution.py:207
  53.1 3.8 %part_in.2 = (bf16[1024,768]{1,0:T(8,128)(2,1)S(1)}, bf16[1024,768]{1,0:T(8,128)(2,1)S(1)}, bf16[1024,128]{1,0:T(8,128)(2,1)S(1)}) custom-call(s32[16]{0:T(128)S(1)} %get-tuple-element.102.order_ref, f32[2048,768]{1,0:T(8,128)S(1)} %copy-done, f32[2048,768]{1,0:T(8,128)S(1)} %copy-done, f32[2048,768]{1,0:T(8,128)S(1)} %copy-done, f32[2048,768]{1,0:T(8,128)S(1)} %copy-done, ...), custom_call_target="tpu_custom_call" | custom-call | flops 1 | bytes 1 | tf_op jit(solution)/shard_map/part_in/pallas_call | solution.py:292
  57.1 1.5 %collective-permute-start.8 = (bf16[2,2,2,2,64,768]{5,4,3,2,0,1:T(8,128)(2,1)S(1)}, bf16[2,2,2,2,64,768]{5,4,3,2,0,1:T(8,128)(2,1)S(1)}, u32[]{:S(2)}, u32[]{:S(2)}) collective-permute-start(bf16[2,2,2,2,64,768]{5,4,3,2,0,1:T(8,128)(2,1)S(1)} %copy.25), channel_id=1, source_target_pairs={{0,2},{1,3},{2,0},{3,1},{4,6},{5,7},{6,4},{7,5},{8,10},{9,11},{10,... | collective-permute-start | bytes 4718600 | tf_op jit(solution)/shard_map/ppermute | solution.py:358
  58.6 3.8 %part_in.3 = (bf16[1024,768]{1,0:T(8,128)(2,1)S(1)}, bf16[1024,768]{1,0:T(8,128)(2,1)S(1)}, bf16[1024,128]{1,0:T(8,128)(2,1)S(1)}) custom-call(s32[16]{0:T(128)S(1)} %get-tuple-element.103.order_ref, f32[2048,768]{1,0:T(8,128)S(1)} %copy-done, f32[2048,768]{1,0:T(8,128)S(1)} %copy-done, f32[2048,768]{1,0:T(8,128)S(1)} %copy-done, f32[2048,768]{1,0:T(8,128)S(1)} %copy-done, ...), custom_call_target="tpu_custom_call" | custom-call | flops 1 | bytes 1 | tf_op jit(solution)/shard_map/part_in/pallas_call | solution.py:292
  63.0 2.0 %part_out.2 = bf16[1024,640]{1,0:T(8,128)(2,1)S(1)} custom-call(s32[16]{0:T(128)S(1)} %get-tuple-element.102.order_ref, bf16[2048,768]{1,0:T(8,128)(2,1)S(1)} %get-tuple-element.55.refs_0_.refs_1_.refs_2_.refs_3_, bf16[2048,768]{1,0:T(8,128)(2,1)S(1)} %get-tuple-element.55.refs_0_.refs_1_.refs_2_.refs_3_, ...), custom_call_target="tpu_custom_call" | custom-call | flops 1 | bytes 1 | tf_op jit(solution)/shard_map/part_out/pallas_call | solution.py:292
  65.3 3.0 %collective-permute-start.10 = (bf16[2,2,2,32,768]{4,3,2,1,0:T(8,128)(2,1)S(1)}, bf16[2,2,2,32,768]{4,3,2,1,0:T(8,128)(2,1)S(1)}, u32[]{:S(2)}, u32[]{:S(2)}) collective-permute-start(bf16[2,2,2,32,768]{4,3,2,1,0:T(8,128)(2,1)S(1)} %get-tuple-element.80), channel_id=1, source_target_pairs={{0,1},{1,0},{2,3},{3,2},{4,5},{5,4},{6,7},{7,6},{8,9},{9,8},{10,11... | collective-permute-start | bytes 1179656 | tf_op jit(solution)/shard_map/ppermute | solution.py:358
  68.3 4.2 %collective-permute-start.11 = (bf16[2,2,2,32,768]{4,3,2,1,0:T(8,128)(2,1)S(1)}, bf16[2,2,2,32,768]{4,3,2,1,0:T(8,128)(2,1)S(1)}, u32[]{:S(2)}, u32[]{:S(2)}) collective-permute-start(bf16[2,2,2,32,768]{4,3,2,1,0:T(8,128)(2,1)S(1)} %get-tuple-element.82), channel_id=1, source_target_pairs={{0,4},{1,5},{2,6},{3,7},{4,0},{5,1},{6,2},{7,3},{8,12},{9,13},{10,... | collective-permute-start | bytes 1179656 | tf_op jit(solution)/shard_map/ppermute | solution.py:358
  72.5 2.0 %part_out.3 = bf16[1024,640]{1,0:T(8,128)(2,1)S(1)} custom-call(s32[16]{0:T(128)S(1)} %get-tuple-element.103.order_ref, bf16[2048,768]{1,0:T(8,128)(2,1)S(1)} %get-tuple-element.55.refs_0_.refs_1_.refs_2_.refs_3_, bf16[2048,768]{1,0:T(8,128)(2,1)S(1)} %get-tuple-element.55.refs_0_.refs_1_.refs_2_.refs_3_, ...), custom_call_target="tpu_custom_call" | custom-call | flops 1 | bytes 1 | tf_op jit(solution)/shard_map/part_out/pallas_call | solution.py:292
  75.1 1.6 %collective-permute-start.12 = (bf16[2,2,2,64,640]{4,3,2,0,1:T(8,128)(2,1)S(1)}, bf16[2,2,2,64,640]{4,3,2,0,1:T(8,128)(2,1)S(1)}, u32[]{:S(2)}, u32[]{:S(2)}) collective-permute-start(bf16[2,2,2,64,640]{4,3,2,0,1:T(8,128)(2,1)S(1)} %get-tuple-element.84), channel_id=1, source_target_pairs={{0,8},{1,9},{2,10},{3,11},{4,12},{5,13},{6,14},{7,15},{8,0},{9,1},... | collective-permute-start | bytes 1966088 | tf_op jit(solution)/shard_map/ppermute | solution.py:358
  76.7 6.2 %feat_grad.1 = (bf16[384,768]{1,0:T(8,128)(2,1)}, bf16[384,768]{1,0:T(8,128)(2,1)}) custom-call(s32[32]{0:T(128)S(1)} %fusion.31.order_ref, bf16[2048,768]{1,0:T(8,128)(2,1)S(1)} %copy-done.2, bf16[2048,768]{1,0:T(8,128)(2,1)S(1)} %copy-done.2, bf16[2048,768]{1,0:T(8,128)(2,1)S(1)} %copy-done.2, bf16[2048,768]{1,0:T(8,128)(2,1)S(1)} %copy-done.2, ...), custom_call_target="tpu_custom_call" | custom-call | flops 1 | bytes 1 | tf_op jit(solution)/shard_map/feat_grad/pallas_call | solution.py:292
  83.3 1.1 collective-permute-start.14
  84.4 7.3 %collective-permute-done.12 = bf16[2,2,2,64,640]{4,3,2,0,1:T(8,128)(2,1)S(1)} collective-permute-done((bf16[2,2,2,64,640]{4,3,2,0,1:T(8,128)(2,1)S(1)}, bf16[2,2,2,64,640]{4,3,2,0,1:T(8,128)(2,1)S(1)}, u32[]{:S(2)}, u32[]{:S(2)}) %collective-permute-start.12) | collective-permute-done | bytes 655392 | tf_op jit(solution)/shard_map/ppermute | solution.py:358
  92.3 0.9 collective-permute-start.15
  93.3 1.6 %collective-permute-start.17 = (bf16[2,64,768]{2,1,0:T(8,128)(2,1)S(1)}, bf16[2,64,768]{2,1,0:T(8,128)(2,1)S(1)}, u32[]{:S(2)}, u32[]{:S(2)}) collective-permute-start(bf16[2,64,768]{2,1,0:T(8,128)(2,1)S(1)} %get-tuple-element.90), channel_id=1, source_target_pairs={{0,8},{1,9},{2,10},{3,11},{4,12},{5,13},{6,14},{7,15},{8,0},{9,1},... | collective-permute-start | bytes 589832 | tf_op jit(solution)/shard_map/ppermute | solution.py:358
  95.0 2.3 %collective-permute-done.16 = bf16[2,2,32,640]{3,2,1,0:T(8,128)(2,1)S(1)} collective-permute-done((bf16[2,2,32,640]{3,2,1,0:T(8,128)(2,1)S(1)}, bf16[2,2,32,640]{3,2,1,0:T(8,128)(2,1)S(1)}, u32[]{:S(2)}, u32[]{:S(2)}) %collective-permute-start.16) | collective-permute-done | bytes 163872 | tf_op jit(solution)/shard_map/ppermute | solution.py:358
  97.8 2.3 %collective-permute-start.19 = (bf16[2,32,640]{2,1,0:T(8,128)(2,1)S(1)}, bf16[2,32,640]{2,1,0:T(8,128)(2,1)S(1)}, u32[]{:S(2)}, u32[]{:S(2)}) collective-permute-start(bf16[2,32,640]{2,1,0:T(8,128)(2,1)S(1)} %get-tuple-element.98), channel_id=1, source_target_pairs={{0,4},{1,5},{2,6},{3,7},{4,0},{5,1},{6,2},{7,3},{8,12},{9,13},{10,... | collective-permute-start | bytes 245768 | tf_op jit(solution)/shard_map/ppermute | solution.py:358
  100.1 2.6 %collective-permute-start.18 = (bf16[64,768]{1,0:T(8,128)(2,1)S(1)}, bf16[64,768]{1,0:T(8,128)(2,1)S(1)}, u32[]{:S(2)}, u32[]{:S(2)}) collective-permute-start(bf16[64,768]{1,0:T(8,128)(2,1)S(1)} %slice_bitcast_fusion.14), channel_id=1, source_target_pairs={{0,16},{1,17},{2,18},{3,19},{4,20},{5,21},{6,22},{7,23},{8,24},{9,... | collective-permute-start | bytes 294920 | tf_op jit(solution)/shard_map/ppermute | solution.py:358
  102.9 2.3 %collective-permute-start.21 = (bf16[64,640]{1,0:T(8,128)(2,1)S(1)}, bf16[64,640]{1,0:T(8,128)(2,1)S(1)}, u32[]{:S(2)}, u32[]{:S(2)}) collective-permute-start(bf16[64,640]{1,0:T(8,128)(2,1)S(1)} %get-tuple-element.96), channel_id=1, source_target_pairs={{0,16},{1,17},{2,18},{3,19},{4,20},{5,21},{6,22},{7,23},{8,24},{9,... | collective-permute-start | bytes 245768 | tf_op jit(solution)/shard_map/ppermute | solution.py:358
  105.2 1.9 %collective-permute-done.18 = bf16[64,768]{1,0:T(8,128)(2,1)S(1)} collective-permute-done((bf16[64,768]{1,0:T(8,128)(2,1)S(1)}, bf16[64,768]{1,0:T(8,128)(2,1)S(1)}, u32[]{:S(2)}, u32[]{:S(2)}) %collective-permute-start.18) | collective-permute-done | bytes 98336 | tf_op jit(solution)/shard_map/ppermute | solution.py:358
  107.8 1.4 %collective-permute-done.21 = bf16[64,640]{1,0:T(8,128)(2,1)S(1)} collective-permute-done((bf16[64,640]{1,0:T(8,128)(2,1)S(1)}, bf16[64,640]{1,0:T(8,128)(2,1)S(1)}, u32[]{:S(2)}, u32[]{:S(2)}) %collective-permute-start.21) | collective-permute-done | bytes 81952 | tf_op jit(solution)/shard_map/ppermute | solution.py:358
  (77 shorter events, 7.4 us)
Async XLA Ops:
  0.6 23.3 %copy-start.6 = (f32[2048]{0:T(1024)S(1)}, f32[2048]{0:T(1024)}, u32[]{:S(2)}) copy-start(f32[2048]{0:T(1024)} %param.17) | copy-start | bytes 24580
  2.7 16.9 %copy-start.5 = (s32[3,12]{1,0:T(4,128)S(1)}, s32[3,12]{1,0:T(4,128)}, u32[]{:S(2)}) copy-start(s32[3,12]{1,0:T(4,128)} %get-tuple-element.40) | copy-start | bytes 436
  2.7 16.9 %collective-permute-start.1 = (s32[3,12]{1,0:T(4,128)}, s32[3,12]{1,0:T(4,128)S(1)}, u32[]{:S(2)}, u32[]{:S(2)}) collective-permute-start(s32[3,12]{1,0:T(4,128)} %get-tuple-element.40), channel_id=1, source_target_pairs={{1,4},{3,6},{5,8},{7,10},{9,12},{11,14},{13,16},{15,18},{17,20},{1... | collective-permute-start | bytes 440 | tf_op jit(solution)/shard_map/ppermute | solution.py:417
  3.5 7.5 %collective-permute-start = (s32[3,12]{1,0:T(4,128)}, s32[3,12]{1,0:T(4,128)S(1)}, u32[]{:S(2)}, u32[]{:S(2)}) collective-permute-start(s32[3,12]{1,0:T(4,128)} %get-tuple-element.40), channel_id=1, source_target_pairs={{0,1},{1,0},{2,3},{3,2},{4,5},{5,4},{6,7},{7,6},{8,9},{9,8},{10,11... | collective-permute-start | bytes 440 | tf_op jit(solution)/shard_map/ppermute | solution.py:358
  11.0 20.4 %collective-permute-start.6 = (bf16[768,512]{1,0:T(8,128)(2,1)}, bf16[768,512]{1,0:T(8,128)(2,1)}, u32[]{:S(2)}, u32[]{:S(2)}) collective-permute-start(bf16[768,512]{1,0:T(8,128)(2,1)} %get-tuple-element.42.r_2_), channel_id=1, source_target_pairs={{0,1},{1,0},{2,3},{3,2},{4,5},{5,4},{6,7},{7,6},{8,9},{9,8},{10,11... | collective-permute-start | bytes 2359304 | tf_op jit(solution)/shard_map/ppermute | solution.py:358
  13.1 29.5 %collective-permute-start.5 = (bf16[768,512]{1,0:T(8,128)(2,1)}, bf16[768,512]{1,0:T(8,128)(2,1)}, u32[]{:S(2)}, u32[]{:S(2)}) collective-permute-start(bf16[768,512]{1,0:T(8,128)(2,1)} %get-tuple-element.42.r_2_), channel_id=1, source_target_pairs={{2,0},{3,1},{4,2},{5,3},{6,4},{7,5},{8,6},{9,7},{10,8},{11,9},{12,... | collective-permute-start | bytes 2359304 | tf_op jit(solution)/shard_map/ppermute | solution.py:354
  14.3 28.2 %collective-permute-start.4 = (bf16[768,512]{1,0:T(8,128)(2,1)}, bf16[768,512]{1,0:T(8,128)(2,1)}, u32[]{:S(2)}, u32[]{:S(2)}) collective-permute-start(bf16[768,512]{1,0:T(8,128)(2,1)} %get-tuple-element.42.r_2_), channel_id=1, source_target_pairs={{0,2},{1,3},{2,4},{3,5},{4,6},{5,7},{6,8},{7,9},{8,10},{9,11},{10,... | collective-permute-start | bytes 2359304 | tf_op jit(solution)/shard_map/ppermute | solution.py:354
  19.6 11.8 %copy-start.3 = (bf16[768,768]{1,0:T(8,128)(2,1)}, bf16[768,768]{1,0:T(8,128)(2,1)S(1)}, u32[]{:S(2)}) copy-start(bf16[768,768]{1,0:T(8,128)(2,1)S(1)} %pad_maximum_fusion.refs_9_) | copy-start | bytes 3538948
  19.6 16.1 %collective-permute-start.3 = (s32[6,12]{1,0:T(8,128)S(1)}, s32[6,12]{1,0:T(8,128)S(1)}, u32[]{:S(2)}, u32[]{:S(2)}) collective-permute-start(s32[6,12]{1,0:T(8,128)S(1)} %add_select_fusion.1), channel_id=1, source_target_pairs={{2,0},{3,1},{4,2},{5,3},{6,4},{7,5},{8,6},{9,7},{10,8},{11,9},{12,... | collective-permute-start | bytes 872 | tf_op jit(solution)/shard_map/ppermute | solution.py:354
  20.9 14.8 %collective-permute-start.2 = (s32[6,12]{1,0:T(8,128)S(1)}, s32[6,12]{1,0:T(8,128)S(1)}, u32[]{:S(2)}, u32[]{:S(2)}) collective-permute-start(s32[6,12]{1,0:T(8,128)S(1)} %add_select_fusion.1), channel_id=1, source_target_pairs={{0,2},{1,3},{2,4},{3,5},{4,6},{5,7},{6,8},{7,9},{8,10},{9,11},{10,... | collective-permute-start | bytes 872 | tf_op jit(solution)/shard_map/ppermute | solution.py:354
  31.4 11.2 %collective-permute-start.7 = (bf16[768,512]{1,0:T(8,128)(2,1)}, bf16[768,512]{1,0:T(8,128)(2,1)}, u32[]{:S(2)}, u32[]{:S(2)}) collective-permute-start(bf16[768,512]{1,0:T(8,128)(2,1)} %collective-permute-done.6.r_5_), channel_id=1, source_target_pairs={{0,2},{2,4},{4,6},{6,8},{8,10},{10,12},{12,14},{14,16},{16,18},{18... | collective-permute-start | bytes 2359304 | tf_op jit(solution)/shard_map/ppermute | solution.py:424
  42.6 10.5 %copy-start = (f32[2048,768]{1,0:T(8,128)S(1)}, f32[2048,768]{1,0:T(8,128)}, u32[]{:S(2)}) copy-start(f32[2048,768]{1,0:T(8,128)} %get-tuple-element.45.refs_0_.refs_1_.refs_2_.refs_3_) | copy-start | bytes 18874372
  42.6 10.5 %copy-start.1 = (bf16[2048,512]{1,0:T(8,128)(2,1)S(1)}, bf16[2048,512]{1,0:T(8,128)(2,1)}, u32[]{:S(2)}) copy-start(bf16[2048,512]{1,0:T(8,128)(2,1)} %refs_7_.3) | copy-start | bytes 6291460
  42.6 10.5 %copy-start.4 = (bf16[768,768]{1,0:T(8,128)(2,1)S(1)}, bf16[768,768]{1,0:T(8,128)(2,1)}, u32[]{:S(2)}) copy-start(bf16[768,768]{1,0:T(8,128)(2,1)} %copy-done.3) | copy-start | bytes 3538948
  57.1 5.4 %collective-permute-start.8 = (bf16[2,2,2,2,64,768]{5,4,3,2,0,1:T(8,128)(2,1)S(1)}, bf16[2,2,2,2,64,768]{5,4,3,2,0,1:T(8,128)(2,1)S(1)}, u32[]{:S(2)}, u32[]{:S(2)}) collective-permute-start(bf16[2,2,2,2,64,768]{5,4,3,2,0,1:T(8,128)(2,1)S(1)} %copy.25), channel_id=1, source_target_pairs={{0,2},{1,3},{2,0},{3,1},{4,6},{5,7},{6,4},{7,5},{8,10},{9,11},{10,... | collective-permute-start | bytes 4718600 | tf_op jit(solution)/shard_map/ppermute | solution.py:358
  65.2 9.4 %collective-permute-start.9 = (bf16[2,2,2,2,64,640]{5,4,3,0,1,2:T(8,128)(2,1)S(1)}, bf16[2,2,2,2,64,640]{5,4,3,0,1,2:T(8,128)(2,1)S(1)}, u32[]{:S(2)}, u32[]{:S(2)}) collective-permute-start(bf16[2,2,2,2,64,640]{5,4,3,0,1,2:T(8,128)(2,1)S(1)} %copy.28), channel_id=1, source_target_pairs={{0,2},{1,3},{2,0},{3,1},{4,6},{5,7},{6,4},{7,5},{8,10},{9,11},{10,... | collective-permute-start | bytes 3932168 | tf_op jit(solution)/shard_map/ppermute | solution.py:358
  65.3 17.7 %collective-permute-start.10 = (bf16[2,2,2,32,768]{4,3,2,1,0:T(8,128)(2,1)S(1)}, bf16[2,2,2,32,768]{4,3,2,1,0:T(8,128)(2,1)S(1)}, u32[]{:S(2)}, u32[]{:S(2)}) collective-permute-start(bf16[2,2,2,32,768]{4,3,2,1,0:T(8,128)(2,1)S(1)} %get-tuple-element.80), channel_id=1, source_target_pairs={{0,1},{1,0},{2,3},{3,2},{4,5},{5,4},{6,7},{7,6},{8,9},{9,8},{10,11... | collective-permute-start | bytes 1179656 | tf_op jit(solution)/shard_map/ppermute | solution.py:358
  68.3 14.9 %collective-permute-start.11 = (bf16[2,2,2,32,768]{4,3,2,1,0:T(8,128)(2,1)S(1)}, bf16[2,2,2,32,768]{4,3,2,1,0:T(8,128)(2,1)S(1)}, u32[]{:S(2)}, u32[]{:S(2)}) collective-permute-start(bf16[2,2,2,32,768]{4,3,2,1,0:T(8,128)(2,1)S(1)} %get-tuple-element.82), channel_id=1, source_target_pairs={{0,4},{1,5},{2,6},{3,7},{4,0},{5,1},{6,2},{7,3},{8,12},{9,13},{10,... | collective-permute-start | bytes 1179656 | tf_op jit(solution)/shard_map/ppermute | solution.py:358
  74.6 2.2 %copy-start.2 = (bf16[2048,768]{1,0:T(8,128)(2,1)S(1)}, bf16[2048,768]{1,0:T(8,128)(2,1)}, u32[]{:S(2)}) copy-start(bf16[2048,768]{1,0:T(8,128)(2,1)} %refs_3_.1) | copy-start | bytes 9437188
  75.1 16.6 %collective-permute-start.12 = (bf16[2,2,2,64,640]{4,3,2,0,1:T(8,128)(2,1)S(1)}, bf16[2,2,2,64,640]{4,3,2,0,1:T(8,128)(2,1)S(1)}, u32[]{:S(2)}, u32[]{:S(2)}) collective-permute-start(bf16[2,2,2,64,640]{4,3,2,0,1:T(8,128)(2,1)S(1)} %get-tuple-element.84), channel_id=1, source_target_pairs={{0,8},{1,9},{2,10},{3,11},{4,12},{5,13},{6,14},{7,15},{8,0},{9,1},... | collective-permute-start | bytes 1966088 | tf_op jit(solution)/shard_map/ppermute | solution.py:358
  83.1 10.2 %collective-permute-start.13 = (bf16[2,2,32,768]{3,2,1,0:T(8,128)(2,1)S(1)}, bf16[2,2,32,768]{3,2,1,0:T(8,128)(2,1)S(1)}, u32[]{:S(2)}, u32[]{:S(2)}) collective-permute-start(bf16[2,2,32,768]{3,2,1,0:T(8,128)(2,1)S(1)} %get-tuple-element.92), channel_id=1, source_target_pairs={{0,4},{1,5},{2,6},{3,7},{4,0},{5,1},{6,2},{7,3},{8,12},{9,13},{10,... | collective-permute-start | bytes 589832 | tf_op jit(solution)/shard_map/ppermute | solution.py:358
  83.3 9.9 %collective-permute-start.14 = (bf16[2,2,32,768]{3,2,1,0:T(8,128)(2,1)S(1)}, bf16[2,2,32,768]{3,2,1,0:T(8,128)(2,1)S(1)}, u32[]{:S(2)}, u32[]{:S(2)}) collective-permute-start(bf16[2,2,32,768]{3,2,1,0:T(8,128)(2,1)S(1)} %get-tuple-element.94), channel_id=1, source_target_pairs={{0,1},{1,0},{2,3},{3,2},{4,5},{5,4},{6,7},{7,6},{8,9},{9,8},{10,11... | collective-permute-start | bytes 589832 | tf_op jit(solution)/shard_map/ppermute | solution.py:358
  91.9 5.4 %collective-permute-start.16 = (bf16[2,2,32,640]{3,2,1,0:T(8,128)(2,1)S(1)}, bf16[2,2,32,640]{3,2,1,0:T(8,128)(2,1)S(1)}, u32[]{:S(2)}, u32[]{:S(2)}) collective-permute-start(bf16[2,2,32,640]{3,2,1,0:T(8,128)(2,1)S(1)} %get-tuple-element.86), channel_id=1, source_target_pairs={{0,4},{1,5},{2,6},{3,7},{4,0},{5,1},{6,2},{7,3},{8,12},{9,13},{10,... | collective-permute-start | bytes 491528 | tf_op jit(solution)/shard_map/ppermute | solution.py:358
  92.3 5.4 %collective-permute-start.15 = (bf16[2,2,32,640]{3,2,1,0:T(8,128)(2,1)S(1)}, bf16[2,2,32,640]{3,2,1,0:T(8,128)(2,1)S(1)}, u32[]{:S(2)}, u32[]{:S(2)}) collective-permute-start(bf16[2,2,32,640]{3,2,1,0:T(8,128)(2,1)S(1)} %get-tuple-element.88), channel_id=1, source_target_pairs={{0,1},{1,0},{2,3},{3,2},{4,5},{5,4},{6,7},{7,6},{8,9},{9,8},{10,11... | collective-permute-start | bytes 491528 | tf_op jit(solution)/shard_map/ppermute | solution.py:358
  93.3 6.7 %collective-permute-start.17 = (bf16[2,64,768]{2,1,0:T(8,128)(2,1)S(1)}, bf16[2,64,768]{2,1,0:T(8,128)(2,1)S(1)}, u32[]{:S(2)}, u32[]{:S(2)}) collective-permute-start(bf16[2,64,768]{2,1,0:T(8,128)(2,1)S(1)} %get-tuple-element.90), channel_id=1, source_target_pairs={{0,8},{1,9},{2,10},{3,11},{4,12},{5,13},{6,14},{7,15},{8,0},{9,1},... | collective-permute-start | bytes 589832 | tf_op jit(solution)/shard_map/ppermute | solution.py:358
  97.3 5.5 %collective-permute-start.20 = (bf16[2,32,640]{2,1,0:T(8,128)(2,1)S(1)}, bf16[2,32,640]{2,1,0:T(8,128)(2,1)S(1)}, u32[]{:S(2)}, u32[]{:S(2)}) collective-permute-start(bf16[2,32,640]{2,1,0:T(8,128)(2,1)S(1)} %get-tuple-element.100), channel_id=1, source_target_pairs={{0,1},{1,0},{2,3},{3,2},{4,5},{5,4},{6,7},{7,6},{8,9},{9,8},{10,11... | collective-permute-start | bytes 245768 | tf_op jit(solution)/shard_map/ppermute | solution.py:358
  97.8 5.1 %collective-permute-start.19 = (bf16[2,32,640]{2,1,0:T(8,128)(2,1)S(1)}, bf16[2,32,640]{2,1,0:T(8,128)(2,1)S(1)}, u32[]{:S(2)}, u32[]{:S(2)}) collective-permute-start(bf16[2,32,640]{2,1,0:T(8,128)(2,1)S(1)} %get-tuple-element.98), channel_id=1, source_target_pairs={{0,4},{1,5},{2,6},{3,7},{4,0},{5,1},{6,2},{7,3},{8,12},{9,13},{10,... | collective-permute-start | bytes 245768 | tf_op jit(solution)/shard_map/ppermute | solution.py:358
  100.1 6.9 %collective-permute-start.18 = (bf16[64,768]{1,0:T(8,128)(2,1)S(1)}, bf16[64,768]{1,0:T(8,128)(2,1)S(1)}, u32[]{:S(2)}, u32[]{:S(2)}) collective-permute-start(bf16[64,768]{1,0:T(8,128)(2,1)S(1)} %slice_bitcast_fusion.14), channel_id=1, source_target_pairs={{0,16},{1,17},{2,18},{3,19},{4,20},{5,21},{6,22},{7,23},{8,24},{9,... | collective-permute-start | bytes 294920 | tf_op jit(solution)/shard_map/ppermute | solution.py:358
  102.9 6.3 %collective-permute-start.21 = (bf16[64,640]{1,0:T(8,128)(2,1)S(1)}, bf16[64,640]{1,0:T(8,128)(2,1)S(1)}, u32[]{:S(2)}, u32[]{:S(2)}) collective-permute-start(bf16[64,640]{1,0:T(8,128)(2,1)S(1)} %get-tuple-element.96), channel_id=1, source_target_pairs={{0,16},{1,17},{2,18},{3,19},{4,20},{5,21},{6,22},{7,23},{8,24},{9,... | collective-permute-start | bytes 245768 | tf_op jit(solution)/shard_map/ppermute | solution.py:358

commit v13 on v10

--- a/solution.py
+++ b/solution.py
@@ -59,6 +59,8 @@
             d = jnp.sum(total, axis=1, keepdims=True)
             n = jnp.where(d > 0.0, lax.rsqrt(d), 0.0)
             nimg_ref[q - tiles] = jnp.broadcast_to(n, (TILE, TILE))
+            for k, (src, dst) in enumerate(zip((pat_ref, pat_t_ref, nimg_ref), outs)):
+                pltpu.make_async_copy(src.at[q - tiles], dst.at[q - tiles], sems.at[k]).start()
 
     def edge_body(q, c):
         one(q, False)
@@ -74,8 +76,6 @@
         pltpu.make_async_copy(src, dst, sems.at[k])
         for k, (src, dst) in enumerate(zip((pat_ref, pat_t_ref, nimg_ref, ncap_ref), outs))
     ]
-    for copy in copies[:3]:
-        copy.start()
     lax.fori_loop(tiles + mid, all_tiles, edge_body, 0)
     for m in range(mid):
         d = deg_ref[m + 2 * tiles]

time: 110 us -> 110 us (level)
  Pallas kernels: 38.3 us -> 36.5 us
  starting transfers between devices: 41.7 us -> 43.5 us
    ppermute x16, starting transfers between devices: 27.2 us -> 29 us  [flipped(): return lax.ppermute(array, AXES, [(i, i ^ mask) for i in range(count)])]
    pallas_call x1, Pallas kernels: 7.82 us -> 6.06 us  [make_tiles(): pl.pallas_call(lambda *r: tiles_kernel(*r, tiles=tiles, slots=slots), out...]
  transfers between devices with their start and end apart: 22 -> 22, of which waited for: 9 -> 9; matrix products, arithmetic and copies ran while one was open for 12% -> 12% of each run, Pallas kernels for 18% -> 17%
where the time goes in v13:
time: 110 us; the launch traced here: 109 us
  starting transfers between devices  43.5 us (40%)
  Pallas kernels  36.5 us (33%)
  waiting for transfers between devices  13.1 us (12%)
  matrix products  7.41 us (7%)
  other arithmetic  6.62 us (6%)
  local copies, waits for them, and re-layouts  1.22 us (1%)
    ppermute x16, starting transfers between devices, flipped(): return lax.ppermute(array, AXES, [(i, i ^ mask) for i in range(count)])  29 us
    pallas_call x5, Pallas kernels, over_hidden(): pl.pallas_call(kernel, out_shape=out_shape, grid_spec=pltpu.PrefetchScala...  17.9 us
    ppermute x16, waiting for transfers between devices, flipped(): return lax.ppermute(array, AXES, [(i, i ^ mask) for i in range(count)])  13.1 us
    pallas_call x1, Pallas kernels, propagate(): pl.pallas_call(lambda *r: hops_kernel(*r, tiles=tiles, slots=slots, width...  10.4 us
    ppermute x4, starting transfers between devices, moved(): lax.ppermute(array, AXES, [(i, i + by) for i in range(count) if 0 <= i +...  9.53 us
    dot_general x1, matrix products, per_device(): lax.dot_general(w_in, feats, across, preferred_element_type=F32)  7.41 us
    pallas_call x1, Pallas kernels, make_tiles(): pl.pallas_call(lambda *r: tiles_kernel(*r, tiles=tiles, slots=slots), out...  6.06 us
    ppermute x1, starting transfers between devices, per_device(): far = lax.ppermute(mate, AXES, nearest_pair(count, 2))  4.29 us
  transfers between devices with their start and end apart: 22, of which 9 were waited for; matrix products, arithmetic and copies ran while one was open for 12% of the time, Pallas kernels for 17%

profile of v13, /device:TPU:0, one launch (start us, length us, event | category | flops | bytes accessed | tf_op | source)
XLA Modules:
  0.0 109.4 jit_solution(9351431525560021752)
XLA Ops:
  0.6 2.1 %stack.1 = (bf16[768,512]{1,0:T(8,128)(2,1)}, s32[3,12]{1,0:T(4,128)}) custom-call(s32[3]{0:T(128)} %count_ref.1, bf16[384,512]{1,0:T(8,128)(2,1)} %top_ref.1, bf16[384,512]{1,0:T(8,128)(2,1)} %bottom_ref.1, s32[3,4]{1,0:T(4,128)} %seed_ref.1, s32[3,4]{1,0:T(4,128)} %cols_ref.1), custom_call_target="tpu_custom_call" | custom-call | flops 1 | bytes 1 | tf_op jit(solution)/shard_map/stack/pallas_call | solution.py:338
  3.4 5.7 %collective-permute-start = (s32[3,12]{1,0:T(4,128)}, s32[3,12]{1,0:T(4,128)S(1)}, u32[]{:S(2)}, u32[]{:S(2)}) collective-permute-start(s32[3,12]{1,0:T(4,128)} %get-tuple-element.38), channel_id=1, source_target_pairs={{0,1},{1,0},{2,3},{3,2},{4,5},{5,4},{6,7},{7,6},{8,9},{9,8},{10,11... | collective-permute-start | bytes 440 | tf_op jit(solution)/shard_map/ppermute | solution.py:357
  9.9 1.0 collective-permute-done
  10.9 2.0 %collective-permute-start.6 = (bf16[768,512]{1,0:T(8,128)(2,1)}, bf16[768,512]{1,0:T(8,128)(2,1)}, u32[]{:S(2)}, u32[]{:S(2)}) collective-permute-start(bf16[768,512]{1,0:T(8,128)(2,1)} %get-tuple-element.40.r_2_), channel_id=1, source_target_pairs={{0,1},{1,0},{2,3},{3,2},{4,5},{5,4},{6,7},{7,6},{8,9},{9,8},{10,11... | collective-permute-start | bytes 2359304 | tf_op jit(solution)/shard_map/ppermute | solution.py:357
  12.9 1.3 %collective-permute-start.5 = (bf16[768,512]{1,0:T(8,128)(2,1)}, bf16[768,512]{1,0:T(8,128)(2,1)}, u32[]{:S(2)}, u32[]{:S(2)}) collective-permute-start(bf16[768,512]{1,0:T(8,128)(2,1)} %get-tuple-element.40.r_2_), channel_id=1, source_target_pairs={{2,0},{3,1},{4,2},{5,3},{6,4},{7,5},{8,6},{9,7},{10,8},{11,9},{12,... | collective-permute-start | bytes 2359304 | tf_op jit(solution)/shard_map/ppermute | solution.py:353
  14.2 3.9 %collective-permute-start.4 = (bf16[768,512]{1,0:T(8,128)(2,1)}, bf16[768,512]{1,0:T(8,128)(2,1)}, u32[]{:S(2)}, u32[]{:S(2)}) collective-permute-start(bf16[768,512]{1,0:T(8,128)(2,1)} %get-tuple-element.40.r_2_), channel_id=1, source_target_pairs={{0,2},{1,3},{2,4},{3,5},{4,6},{5,7},{6,8},{7,9},{8,10},{9,11},{10,... | collective-permute-start | bytes 2359304 | tf_op jit(solution)/shard_map/ppermute | solution.py:353
  18.1 1.3 %pad_maximum_fusion.refs_9_ = bf16[768,768]{1,0:T(8,128)(2,1)S(1)} fusion(bf16[384,768]{1,0:T(8,128)(2,1)} %param.13, bf16[384,768]{1,0:T(8,128)(2,1)} %param.12), kind=kLoop, calls=%fused_computation.15 | loop fusion | flops 2359296 | bytes 2359296 | tf_op jit(solution)/shard_map/concatenate | solution.py:425
  20.2 1.3 %collective-permute-start.3 = (s32[6,12]{1,0:T(8,128)S(1)}, s32[6,12]{1,0:T(8,128)S(1)}, u32[]{:S(2)}, u32[]{:S(2)}) collective-permute-start(s32[6,12]{1,0:T(8,128)S(1)} %add_select_fusion.1), channel_id=1, source_target_pairs={{2,0},{3,1},{4,2},{5,3},{6,4},{7,5},{8,6},{9,7},{10,8},{11,9},{12,... | collective-permute-start | bytes 872 | tf_op jit(solution)/shard_map/ppermute | solution.py:353
  21.5 3.0 %collective-permute-start.2 = (s32[6,12]{1,0:T(8,128)S(1)}, s32[6,12]{1,0:T(8,128)S(1)}, u32[]{:S(2)}, u32[]{:S(2)}) collective-permute-start(s32[6,12]{1,0:T(8,128)S(1)} %add_select_fusion.1), channel_id=1, source_target_pairs={{0,2},{1,3},{2,4},{3,5},{4,6},{5,7},{6,8},{7,9},{8,10},{9,11},{10,... | collective-permute-start | bytes 872 | tf_op jit(solution)/shard_map/ppermute | solution.py:353
  24.6 7.4 %fusion.3 = (f32[2048,768]{1,0:T(8,128)}, bf16[2048,768]{1,0:T(8,128)(2,1)S(1)}) fusion(f32[2048]{0:T(1024)S(1)} %copy-done.5, bf16[768,768]{1,0:T(8,128)(2,1)S(1)} %pad_maximum_fusion.refs_9_, bf16[2048,768]{1,0:T(8,128)(2,1)} %refs_3_.1), kind=kOutput, calls=%fused_computation.4 | convolution fusion | flops 2433220608 | bytes 13770752 | tf_op jit(solution)/shard_map/dot_general | solution.py:460
  32.0 4.3 %collective-permute-start.7 = (bf16[768,512]{1,0:T(8,128)(2,1)}, bf16[768,512]{1,0:T(8,128)(2,1)}, u32[]{:S(2)}, u32[]{:S(2)}) collective-permute-start(bf16[768,512]{1,0:T(8,128)(2,1)} %collective-permute-done.6.r_5_), channel_id=1, source_target_pairs={{0,2},{2,4},{4,6},{6,8},{8,10},{10,12},{12,14},{14,16},{16,18},{18... | collective-permute-start | bytes 2359304 | tf_op jit(solution)/shard_map/ppermute | solution.py:423
  37.0 6.1 %tiles.1 = (bf16[15,128,512]{2,1,0:T(8,128)(2,1)}, bf16[15,512,128]{2,1,0:T(8,128)(2,1)}, f32[15,128,128]{2,1,0:T(8,128)}, f32[15,128,128]{2,1,0:T(8,128)}) custom-call(s32[84]{0:T(128)S(1)} %reshape.40.r_0_, s32[84]{0:T(128)S(1)} %reshape.41.r_1_, s32[21]{0:T(128)S(1)} %slice_reduce_fusion.r_2_), custom_call_target="tpu_custom_call" | custom-call | flops 1 | bytes 1 | tf_op jit(solution)/shard_map/tiles/pallas_call | solution.py:103
  43.2 10.4 %hops.1.refs_8_.refs_4_ = bf16[768,512]{1,0:T(8,128)(2,1)S(1)} custom-call(s32[60]{0:T(128)S(1)} %reshape.39.r_0_, s32[2]{0:T(128)S(1)} %fusion.18.r_1_, bf16[768,512]{1,0:T(8,128)(2,1)} %get-tuple-element.40.r_2_, bf16[768,512]{1,0:T(8,128)(2,1)} %collective-permute-done.4.r_3_, bf16[768,512]{1,0:T(8,128)(2,1)} %collective-permute-done.5.r_4_, ...), custom_call_target="tpu_custom_call" | custom-call | flops 1 | bytes 1 | tf_op jit(solution)/shard_map/hops/pallas_call | solution.py:207
  53.7 3.8 %part_in.2 = (bf16[1024,896]{1,0:T(8,128)(2,1)S(1)}, bf16[1024,768]{1,0:T(8,128)(2,1)S(1)}) custom-call(s32[16]{0:T(128)S(1)} %get-tuple-element.98.order_ref, f32[2048,768]{1,0:T(8,128)S(1)} %copy-done, f32[2048,768]{1,0:T(8,128)S(1)} %copy-done, f32[2048,768]{1,0:T(8,128)S(1)} %copy-done, f32[2048,768]{1,0:T(8,128)S(1)} %copy-done, ...), custom_call_target="tpu_custom_call" | custom-call | flops 1 | bytes 1 | tf_op jit(solution)/shard_map/part_in/pallas_call | solution.py:291
  57.7 1.5 %collective-permute-start.8 = (bf16[2,2,2,2,64,896]{5,4,3,2,0,1:T(8,128)(2,1)S(1)}, bf16[2,2,2,2,64,896]{5,4,3,2,0,1:T(8,128)(2,1)S(1)}, u32[]{:S(2)}, u32[]{:S(2)}) collective-permute-start(bf16[2,2,2,2,64,896]{5,4,3,2,0,1:T(8,128)(2,1)S(1)} %copy.25), channel_id=1, source_target_pairs={{0,2},{1,3},{2,0},{3,1},{4,6},{5,7},{6,4},{7,5},{8,10},{9,11},{10,... | collective-permute-start | bytes 5505032 | tf_op jit(solution)/shard_map/ppermute | solution.py:357
  59.2 3.8 %part_in.3 = (bf16[1024,896]{1,0:T(8,128)(2,1)S(1)}, bf16[1024,768]{1,0:T(8,128)(2,1)S(1)}) custom-call(s32[16]{0:T(128)S(1)} %get-tuple-element.99.order_ref, f32[2048,768]{1,0:T(8,128)S(1)} %copy-done, f32[2048,768]{1,0:T(8,128)S(1)} %copy-done, f32[2048,768]{1,0:T(8,128)S(1)} %copy-done, f32[2048,768]{1,0:T(8,128)S(1)} %copy-done, ...), custom_call_target="tpu_custom_call" | custom-call | flops 1 | bytes 1 | tf_op jit(solution)/shard_map/part_in/pallas_call | solution.py:291
  63.8 2.0 %part_out.2 = bf16[1024,512]{1,0:T(8,128)(2,1)S(1)} custom-call(s32[16]{0:T(128)S(1)} %get-tuple-element.98.order_ref, bf16[2048,768]{1,0:T(8,128)(2,1)S(1)} %get-tuple-element.53.refs_0_.refs_1_.refs_2_.refs_3_, bf16[2048,768]{1,0:T(8,128)(2,1)S(1)} %get-tuple-element.53.refs_0_.refs_1_.refs_2_.refs_3_, ...), custom_call_target="tpu_custom_call" | custom-call | flops 1 | bytes 1 | tf_op jit(solution)/shard_map/part_out/pallas_call | solution.py:291
  66.0 3.0 %collective-permute-start.10 = (bf16[2,2,2,32,896]{4,3,2,1,0:T(8,128)(2,1)S(1)}, bf16[2,2,2,32,896]{4,3,2,1,0:T(8,128)(2,1)S(1)}, u32[]{:S(2)}, u32[]{:S(2)}) collective-permute-start(bf16[2,2,2,32,896]{4,3,2,1,0:T(8,128)(2,1)S(1)} %get-tuple-element.76), channel_id=1, source_target_pairs={{0,1},{1,0},{2,3},{3,2},{4,5},{5,4},{6,7},{7,6},{8,9},{9,8},{10,11... | collective-permute-start | bytes 1376264 | tf_op jit(solution)/shard_map/ppermute | solution.py:357
  69.0 4.2 %collective-permute-start.11 = (bf16[2,2,2,32,896]{4,3,2,1,0:T(8,128)(2,1)S(1)}, bf16[2,2,2,32,896]{4,3,2,1,0:T(8,128)(2,1)S(1)}, u32[]{:S(2)}, u32[]{:S(2)}) collective-permute-start(bf16[2,2,2,32,896]{4,3,2,1,0:T(8,128)(2,1)S(1)} %get-tuple-element.78), channel_id=1, source_target_pairs={{0,4},{1,5},{2,6},{3,7},{4,0},{5,1},{6,2},{7,3},{8,12},{9,13},{10,... | collective-permute-start | bytes 1376264 | tf_op jit(solution)/shard_map/ppermute | solution.py:357
  73.2 2.0 %part_out.3 = bf16[1024,512]{1,0:T(8,128)(2,1)S(1)} custom-call(s32[16]{0:T(128)S(1)} %get-tuple-element.99.order_ref, bf16[2048,768]{1,0:T(8,128)(2,1)S(1)} %get-tuple-element.53.refs_0_.refs_1_.refs_2_.refs_3_, bf16[2048,768]{1,0:T(8,128)(2,1)S(1)} %get-tuple-element.53.refs_0_.refs_1_.refs_2_.refs_3_, ...), custom_call_target="tpu_custom_call" | custom-call | flops 1 | bytes 1 | tf_op jit(solution)/shard_map/part_out/pallas_call | solution.py:291
  75.7 1.7 %collective-permute-start.12 = (bf16[2,2,2,64,512]{4,3,2,0,1:T(8,128)(2,1)S(1)}, bf16[2,2,2,64,512]{4,3,2,0,1:T(8,128)(2,1)S(1)}, u32[]{:S(2)}, u32[]{:S(2)}) collective-permute-start(bf16[2,2,2,64,512]{4,3,2,0,1:T(8,128)(2,1)S(1)} %get-tuple-element.80), channel_id=1, source_target_pairs={{0,8},{1,9},{2,10},{3,11},{4,12},{5,13},{6,14},{7,15},{8,0},{9,1},... | collective-permute-start | bytes 1572872 | tf_op jit(solution)/shard_map/ppermute | solution.py:357
  77.4 6.2 %feat_grad.1 = (bf16[384,768]{1,0:T(8,128)(2,1)}, bf16[384,768]{1,0:T(8,128)(2,1)}) custom-call(s32[32]{0:T(128)S(1)} %fusion.31.order_ref, bf16[2048,768]{1,0:T(8,128)(2,1)S(1)} %copy-done.2, bf16[2048,768]{1,0:T(8,128)(2,1)S(1)} %copy-done.2, bf16[2048,768]{1,0:T(8,128)(2,1)S(1)} %copy-done.2, bf16[2048,768]{1,0:T(8,128)(2,1)S(1)} %copy-done.2, ...), custom_call_target="tpu_custom_call" | custom-call | flops 1 | bytes 1 | tf_op jit(solution)/shard_map/feat_grad/pallas_call | solution.py:291
  84.8 1.8 %collective-permute-start.14 = (bf16[2,2,32,896]{3,2,1,0:T(8,128)(2,1)S(1)}, bf16[2,2,32,896]{3,2,1,0:T(8,128)(2,1)S(1)}, u32[]{:S(2)}, u32[]{:S(2)}) collective-permute-start(bf16[2,2,32,896]{3,2,1,0:T(8,128)(2,1)S(1)} %get-tuple-element.90), channel_id=1, source_target_pairs={{0,1},{1,0},{2,3},{3,2},{4,5},{5,4},{6,7},{7,6},{8,9},{9,8},{10,11... | collective-permute-start | bytes 688136 | tf_op jit(solution)/shard_map/ppermute | solution.py:357
  86.6 2.9 %collective-permute-done.12 = bf16[2,2,2,64,512]{4,3,2,0,1:T(8,128)(2,1)S(1)} collective-permute-done((bf16[2,2,2,64,512]{4,3,2,0,1:T(8,128)(2,1)S(1)}, bf16[2,2,2,64,512]{4,3,2,0,1:T(8,128)(2,1)S(1)}, u32[]{:S(2)}, u32[]{:S(2)}) %collective-permute-start.12) | collective-permute-done | bytes 524320 | tf_op jit(solution)/shard_map/ppermute | solution.py:357
  90.6 1.6 %collective-permute-done.14 = bf16[2,2,32,896]{3,2,1,0:T(8,128)(2,1)S(1)} collective-permute-done((bf16[2,2,32,896]{3,2,1,0:T(8,128)(2,1)S(1)}, bf16[2,2,32,896]{3,2,1,0:T(8,128)(2,1)S(1)}, u32[]{:S(2)}, u32[]{:S(2)}) %collective-permute-start.14) | collective-permute-done | bytes 229408 | tf_op jit(solution)/shard_map/ppermute | solution.py:357
  92.4 1.7 %collective-permute-start.17 = (bf16[2,64,896]{2,1,0:T(8,128)(2,1)S(1)}, bf16[2,64,896]{2,1,0:T(8,128)(2,1)S(1)}, u32[]{:S(2)}, u32[]{:S(2)}) collective-permute-start(bf16[2,64,896]{2,1,0:T(8,128)(2,1)S(1)} %get-tuple-element.86), channel_id=1, source_target_pairs={{0,8},{1,9},{2,10},{3,11},{4,12},{5,13},{6,14},{7,15},{8,0},{9,1},... | collective-permute-start | bytes 688136 | tf_op jit(solution)/shard_map/ppermute | solution.py:357
  94.8 1.9 %collective-permute-start.20 = (bf16[2,32,512]{2,1,0:T(8,128)(2,1)S(1)}, bf16[2,32,512]{2,1,0:T(8,128)(2,1)S(1)}, u32[]{:S(2)}, u32[]{:S(2)}) collective-permute-start(bf16[2,32,512]{2,1,0:T(8,128)(2,1)S(1)} %get-tuple-element.96), channel_id=1, source_target_pairs={{0,1},{1,0},{2,3},{3,2},{4,5},{5,4},{6,7},{7,6},{8,9},{9,8},{10,11... | collective-permute-start | bytes 196616 | tf_op jit(solution)/shard_map/ppermute | solution.py:357
  97.4 1.0 collective-permute-done.17
  99.1 1.9 %collective-permute-done.19 = bf16[2,32,512]{2,1,0:T(8,128)(2,1)S(1)} collective-permute-done((bf16[2,32,512]{2,1,0:T(8,128)(2,1)S(1)}, bf16[2,32,512]{2,1,0:T(8,128)(2,1)S(1)}, u32[]{:S(2)}, u32[]{:S(2)}) %collective-permute-start.19) | collective-permute-done | bytes 65568 | tf_op jit(solution)/shard_map/ppermute | solution.py:357
  101.1 1.3 %collective-permute-start.21 = (bf16[64,512]{1,0:T(8,128)(2,1)S(1)}, bf16[64,512]{1,0:T(8,128)(2,1)S(1)}, u32[]{:S(2)}, u32[]{:S(2)}) collective-permute-start(bf16[64,512]{1,0:T(8,128)(2,1)S(1)} %fusion.16), channel_id=1, source_target_pairs={{0,16},{1,17},{2,18},{3,19},{4,20},{5,21},{6,22},{7,23},{8,24},{9,... | collective-permute-start | bytes 196616 | tf_op jit(solution)/shard_map/ppermute | solution.py:357
  102.4 1.7 %collective-permute-start.18 = (bf16[64,896]{1,0:T(8,128)(2,1)S(1)}, bf16[64,896]{1,0:T(8,128)(2,1)S(1)}, u32[]{:S(2)}, u32[]{:S(2)}) collective-permute-start(bf16[64,896]{1,0:T(8,128)(2,1)S(1)} %get-tuple-element.92), channel_id=1, source_target_pairs={{0,16},{1,17},{2,18},{3,19},{4,20},{5,21},{6,22},{7,23},{8,24},{9,... | collective-permute-start | bytes 344072 | tf_op jit(solution)/shard_map/ppermute | solution.py:357
  104.0 2.8 %collective-permute-done.21 = bf16[64,512]{1,0:T(8,128)(2,1)S(1)} collective-permute-done((bf16[64,512]{1,0:T(8,128)(2,1)S(1)}, bf16[64,512]{1,0:T(8,128)(2,1)S(1)}, u32[]{:S(2)}, u32[]{:S(2)}) %collective-permute-start.21) | collective-permute-done | bytes 65568 | tf_op jit(solution)/shard_map/ppermute | solution.py:357
  (75 shorter events, 11.6 us)
Async XLA Ops:
  0.6 23.9 %copy-start.5 = (f32[2048]{0:T(1024)S(1)}, f32[2048]{0:T(1024)}, u32[]{:S(2)}) copy-start(f32[2048]{0:T(1024)} %param.17) | copy-start | bytes 24580
  2.7 17.5 %collective-permute-start.1 = (s32[3,12]{1,0:T(4,128)}, s32[3,12]{1,0:T(4,128)S(1)}, u32[]{:S(2)}, u32[]{:S(2)}) collective-permute-start(s32[3,12]{1,0:T(4,128)} %get-tuple-element.38), channel_id=1, source_target_pairs={{1,4},{3,6},{5,8},{7,10},{9,12},{11,14},{13,16},{15,18},{17,20},{1... | collective-permute-start | bytes 440 | tf_op jit(solution)/shard_map/ppermute | solution.py:416
  3.4 7.5 %collective-permute-start = (s32[3,12]{1,0:T(4,128)}, s32[3,12]{1,0:T(4,128)S(1)}, u32[]{:S(2)}, u32[]{:S(2)}) collective-permute-start(s32[3,12]{1,0:T(4,128)} %get-tuple-element.38), channel_id=1, source_target_pairs={{0,1},{1,0},{2,3},{3,2},{4,5},{5,4},{6,7},{7,6},{8,9},{9,8},{10,11... | collective-permute-start | bytes 440 | tf_op jit(solution)/shard_map/ppermute | solution.py:357
  10.9 21.1 %collective-permute-start.6 = (bf16[768,512]{1,0:T(8,128)(2,1)}, bf16[768,512]{1,0:T(8,128)(2,1)}, u32[]{:S(2)}, u32[]{:S(2)}) collective-permute-start(bf16[768,512]{1,0:T(8,128)(2,1)} %get-tuple-element.40.r_2_), channel_id=1, source_target_pairs={{0,1},{1,0},{2,3},{3,2},{4,5},{5,4},{6,7},{7,6},{8,9},{9,8},{10,11... | collective-permute-start | bytes 2359304 | tf_op jit(solution)/shard_map/ppermute | solution.py:357
  12.9 30.2 %collective-permute-start.5 = (bf16[768,512]{1,0:T(8,128)(2,1)}, bf16[768,512]{1,0:T(8,128)(2,1)}, u32[]{:S(2)}, u32[]{:S(2)}) collective-permute-start(bf16[768,512]{1,0:T(8,128)(2,1)} %get-tuple-element.40.r_2_), channel_id=1, source_target_pairs={{2,0},{3,1},{4,2},{5,3},{6,4},{7,5},{8,6},{9,7},{10,8},{11,9},{12,... | collective-permute-start | bytes 2359304 | tf_op jit(solution)/shard_map/ppermute | solution.py:353
  14.2 28.9 %collective-permute-start.4 = (bf16[768,512]{1,0:T(8,128)(2,1)}, bf16[768,512]{1,0:T(8,128)(2,1)}, u32[]{:S(2)}, u32[]{:S(2)}) collective-permute-start(bf16[768,512]{1,0:T(8,128)(2,1)} %get-tuple-element.40.r_2_), channel_id=1, source_target_pairs={{0,2},{1,3},{2,4},{3,5},{4,6},{5,7},{6,8},{7,9},{8,10},{9,11},{10,... | collective-permute-start | bytes 2359304 | tf_op jit(solution)/shard_map/ppermute | solution.py:353
  19.4 12.6 %copy-start.3 = (bf16[768,768]{1,0:T(8,128)(2,1)}, bf16[768,768]{1,0:T(8,128)(2,1)S(1)}, u32[]{:S(2)}) copy-start(bf16[768,768]{1,0:T(8,128)(2,1)S(1)} %pad_maximum_fusion.refs_9_) | copy-start | bytes 3538948
  20.2 16.1 %collective-permute-start.3 = (s32[6,12]{1,0:T(8,128)S(1)}, s32[6,12]{1,0:T(8,128)S(1)}, u32[]{:S(2)}, u32[]{:S(2)}) collective-permute-start(s32[6,12]{1,0:T(8,128)S(1)} %add_select_fusion.1), channel_id=1, source_target_pairs={{2,0},{3,1},{4,2},{5,3},{6,4},{7,5},{8,6},{9,7},{10,8},{11,9},{12,... | collective-permute-start | bytes 872 | tf_op jit(solution)/shard_map/ppermute | solution.py:353
  21.5 14.8 %collective-permute-start.2 = (s32[6,12]{1,0:T(8,128)S(1)}, s32[6,12]{1,0:T(8,128)S(1)}, u32[]{:S(2)}, u32[]{:S(2)}) collective-permute-start(s32[6,12]{1,0:T(8,128)S(1)} %add_select_fusion.1), channel_id=1, source_target_pairs={{0,2},{1,3},{2,4},{3,5},{4,6},{5,7},{6,8},{7,9},{8,10},{9,11},{10,... | collective-permute-start | bytes 872 | tf_op jit(solution)/shard_map/ppermute | solution.py:353
  32.0 11.2 %collective-permute-start.7 = (bf16[768,512]{1,0:T(8,128)(2,1)}, bf16[768,512]{1,0:T(8,128)(2,1)}, u32[]{:S(2)}, u32[]{:S(2)}) collective-permute-start(bf16[768,512]{1,0:T(8,128)(2,1)} %collective-permute-done.6.r_5_), channel_id=1, source_target_pairs={{0,2},{2,4},{4,6},{6,8},{8,10},{10,12},{12,14},{14,16},{16,18},{18... | collective-permute-start | bytes 2359304 | tf_op jit(solution)/shard_map/ppermute | solution.py:423
  43.2 10.5 %copy-start = (f32[2048,768]{1,0:T(8,128)S(1)}, f32[2048,768]{1,0:T(8,128)}, u32[]{:S(2)}) copy-start(f32[2048,768]{1,0:T(8,128)} %get-tuple-element.43.refs_0_.refs_1_.refs_2_.refs_3_) | copy-start | bytes 18874372
  43.2 10.5 %copy-start.1 = (bf16[2048,512]{1,0:T(8,128)(2,1)S(1)}, bf16[2048,512]{1,0:T(8,128)(2,1)}, u32[]{:S(2)}) copy-start(bf16[2048,512]{1,0:T(8,128)(2,1)} %refs_7_.3) | copy-start | bytes 6291460
  43.2 10.5 %copy-start.4 = (bf16[768,768]{1,0:T(8,128)(2,1)S(1)}, bf16[768,768]{1,0:T(8,128)(2,1)}, u32[]{:S(2)}) copy-start(bf16[768,768]{1,0:T(8,128)(2,1)} %copy-done.3) | copy-start | bytes 3538948
  57.7 5.4 %collective-permute-start.8 = (bf16[2,2,2,2,64,896]{5,4,3,2,0,1:T(8,128)(2,1)S(1)}, bf16[2,2,2,2,64,896]{5,4,3,2,0,1:T(8,128)(2,1)S(1)}, u32[]{:S(2)}, u32[]{:S(2)}) collective-permute-start(bf16[2,2,2,2,64,896]{5,4,3,2,0,1:T(8,128)(2,1)S(1)} %copy.25), channel_id=1, source_target_pairs={{0,2},{1,3},{2,0},{3,1},{4,6},{5,7},{6,4},{7,5},{8,10},{9,11},{10,... | collective-permute-start | bytes 5505032 | tf_op jit(solution)/shard_map/ppermute | solution.py:357
  65.9 9.4 %collective-permute-start.9 = (bf16[2,2,2,2,64,512]{5,4,3,0,1,2:T(8,128)(2,1)S(1)}, bf16[2,2,2,2,64,512]{5,4,3,0,1,2:T(8,128)(2,1)S(1)}, u32[]{:S(2)}, u32[]{:S(2)}) collective-permute-start(bf16[2,2,2,2,64,512]{5,4,3,0,1,2:T(8,128)(2,1)S(1)} %copy.28), channel_id=1, source_target_pairs={{0,2},{1,3},{2,0},{3,1},{4,6},{5,7},{6,4},{7,5},{8,10},{9,11},{10,... | collective-permute-start | bytes 3145736 | tf_op jit(solution)/shard_map/ppermute | solution.py:357
  66.0 17.6 %collective-permute-start.10 = (bf16[2,2,2,32,896]{4,3,2,1,0:T(8,128)(2,1)S(1)}, bf16[2,2,2,32,896]{4,3,2,1,0:T(8,128)(2,1)S(1)}, u32[]{:S(2)}, u32[]{:S(2)}) collective-permute-start(bf16[2,2,2,32,896]{4,3,2,1,0:T(8,128)(2,1)S(1)} %get-tuple-element.76), channel_id=1, source_target_pairs={{0,1},{1,0},{2,3},{3,2},{4,5},{5,4},{6,7},{7,6},{8,9},{9,8},{10,11... | collective-permute-start | bytes 1376264 | tf_op jit(solution)/shard_map/ppermute | solution.py:357
  69.0 15.6 %collective-permute-start.11 = (bf16[2,2,2,32,896]{4,3,2,1,0:T(8,128)(2,1)S(1)}, bf16[2,2,2,32,896]{4,3,2,1,0:T(8,128)(2,1)S(1)}, u32[]{:S(2)}, u32[]{:S(2)}) collective-permute-start(bf16[2,2,2,32,896]{4,3,2,1,0:T(8,128)(2,1)S(1)} %get-tuple-element.78), channel_id=1, source_target_pairs={{0,4},{1,5},{2,6},{3,7},{4,0},{5,1},{6,2},{7,3},{8,12},{9,13},{10,... | collective-permute-start | bytes 1376264 | tf_op jit(solution)/shard_map/ppermute | solution.py:357
  75.3 2.1 %copy-start.2 = (bf16[2048,768]{1,0:T(8,128)(2,1)S(1)}, bf16[2048,768]{1,0:T(8,128)(2,1)}, u32[]{:S(2)}) copy-start(bf16[2048,768]{1,0:T(8,128)(2,1)} %refs_3_.1) | copy-start | bytes 9437188
  75.7 13.8 %collective-permute-start.12 = (bf16[2,2,2,64,512]{4,3,2,0,1:T(8,128)(2,1)S(1)}, bf16[2,2,2,64,512]{4,3,2,0,1:T(8,128)(2,1)S(1)}, u32[]{:S(2)}, u32[]{:S(2)}) collective-permute-start(bf16[2,2,2,64,512]{4,3,2,0,1:T(8,128)(2,1)S(1)} %get-tuple-element.80), channel_id=1, source_target_pairs={{0,8},{1,9},{2,10},{3,11},{4,12},{5,13},{6,14},{7,15},{8,0},{9,1},... | collective-permute-start | bytes 1572872 | tf_op jit(solution)/shard_map/ppermute | solution.py:357
  83.7 8.5 %collective-permute-start.13 = (bf16[2,2,32,896]{3,2,1,0:T(8,128)(2,1)S(1)}, bf16[2,2,32,896]{3,2,1,0:T(8,128)(2,1)S(1)}, u32[]{:S(2)}, u32[]{:S(2)}) collective-permute-start(bf16[2,2,32,896]{3,2,1,0:T(8,128)(2,1)S(1)} %get-tuple-element.88), channel_id=1, source_target_pairs={{0,4},{1,5},{2,6},{3,7},{4,0},{5,1},{6,2},{7,3},{8,12},{9,13},{10,... | collective-permute-start | bytes 688136 | tf_op jit(solution)/shard_map/ppermute | solution.py:357
  84.8 7.4 %collective-permute-start.14 = (bf16[2,2,32,896]{3,2,1,0:T(8,128)(2,1)S(1)}, bf16[2,2,32,896]{3,2,1,0:T(8,128)(2,1)S(1)}, u32[]{:S(2)}, u32[]{:S(2)}) collective-permute-start(bf16[2,2,32,896]{3,2,1,0:T(8,128)(2,1)S(1)} %get-tuple-element.90), channel_id=1, source_target_pairs={{0,1},{1,0},{2,3},{3,2},{4,5},{5,4},{6,7},{7,6},{8,9},{9,8},{10,11... | collective-permute-start | bytes 688136 | tf_op jit(solution)/shard_map/ppermute | solution.py:357
  89.7 5.0 %collective-permute-start.16 = (bf16[2,2,32,512]{3,2,1,0:T(8,128)(2,1)S(1)}, bf16[2,2,32,512]{3,2,1,0:T(8,128)(2,1)S(1)}, u32[]{:S(2)}, u32[]{:S(2)}) collective-permute-start(bf16[2,2,32,512]{3,2,1,0:T(8,128)(2,1)S(1)} %get-tuple-element.82), channel_id=1, source_target_pairs={{0,4},{1,5},{2,6},{3,7},{4,0},{5,1},{6,2},{7,3},{8,12},{9,13},{10,... | collective-permute-start | bytes 393224 | tf_op jit(solution)/shard_map/ppermute | solution.py:357
  90.0 6.6 %collective-permute-start.15 = (bf16[2,2,32,512]{3,2,1,0:T(8,128)(2,1)S(1)}, bf16[2,2,32,512]{3,2,1,0:T(8,128)(2,1)S(1)}, u32[]{:S(2)}, u32[]{:S(2)}) collective-permute-start(bf16[2,2,32,512]{3,2,1,0:T(8,128)(2,1)S(1)} %get-tuple-element.84), channel_id=1, source_target_pairs={{0,1},{1,0},{2,3},{3,2},{4,5},{5,4},{6,7},{7,6},{8,9},{9,8},{10,11... | collective-permute-start | bytes 393224 | tf_op jit(solution)/shard_map/ppermute | solution.py:357
  92.4 6.1 %collective-permute-start.17 = (bf16[2,64,896]{2,1,0:T(8,128)(2,1)S(1)}, bf16[2,64,896]{2,1,0:T(8,128)(2,1)S(1)}, u32[]{:S(2)}, u32[]{:S(2)}) collective-permute-start(bf16[2,64,896]{2,1,0:T(8,128)(2,1)S(1)} %get-tuple-element.86), channel_id=1, source_target_pairs={{0,8},{1,9},{2,10},{3,11},{4,12},{5,13},{6,14},{7,15},{8,0},{9,1},... | collective-permute-start | bytes 688136 | tf_op jit(solution)/shard_map/ppermute | solution.py:357
  94.8 4.3 %collective-permute-start.20 = (bf16[2,32,512]{2,1,0:T(8,128)(2,1)S(1)}, bf16[2,32,512]{2,1,0:T(8,128)(2,1)S(1)}, u32[]{:S(2)}, u32[]{:S(2)}) collective-permute-start(bf16[2,32,512]{2,1,0:T(8,128)(2,1)S(1)} %get-tuple-element.96), channel_id=1, source_target_pairs={{0,1},{1,0},{2,3},{3,2},{4,5},{5,4},{6,7},{7,6},{8,9},{9,8},{10,11... | collective-permute-start | bytes 196616 | tf_op jit(solution)/shard_map/ppermute | solution.py:357
  96.7 4.3 %collective-permute-start.19 = (bf16[2,32,512]{2,1,0:T(8,128)(2,1)S(1)}, bf16[2,32,512]{2,1,0:T(8,128)(2,1)S(1)}, u32[]{:S(2)}, u32[]{:S(2)}) collective-permute-start(bf16[2,32,512]{2,1,0:T(8,128)(2,1)S(1)} %get-tuple-element.94), channel_id=1, source_target_pairs={{0,4},{1,5},{2,6},{3,7},{4,0},{5,1},{6,2},{7,3},{8,12},{9,13},{10,... | collective-permute-start | bytes 196616 | tf_op jit(solution)/shard_map/ppermute | solution.py:357
  101.1 5.8 %collective-permute-start.21 = (bf16[64,512]{1,0:T(8,128)(2,1)S(1)}, bf16[64,512]{1,0:T(8,128)(2,1)S(1)}, u32[]{:S(2)}, u32[]{:S(2)}) collective-permute-start(bf16[64,512]{1,0:T(8,128)(2,1)S(1)} %fusion.16), channel_id=1, source_target_pairs={{0,16},{1,17},{2,18},{3,19},{4,20},{5,21},{6,22},{7,23},{8,24},{9,... | collective-permute-start | bytes 196616 | tf_op jit(solution)/shard_map/ppermute | solution.py:357
  102.4 5.7 %collective-permute-start.18 = (bf16[64,896]{1,0:T(8,128)(2,1)S(1)}, bf16[64,896]{1,0:T(8,128)(2,1)S(1)}, u32[]{:S(2)}, u32[]{:S(2)}) collective-permute-start(bf16[64,896]{1,0:T(8,128)(2,1)S(1)} %get-tuple-element.92), channel_id=1, source_target_pairs={{0,16},{1,17},{2,18},{3,19},{4,20},{5,21},{6,22},{7,23},{8,24},{9,... | collective-permute-start | bytes 344072 | tf_op jit(solution)/shard_map/ppermute | solution.py:357

commit v14 on v13

--- a/solution.py
+++ b/solution.py
@@ -416,13 +416,13 @@
     third = lax.ppermute(
         meta, AXES, [(i, i + 3) for i in range(1, count - 3, 2)] + [(i, i - 3) for i in range(4, count, 2)]
     )
-    block = after(block, other)
-    mate = flipped(block, count, 1)
+    behind = after(block, other)
+    mate = flipped(behind, count, 1)
     low = moved(block, count, 2)
     high = moved(block, count, -2)
     far = lax.ppermute(mate, AXES, nearest_pair(count, 2))
     pair = jnp.where(even, jnp.concatenate([meta, other]), jnp.concatenate([other, meta]))
-    feats = jnp.concatenate([after(feats_img, block), feats_cap], axis=0)
+    feats = jnp.concatenate([after(feats_img, behind), feats_cap], axis=0)
     pair, feats, third = lax.optimization_barrier((pair, feats, third))
     pair_low = moved(pair, count, 2)
     pair_high = moved(pair, count, -2)

time: 110 us -> 111 us (level)
  waiting for transfers between devices: 13.1 us -> 18.1 us
  starting transfers between devices: 43.5 us -> 39.4 us
    ppermute x16, waiting for transfers between devices: 13.1 us -> 18 us  [flipped(): return lax.ppermute(array, AXES, [(i, i ^ mask) for i in range(count)])]
    ppermute x1, starting transfers between devices: 4.29 us -> 2.25 us  [per_device(): far = lax.ppermute(mate, AXES, nearest_pair(count, 2))]
    ppermute x16, starting transfers between devices: 29 us -> 27 us  [flipped(): return lax.ppermute(array, AXES, [(i, i ^ mask) for i in range(count)])]
  transfers between devices with their start and end apart: 22 -> 22, of which waited for: 9 -> 8; matrix products, arithmetic and copies ran while one was open for 12% -> 12% of each run, Pallas kernels for 17% -> 16%
where the time goes in v14:
time: 111 us; the launch traced here: 110 us
  starting transfers between devices  39.4 us (35%)
  Pallas kernels  36.5 us (33%)
  waiting for transfers between devices  18.1 us (16%)
  matrix products  7.4 us (7%)
  other arithmetic  6.62 us (6%)
  local copies, waits for them, and re-layouts  1.22 us (1%)
    ppermute x16, starting transfers between devices, flipped(): return lax.ppermute(array, AXES, [(i, i ^ mask) for i in range(count)])  27 us
    ppermute x16, waiting for transfers between devices, flipped(): return lax.ppermute(array, AXES, [(i, i ^ mask) for i in range(count)])  18 us
    pallas_call x5, Pallas kernels, over_hidden(): pl.pallas_call(kernel, out_shape=out_shape, grid_spec=pltpu.PrefetchScala...  17.9 us
    pallas_call x1, Pallas kernels, propagate(): pl.pallas_call(lambda *r: hops_kernel(*r, tiles=tiles, slots=slots, width...  10.4 us
    ppermute x4, starting transfers between devices, moved(): lax.ppermute(array, AXES, [(i, i + by) for i in range(count) if 0 <= i +...  9.53 us
    dot_general x1, matrix products, per_device(): lax.dot_general(w_in, feats, across, preferred_element_type=F32)  7.4 us
    pallas_call x1, Pallas kernels, make_tiles(): pl.pallas_call(lambda *r: tiles_kernel(*r, tiles=tiles, slots=slots), out...  6.06 us
    ppermute x1, starting transfers between devices, per_device(): far = lax.ppermute(mate, AXES, nearest_pair(count, 2))  2.25 us
  transfers between devices with their start and end apart: 22, of which 8 were waited for; matrix products, arithmetic and copies ran while one was open for 12% of the time, Pallas kernels for 16%

profile of v14, /device:TPU:0, one launch (start us, length us, event | category | flops | bytes accessed | tf_op | source)
XLA Modules:
  0.0 110.3 jit_solution(14165102858946914937)
XLA Ops:
  0.6 2.1 %stack.1 = (bf16[768,512]{1,0:T(8,128)(2,1)}, s32[3,12]{1,0:T(4,128)}) custom-call(s32[3]{0:T(128)} %count_ref.1, bf16[384,512]{1,0:T(8,128)(2,1)} %top_ref.1, bf16[384,512]{1,0:T(8,128)(2,1)} %bottom_ref.1, s32[3,4]{1,0:T(4,128)} %seed_ref.1, s32[3,4]{1,0:T(4,128)} %cols_ref.1), custom_call_target="tpu_custom_call" | custom-call | flops 1 | bytes 1 | tf_op jit(solution)/shard_map/stack/pallas_call | solution.py:338
  3.4 5.7 %collective-permute-start = (s32[3,12]{1,0:T(4,128)}, s32[3,12]{1,0:T(4,128)S(1)}, u32[]{:S(2)}, u32[]{:S(2)}) collective-permute-start(s32[3,12]{1,0:T(4,128)} %get-tuple-element.38), channel_id=1, source_target_pairs={{0,1},{1,0},{2,3},{3,2},{4,5},{5,4},{6,7},{7,6},{8,9},{9,8},{10,11... | collective-permute-start | bytes 440 | tf_op jit(solution)/shard_map/ppermute | solution.py:357
  9.1 1.3 %collective-permute-start.5 = (bf16[768,512]{1,0:T(8,128)(2,1)}, bf16[768,512]{1,0:T(8,128)(2,1)}, u32[]{:S(2)}, u32[]{:S(2)}) collective-permute-start(bf16[768,512]{1,0:T(8,128)(2,1)} %get-tuple-element.40.r_2_), channel_id=1, source_target_pairs={{2,0},{3,1},{4,2},{5,3},{6,4},{7,5},{8,6},{9,7},{10,8},{11,9},{12,... | collective-permute-start | bytes 2359304 | tf_op jit(solution)/shard_map/ppermute | solution.py:353
  10.4 3.9 %collective-permute-start.4 = (bf16[768,512]{1,0:T(8,128)(2,1)}, bf16[768,512]{1,0:T(8,128)(2,1)}, u32[]{:S(2)}, u32[]{:S(2)}) collective-permute-start(bf16[768,512]{1,0:T(8,128)(2,1)} %get-tuple-element.40.r_2_), channel_id=1, source_target_pairs={{0,2},{1,3},{2,4},{3,5},{4,6},{5,7},{6,8},{7,9},{8,10},{9,11},{10,... | collective-permute-start | bytes 2359304 | tf_op jit(solution)/shard_map/ppermute | solution.py:353
  15.1 1.3 %pad_maximum_fusion.refs_9_ = bf16[768,768]{1,0:T(8,128)(2,1)S(1)} fusion(bf16[384,768]{1,0:T(8,128)(2,1)} %param.13, bf16[384,768]{1,0:T(8,128)(2,1)} %param.12), kind=kLoop, calls=%fused_computation.15 | loop fusion | flops 2359296 | bytes 2359296 | tf_op jit(solution)/shard_map/concatenate | solution.py:425
  17.2 1.3 %collective-permute-start.3 = (s32[6,12]{1,0:T(8,128)S(1)}, s32[6,12]{1,0:T(8,128)S(1)}, u32[]{:S(2)}, u32[]{:S(2)}) collective-permute-start(s32[6,12]{1,0:T(8,128)S(1)} %add_select_fusion.1), channel_id=1, source_target_pairs={{2,0},{3,1},{4,2},{5,3},{6,4},{7,5},{8,6},{9,7},{10,8},{11,9},{12,... | collective-permute-start | bytes 872 | tf_op jit(solution)/shard_map/ppermute | solution.py:353
  18.5 3.0 %collective-permute-start.2 = (s32[6,12]{1,0:T(8,128)S(1)}, s32[6,12]{1,0:T(8,128)S(1)}, u32[]{:S(2)}, u32[]{:S(2)}) collective-permute-start(s32[6,12]{1,0:T(8,128)S(1)} %add_select_fusion.1), channel_id=1, source_target_pairs={{0,2},{1,3},{2,4},{3,5},{4,6},{5,7},{6,8},{7,9},{8,10},{9,11},{10,... | collective-permute-start | bytes 872 | tf_op jit(solution)/shard_map/ppermute | solution.py:353
  21.6 7.4 %fusion.3 = (f32[2048,768]{1,0:T(8,128)}, bf16[2048,768]{1,0:T(8,128)(2,1)S(1)}) fusion(f32[2048]{0:T(1024)S(1)} %copy-done.5, bf16[768,768]{1,0:T(8,128)(2,1)S(1)} %pad_maximum_fusion.refs_9_, bf16[2048,768]{1,0:T(8,128)(2,1)} %refs_3_.1), kind=kOutput, calls=%fused_computation.4 | convolution fusion | flops 2433220608 | bytes 13770752 | tf_op jit(solution)/shard_map/dot_general | solution.py:460
  29.0 6.1 %collective-permute-done.6.r_5_ = bf16[768,512]{1,0:T(8,128)(2,1)} collective-permute-done((bf16[768,512]{1,0:T(8,128)(2,1)}, bf16[768,512]{1,0:T(8,128)(2,1)}, u32[]{:S(2)}, u32[]{:S(2)}) %collective-permute-start.6) | collective-permute-done | bytes 786464 | tf_op jit(solution)/shard_map/ppermute | solution.py:357
  35.1 2.2 %collective-permute-start.7 = (bf16[768,512]{1,0:T(8,128)(2,1)}, bf16[768,512]{1,0:T(8,128)(2,1)}, u32[]{:S(2)}, u32[]{:S(2)}) collective-permute-start(bf16[768,512]{1,0:T(8,128)(2,1)} %collective-permute-done.6.r_5_), channel_id=1, source_target_pairs={{0,2},{2,4},{4,6},{6,8},{8,10},{10,12},{12,14},{14,16},{16,18},{18... | collective-permute-start | bytes 2359304 | tf_op jit(solution)/shard_map/ppermute | solution.py:423
  38.0 6.1 %tiles.1 = (bf16[15,128,512]{2,1,0:T(8,128)(2,1)}, bf16[15,512,128]{2,1,0:T(8,128)(2,1)}, f32[15,128,128]{2,1,0:T(8,128)}, f32[15,128,128]{2,1,0:T(8,128)}) custom-call(s32[84]{0:T(128)S(1)} %reshape.40.r_0_, s32[84]{0:T(128)S(1)} %reshape.41.r_1_, s32[21]{0:T(128)S(1)} %slice_reduce_fusion.r_2_), custom_call_target="tpu_custom_call" | custom-call | flops 1 | bytes 1 | tf_op jit(solution)/shard_map/tiles/pallas_call | solution.py:103
  44.3 10.4 %hops.1.refs_8_.refs_4_ = bf16[768,512]{1,0:T(8,128)(2,1)S(1)} custom-call(s32[60]{0:T(128)S(1)} %reshape.39.r_0_, s32[2]{0:T(128)S(1)} %fusion.18.r_1_, bf16[768,512]{1,0:T(8,128)(2,1)} %get-tuple-element.40.r_2_, bf16[768,512]{1,0:T(8,128)(2,1)} %collective-permute-done.4.r_3_, bf16[768,512]{1,0:T(8,128)(2,1)} %collective-permute-done.5.r_4_, ...), custom_call_target="tpu_custom_call" | custom-call | flops 1 | bytes 1 | tf_op jit(solution)/shard_map/hops/pallas_call | solution.py:207
  54.7 3.8 %part_in.2 = (bf16[1024,896]{1,0:T(8,128)(2,1)S(1)}, bf16[1024,768]{1,0:T(8,128)(2,1)S(1)}) custom-call(s32[16]{0:T(128)S(1)} %get-tuple-element.98.order_ref, f32[2048,768]{1,0:T(8,128)S(1)} %copy-done, f32[2048,768]{1,0:T(8,128)S(1)} %copy-done, f32[2048,768]{1,0:T(8,128)S(1)} %copy-done, f32[2048,768]{1,0:T(8,128)S(1)} %copy-done, ...), custom_call_target="tpu_custom_call" | custom-call | flops 1 | bytes 1 | tf_op jit(solution)/shard_map/part_in/pallas_call | solution.py:291
  58.8 3.2 %collective-permute-start.8 = (bf16[2,2,2,2,64,896]{5,4,3,2,0,1:T(8,128)(2,1)S(1)}, bf16[2,2,2,2,64,896]{5,4,3,2,0,1:T(8,128)(2,1)S(1)}, u32[]{:S(2)}, u32[]{:S(2)}) collective-permute-start(bf16[2,2,2,2,64,896]{5,4,3,2,0,1:T(8,128)(2,1)S(1)} %copy.25), channel_id=1, source_target_pairs={{0,2},{1,3},{2,0},{3,1},{4,6},{5,7},{6,4},{7,5},{8,10},{9,11},{10,... | collective-permute-start | bytes 5505032 | tf_op jit(solution)/shard_map/ppermute | solution.py:357
  61.9 3.8 %part_in.3 = (bf16[1024,896]{1,0:T(8,128)(2,1)S(1)}, bf16[1024,768]{1,0:T(8,128)(2,1)S(1)}) custom-call(s32[16]{0:T(128)S(1)} %get-tuple-element.99.order_ref, f32[2048,768]{1,0:T(8,128)S(1)} %copy-done, f32[2048,768]{1,0:T(8,128)S(1)} %copy-done, f32[2048,768]{1,0:T(8,128)S(1)} %copy-done, f32[2048,768]{1,0:T(8,128)S(1)} %copy-done, ...), custom_call_target="tpu_custom_call" | custom-call | flops 1 | bytes 1 | tf_op jit(solution)/shard_map/part_in/pallas_call | solution.py:291
  66.5 2.0 %part_out.2 = bf16[1024,512]{1,0:T(8,128)(2,1)S(1)} custom-call(s32[16]{0:T(128)S(1)} %get-tuple-element.98.order_ref, bf16[2048,768]{1,0:T(8,128)(2,1)S(1)} %get-tuple-element.53.refs_0_.refs_1_.refs_2_.refs_3_, bf16[2048,768]{1,0:T(8,128)(2,1)S(1)} %get-tuple-element.53.refs_0_.refs_1_.refs_2_.refs_3_, ...), custom_call_target="tpu_custom_call" | custom-call | flops 1 | bytes 1 | tf_op jit(solution)/shard_map/part_out/pallas_call | solution.py:291
  68.7 1.8 %collective-permute-start.10 = (bf16[2,2,2,32,896]{4,3,2,1,0:T(8,128)(2,1)S(1)}, bf16[2,2,2,32,896]{4,3,2,1,0:T(8,128)(2,1)S(1)}, u32[]{:S(2)}, u32[]{:S(2)}) collective-permute-start(bf16[2,2,2,32,896]{4,3,2,1,0:T(8,128)(2,1)S(1)} %get-tuple-element.76), channel_id=1, source_target_pairs={{0,1},{1,0},{2,3},{3,2},{4,5},{5,4},{6,7},{7,6},{8,9},{9,8},{10,11... | collective-permute-start | bytes 1376264 | tf_op jit(solution)/shard_map/ppermute | solution.py:357
  70.5 2.2 %collective-permute-start.11 = (bf16[2,2,2,32,896]{4,3,2,1,0:T(8,128)(2,1)S(1)}, bf16[2,2,2,32,896]{4,3,2,1,0:T(8,128)(2,1)S(1)}, u32[]{:S(2)}, u32[]{:S(2)}) collective-permute-start(bf16[2,2,2,32,896]{4,3,2,1,0:T(8,128)(2,1)S(1)} %get-tuple-element.78), channel_id=1, source_target_pairs={{0,4},{1,5},{2,6},{3,7},{4,0},{5,1},{6,2},{7,3},{8,12},{9,13},{10,... | collective-permute-start | bytes 1376264 | tf_op jit(solution)/shard_map/ppermute | solution.py:357
  72.7 2.0 %part_out.3 = bf16[1024,512]{1,0:T(8,128)(2,1)S(1)} custom-call(s32[16]{0:T(128)S(1)} %get-tuple-element.99.order_ref, bf16[2048,768]{1,0:T(8,128)(2,1)S(1)} %get-tuple-element.53.refs_0_.refs_1_.refs_2_.refs_3_, bf16[2048,768]{1,0:T(8,128)(2,1)S(1)} %get-tuple-element.53.refs_0_.refs_1_.refs_2_.refs_3_, ...), custom_call_target="tpu_custom_call" | custom-call | flops 1 | bytes 1 | tf_op jit(solution)/shard_map/part_out/pallas_call | solution.py:291
  75.2 1.6 %collective-permute-start.12 = (bf16[2,2,2,64,512]{4,3,2,0,1:T(8,128)(2,1)S(1)}, bf16[2,2,2,64,512]{4,3,2,0,1:T(8,128)(2,1)S(1)}, u32[]{:S(2)}, u32[]{:S(2)}) collective-permute-start(bf16[2,2,2,64,512]{4,3,2,0,1:T(8,128)(2,1)S(1)} %get-tuple-element.80), channel_id=1, source_target_pairs={{0,8},{1,9},{2,10},{3,11},{4,12},{5,13},{6,14},{7,15},{8,0},{9,1},... | collective-permute-start | bytes 1572872 | tf_op jit(solution)/shard_map/ppermute | solution.py:357
  76.8 6.2 %feat_grad.1 = (bf16[384,768]{1,0:T(8,128)(2,1)}, bf16[384,768]{1,0:T(8,128)(2,1)}) custom-call(s32[32]{0:T(128)S(1)} %fusion.31.order_ref, bf16[2048,768]{1,0:T(8,128)(2,1)S(1)} %copy-done.2, bf16[2048,768]{1,0:T(8,128)(2,1)S(1)} %copy-done.2, bf16[2048,768]{1,0:T(8,128)(2,1)S(1)} %copy-done.2, bf16[2048,768]{1,0:T(8,128)(2,1)S(1)} %copy-done.2, ...), custom_call_target="tpu_custom_call" | custom-call | flops 1 | bytes 1 | tf_op jit(solution)/shard_map/feat_grad/pallas_call | solution.py:291
  83.2 1.1 %collective-permute-start.13 = (bf16[2,2,32,896]{3,2,1,0:T(8,128)(2,1)S(1)}, bf16[2,2,32,896]{3,2,1,0:T(8,128)(2,1)S(1)}, u32[]{:S(2)}, u32[]{:S(2)}) collective-permute-start(bf16[2,2,32,896]{3,2,1,0:T(8,128)(2,1)S(1)} %get-tuple-element.88), channel_id=1, source_target_pairs={{0,4},{1,5},{2,6},{3,7},{4,0},{5,1},{6,2},{7,3},{8,12},{9,13},{10,... | collective-permute-start | bytes 688136 | tf_op jit(solution)/shard_map/ppermute | solution.py:357
  84.5 1.6 %collective-permute-start.14 = (bf16[2,2,32,896]{3,2,1,0:T(8,128)(2,1)S(1)}, bf16[2,2,32,896]{3,2,1,0:T(8,128)(2,1)S(1)}, u32[]{:S(2)}, u32[]{:S(2)}) collective-permute-start(bf16[2,2,32,896]{3,2,1,0:T(8,128)(2,1)S(1)} %get-tuple-element.90), channel_id=1, source_target_pairs={{0,1},{1,0},{2,3},{3,2},{4,5},{5,4},{6,7},{7,6},{8,9},{9,8},{10,11... | collective-permute-start | bytes 688136 | tf_op jit(solution)/shard_map/ppermute | solution.py:357
  86.0 2.9 %collective-permute-done.12 = bf16[2,2,2,64,512]{4,3,2,0,1:T(8,128)(2,1)S(1)} collective-permute-done((bf16[2,2,2,64,512]{4,3,2,0,1:T(8,128)(2,1)S(1)}, bf16[2,2,2,64,512]{4,3,2,0,1:T(8,128)(2,1)S(1)}, u32[]{:S(2)}, u32[]{:S(2)}) %collective-permute-start.12) | collective-permute-done | bytes 524320 | tf_op jit(solution)/shard_map/ppermute | solution.py:357
  89.5 1.7 %collective-permute-start.15 = (bf16[2,2,32,512]{3,2,1,0:T(8,128)(2,1)S(1)}, bf16[2,2,32,512]{3,2,1,0:T(8,128)(2,1)S(1)}, u32[]{:S(2)}, u32[]{:S(2)}) collective-permute-start(bf16[2,2,32,512]{3,2,1,0:T(8,128)(2,1)S(1)} %get-tuple-element.84), channel_id=1, source_target_pairs={{0,1},{1,0},{2,3},{3,2},{4,5},{5,4},{6,7},{7,6},{8,9},{9,8},{10,11... | collective-permute-start | bytes 393224 | tf_op jit(solution)/shard_map/ppermute | solution.py:357
  91.5 1.8 %collective-permute-start.17 = (bf16[2,64,896]{2,1,0:T(8,128)(2,1)S(1)}, bf16[2,64,896]{2,1,0:T(8,128)(2,1)S(1)}, u32[]{:S(2)}, u32[]{:S(2)}) collective-permute-start(bf16[2,64,896]{2,1,0:T(8,128)(2,1)S(1)} %get-tuple-element.86), channel_id=1, source_target_pairs={{0,8},{1,9},{2,10},{3,11},{4,12},{5,13},{6,14},{7,15},{8,0},{9,1},... | collective-permute-start | bytes 688136 | tf_op jit(solution)/shard_map/ppermute | solution.py:357
  94.2 1.2 %collective-permute-start.20 = (bf16[2,32,512]{2,1,0:T(8,128)(2,1)S(1)}, bf16[2,32,512]{2,1,0:T(8,128)(2,1)S(1)}, u32[]{:S(2)}, u32[]{:S(2)}) collective-permute-start(bf16[2,32,512]{2,1,0:T(8,128)(2,1)S(1)} %get-tuple-element.96), channel_id=1, source_target_pairs={{0,1},{1,0},{2,3},{3,2},{4,5},{5,4},{6,7},{7,6},{8,9},{9,8},{10,11... | collective-permute-start | bytes 196616 | tf_op jit(solution)/shard_map/ppermute | solution.py:357
  95.5 1.7 %collective-permute-start.19 = (bf16[2,32,512]{2,1,0:T(8,128)(2,1)S(1)}, bf16[2,32,512]{2,1,0:T(8,128)(2,1)S(1)}, u32[]{:S(2)}, u32[]{:S(2)}) collective-permute-start(bf16[2,32,512]{2,1,0:T(8,128)(2,1)S(1)} %get-tuple-element.94), channel_id=1, source_target_pairs={{0,4},{1,5},{2,6},{3,7},{4,0},{5,1},{6,2},{7,3},{8,12},{9,13},{10,... | collective-permute-start | bytes 196616 | tf_op jit(solution)/shard_map/ppermute | solution.py:357
  98.6 1.2 %collective-permute-done.19 = bf16[2,32,512]{2,1,0:T(8,128)(2,1)S(1)} collective-permute-done((bf16[2,32,512]{2,1,0:T(8,128)(2,1)S(1)}, bf16[2,32,512]{2,1,0:T(8,128)(2,1)S(1)}, u32[]{:S(2)}, u32[]{:S(2)}) %collective-permute-start.19) | collective-permute-done | bytes 65568 | tf_op jit(solution)/shard_map/ppermute | solution.py:357
  99.8 2.2 %collective-permute-start.21 = (bf16[64,512]{1,0:T(8,128)(2,1)S(1)}, bf16[64,512]{1,0:T(8,128)(2,1)S(1)}, u32[]{:S(2)}, u32[]{:S(2)}) collective-permute-start(bf16[64,512]{1,0:T(8,128)(2,1)S(1)} %fusion.16), channel_id=1, source_target_pairs={{0,16},{1,17},{2,18},{3,19},{4,20},{5,21},{6,22},{7,23},{8,24},{9,... | collective-permute-start | bytes 196616 | tf_op jit(solution)/shard_map/ppermute | solution.py:357
  102.8 3.1 %collective-permute-done.21 = bf16[64,512]{1,0:T(8,128)(2,1)S(1)} collective-permute-done((bf16[64,512]{1,0:T(8,128)(2,1)S(1)}, bf16[64,512]{1,0:T(8,128)(2,1)S(1)}, u32[]{:S(2)}, u32[]{:S(2)}) %collective-permute-start.21) | collective-permute-done | bytes 65568 | tf_op jit(solution)/shard_map/ppermute | solution.py:357
  106.6 2.4 %collective-permute-done.18 = bf16[64,896]{1,0:T(8,128)(2,1)S(1)} collective-permute-done((bf16[64,896]{1,0:T(8,128)(2,1)S(1)}, bf16[64,896]{1,0:T(8,128)(2,1)S(1)}, u32[]{:S(2)}, u32[]{:S(2)}) %collective-permute-start.18) | collective-permute-done | bytes 114720 | tf_op jit(solution)/shard_map/ppermute | solution.py:357
  (75 shorter events, 10.7 us)
Async XLA Ops:
  0.6 20.9 %copy-start.5 = (f32[2048]{0:T(1024)S(1)}, f32[2048]{0:T(1024)}, u32[]{:S(2)}) copy-start(f32[2048]{0:T(1024)} %param.17) | copy-start | bytes 24580
  2.7 14.5 %collective-permute-start.1 = (s32[3,12]{1,0:T(4,128)}, s32[3,12]{1,0:T(4,128)S(1)}, u32[]{:S(2)}, u32[]{:S(2)}) collective-permute-start(s32[3,12]{1,0:T(4,128)} %get-tuple-element.38), channel_id=1, source_target_pairs={{1,4},{3,6},{5,8},{7,10},{9,12},{11,14},{13,16},{15,18},{17,20},{1... | collective-permute-start | bytes 440 | tf_op jit(solution)/shard_map/ppermute | solution.py:416
  3.4 11.7 %collective-permute-start = (s32[3,12]{1,0:T(4,128)}, s32[3,12]{1,0:T(4,128)S(1)}, u32[]{:S(2)}, u32[]{:S(2)}) collective-permute-start(s32[3,12]{1,0:T(4,128)} %get-tuple-element.38), channel_id=1, source_target_pairs={{0,1},{1,0},{2,3},{3,2},{4,5},{5,4},{6,7},{7,6},{8,9},{9,8},{10,11... | collective-permute-start | bytes 440 | tf_op jit(solution)/shard_map/ppermute | solution.py:357
  9.1 35.1 %collective-permute-start.5 = (bf16[768,512]{1,0:T(8,128)(2,1)}, bf16[768,512]{1,0:T(8,128)(2,1)}, u32[]{:S(2)}, u32[]{:S(2)}) collective-permute-start(bf16[768,512]{1,0:T(8,128)(2,1)} %get-tuple-element.40.r_2_), channel_id=1, source_target_pairs={{2,0},{3,1},{4,2},{5,3},{6,4},{7,5},{8,6},{9,7},{10,8},{11,9},{12,... | collective-permute-start | bytes 2359304 | tf_op jit(solution)/shard_map/ppermute | solution.py:353
  10.4 33.8 %collective-permute-start.4 = (bf16[768,512]{1,0:T(8,128)(2,1)}, bf16[768,512]{1,0:T(8,128)(2,1)}, u32[]{:S(2)}, u32[]{:S(2)}) collective-permute-start(bf16[768,512]{1,0:T(8,128)(2,1)} %get-tuple-element.40.r_2_), channel_id=1, source_target_pairs={{0,2},{1,3},{2,4},{3,5},{4,6},{5,7},{6,8},{7,9},{8,10},{9,11},{10,... | collective-permute-start | bytes 2359304 | tf_op jit(solution)/shard_map/ppermute | solution.py:353
  15.1 20.0 %collective-permute-start.6 = (bf16[768,512]{1,0:T(8,128)(2,1)}, bf16[768,512]{1,0:T(8,128)(2,1)}, u32[]{:S(2)}, u32[]{:S(2)}) collective-permute-start(bf16[768,512]{1,0:T(8,128)(2,1)} %get-tuple-element.40.r_2_), channel_id=1, source_target_pairs={{0,1},{1,0},{2,3},{3,2},{4,5},{5,4},{6,7},{7,6},{8,9},{9,8},{10,11... | collective-permute-start | bytes 2359304 | tf_op jit(solution)/shard_map/ppermute | solution.py:357
  16.4 12.5 %copy-start.3 = (bf16[768,768]{1,0:T(8,128)(2,1)}, bf16[768,768]{1,0:T(8,128)(2,1)S(1)}, u32[]{:S(2)}) copy-start(bf16[768,768]{1,0:T(8,128)(2,1)S(1)} %pad_maximum_fusion.refs_9_) | copy-start | bytes 3538948
  17.2 20.1 %collective-permute-start.3 = (s32[6,12]{1,0:T(8,128)S(1)}, s32[6,12]{1,0:T(8,128)S(1)}, u32[]{:S(2)}, u32[]{:S(2)}) collective-permute-start(s32[6,12]{1,0:T(8,128)S(1)} %add_select_fusion.1), channel_id=1, source_target_pairs={{2,0},{3,1},{4,2},{5,3},{6,4},{7,5},{8,6},{9,7},{10,8},{11,9},{12,... | collective-permute-start | bytes 872 | tf_op jit(solution)/shard_map/ppermute | solution.py:353
  18.5 18.8 %collective-permute-start.2 = (s32[6,12]{1,0:T(8,128)S(1)}, s32[6,12]{1,0:T(8,128)S(1)}, u32[]{:S(2)}, u32[]{:S(2)}) collective-permute-start(s32[6,12]{1,0:T(8,128)S(1)} %add_select_fusion.1), channel_id=1, source_target_pairs={{0,2},{1,3},{2,4},{3,5},{4,6},{5,7},{6,8},{7,9},{8,10},{9,11},{10,... | collective-permute-start | bytes 872 | tf_op jit(solution)/shard_map/ppermute | solution.py:353
  35.1 9.1 %collective-permute-start.7 = (bf16[768,512]{1,0:T(8,128)(2,1)}, bf16[768,512]{1,0:T(8,128)(2,1)}, u32[]{:S(2)}, u32[]{:S(2)}) collective-permute-start(bf16[768,512]{1,0:T(8,128)(2,1)} %collective-permute-done.6.r_5_), channel_id=1, source_target_pairs={{0,2},{2,4},{4,6},{6,8},{8,10},{10,12},{12,14},{14,16},{16,18},{18... | collective-permute-start | bytes 2359304 | tf_op jit(solution)/shard_map/ppermute | solution.py:423
  44.2 10.5 %copy-start = (f32[2048,768]{1,0:T(8,128)S(1)}, f32[2048,768]{1,0:T(8,128)}, u32[]{:S(2)}) copy-start(f32[2048,768]{1,0:T(8,128)} %get-tuple-element.43.refs_0_.refs_1_.refs_2_.refs_3_) | copy-start | bytes 18874372
  44.2 10.5 %copy-start.1 = (bf16[2048,512]{1,0:T(8,128)(2,1)S(1)}, bf16[2048,512]{1,0:T(8,128)(2,1)}, u32[]{:S(2)}) copy-start(bf16[2048,512]{1,0:T(8,128)(2,1)} %refs_7_.3) | copy-start | bytes 6291460
  44.2 10.5 %copy-start.4 = (bf16[768,768]{1,0:T(8,128)(2,1)S(1)}, bf16[768,768]{1,0:T(8,128)(2,1)}, u32[]{:S(2)}) copy-start(bf16[768,768]{1,0:T(8,128)(2,1)} %copy-done.3) | copy-start | bytes 3538948
  58.8 7.0 %collective-permute-start.8 = (bf16[2,2,2,2,64,896]{5,4,3,2,0,1:T(8,128)(2,1)S(1)}, bf16[2,2,2,2,64,896]{5,4,3,2,0,1:T(8,128)(2,1)S(1)}, u32[]{:S(2)}, u32[]{:S(2)}) collective-permute-start(bf16[2,2,2,2,64,896]{5,4,3,2,0,1:T(8,128)(2,1)S(1)} %copy.25), channel_id=1, source_target_pairs={{0,2},{1,3},{2,0},{3,1},{4,6},{5,7},{6,4},{7,5},{8,10},{9,11},{10,... | collective-permute-start | bytes 5505032 | tf_op jit(solution)/shard_map/ppermute | solution.py:357
  68.6 6.1 %collective-permute-start.9 = (bf16[2,2,2,2,64,512]{5,4,3,0,1,2:T(8,128)(2,1)S(1)}, bf16[2,2,2,2,64,512]{5,4,3,0,1,2:T(8,128)(2,1)S(1)}, u32[]{:S(2)}, u32[]{:S(2)}) collective-permute-start(bf16[2,2,2,2,64,512]{5,4,3,0,1,2:T(8,128)(2,1)S(1)} %copy.28), channel_id=1, source_target_pairs={{0,2},{1,3},{2,0},{3,1},{4,6},{5,7},{6,4},{7,5},{8,10},{9,11},{10,... | collective-permute-start | bytes 3145736 | tf_op jit(solution)/shard_map/ppermute | solution.py:357
  68.7 14.3 %collective-permute-start.10 = (bf16[2,2,2,32,896]{4,3,2,1,0:T(8,128)(2,1)S(1)}, bf16[2,2,2,32,896]{4,3,2,1,0:T(8,128)(2,1)S(1)}, u32[]{:S(2)}, u32[]{:S(2)}) collective-permute-start(bf16[2,2,2,32,896]{4,3,2,1,0:T(8,128)(2,1)S(1)} %get-tuple-element.76), channel_id=1, source_target_pairs={{0,1},{1,0},{2,3},{3,2},{4,5},{5,4},{6,7},{7,6},{8,9},{9,8},{10,11... | collective-permute-start | bytes 1376264 | tf_op jit(solution)/shard_map/ppermute | solution.py:357
  70.5 13.8 %collective-permute-start.11 = (bf16[2,2,2,32,896]{4,3,2,1,0:T(8,128)(2,1)S(1)}, bf16[2,2,2,32,896]{4,3,2,1,0:T(8,128)(2,1)S(1)}, u32[]{:S(2)}, u32[]{:S(2)}) collective-permute-start(bf16[2,2,2,32,896]{4,3,2,1,0:T(8,128)(2,1)S(1)} %get-tuple-element.78), channel_id=1, source_target_pairs={{0,4},{1,5},{2,6},{3,7},{4,0},{5,1},{6,2},{7,3},{8,12},{9,13},{10,... | collective-permute-start | bytes 1376264 | tf_op jit(solution)/shard_map/ppermute | solution.py:357
  74.8 2.1 %copy-start.2 = (bf16[2048,768]{1,0:T(8,128)(2,1)S(1)}, bf16[2048,768]{1,0:T(8,128)(2,1)}, u32[]{:S(2)}) copy-start(bf16[2048,768]{1,0:T(8,128)(2,1)} %refs_3_.1) | copy-start | bytes 9437188
  75.2 13.8 %collective-permute-start.12 = (bf16[2,2,2,64,512]{4,3,2,0,1:T(8,128)(2,1)S(1)}, bf16[2,2,2,64,512]{4,3,2,0,1:T(8,128)(2,1)S(1)}, u32[]{:S(2)}, u32[]{:S(2)}) collective-permute-start(bf16[2,2,2,64,512]{4,3,2,0,1:T(8,128)(2,1)S(1)} %get-tuple-element.80), channel_id=1, source_target_pairs={{0,8},{1,9},{2,10},{3,11},{4,12},{5,13},{6,14},{7,15},{8,0},{9,1},... | collective-permute-start | bytes 1572872 | tf_op jit(solution)/shard_map/ppermute | solution.py:357
  83.2 8.1 %collective-permute-start.13 = (bf16[2,2,32,896]{3,2,1,0:T(8,128)(2,1)S(1)}, bf16[2,2,32,896]{3,2,1,0:T(8,128)(2,1)S(1)}, u32[]{:S(2)}, u32[]{:S(2)}) collective-permute-start(bf16[2,2,32,896]{3,2,1,0:T(8,128)(2,1)S(1)} %get-tuple-element.88), channel_id=1, source_target_pairs={{0,4},{1,5},{2,6},{3,7},{4,0},{5,1},{6,2},{7,3},{8,12},{9,13},{10,... | collective-permute-start | bytes 688136 | tf_op jit(solution)/shard_map/ppermute | solution.py:357
  84.5 6.8 %collective-permute-start.14 = (bf16[2,2,32,896]{3,2,1,0:T(8,128)(2,1)S(1)}, bf16[2,2,32,896]{3,2,1,0:T(8,128)(2,1)S(1)}, u32[]{:S(2)}, u32[]{:S(2)}) collective-permute-start(bf16[2,2,32,896]{3,2,1,0:T(8,128)(2,1)S(1)} %get-tuple-element.90), channel_id=1, source_target_pairs={{0,1},{1,0},{2,3},{3,2},{4,5},{5,4},{6,7},{7,6},{8,9},{9,8},{10,11... | collective-permute-start | bytes 688136 | tf_op jit(solution)/shard_map/ppermute | solution.py:357
  89.1 5.0 %collective-permute-start.16 = (bf16[2,2,32,512]{3,2,1,0:T(8,128)(2,1)S(1)}, bf16[2,2,32,512]{3,2,1,0:T(8,128)(2,1)S(1)}, u32[]{:S(2)}, u32[]{:S(2)}) collective-permute-start(bf16[2,2,32,512]{3,2,1,0:T(8,128)(2,1)S(1)} %get-tuple-element.82), channel_id=1, source_target_pairs={{0,4},{1,5},{2,6},{3,7},{4,0},{5,1},{6,2},{7,3},{8,12},{9,13},{10,... | collective-permute-start | bytes 393224 | tf_op jit(solution)/shard_map/ppermute | solution.py:357
  89.5 5.9 %collective-permute-start.15 = (bf16[2,2,32,512]{3,2,1,0:T(8,128)(2,1)S(1)}, bf16[2,2,32,512]{3,2,1,0:T(8,128)(2,1)S(1)}, u32[]{:S(2)}, u32[]{:S(2)}) collective-permute-start(bf16[2,2,32,512]{3,2,1,0:T(8,128)(2,1)S(1)} %get-tuple-element.84), channel_id=1, source_target_pairs={{0,1},{1,0},{2,3},{3,2},{4,5},{5,4},{6,7},{7,6},{8,9},{9,8},{10,11... | collective-permute-start | bytes 393224 | tf_op jit(solution)/shard_map/ppermute | solution.py:357
  91.5 6.1 %collective-permute-start.17 = (bf16[2,64,896]{2,1,0:T(8,128)(2,1)S(1)}, bf16[2,64,896]{2,1,0:T(8,128)(2,1)S(1)}, u32[]{:S(2)}, u32[]{:S(2)}) collective-permute-start(bf16[2,64,896]{2,1,0:T(8,128)(2,1)S(1)} %get-tuple-element.86), channel_id=1, source_target_pairs={{0,8},{1,9},{2,10},{3,11},{4,12},{5,13},{6,14},{7,15},{8,0},{9,1},... | collective-permute-start | bytes 688136 | tf_op jit(solution)/shard_map/ppermute | solution.py:357
  94.2 4.3 %collective-permute-start.20 = (bf16[2,32,512]{2,1,0:T(8,128)(2,1)S(1)}, bf16[2,32,512]{2,1,0:T(8,128)(2,1)S(1)}, u32[]{:S(2)}, u32[]{:S(2)}) collective-permute-start(bf16[2,32,512]{2,1,0:T(8,128)(2,1)S(1)} %get-tuple-element.96), channel_id=1, source_target_pairs={{0,1},{1,0},{2,3},{3,2},{4,5},{5,4},{6,7},{7,6},{8,9},{9,8},{10,11... | collective-permute-start | bytes 196616 | tf_op jit(solution)/shard_map/ppermute | solution.py:357
  95.5 4.3 %collective-permute-start.19 = (bf16[2,32,512]{2,1,0:T(8,128)(2,1)S(1)}, bf16[2,32,512]{2,1,0:T(8,128)(2,1)S(1)}, u32[]{:S(2)}, u32[]{:S(2)}) collective-permute-start(bf16[2,32,512]{2,1,0:T(8,128)(2,1)S(1)} %get-tuple-element.94), channel_id=1, source_target_pairs={{0,4},{1,5},{2,6},{3,7},{4,0},{5,1},{6,2},{7,3},{8,12},{9,13},{10,... | collective-permute-start | bytes 196616 | tf_op jit(solution)/shard_map/ppermute | solution.py:357
  99.8 6.1 %collective-permute-start.21 = (bf16[64,512]{1,0:T(8,128)(2,1)S(1)}, bf16[64,512]{1,0:T(8,128)(2,1)S(1)}, u32[]{:S(2)}, u32[]{:S(2)}) collective-permute-start(bf16[64,512]{1,0:T(8,128)(2,1)S(1)} %fusion.16), channel_id=1, source_target_pairs={{0,16},{1,17},{2,18},{3,19},{4,20},{5,21},{6,22},{7,23},{8,24},{9,... | collective-permute-start | bytes 196616 | tf_op jit(solution)/shard_map/ppermute | solution.py:357
  102.1 6.9 %collective-permute-start.18 = (bf16[64,896]{1,0:T(8,128)(2,1)S(1)}, bf16[64,896]{1,0:T(8,128)(2,1)S(1)}, u32[]{:S(2)}, u32[]{:S(2)}) collective-permute-start(bf16[64,896]{1,0:T(8,128)(2,1)S(1)} %get-tuple-element.92), channel_id=1, source_target_pairs={{0,16},{1,17},{2,18},{3,19},{4,20},{5,21},{6,22},{7,23},{8,24},{9,... | collective-permute-start | bytes 344072 | tf_op jit(solution)/shard_map/ppermute | solution.py:357

commit v15 on v13

--- a/solution.py
+++ b/solution.py
@@ -513,9 +513,10 @@
         r_out.start()
         done = r_out.sent
     grad_scale = 1.0 / math.sqrt(nodes * count)
-    g_out = r_out.result(slice(None)) * grad_scale
     g_in = r_in.result(slice(0, f_in)) * grad_scale
     g_bias = r_in.result(f_in) * grad_scale
+    r_out.kept = [after(r_out.kept[0], g_in, g_bias)]
+    g_out = r_out.result(slice(None)) * grad_scale
     return (grad_img, grad_cap, g_in, g_out, g_bias)
 
 

time: 110 us -> 109 us (level)
  waiting for transfers between devices: 13.1 us -> 11.3 us
    ppermute x16, waiting for transfers between devices: 13.1 us -> 11.3 us  [flipped(): return lax.ppermute(array, AXES, [(i, i ^ mask) for i in range(count)])]
  transfers between devices with their start and end apart: 22 -> 22, of which waited for: 9 -> 6; matrix products, arithmetic and copies ran while one was open for 12% -> 13% of each run, Pallas kernels for 17% -> 17%
where the time goes in v15:
time: 109 us; the launch traced here: 108 us
  starting transfers between devices  44.2 us (41%)
  Pallas kernels  36.5 us (33%)
  waiting for transfers between devices  11.3 us (10%)
  matrix products  7.41 us (7%)
  other arithmetic  6.63 us (6%)
  local copies, waits for them, and re-layouts  1.22 us (1%)
    ppermute x16, starting transfers between devices, flipped(): return lax.ppermute(array, AXES, [(i, i ^ mask) for i in range(count)])  29.8 us
    pallas_call x5, Pallas kernels, over_hidden(): pl.pallas_call(kernel, out_shape=out_shape, grid_spec=pltpu.PrefetchScala...  17.9 us
    ppermute x16, waiting for transfers between devices, flipped(): return lax.ppermute(array, AXES, [(i, i ^ mask) for i in range(count)])  11.3 us
    pallas_call x1, Pallas kernels, propagate(): pl.pallas_call(lambda *r: hops_kernel(*r, tiles=tiles, slots=slots, width...  10.4 us
    ppermute x4, starting transfers between devices, moved(): lax.ppermute(array, AXES, [(i, i + by) for i in range(count) if 0 <= i +...  9.52 us
    dot_general x1, matrix products, per_device(): lax.dot_general(w_in, feats, across, preferred_element_type=F32)  7.41 us
    pallas_call x1, Pallas kernels, make_tiles(): pl.pallas_call(lambda *r: tiles_kernel(*r, tiles=tiles, slots=slots), out...  6.06 us
    ppermute x1, starting transfers between devices, per_device(): far = lax.ppermute(mate, AXES, nearest_pair(count, 2))  4.3 us
  transfers between devices with their start and end apart: 22, of which 6 were waited for; matrix products, arithmetic and copies ran while one was open for 13% of the time, Pallas kernels for 17%

profile of v15, /device:TPU:0, one launch (start us, length us, event | category | flops | bytes accessed | tf_op | source)
XLA Modules:
  0.0 108.4 jit_solution(18269643416592479381)
XLA Ops:
  0.6 2.1 %stack.1 = (bf16[768,512]{1,0:T(8,128)(2,1)}, s32[3,12]{1,0:T(4,128)}) custom-call(s32[3]{0:T(128)} %count_ref.1, bf16[384,512]{1,0:T(8,128)(2,1)} %top_ref.1, bf16[384,512]{1,0:T(8,128)(2,1)} %bottom_ref.1, s32[3,4]{1,0:T(4,128)} %seed_ref.1, s32[3,4]{1,0:T(4,128)} %cols_ref.1), custom_call_target="tpu_custom_call" | custom-call | flops 1 | bytes 1 | tf_op jit(solution)/shard_map/stack/pallas_call | solution.py:338
  3.4 5.7 %collective-permute-start = (s32[3,12]{1,0:T(4,128)}, s32[3,12]{1,0:T(4,128)S(1)}, u32[]{:S(2)}, u32[]{:S(2)}) collective-permute-start(s32[3,12]{1,0:T(4,128)} %get-tuple-element.39), channel_id=1, source_target_pairs={{0,1},{1,0},{2,3},{3,2},{4,5},{5,4},{6,7},{7,6},{8,9},{9,8},{10,11... | collective-permute-start | bytes 440 | tf_op jit(solution)/shard_map/ppermute | solution.py:357
  9.9 1.0 collective-permute-done
  10.9 2.0 %collective-permute-start.6 = (bf16[768,512]{1,0:T(8,128)(2,1)}, bf16[768,512]{1,0:T(8,128)(2,1)}, u32[]{:S(2)}, u32[]{:S(2)}) collective-permute-start(bf16[768,512]{1,0:T(8,128)(2,1)} %get-tuple-element.41.r_2_), channel_id=1, source_target_pairs={{0,1},{1,0},{2,3},{3,2},{4,5},{5,4},{6,7},{7,6},{8,9},{9,8},{10,11... | collective-permute-start | bytes 2359304 | tf_op jit(solution)/shard_map/ppermute | solution.py:357
  12.9 1.3 %collective-permute-start.5 = (bf16[768,512]{1,0:T(8,128)(2,1)}, bf16[768,512]{1,0:T(8,128)(2,1)}, u32[]{:S(2)}, u32[]{:S(2)}) collective-permute-start(bf16[768,512]{1,0:T(8,128)(2,1)} %get-tuple-element.41.r_2_), channel_id=1, source_target_pairs={{2,0},{3,1},{4,2},{5,3},{6,4},{7,5},{8,6},{9,7},{10,8},{11,9},{12,... | collective-permute-start | bytes 2359304 | tf_op jit(solution)/shard_map/ppermute | solution.py:353
  14.2 3.9 %collective-permute-start.4 = (bf16[768,512]{1,0:T(8,128)(2,1)}, bf16[768,512]{1,0:T(8,128)(2,1)}, u32[]{:S(2)}, u32[]{:S(2)}) collective-permute-start(bf16[768,512]{1,0:T(8,128)(2,1)} %get-tuple-element.41.r_2_), channel_id=1, source_target_pairs={{0,2},{1,3},{2,4},{3,5},{4,6},{5,7},{6,8},{7,9},{8,10},{9,11},{10,... | collective-permute-start | bytes 2359304 | tf_op jit(solution)/shard_map/ppermute | solution.py:353
  18.1 1.3 %pad_maximum_fusion.refs_9_ = bf16[768,768]{1,0:T(8,128)(2,1)S(1)} fusion(bf16[384,768]{1,0:T(8,128)(2,1)} %param.13, bf16[384,768]{1,0:T(8,128)(2,1)} %param.12), kind=kLoop, calls=%fused_computation.15 | loop fusion | flops 2359296 | bytes 2359296 | tf_op jit(solution)/shard_map/concatenate | solution.py:425
  20.2 1.3 %collective-permute-start.3 = (s32[6,12]{1,0:T(8,128)S(1)}, s32[6,12]{1,0:T(8,128)S(1)}, u32[]{:S(2)}, u32[]{:S(2)}) collective-permute-start(s32[6,12]{1,0:T(8,128)S(1)} %add_select_fusion.1), channel_id=1, source_target_pairs={{2,0},{3,1},{4,2},{5,3},{6,4},{7,5},{8,6},{9,7},{10,8},{11,9},{12,... | collective-permute-start | bytes 872 | tf_op jit(solution)/shard_map/ppermute | solution.py:353
  21.5 3.0 %collective-permute-start.2 = (s32[6,12]{1,0:T(8,128)S(1)}, s32[6,12]{1,0:T(8,128)S(1)}, u32[]{:S(2)}, u32[]{:S(2)}) collective-permute-start(s32[6,12]{1,0:T(8,128)S(1)} %add_select_fusion.1), channel_id=1, source_target_pairs={{0,2},{1,3},{2,4},{3,5},{4,6},{5,7},{6,8},{7,9},{8,10},{9,11},{10,... | collective-permute-start | bytes 872 | tf_op jit(solution)/shard_map/ppermute | solution.py:353
  24.6 7.4 %fusion.3 = (f32[2048,768]{1,0:T(8,128)}, bf16[2048,768]{1,0:T(8,128)(2,1)S(1)}) fusion(f32[2048]{0:T(1024)S(1)} %copy-done.5, bf16[768,768]{1,0:T(8,128)(2,1)S(1)} %pad_maximum_fusion.refs_9_, bf16[2048,768]{1,0:T(8,128)(2,1)} %refs_3_.1), kind=kOutput, calls=%fused_computation.4 | convolution fusion | flops 2433220608 | bytes 13770752 | tf_op jit(solution)/shard_map/dot_general | solution.py:460
  32.0 4.3 %collective-permute-start.7 = (bf16[768,512]{1,0:T(8,128)(2,1)}, bf16[768,512]{1,0:T(8,128)(2,1)}, u32[]{:S(2)}, u32[]{:S(2)}) collective-permute-start(bf16[768,512]{1,0:T(8,128)(2,1)} %collective-permute-done.6.r_5_), channel_id=1, source_target_pairs={{0,2},{2,4},{4,6},{6,8},{8,10},{10,12},{12,14},{14,16},{16,18},{18... | collective-permute-start | bytes 2359304 | tf_op jit(solution)/shard_map/ppermute | solution.py:423
  37.0 6.1 %tiles.1 = (bf16[15,128,512]{2,1,0:T(8,128)(2,1)}, bf16[15,512,128]{2,1,0:T(8,128)(2,1)}, f32[15,128,128]{2,1,0:T(8,128)}, f32[15,128,128]{2,1,0:T(8,128)}) custom-call(s32[84]{0:T(128)S(1)} %reshape.38.r_0_, s32[84]{0:T(128)S(1)} %reshape.39.r_1_, s32[21]{0:T(128)S(1)} %slice_reduce_fusion.r_2_), custom_call_target="tpu_custom_call" | custom-call | flops 1 | bytes 1 | tf_op jit(solution)/shard_map/tiles/pallas_call | solution.py:103
  43.2 10.4 %hops.1.refs_8_.refs_4_ = bf16[768,512]{1,0:T(8,128)(2,1)S(1)} custom-call(s32[60]{0:T(128)S(1)} %reshape.37.r_0_, s32[2]{0:T(128)S(1)} %fusion.17.r_1_, bf16[768,512]{1,0:T(8,128)(2,1)} %get-tuple-element.41.r_2_, bf16[768,512]{1,0:T(8,128)(2,1)} %collective-permute-done.4.r_3_, bf16[768,512]{1,0:T(8,128)(2,1)} %collective-permute-done.5.r_4_, ...), custom_call_target="tpu_custom_call" | custom-call | flops 1 | bytes 1 | tf_op jit(solution)/shard_map/hops/pallas_call | solution.py:207
  53.7 3.8 %part_in.2 = (bf16[1024,896]{1,0:T(8,128)(2,1)S(1)}, bf16[1024,768]{1,0:T(8,128)(2,1)S(1)}) custom-call(s32[16]{0:T(128)S(1)} %get-tuple-element.102.order_ref, f32[2048,768]{1,0:T(8,128)S(1)} %copy-done, f32[2048,768]{1,0:T(8,128)S(1)} %copy-done, f32[2048,768]{1,0:T(8,128)S(1)} %copy-done, f32[2048,768]{1,0:T(8,128)S(1)} %copy-done, ...), custom_call_target="tpu_custom_call" | custom-call | flops 1 | bytes 1 | tf_op jit(solution)/shard_map/part_in/pallas_call | solution.py:291
  57.7 1.5 %collective-permute-start.8 = (bf16[2,2,2,2,64,896]{5,4,3,2,0,1:T(8,128)(2,1)S(1)}, bf16[2,2,2,2,64,896]{5,4,3,2,0,1:T(8,128)(2,1)S(1)}, u32[]{:S(2)}, u32[]{:S(2)}) collective-permute-start(bf16[2,2,2,2,64,896]{5,4,3,2,0,1:T(8,128)(2,1)S(1)} %copy.25), channel_id=1, source_target_pairs={{0,2},{1,3},{2,0},{3,1},{4,6},{5,7},{6,4},{7,5},{8,10},{9,11},{10,... | collective-permute-start | bytes 5505032 | tf_op jit(solution)/shard_map/ppermute | solution.py:357
  59.2 3.8 %part_in.3 = (bf16[1024,896]{1,0:T(8,128)(2,1)S(1)}, bf16[1024,768]{1,0:T(8,128)(2,1)S(1)}) custom-call(s32[16]{0:T(128)S(1)} %get-tuple-element.103.order_ref, f32[2048,768]{1,0:T(8,128)S(1)} %copy-done, f32[2048,768]{1,0:T(8,128)S(1)} %copy-done, f32[2048,768]{1,0:T(8,128)S(1)} %copy-done, f32[2048,768]{1,0:T(8,128)S(1)} %copy-done, ...), custom_call_target="tpu_custom_call" | custom-call | flops 1 | bytes 1 | tf_op jit(solution)/shard_map/part_in/pallas_call | solution.py:291
  63.8 2.0 %part_out.2 = bf16[1024,512]{1,0:T(8,128)(2,1)S(1)} custom-call(s32[16]{0:T(128)S(1)} %get-tuple-element.102.order_ref, bf16[2048,768]{1,0:T(8,128)(2,1)S(1)} %get-tuple-element.54.refs_0_.refs_1_.refs_2_.refs_3_, bf16[2048,768]{1,0:T(8,128)(2,1)S(1)} %get-tuple-element.54.refs_0_.refs_1_.refs_2_.refs_3_, ...), custom_call_target="tpu_custom_call" | custom-call | flops 1 | bytes 1 | tf_op jit(solution)/shard_map/part_out/pallas_call | solution.py:291
  66.0 3.0 %collective-permute-start.10 = (bf16[2,2,2,32,896]{4,3,2,1,0:T(8,128)(2,1)S(1)}, bf16[2,2,2,32,896]{4,3,2,1,0:T(8,128)(2,1)S(1)}, u32[]{:S(2)}, u32[]{:S(2)}) collective-permute-start(bf16[2,2,2,32,896]{4,3,2,1,0:T(8,128)(2,1)S(1)} %get-tuple-element.78), channel_id=1, source_target_pairs={{0,1},{1,0},{2,3},{3,2},{4,5},{5,4},{6,7},{7,6},{8,9},{9,8},{10,11... | collective-permute-start | bytes 1376264 | tf_op jit(solution)/shard_map/ppermute | solution.py:357
  69.1 4.2 %collective-permute-start.11 = (bf16[2,2,2,32,896]{4,3,2,1,0:T(8,128)(2,1)S(1)}, bf16[2,2,2,32,896]{4,3,2,1,0:T(8,128)(2,1)S(1)}, u32[]{:S(2)}, u32[]{:S(2)}) collective-permute-start(bf16[2,2,2,32,896]{4,3,2,1,0:T(8,128)(2,1)S(1)} %get-tuple-element.80), channel_id=1, source_target_pairs={{0,4},{1,5},{2,6},{3,7},{4,0},{5,1},{6,2},{7,3},{8,12},{9,13},{10,... | collective-permute-start | bytes 1376264 | tf_op jit(solution)/shard_map/ppermute | solution.py:357
  73.3 2.0 %part_out.3 = bf16[1024,512]{1,0:T(8,128)(2,1)S(1)} custom-call(s32[16]{0:T(128)S(1)} %get-tuple-element.103.order_ref, bf16[2048,768]{1,0:T(8,128)(2,1)S(1)} %get-tuple-element.54.refs_0_.refs_1_.refs_2_.refs_3_, bf16[2048,768]{1,0:T(8,128)(2,1)S(1)} %get-tuple-element.54.refs_0_.refs_1_.refs_2_.refs_3_, ...), custom_call_target="tpu_custom_call" | custom-call | flops 1 | bytes 1 | tf_op jit(solution)/shard_map/part_out/pallas_call | solution.py:291
  75.8 1.6 %collective-permute-start.12 = (bf16[2,2,2,64,512]{4,3,2,0,1:T(8,128)(2,1)S(1)}, bf16[2,2,2,64,512]{4,3,2,0,1:T(8,128)(2,1)S(1)}, u32[]{:S(2)}, u32[]{:S(2)}) collective-permute-start(bf16[2,2,2,64,512]{4,3,2,0,1:T(8,128)(2,1)S(1)} %get-tuple-element.82), channel_id=1, source_target_pairs={{0,8},{1,9},{2,10},{3,11},{4,12},{5,13},{6,14},{7,15},{8,0},{9,1},... | collective-permute-start | bytes 1572872 | tf_op jit(solution)/shard_map/ppermute | solution.py:357
  77.4 6.2 %feat_grad.1 = (bf16[384,768]{1,0:T(8,128)(2,1)}, bf16[384,768]{1,0:T(8,128)(2,1)}) custom-call(s32[32]{0:T(128)S(1)} %fusion.30.order_ref, bf16[2048,768]{1,0:T(8,128)(2,1)S(1)} %copy-done.2, bf16[2048,768]{1,0:T(8,128)(2,1)S(1)} %copy-done.2, bf16[2048,768]{1,0:T(8,128)(2,1)S(1)} %copy-done.2, bf16[2048,768]{1,0:T(8,128)(2,1)S(1)} %copy-done.2, ...), custom_call_target="tpu_custom_call" | custom-call | flops 1 | bytes 1 | tf_op jit(solution)/shard_map/feat_grad/pallas_call | solution.py:291
  83.8 0.8 collective-permute-start.13
  84.8 1.8 %collective-permute-start.14 = (bf16[2,2,32,896]{3,2,1,0:T(8,128)(2,1)S(1)}, bf16[2,2,32,896]{3,2,1,0:T(8,128)(2,1)S(1)}, u32[]{:S(2)}, u32[]{:S(2)}) collective-permute-start(bf16[2,2,32,896]{3,2,1,0:T(8,128)(2,1)S(1)} %get-tuple-element.92), channel_id=1, source_target_pairs={{0,1},{1,0},{2,3},{3,2},{4,5},{5,4},{6,7},{7,6},{8,9},{9,8},{10,11... | collective-permute-start | bytes 688136 | tf_op jit(solution)/shard_map/ppermute | solution.py:357
  86.6 2.9 %collective-permute-done.12 = bf16[2,2,2,64,512]{4,3,2,0,1:T(8,128)(2,1)S(1)} collective-permute-done((bf16[2,2,2,64,512]{4,3,2,0,1:T(8,128)(2,1)S(1)}, bf16[2,2,2,64,512]{4,3,2,0,1:T(8,128)(2,1)S(1)}, u32[]{:S(2)}, u32[]{:S(2)}) %collective-permute-start.12) | collective-permute-done | bytes 524320 | tf_op jit(solution)/shard_map/ppermute | solution.py:357
  90.6 1.6 %collective-permute-done.14 = bf16[2,2,32,896]{3,2,1,0:T(8,128)(2,1)S(1)} collective-permute-done((bf16[2,2,32,896]{3,2,1,0:T(8,128)(2,1)S(1)}, bf16[2,2,32,896]{3,2,1,0:T(8,128)(2,1)S(1)}, u32[]{:S(2)}, u32[]{:S(2)}) %collective-permute-start.14) | collective-permute-done | bytes 229408 | tf_op jit(solution)/shard_map/ppermute | solution.py:357
  92.4 1.6 %collective-permute-start.17 = (bf16[2,64,896]{2,1,0:T(8,128)(2,1)S(1)}, bf16[2,64,896]{2,1,0:T(8,128)(2,1)S(1)}, u32[]{:S(2)}, u32[]{:S(2)}) collective-permute-start(bf16[2,64,896]{2,1,0:T(8,128)(2,1)S(1)} %get-tuple-element.88), channel_id=1, source_target_pairs={{0,8},{1,9},{2,10},{3,11},{4,12},{5,13},{6,14},{7,15},{8,0},{9,1},... | collective-permute-start | bytes 688136 | tf_op jit(solution)/shard_map/ppermute | solution.py:357
  94.8 1.8 %collective-permute-start.20 = (bf16[2,32,512]{2,1,0:T(8,128)(2,1)S(1)}, bf16[2,32,512]{2,1,0:T(8,128)(2,1)S(1)}, u32[]{:S(2)}, u32[]{:S(2)}) collective-permute-start(bf16[2,32,512]{2,1,0:T(8,128)(2,1)S(1)} %get-tuple-element.100), channel_id=1, source_target_pairs={{0,1},{1,0},{2,3},{3,2},{4,5},{5,4},{6,7},{7,6},{8,9},{9,8},{10,11... | collective-permute-start | bytes 196616 | tf_op jit(solution)/shard_map/ppermute | solution.py:357
  97.5 1.0 collective-permute-done.17
  98.6 2.7 %collective-permute-start.18 = (bf16[64,896]{1,0:T(8,128)(2,1)S(1)}, bf16[64,896]{1,0:T(8,128)(2,1)S(1)}, u32[]{:S(2)}, u32[]{:S(2)}) collective-permute-start(bf16[64,896]{1,0:T(8,128)(2,1)S(1)} %get-tuple-element.94), channel_id=1, source_target_pairs={{0,16},{1,17},{2,18},{3,19},{4,20},{5,21},{6,22},{7,23},{8,24},{9,... | collective-permute-start | bytes 344072 | tf_op jit(solution)/shard_map/ppermute | solution.py:357
  101.4 1.0 collective-permute-start.21
  102.4 4.0 %collective-permute-done.18 = bf16[64,896]{1,0:T(8,128)(2,1)S(1)} collective-permute-done((bf16[64,896]{1,0:T(8,128)(2,1)S(1)}, bf16[64,896]{1,0:T(8,128)(2,1)S(1)}, u32[]{:S(2)}, u32[]{:S(2)}) %collective-permute-start.18) | collective-permute-done | bytes 114720 | tf_op jit(solution)/shard_map/ppermute | solution.py:357
  (75 shorter events, 9.6 us)
Async XLA Ops:
  0.6 24.0 %copy-start.5 = (f32[2048]{0:T(1024)S(1)}, f32[2048]{0:T(1024)}, u32[]{:S(2)}) copy-start(f32[2048]{0:T(1024)} %param.17) | copy-start | bytes 24580
  2.7 17.5 %collective-permute-start.1 = (s32[3,12]{1,0:T(4,128)}, s32[3,12]{1,0:T(4,128)S(1)}, u32[]{:S(2)}, u32[]{:S(2)}) collective-permute-start(s32[3,12]{1,0:T(4,128)} %get-tuple-element.39), channel_id=1, source_target_pairs={{1,4},{3,6},{5,8},{7,10},{9,12},{11,14},{13,16},{15,18},{17,20},{1... | collective-permute-start | bytes 440 | tf_op jit(solution)/shard_map/ppermute | solution.py:416
  3.4 7.5 %collective-permute-start = (s32[3,12]{1,0:T(4,128)}, s32[3,12]{1,0:T(4,128)S(1)}, u32[]{:S(2)}, u32[]{:S(2)}) collective-permute-start(s32[3,12]{1,0:T(4,128)} %get-tuple-element.39), channel_id=1, source_target_pairs={{0,1},{1,0},{2,3},{3,2},{4,5},{5,4},{6,7},{7,6},{8,9},{9,8},{10,11... | collective-permute-start | bytes 440 | tf_op jit(solution)/shard_map/ppermute | solution.py:357
  10.9 21.1 %collective-permute-start.6 = (bf16[768,512]{1,0:T(8,128)(2,1)}, bf16[768,512]{1,0:T(8,128)(2,1)}, u32[]{:S(2)}, u32[]{:S(2)}) collective-permute-start(bf16[768,512]{1,0:T(8,128)(2,1)} %get-tuple-element.41.r_2_), channel_id=1, source_target_pairs={{0,1},{1,0},{2,3},{3,2},{4,5},{5,4},{6,7},{7,6},{8,9},{9,8},{10,11... | collective-permute-start | bytes 2359304 | tf_op jit(solution)/shard_map/ppermute | solution.py:357
  12.9 30.2 %collective-permute-start.5 = (bf16[768,512]{1,0:T(8,128)(2,1)}, bf16[768,512]{1,0:T(8,128)(2,1)}, u32[]{:S(2)}, u32[]{:S(2)}) collective-permute-start(bf16[768,512]{1,0:T(8,128)(2,1)} %get-tuple-element.41.r_2_), channel_id=1, source_target_pairs={{2,0},{3,1},{4,2},{5,3},{6,4},{7,5},{8,6},{9,7},{10,8},{11,9},{12,... | collective-permute-start | bytes 2359304 | tf_op jit(solution)/shard_map/ppermute | solution.py:353
  14.2 28.9 %collective-permute-start.4 = (bf16[768,512]{1,0:T(8,128)(2,1)}, bf16[768,512]{1,0:T(8,128)(2,1)}, u32[]{:S(2)}, u32[]{:S(2)}) collective-permute-start(bf16[768,512]{1,0:T(8,128)(2,1)} %get-tuple-element.41.r_2_), channel_id=1, source_target_pairs={{0,2},{1,3},{2,4},{3,5},{4,6},{5,7},{6,8},{7,9},{8,10},{9,11},{10,... | collective-permute-start | bytes 2359304 | tf_op jit(solution)/shard_map/ppermute | solution.py:353
  19.4 12.6 %copy-start.3 = (bf16[768,768]{1,0:T(8,128)(2,1)}, bf16[768,768]{1,0:T(8,128)(2,1)S(1)}, u32[]{:S(2)}) copy-start(bf16[768,768]{1,0:T(8,128)(2,1)S(1)} %pad_maximum_fusion.refs_9_) | copy-start | bytes 3538948
  20.2 16.1 %collective-permute-start.3 = (s32[6,12]{1,0:T(8,128)S(1)}, s32[6,12]{1,0:T(8,128)S(1)}, u32[]{:S(2)}, u32[]{:S(2)}) collective-permute-start(s32[6,12]{1,0:T(8,128)S(1)} %add_select_fusion.1), channel_id=1, source_target_pairs={{2,0},{3,1},{4,2},{5,3},{6,4},{7,5},{8,6},{9,7},{10,8},{11,9},{12,... | collective-permute-start | bytes 872 | tf_op jit(solution)/shard_map/ppermute | solution.py:353
  21.5 14.8 %collective-permute-start.2 = (s32[6,12]{1,0:T(8,128)S(1)}, s32[6,12]{1,0:T(8,128)S(1)}, u32[]{:S(2)}, u32[]{:S(2)}) collective-permute-start(s32[6,12]{1,0:T(8,128)S(1)} %add_select_fusion.1), channel_id=1, source_target_pairs={{0,2},{1,3},{2,4},{3,5},{4,6},{5,7},{6,8},{7,9},{8,10},{9,11},{10,... | collective-permute-start | bytes 872 | tf_op jit(solution)/shard_map/ppermute | solution.py:353
  32.0 11.2 %collective-permute-start.7 = (bf16[768,512]{1,0:T(8,128)(2,1)}, bf16[768,512]{1,0:T(8,128)(2,1)}, u32[]{:S(2)}, u32[]{:S(2)}) collective-permute-start(bf16[768,512]{1,0:T(8,128)(2,1)} %collective-permute-done.6.r_5_), channel_id=1, source_target_pairs={{0,2},{2,4},{4,6},{6,8},{8,10},{10,12},{12,14},{14,16},{16,18},{18... | collective-permute-start | bytes 2359304 | tf_op jit(solution)/shard_map/ppermute | solution.py:423
  43.2 10.5 %copy-start = (f32[2048,768]{1,0:T(8,128)S(1)}, f32[2048,768]{1,0:T(8,128)}, u32[]{:S(2)}) copy-start(f32[2048,768]{1,0:T(8,128)} %get-tuple-element.44.refs_0_.refs_1_.refs_2_.refs_3_) | copy-start | bytes 18874372
  43.2 10.5 %copy-start.1 = (bf16[2048,512]{1,0:T(8,128)(2,1)S(1)}, bf16[2048,512]{1,0:T(8,128)(2,1)}, u32[]{:S(2)}) copy-start(bf16[2048,512]{1,0:T(8,128)(2,1)} %refs_7_.3) | copy-start | bytes 6291460
  43.2 10.5 %copy-start.4 = (bf16[768,768]{1,0:T(8,128)(2,1)S(1)}, bf16[768,768]{1,0:T(8,128)(2,1)}, u32[]{:S(2)}) copy-start(bf16[768,768]{1,0:T(8,128)(2,1)} %copy-done.3) | copy-start | bytes 3538948
  57.7 5.4 %collective-permute-start.8 = (bf16[2,2,2,2,64,896]{5,4,3,2,0,1:T(8,128)(2,1)S(1)}, bf16[2,2,2,2,64,896]{5,4,3,2,0,1:T(8,128)(2,1)S(1)}, u32[]{:S(2)}, u32[]{:S(2)}) collective-permute-start(bf16[2,2,2,2,64,896]{5,4,3,2,0,1:T(8,128)(2,1)S(1)} %copy.25), channel_id=1, source_target_pairs={{0,2},{1,3},{2,0},{3,1},{4,6},{5,7},{6,4},{7,5},{8,10},{9,11},{10,... | collective-permute-start | bytes 5505032 | tf_op jit(solution)/shard_map/ppermute | solution.py:357
  66.0 9.4 %collective-permute-start.9 = (bf16[2,2,2,2,64,512]{5,4,3,0,1,2:T(8,128)(2,1)S(1)}, bf16[2,2,2,2,64,512]{5,4,3,0,1,2:T(8,128)(2,1)S(1)}, u32[]{:S(2)}, u32[]{:S(2)}) collective-permute-start(bf16[2,2,2,2,64,512]{5,4,3,0,1,2:T(8,128)(2,1)S(1)} %copy.28), channel_id=1, source_target_pairs={{0,2},{1,3},{2,0},{3,1},{4,6},{5,7},{6,4},{7,5},{8,10},{9,11},{10,... | collective-permute-start | bytes 3145736 | tf_op jit(solution)/shard_map/ppermute | solution.py:357
  66.0 17.6 %collective-permute-start.10 = (bf16[2,2,2,32,896]{4,3,2,1,0:T(8,128)(2,1)S(1)}, bf16[2,2,2,32,896]{4,3,2,1,0:T(8,128)(2,1)S(1)}, u32[]{:S(2)}, u32[]{:S(2)}) collective-permute-start(bf16[2,2,2,32,896]{4,3,2,1,0:T(8,128)(2,1)S(1)} %get-tuple-element.78), channel_id=1, source_target_pairs={{0,1},{1,0},{2,3},{3,2},{4,5},{5,4},{6,7},{7,6},{8,9},{9,8},{10,11... | collective-permute-start | bytes 1376264 | tf_op jit(solution)/shard_map/ppermute | solution.py:357
  69.1 15.6 %collective-permute-start.11 = (bf16[2,2,2,32,896]{4,3,2,1,0:T(8,128)(2,1)S(1)}, bf16[2,2,2,32,896]{4,3,2,1,0:T(8,128)(2,1)S(1)}, u32[]{:S(2)}, u32[]{:S(2)}) collective-permute-start(bf16[2,2,2,32,896]{4,3,2,1,0:T(8,128)(2,1)S(1)} %get-tuple-element.80), channel_id=1, source_target_pairs={{0,4},{1,5},{2,6},{3,7},{4,0},{5,1},{6,2},{7,3},{8,12},{9,13},{10,... | collective-permute-start | bytes 1376264 | tf_op jit(solution)/shard_map/ppermute | solution.py:357
  75.3 2.1 %copy-start.2 = (bf16[2048,768]{1,0:T(8,128)(2,1)S(1)}, bf16[2048,768]{1,0:T(8,128)(2,1)}, u32[]{:S(2)}) copy-start(bf16[2048,768]{1,0:T(8,128)(2,1)} %refs_3_.1) | copy-start | bytes 9437188
  75.8 13.8 %collective-permute-start.12 = (bf16[2,2,2,64,512]{4,3,2,0,1:T(8,128)(2,1)S(1)}, bf16[2,2,2,64,512]{4,3,2,0,1:T(8,128)(2,1)S(1)}, u32[]{:S(2)}, u32[]{:S(2)}) collective-permute-start(bf16[2,2,2,64,512]{4,3,2,0,1:T(8,128)(2,1)S(1)} %get-tuple-element.82), channel_id=1, source_target_pairs={{0,8},{1,9},{2,10},{3,11},{4,12},{5,13},{6,14},{7,15},{8,0},{9,1},... | collective-permute-start | bytes 1572872 | tf_op jit(solution)/shard_map/ppermute | solution.py:357
  83.8 8.5 %collective-permute-start.13 = (bf16[2,2,32,896]{3,2,1,0:T(8,128)(2,1)S(1)}, bf16[2,2,32,896]{3,2,1,0:T(8,128)(2,1)S(1)}, u32[]{:S(2)}, u32[]{:S(2)}) collective-permute-start(bf16[2,2,32,896]{3,2,1,0:T(8,128)(2,1)S(1)} %get-tuple-element.90), channel_id=1, source_target_pairs={{0,4},{1,5},{2,6},{3,7},{4,0},{5,1},{6,2},{7,3},{8,12},{9,13},{10,... | collective-permute-start | bytes 688136 | tf_op jit(solution)/shard_map/ppermute | solution.py:357
  84.8 7.4 %collective-permute-start.14 = (bf16[2,2,32,896]{3,2,1,0:T(8,128)(2,1)S(1)}, bf16[2,2,32,896]{3,2,1,0:T(8,128)(2,1)S(1)}, u32[]{:S(2)}, u32[]{:S(2)}) collective-permute-start(bf16[2,2,32,896]{3,2,1,0:T(8,128)(2,1)S(1)} %get-tuple-element.92), channel_id=1, source_target_pairs={{0,1},{1,0},{2,3},{3,2},{4,5},{5,4},{6,7},{7,6},{8,9},{9,8},{10,11... | collective-permute-start | bytes 688136 | tf_op jit(solution)/shard_map/ppermute | solution.py:357
  89.7 5.0 %collective-permute-start.16 = (bf16[2,2,32,512]{3,2,1,0:T(8,128)(2,1)S(1)}, bf16[2,2,32,512]{3,2,1,0:T(8,128)(2,1)S(1)}, u32[]{:S(2)}, u32[]{:S(2)}) collective-permute-start(bf16[2,2,32,512]{3,2,1,0:T(8,128)(2,1)S(1)} %get-tuple-element.84), channel_id=1, source_target_pairs={{0,4},{1,5},{2,6},{3,7},{4,0},{5,1},{6,2},{7,3},{8,12},{9,13},{10,... | collective-permute-start | bytes 393224 | tf_op jit(solution)/shard_map/ppermute | solution.py:357
  90.1 6.6 %collective-permute-start.15 = (bf16[2,2,32,512]{3,2,1,0:T(8,128)(2,1)S(1)}, bf16[2,2,32,512]{3,2,1,0:T(8,128)(2,1)S(1)}, u32[]{:S(2)}, u32[]{:S(2)}) collective-permute-start(bf16[2,2,32,512]{3,2,1,0:T(8,128)(2,1)S(1)} %get-tuple-element.86), channel_id=1, source_target_pairs={{0,1},{1,0},{2,3},{3,2},{4,5},{5,4},{6,7},{7,6},{8,9},{9,8},{10,11... | collective-permute-start | bytes 393224 | tf_op jit(solution)/shard_map/ppermute | solution.py:357
  92.4 6.1 %collective-permute-start.17 = (bf16[2,64,896]{2,1,0:T(8,128)(2,1)S(1)}, bf16[2,64,896]{2,1,0:T(8,128)(2,1)S(1)}, u32[]{:S(2)}, u32[]{:S(2)}) collective-permute-start(bf16[2,64,896]{2,1,0:T(8,128)(2,1)S(1)} %get-tuple-element.88), channel_id=1, source_target_pairs={{0,8},{1,9},{2,10},{3,11},{4,12},{5,13},{6,14},{7,15},{8,0},{9,1},... | collective-permute-start | bytes 688136 | tf_op jit(solution)/shard_map/ppermute | solution.py:357
  94.8 6.5 %collective-permute-start.20 = (bf16[2,32,512]{2,1,0:T(8,128)(2,1)S(1)}, bf16[2,32,512]{2,1,0:T(8,128)(2,1)S(1)}, u32[]{:S(2)}, u32[]{:S(2)}) collective-permute-start(bf16[2,32,512]{2,1,0:T(8,128)(2,1)S(1)} %get-tuple-element.100), channel_id=1, source_target_pairs={{0,1},{1,0},{2,3},{3,2},{4,5},{5,4},{6,7},{7,6},{8,9},{9,8},{10,11... | collective-permute-start | bytes 196616 | tf_op jit(solution)/shard_map/ppermute | solution.py:357
  96.7 4.6 %collective-permute-start.19 = (bf16[2,32,512]{2,1,0:T(8,128)(2,1)S(1)}, bf16[2,32,512]{2,1,0:T(8,128)(2,1)S(1)}, u32[]{:S(2)}, u32[]{:S(2)}) collective-permute-start(bf16[2,32,512]{2,1,0:T(8,128)(2,1)S(1)} %get-tuple-element.98), channel_id=1, source_target_pairs={{0,4},{1,5},{2,6},{3,7},{4,0},{5,1},{6,2},{7,3},{8,12},{9,13},{10,... | collective-permute-start | bytes 196616 | tf_op jit(solution)/shard_map/ppermute | solution.py:357
  98.6 7.8 %collective-permute-start.18 = (bf16[64,896]{1,0:T(8,128)(2,1)S(1)}, bf16[64,896]{1,0:T(8,128)(2,1)S(1)}, u32[]{:S(2)}, u32[]{:S(2)}) collective-permute-start(bf16[64,896]{1,0:T(8,128)(2,1)S(1)} %get-tuple-element.94), channel_id=1, source_target_pairs={{0,16},{1,17},{2,18},{3,19},{4,20},{5,21},{6,22},{7,23},{8,24},{9,... | collective-permute-start | bytes 344072 | tf_op jit(solution)/shard_map/ppermute | solution.py:357
  101.4 6.4 %collective-permute-start.21 = (bf16[64,512]{1,0:T(8,128)(2,1)S(1)}, bf16[64,512]{1,0:T(8,128)(2,1)S(1)}, u32[]{:S(2)}, u32[]{:S(2)}) collective-permute-start(bf16[64,512]{1,0:T(8,128)(2,1)S(1)} %get-tuple-element.96), channel_id=1, source_target_pairs={{0,16},{1,17},{2,18},{3,19},{4,20},{5,21},{6,22},{7,23},{8,24},{9,... | collective-permute-start | bytes 196616 | tf_op jit(solution)/shard_map/ppermute | solution.py:357
